TPU v7x, 32 devices: a whole 2x2x4 slice. The times are simulated.
32 devices in a mesh: fsdp: 4 (over z), ctx: 2 (over y), tp: 4 (over x, core).
Axes of the slice: x: 2, y: 2, z: 4, core: 2. Of those that a mesh axis runs over, the one named last changes fastest.
Arguments:
- hidden_in: bfloat16 [16, 1024, 1536], P('fsdp', 'ctx'), may hold values from -6 to 6
- cotangent: bfloat16 [16, 1024, 1536], P('fsdp', 'ctx'), may hold values from -6 to 6
- seq_lengths: int32 [16], replicated, may hold values from 128 to 1024, as said below
- positions: int32 [16, 1024], P(None, 'ctx'), may hold values from 0 to 1023, as said below
- permutation: int32 [16], replicated, may hold values from 0 to 15, as said below
- query_weight: bfloat16 [1536, 1536], P(('fsdp', 'ctx'), 'tp'), may hold values from -0.15625 to 0.15625
- keyval_weight: bfloat16 [1536, 512], P(('fsdp', 'ctx')), may hold values from -0.15625 to 0.15625
- output_weight: bfloat16 [1536, 1536], P('tp', ('fsdp', 'ctx')), may hold values from -2 to 2
- norm_gains: bfloat16 [2, 1536], P(None, ('fsdp', 'ctx')), may hold values from 0.25 to 1.75
- bias_query: bfloat16 [12, 128], P('tp'), may hold values from -3 to 3
- bias_keyval: bfloat16 [4, 128], replicated, may hold values from -3 to 3
- gate_weight: bfloat16 [1536, 8960], P(('fsdp', 'ctx'), 'tp'), may hold values from -0.15625 to 0.15625
- up_weight: bfloat16 [1536, 8960], P(('fsdp', 'ctx'), 'tp'), may hold values from -0.15625 to 0.15625
- down_weight: bfloat16 [8960, 1536], P('tp', ('fsdp', 'ctx')), may hold values from -0.09375 to 0.09375
Outputs:
- block_out: bfloat16 [16, 1024, 1536], P('fsdp', 'ctx')
- input_grad: bfloat16 [16, 1024, 1536], P('fsdp', 'ctx')
- query_weight_grad: float32 [1536, 1536], P(('fsdp', 'ctx'), 'tp')
- keyval_weight_grad: float32 [1536, 512], P(('fsdp', 'ctx'), 'tp')
- output_weight_grad: float32 [1536, 1536], P('tp', ('fsdp', 'ctx'))
- norm_gain_grad: float32 [2, 1536], P(None, ('fsdp', 'ctx'))
- query_bias_grad: float32 [12, 128], P('tp', ('fsdp', 'ctx'))
- keyval_bias_grad: float32 [4, 128], P('tp', ('fsdp', 'ctx'))
- gate_weight_grad: float32 [1536, 8960], P(('fsdp', 'ctx'), 'tp')
- up_weight_grad: float32 [1536, 8960], P(('fsdp', 'ctx'), 'tp')
- down_weight_grad: float32 [8960, 1536], P('tp', ('fsdp', 'ctx'))
Inputs may be any that keep to these rules, and one draw needn't show every extreme that they name: `seq_lengths`: tokens at or after the length of a home sequence are padding, never visible as keys; one sequence has all 1024 tokens and one has 128. Along a home sequence the positions rise by one from token to token and fall back to 0 where a document starts; home sequence 0 is one document. A permutation of the 16 home sequences; group f of fsdp holds the working slots f * 4 to (f + 1) * 4 - 1 and receives exactly 1 sequence from the home range of each group.
All inputs are finite; a program needn't handle non-finite values.
Results may differ from a plain program's by a relative error of at most 0.015.
Values may be sent and summed in bfloat16 or wider, within the bound.
A program may use at most 256 MiB of HBM per device.

v0:
```python
import math

import jax
import jax.numpy as jnp
from jax import lax
from jax.sharding import PartitionSpec as P

EPS = 1e-06
ROPE_BASE = 10000.0
NEG_FILL = -1e30


def from_partner(value, axis, apart):
    mask = 2**apart
    pairs = [(source, source ^ mask) for source in range(lax.axis_size(axis))]
    return lax.ppermute(value, axis, pairs)


def rope_tables(positions, head_dim):
    frequency = 1.0 / ROPE_BASE ** (jnp.arange(0, head_dim, 2, dtype=jnp.float32) / head_dim)
    angles = positions.astype(jnp.float32)[..., None] * frequency
    return (jnp.cos(angles), jnp.sin(angles))


def rotate(values, cosine, sine_part):
    half_width = values.shape[-1] // 2
    first_half = values[..., :half_width]
    second_half = values[..., half_width:]
    return jnp.concatenate(
        [
            first_half * cosine - second_half * sine_part,
            second_half * cosine + first_half * sine_part,
        ],
        axis=-1,
    )


def rotate_back(grad_block, cosine, sine_part):
    half_width = grad_block.shape[-1] // 2
    first_half = grad_block[..., :half_width]
    second_half = grad_block[..., half_width:]
    return jnp.concatenate(
        [
            first_half * cosine + second_half * sine_part,
            second_half * cosine - first_half * sine_part,
        ],
        axis=-1,
    )


def norm_forward(values, gain_row):
    scale_inv = lax.rsqrt(jnp.mean(values * values, axis=-1, keepdims=True) + EPS)
    return ((values * scale_inv * gain_row).astype(jnp.bfloat16), scale_inv)


def norm_backward(values, scale_inv, gain_row, upstream):
    scaled = gain_row * upstream
    inner_mean = jnp.mean(values * scaled, axis=-1, keepdims=True)
    grad_in = scale_inv * scaled - values * (scale_inv * scale_inv * scale_inv) * inner_mean
    gain_grad = jnp.sum(upstream * values * scale_inv, axis=0)
    return (grad_in, gain_grad)


def product(left_side, right_side):
    return jnp.dot(left_side, right_side, preferred_element_type=jnp.float32)


def contract_rows(left_side, right_side):
    return lax.dot_general(
        left_side, right_side, (((0,), (0,)), ((), ())), preferred_element_type=jnp.float32
    )


def contract_cols(left_side, right_side):
    return lax.dot_general(
        left_side, right_side, (((1,), (1,)), ((), ())), preferred_element_type=jnp.float32
    )


def send_table(permutation, group_rank, seq_grp, fsdp_count, per_peer):
    slot_table = permutation.reshape(fsdp_count, seq_grp)
    from_here = slot_table // seq_grp == group_rank
    slot_rank = jnp.cumsum(from_here.astype(jnp.int32), axis=1) - 1
    local_index = slot_table - group_rank * seq_grp
    hits = (
        from_here[:, :, None, None]
        & (slot_rank[:, :, None, None] == jnp.arange(per_peer)[None, None, :, None])
        & (local_index[:, :, None, None] == jnp.arange(seq_grp)[None, None, None, :])
    )
    return jnp.sum(hits.astype(jnp.float32), axis=1).astype(jnp.bfloat16)


def arrive_table(permutation, group_rank, seq_grp, per_peer):
    slot_seqs = lax.dynamic_slice_in_dim(permutation, group_rank * seq_grp, seq_grp)
    source = slot_seqs // seq_grp
    slot_index = jnp.arange(seq_grp)
    earlier = (source[None, :] == source[:, None]) & (slot_index[None, :] < slot_index[:, None])
    arrival = source * per_peer + jnp.sum(earlier.astype(jnp.int32), axis=1)
    return ((arrival[:, None] == slot_index[None, :]).astype(jnp.bfloat16), slot_seqs)


def visible_mask(length, row_count, heads_local, key_count, offset):
    query_pos = offset + jnp.arange(row_count) // heads_local
    key_pos = jnp.arange(key_count)
    return (key_pos[None, :] <= query_pos[:, None]) & (key_pos[None, :] < length)


def attend_forward(query_rows, key_block, value_block, length, offset, heads_local, score_scale):
    scores = contract_cols(query_rows, key_block) * score_scale
    visible = visible_mask(length, query_rows.shape[0], heads_local, key_block.shape[0], offset)
    masked = jnp.where(visible, scores, NEG_FILL)
    row_max = jnp.max(masked, axis=1, keepdims=True)
    exponent = jnp.exp(masked - row_max)
    row_total = jnp.sum(exponent, axis=1, keepdims=True)
    probs = (exponent / row_total).astype(jnp.bfloat16)
    mixed_rows = product(probs, value_block).astype(jnp.bfloat16)
    return (mixed_rows, (row_max + jnp.log(row_total))[:, 0])


def attend_backward(
    query_rows,
    key_block,
    value_block,
    length,
    log_total,
    grad_rows,
    offset,
    heads_local,
    score_scale,
):
    scores = contract_cols(query_rows, key_block) * score_scale
    visible = visible_mask(length, query_rows.shape[0], heads_local, key_block.shape[0], offset)
    probs = jnp.exp(jnp.where(visible, scores, NEG_FILL) - log_total[:, None])
    grad_probs = contract_cols(grad_rows, value_block)
    row_dot = jnp.sum(probs * grad_probs, axis=1, keepdims=True)
    grad_scores = (probs * (grad_probs - row_dot)).astype(jnp.bfloat16)
    grad_query = product(grad_scores, key_block) * score_scale
    grad_keys = contract_rows(grad_scores, query_rows) * score_scale
    grad_values = contract_rows(probs.astype(jnp.bfloat16), grad_rows)
    return (grad_query, grad_keys, grad_values)


def regroup(grad_term, axis_index, outer_count, inner_count):
    moved = jnp.moveaxis(grad_term, axis_index, 0)
    moved_shape = moved.shape
    blocks = moved.reshape(
        (outer_count, inner_count, moved_shape[0] // (outer_count * inner_count)) + moved_shape[1:]
    )
    swapped = jnp.swapaxes(blocks, 0, 1).reshape(moved_shape)
    return jnp.moveaxis(swapped, 0, axis_index)


def local(
    hidden_in,
    cotangent,
    seq_lengths,
    positions,
    permutation,
    query_weight,
    keyval_weight,
    output_weight,
    norm_gains,
    bias_query,
    bias_keyval,
    gate_weight,
    up_weight,
    down_weight,
):
    group_rank = lax.axis_index("fsdp")
    ctx_rank = lax.axis_index("ctx")
    tensor_rank = lax.axis_index("tp")
    fsdp_count = lax.axis_size("fsdp")
    tensor_count = lax.axis_size("tp")
    seq_grp, local_len, model_width = hidden_in.shape
    heads_local, head_dim = bias_query.shape
    keyval_heads = bias_keyval.shape[0] // 2
    per_peer = seq_grp // fsdp_count
    all_seqs = permutation.shape[0]
    token_count = seq_grp * local_len
    row_share = token_count // tensor_count
    row_start = tensor_rank * row_share
    score_scale = 1.0 / math.sqrt(head_dim)
    send_rows = send_table(permutation, group_rank, seq_grp, fsdp_count, per_peer)
    arrive, slot_seqs = arrive_table(permutation, group_rank, seq_grp, per_peer)
    outgoing = jnp.einsum(
        "fpk,kld->fpld", send_rows, hidden_in, preferred_element_type=jnp.float32
    ).astype(jnp.bfloat16)
    incoming = lax.all_to_all(outgoing, "fsdp", split_axis=0, concat_axis=0, tiled=True)
    incoming = incoming.reshape(seq_grp, local_len, model_width)
    working = jnp.einsum("ja,ald->jld", arrive, incoming, preferred_element_type=jnp.float32)
    slot_pick = (slot_seqs[:, None] == jnp.arange(all_seqs)[None, :]).astype(jnp.int32)
    lengths_now = jnp.sum(slot_pick * seq_lengths[None, :], axis=1)
    positions_now = jnp.sum(slot_pick[:, :, None] * positions[None, :, :], axis=1)
    query_full, keyval_full, output_full, gains_full, gate_full, up_full, down_full = (
        lax.all_gather(query_weight, ("fsdp", "ctx"), axis=0, tiled=True),
        lax.all_gather(keyval_weight, ("fsdp", "ctx"), axis=0, tiled=True),
        lax.all_gather(output_weight, ("fsdp", "ctx"), axis=1, tiled=True),
        lax.all_gather(norm_gains, ("fsdp", "ctx"), axis=1, tiled=True),
        lax.all_gather(gate_weight, ("fsdp", "ctx"), axis=0, tiled=True),
        lax.all_gather(up_weight, ("fsdp", "ctx"), axis=0, tiled=True),
        lax.all_gather(down_weight, ("fsdp", "ctx"), axis=1, tiled=True),
    )
    gains_now = gains_full.astype(jnp.float32)
    flat_in = working.reshape(token_count, model_width)
    normed_one, inv_one = norm_forward(flat_in, gains_now[0])
    query_lin = product(normed_one, query_full) + bias_query.reshape(-1).astype(jnp.float32)
    head_pair = tensor_rank // (tensor_count // keyval_heads)
    parity = tensor_rank % 2
    keyval_head = lax.dynamic_slice_in_dim(
        keyval_full, head_pair * 2 * head_dim, 2 * head_dim, axis=1
    )
    bias_head = (
        lax.dynamic_slice_in_dim(bias_keyval, head_pair * 2, 2, axis=0)
        .reshape(-1)
        .astype(jnp.float32)
    )
    keyval_lin = product(normed_one, keyval_head) + bias_head
    cosine, sine_part = rope_tables(positions_now.reshape(token_count), head_dim)
    query_rot = rotate(
        query_lin.reshape(token_count, heads_local, head_dim),
        cosine[:, None, :],
        sine_part[:, None, :],
    ).astype(jnp.bfloat16)
    key_rot = rotate(keyval_lin[:, :head_dim], cosine, sine_part).astype(jnp.bfloat16)
    value_low = keyval_lin[:, head_dim:].astype(jnp.bfloat16)
    keys_all, values_all = (
        lax.all_gather(key_rot.reshape(seq_grp, local_len, head_dim), "ctx", axis=1, tiled=True),
        lax.all_gather(value_low.reshape(seq_grp, local_len, head_dim), "ctx", axis=1, tiled=True),
    )
    offset = ctx_rank * local_len
    query_seq = query_rot.reshape(seq_grp, local_len * heads_local, head_dim)

    def forward_one(seq_items):
        query_rows, key_block, value_block, length = seq_items
        return attend_forward(
            query_rows, key_block, value_block, length, offset, heads_local, score_scale
        )

    mixed_rows, log_totals = lax.map(forward_one, (query_seq, keys_all, values_all, lengths_now))
    mixed_flat = mixed_rows.reshape(token_count, heads_local * head_dim)
    attn_part = product(mixed_flat, output_full)
    in_share = lax.dynamic_slice_in_dim(flat_in, row_start, row_share, 0)
    middle_share = in_share + lax.psum_scatter(attn_part, "tp", scatter_dimension=0, tiled=True)
    normed_share, inv_two_share = norm_forward(middle_share, gains_now[1])
    normed_two = lax.all_gather(normed_share, "tp", axis=0, tiled=True)
    gate_lin = product(normed_two, gate_full)
    up_lin = product(normed_two, up_full)
    gate_sigmoid = jax.nn.sigmoid(gate_lin)
    silu_gate = gate_lin * gate_sigmoid
    hidden_act = (silu_gate * up_lin).astype(jnp.bfloat16)
    mlp_part = product(hidden_act, down_full)
    block_share = (
        middle_share + lax.psum_scatter(mlp_part, "tp", scatter_dimension=0, tiled=True)
    ).astype(jnp.bfloat16)
    grad_rows = cotangent.reshape(token_count, model_width)
    down_grad = contract_rows(hidden_act, grad_rows)
    grad_hidden = contract_cols(grad_rows, down_full)
    grad_gate = (
        grad_hidden * up_lin * gate_sigmoid * (1.0 + gate_lin * (1.0 - gate_sigmoid))
    ).astype(jnp.bfloat16)
    grad_up = (grad_hidden * silu_gate).astype(jnp.bfloat16)
    gate_grad = contract_rows(normed_two, grad_gate)
    up_grad = contract_rows(normed_two, grad_up)
    mlp_back_part = contract_cols(grad_gate, gate_full) + contract_cols(grad_up, up_full)
    grad_two_share = lax.psum_scatter(mlp_back_part, "tp", scatter_dimension=0, tiled=True)
    grad_norm_two, gain_two = norm_backward(
        middle_share, inv_two_share, gains_now[1], grad_two_share
    )
    cot_share = lax.dynamic_slice_in_dim(grad_rows, row_start, row_share, 0).astype(jnp.float32)
    grad_middle = cot_share + grad_norm_two
    grad_branch = lax.all_gather(grad_middle.astype(jnp.bfloat16), "tp", axis=0, tiled=True)
    output_grad = contract_rows(mixed_flat, grad_branch)
    grad_mixed = (
        contract_cols(grad_branch, output_full)
        .astype(jnp.bfloat16)
        .reshape(seq_grp, local_len * heads_local, head_dim)
    )

    def backward_one(seq_items):
        query_rows, key_block, value_block, length, log_total, grad_now = seq_items
        return attend_backward(
            query_rows,
            key_block,
            value_block,
            length,
            log_total,
            grad_now,
            offset,
            heads_local,
            score_scale,
        )

    grad_query, key_terms, value_terms = lax.map(
        backward_one, (query_seq, keys_all, values_all, lengths_now, log_totals, grad_mixed)
    )
    key_part, value_part = (
        lax.psum_scatter(key_terms, "ctx", scatter_dimension=1, tiled=True),
        lax.psum_scatter(value_terms, "ctx", scatter_dimension=1, tiled=True),
    )
    key_other, value_other = from_partner((key_part, value_part), "tp", 0)
    grad_key_rot = (key_part + key_other).reshape(token_count, head_dim)
    grad_value = (value_part + value_other).reshape(token_count, head_dim).astype(jnp.bfloat16)
    grad_query_lin = (
        rotate_back(
            grad_query.reshape(token_count, heads_local, head_dim),
            cosine[:, None, :],
            sine_part[:, None, :],
        )
        .astype(jnp.bfloat16)
        .reshape(token_count, heads_local * head_dim)
    )
    grad_key_lin = rotate_back(grad_key_rot, cosine, sine_part).astype(jnp.bfloat16)
    own_grad = jnp.where(parity == 0, grad_key_lin, grad_value)
    own_weight = lax.dynamic_slice_in_dim(keyval_head, parity * head_dim, head_dim, axis=1)
    query_grad = contract_rows(normed_one, grad_query_lin)
    keyval_grad = contract_rows(normed_one, own_grad)
    query_bias_grad = jnp.sum(grad_query_lin.astype(jnp.float32), axis=0).reshape(
        heads_local, head_dim
    )
    keyval_bias_grad = jnp.sum(own_grad.astype(jnp.float32), axis=0).reshape(1, head_dim)
    attn_back_part = contract_cols(grad_query_lin, query_full) + contract_cols(own_grad, own_weight)
    grad_one_share = lax.psum_scatter(attn_back_part, "tp", scatter_dimension=0, tiled=True)
    inv_one_share = lax.dynamic_slice_in_dim(inv_one, row_start, row_share, 0)
    grad_norm_one, gain_one = norm_backward(in_share, inv_one_share, gains_now[0], grad_one_share)
    input_share = (grad_middle + grad_norm_one).astype(jnp.bfloat16)
    block_rows, input_rows = (
        lax.all_gather(block_share, "tp", axis=0, tiled=True),
        lax.all_gather(input_share, "tp", axis=0, tiled=True),
    )
    gain_one, gain_two = lax.psum((gain_one, gain_two), "tp")
    out_block = (
        jnp.einsum(
            "ja,jld->ald",
            arrive,
            block_rows.reshape(seq_grp, local_len, model_width),
            preferred_element_type=jnp.float32,
        )
        .astype(jnp.bfloat16)
        .reshape(fsdp_count, per_peer, local_len, model_width)
    )
    out_grad = (
        jnp.einsum(
            "ja,jld->ald",
            arrive,
            input_rows.reshape(seq_grp, local_len, model_width),
            preferred_element_type=jnp.float32,
        )
        .astype(jnp.bfloat16)
        .reshape(fsdp_count, per_peer, local_len, model_width)
    )
    home_block, home_grad = (
        lax.all_to_all(out_block, "fsdp", split_axis=0, concat_axis=0, tiled=True),
        lax.all_to_all(out_grad, "fsdp", split_axis=0, concat_axis=0, tiled=True),
    )
    block_out = jnp.einsum(
        "gpk,gpld->kld", send_rows, home_block, preferred_element_type=jnp.float32
    ).astype(jnp.bfloat16)
    input_grad = jnp.einsum(
        "gpk,gpld->kld", send_rows, home_grad, preferred_element_type=jnp.float32
    ).astype(jnp.bfloat16)
    gain_grad = jnp.stack([gain_one, gain_two])
    ctx_count = lax.axis_size("ctx")
    query_held = regroup(query_grad, 0, fsdp_count, ctx_count)
    keyval_held = regroup(keyval_grad, 0, fsdp_count, ctx_count)
    output_held = regroup(output_grad, 1, fsdp_count, ctx_count)
    gain_held = regroup(gain_grad, 1, fsdp_count, ctx_count)
    gate_held = regroup(gate_grad, 0, fsdp_count, ctx_count)
    up_held = regroup(up_grad, 0, fsdp_count, ctx_count)
    down_held = regroup(down_grad, 1, fsdp_count, ctx_count)
    qbias_held = regroup(query_bias_grad, 1, fsdp_count, ctx_count)
    kvbias_held = regroup(keyval_bias_grad, 1, fsdp_count, ctx_count)
    sectioned = (
        lax.psum_scatter(query_held, "ctx", scatter_dimension=0, tiled=True),
        lax.psum_scatter(keyval_held, "ctx", scatter_dimension=0, tiled=True),
        lax.psum_scatter(output_held, "ctx", scatter_dimension=1, tiled=True),
        lax.psum_scatter(gain_held, "ctx", scatter_dimension=1, tiled=True),
        lax.psum_scatter(gate_held, "ctx", scatter_dimension=0, tiled=True),
        lax.psum_scatter(up_held, "ctx", scatter_dimension=0, tiled=True),
        lax.psum_scatter(down_held, "ctx", scatter_dimension=1, tiled=True),
        lax.psum_scatter(qbias_held, "ctx", scatter_dimension=1, tiled=True),
        lax.psum_scatter(kvbias_held, "ctx", scatter_dimension=1, tiled=True),
    )
    summed = (
        lax.psum_scatter(sectioned[0], "fsdp", scatter_dimension=0, tiled=True),
        lax.psum_scatter(sectioned[1], "fsdp", scatter_dimension=0, tiled=True),
        lax.psum_scatter(sectioned[2], "fsdp", scatter_dimension=1, tiled=True),
        lax.psum_scatter(sectioned[3], "fsdp", scatter_dimension=1, tiled=True),
        lax.psum_scatter(sectioned[4], "fsdp", scatter_dimension=0, tiled=True),
        lax.psum_scatter(sectioned[5], "fsdp", scatter_dimension=0, tiled=True),
        lax.psum_scatter(sectioned[6], "fsdp", scatter_dimension=1, tiled=True),
        lax.psum_scatter(sectioned[7], "fsdp", scatter_dimension=1, tiled=True),
        lax.psum_scatter(sectioned[8], "fsdp", scatter_dimension=1, tiled=True),
    )
    return (
        block_out,
        input_grad,
        summed[0],
        summed[1],
        summed[2],
        summed[3],
        summed[7],
        summed[8],
        summed[4],
        summed[5],
        summed[6],
    )


def solution(mesh):
    placed = (
        P("fsdp", "ctx", None),
        P("fsdp", "ctx", None),
        P(),
        P(None, "ctx"),
        P(),
        P(("fsdp", "ctx"), "tp"),
        P(("fsdp", "ctx"), None),
        P("tp", ("fsdp", "ctx")),
        P(None, ("fsdp", "ctx")),
        P("tp", None),
        P(),
        P(("fsdp", "ctx"), "tp"),
        P(("fsdp", "ctx"), "tp"),
        P("tp", ("fsdp", "ctx")),
    )
    return jax.shard_map(
        local,
        mesh=mesh,
        in_specs=placed,
        out_specs=(
            P("fsdp", "ctx", None),
            P("fsdp", "ctx", None),
            P(("fsdp", "ctx"), "tp"),
            P(("fsdp", "ctx"), "tp"),
            P("tp", ("fsdp", "ctx")),
            P(None, ("fsdp", "ctx")),
            P("tp", ("fsdp", "ctx")),
            P("tp", ("fsdp", "ctx")),
            P(("fsdp", "ctx"), "tp"),
            P(("fsdp", "ctx"), "tp"),
            P("tp", ("fsdp", "ctx")),
        ),
        check_vma=False,
    )
```

profile of v0, /device:TPU:1, one launch (start us, length us, event | category | flops | bytes accessed | tf_op | source)
XLA Modules:
  0.0 2778.3 jit_solution(17800331773113071734)
XLA Ops:
  32.8 129.5 %all-gather = bf16[8,192,2]{1,2,0:T(2,128)(2,1)S(1)} all-gather(bf16[1,192,2]{1,2,0:T(2,128)(2,1)S(1)} %bitcast.325), channel_id=1, replica_groups=mesh['fsdp'=4,'ctx'=2,'tp'=4] {'fsdp','ctx'}, dimensions={0}, use_global_device_ids=true | all-gather | bytes 6912 | tf_op jit(solution)/shard_map/all_gather | solution.py:198
  288.5 55.1 %while.30 = (s32[]{:T(128)}, bf16[4,1536,128]{2,1,0:T(8,128)(2,1)S(1)}, f32[4,1536]{1,0:T(4,128)}, s32[]{:T(128)}, s32[4]{0:T(128)S(1)}, /*index=5*/bf16[4,1536,...) while((s32[]{:T(128)}, ...), condition=%wide.region_9.10_spmd, body=%wide.region_6.9_spmd.sunk | while | flops 821244928 | bytes 45445272 | solution.py:239
  352.9 98.4 %reduce-scatter.37.cloned.1.call-done = f32[512,1536]{1,0:T(8,128)} async-done(((f32[2048,1536]{1,0:T(8,128)}), f32[512,1536]{1,0:T(8,128)}) %reduce-scatter.37.cloned.1.call-update) | async-done | bytes 3145744 | tf_op jit(solution)/shard_map/reduce_scatter | solution.py:243
  459.3 102.6 %all-gather.26.cloned.1.call-done = bf16[1536,2240]{1,0:T(8,128)(2,1)} async-done(((bf16[192,2240]{1,0:T(8,128)(2,1)}), bf16[1536,2240]{1,0:T(8,128)(2,1)}) %all-gather.26.cloned.1.call-update) | async-done | bytes 6881296 | tf_op jit(solution)/shard_map/all_gather | solution.py:199
  561.9 47.6 %all-gather.24.cloned.1.call-done = bf16[2048,1536]{1,0:T(8,128)(2,1)} async-done(((bf16[512,1536]{1,0:T(8,128)(2,1)}), bf16[2048,1536]{1,0:T(8,128)(2,1)}) %all-gather.24.cloned.1.call-update) | async-done | bytes 6291472 | tf_op jit(solution)/shard_map/all_gather | solution.py:245
  630.3 89.4 %all-gather.28.cloned.1.call-done = bf16[1536,2240]{1,0:T(8,128)(2,1)} async-done(((bf16[192,2240]{1,0:T(8,128)(2,1)}), bf16[1536,2240]{1,0:T(8,128)(2,1)}) %all-gather.28.cloned.1.call-update) | async-done | bytes 6881296 | tf_op jit(solution)/shard_map/all_gather | solution.py:200
  740.8 88.0 %all-gather.30.cloned.1.call-done = bf16[2240,1536]{0,1:T(8,128)(2,1)} async-done(((bf16[2240,192]{0,1:T(8,128)(2,1)}), bf16[2240,1536]{0,1:T(8,128)(2,1)}) %all-gather.30.cloned.1.call-update) | async-done | bytes 6881296 | tf_op jit(solution)/shard_map/all_gather | solution.py:201
  828.7 33.2 %multiply_convert_fusion.1 = (bf16[2048,2240]{0,1:T(8,128)(2,1)}, bf16[2048,2240]{0,1:T(8,128)(2,1)}, bf16[2048,2240]{0,1:T(8,128)(2,1)}) fusion(f32[2048,2240]{0,1:T(8,128)} %fusion.120, f32[2048,2240]{0,1:T(8,128)} %fusion.121, bf16[2048,1536]{1,0:T(8,128)(2,1)} %bitcast.301, bf16[2240,1536]{0,1:T(8,128)(2,1)} %all-gather.30.cloned.1.call-done), kind=kOutput, calls=%fused_computation.73 | convolution fusion | flops 14161674240 | bytes 77398016 | tf_op jit(solution)/shard_map/dot_general | solution.py:75
  922.6 76.6 %reduce-scatter.41.cloned.1.call-done = f32[512,1536]{1,0:T(8,128)} async-done(((f32[2048,1536]{1,0:T(8,128)}), f32[512,1536]{1,0:T(8,128)}) %reduce-scatter.41.cloned.1.call-update) | async-done | bytes 3145744 | tf_op jit(solution)/shard_map/reduce_scatter | solution.py:265
  1001.9 98.8 %reduce-scatter.39.cloned.1.call-done = f32[512,1536]{1,0:T(8,128)} async-done(((f32[2048,1536]{1,0:T(8,128)}), f32[512,1536]{1,0:T(8,128)}) %reduce-scatter.39.cloned.1.call-update) | async-done | bytes 3145744 | tf_op jit(solution)/shard_map/reduce_scatter | solution.py:253
  1106.6 46.9 %all-gather.34.cloned.1.call-done = bf16[2048,1536]{1,0:T(8,128)(2,1)} async-done(((bf16[512,1536]{1,0:T(8,128)(2,1)}), bf16[2048,1536]{1,0:T(8,128)(2,1)}) %all-gather.34.cloned.1.call-update) | async-done | bytes 6291472 | tf_op jit(solution)/shard_map/all_gather | solution.py:271
  1163.8 63.3 %while.31 = (s32[]{:T(128)}, f32[4,1536,128]{2,1,0:T(8,128)}, f32[4,1024,128]{2,1,0:T(8,128)}, f32[4,1024,128]{2,1,0:T(8,128)}, s32[]{:T(128)}, /*index=5*/s32[4...) while((s32[]{:T(128)}, f32[4,1536,128]{2,1,0:T(8,128)}, ...), condition=%wide.region_17.18_spmd, body=%wide.region_15.17_spmd.sunk | while | flops 2030908416 | bytes 51434636 | solution.py:293
  1324.2 95.4 %reduce-scatter.47.cloned.1.call-done = f32[512,1536]{1,0:T(8,128)} async-done(((f32[2048,1536]{1,0:T(8,128)}), f32[512,1536]{1,0:T(8,128)}) %reduce-scatter.47.cloned.1.call-update) | async-done | bytes 3145744 | tf_op jit(solution)/shard_map/reduce_scatter | solution.py:322
  1595.0 35.7 %reduce-scatter.61.cloned.1.call-done = f32[768,2240]{1,0:T(8,128)} async-done(((f32[1536,2240]{1,0:T(8,128)}), f32[768,2240]{1,0:T(8,128)}) %reduce-scatter.61.cloned.1.call-update) | async-done | bytes 6881296 | tf_op jit(solution)/shard_map/reduce_scatter | solution.py:377
  1630.8 163.8 %reduce-scatter.65.cloned.1.call-done = f32[768,2240]{1,0:T(8,128)} async-done(((f32[1536,2240]{1,0:T(8,128)}), f32[768,2240]{1,0:T(8,128)}) %reduce-scatter.65.cloned.1.call-update) | async-done | bytes 6881296 | tf_op jit(solution)/shard_map/reduce_scatter | solution.py:378
  1794.9 163.5 %reduce-scatter.69.cloned.1.call-done = f32[2240,768]{0,1:T(8,128)} async-done(((f32[2240,1536]{0,1:T(8,128)}), f32[2240,768]{0,1:T(8,128)}) %reduce-scatter.69.cloned.1.call-update) | async-done | bytes 6881296 | tf_op jit(solution)/shard_map/reduce_scatter | solution.py:379
  1958.5 48.5 %all-gather.32.cloned.1.call-done = bf16[2048,1536]{1,0:T(8,128)(2,1)} async-done(((bf16[512,1536]{1,0:T(8,128)(2,1)}), bf16[2048,1536]{1,0:T(8,128)(2,1)}) %all-gather.32.cloned.1.call-update) | async-done | bytes 6291472 | tf_op jit(solution)/shard_map/all_gather | solution.py:327
  2071.8 98.1 %all-to-all-done.1 = bf16[4,1,512,1536]{3,2,1,0:T(8,128)(2,1)} async-done(((bf16[4,1,512,1536]{3,2,1,0:T(8,128)(2,1)}), bf16[4,1,512,1536]{3,2,1,0:T(8,128)(2,1)}, u32[]{:S(2)}, u32[]{:S(2)}) %all-to-all-start.1) | async-done | bytes 6291488 | tf_op jit(solution)/shard_map/all_to_all | solution.py:352
  2225.5 153.1 %all-to-all-done.2 = bf16[4,1,512,1536]{3,2,1,0:T(8,128)(2,1)} async-done(((bf16[4,1,512,1536]{3,2,1,0:T(8,128)(2,1)}), bf16[4,1,512,1536]{3,2,1,0:T(8,128)(2,1)}, u32[]{:S(2)}, u32[]{:S(2)}) %all-to-all-start.2) | async-done | bytes 6291488 | tf_op jit(solution)/shard_map/all_to_all | solution.py:353
  2391.5 44.1 %reduce-scatter.63.cloned.1.call-done = f32[192,2240]{1,0:T(8,128)} async-done(((f32[768,2240]{1,0:T(8,128)}), f32[192,2240]{1,0:T(8,128)}) %reduce-scatter.63.cloned.1.call-update) | async-done | bytes 1720336 | tf_op jit(solution)/shard_map/reduce_scatter | solution.py:388
  2435.6 124.6 %reduce-scatter.67.cloned.1.call-done = f32[192,2240]{1,0:T(8,128)} async-done(((f32[768,2240]{1,0:T(8,128)}), f32[192,2240]{1,0:T(8,128)}) %reduce-scatter.67.cloned.1.call-update) | async-done | bytes 1720336 | tf_op jit(solution)/shard_map/reduce_scatter | solution.py:389
  2560.2 126.9 %reduce-scatter.71.cloned.1.call-done = f32[2240,192]{0,1:T(8,128)} async-done(((f32[2240,768]{0,1:T(8,128)}), f32[2240,192]{0,1:T(8,128)}) %reduce-scatter.71.cloned.1.call-update) | async-done | bytes 1720336 | tf_op jit(solution)/shard_map/reduce_scatter | solution.py:390
  2687.1 32.5 %reduce-scatter.51.cloned.1.call-done = f32[192,384]{1,0:T(8,128)} async-done(((f32[768,384]{1,0:T(8,128)}), f32[192,384]{1,0:T(8,128)}) %reduce-scatter.51.cloned.1.call-update) | async-done | bytes 294928 | tf_op jit(solution)/shard_map/reduce_scatter | solution.py:384
  2719.7 30.9 %reduce-scatter.59.cloned.1.call-done = f32[384,192]{0,1:T(8,128)} async-done(((f32[384,768]{0,1:T(8,128)}), f32[384,192]{0,1:T(8,128)}) %reduce-scatter.59.cloned.1.call-update) | async-done | bytes 294928 | tf_op jit(solution)/shard_map/reduce_scatter | solution.py:386
  (408 shorter events, 834.4 us)
Async XLA Ops:
  32.4 243.2 %all-gather.18.cloned.1.call-start = ((), (), s32[]{:S(2)}) async-start(), calls=%async_computation.29 | async-start | bytes 1572864 | tf_op jit(solution)/shard_map/all_gather | solution.py:227
  352.8 256.7 %all-gather.24.cloned.1.call-start = ((), (), s32[]{:S(2)}) async-start(), calls=%async_computation.33 | async-start | bytes 7864320 | tf_op jit(solution)/shard_map/all_gather | solution.py:245
  457.7 262.0 %all-gather.28.cloned.1.call-start = ((), (), s32[]{:S(2)}) async-start(), calls=%async_computation.35 | async-start | bytes 7962624 | tf_op jit(solution)/shard_map/all_gather | solution.py:200
  458.5 370.3 %all-gather.30.cloned.1.call-start = ((), (), s32[]{:S(2)}) async-start(), calls=%async_computation.36 | async-start | bytes 7962624 | tf_op jit(solution)/shard_map/all_gather | solution.py:201
  459.1 540.2 %reduce-scatter.41.cloned.1.call-start = ((), (), s32[]{:S(2)}) async-start(), calls=%async_computation.39 | async-start | bytes 15728640 | tf_op jit(solution)/shard_map/reduce_scatter | solution.py:265
  1321.0 266.5 %reduce-scatter.77.cloned.1.call-start = ((), (), s32[]{:S(2)}) async-start(), calls=%async_computation.59 | async-start | bytes 98304
  1322.6 265.4 %reduce-scatter.81.cloned.1.call-start = ((), (), s32[]{:S(2)}) async-start(), calls=%async_computation.61 | async-start | bytes 98304
  1324.1 270.3 %reduce-scatter.73.cloned.1.call-start = ((), (), s32[]{:S(2)}) async-start(), calls=%async_computation.57 | async-start | bytes 1179648
  1467.7 326.9 %reduce-scatter.65.cloned.1.call-start = ((), (), s32[]{:S(2)}) async-start(), calls=%async_computation.53 | async-start | bytes 21233664 | tf_op jit(solution)/shard_map/reduce_scatter | solution.py:378
  1500.3 458.1 %reduce-scatter.69.cloned.1.call-start = ((), (), s32[]{:S(2)}) async-start(), calls=%async_computation.55 | async-start | bytes 21233664 | tf_op jit(solution)/shard_map/reduce_scatter | solution.py:379
  1546.9 460.0 %all-gather.32.cloned.1.call-start = ((), (), s32[]{:S(2)}) async-start(), calls=%async_computation.38 | async-start | bytes 7864320 | tf_op jit(solution)/shard_map/all_gather | solution.py:327
  1547.6 507.2 %all-gather.36.cloned.1.call-start = ((), (), s32[]{:S(2)}) async-start(), calls=%async_computation.44 | async-start | bytes 7864320 | tf_op jit(solution)/shard_map/all_gather | solution.py:328
  1553.5 621.7 %reduce-scatter.49.cloned.1.call-start = ((), (), s32[]{:S(2)}) async-start(), calls=%async_computation.45 | async-start | bytes 3538944 | tf_op jit(solution)/shard_map/reduce_scatter | solution.py:373
  1570.4 605.6 %reduce-scatter.57.cloned.1.call-start = ((), (), s32[]{:S(2)}) async-start(), calls=%async_computation.49 | async-start | bytes 3538944 | tf_op jit(solution)/shard_map/reduce_scatter | solution.py:375
  1587.4 589.5 %reduce-scatter.79.cloned.1.call-start = ((), (), s32[]{:S(2)}) async-start(), calls=%async_computation.60 | async-start | bytes 40960
  1588.0 590.3 %reduce-scatter.83.cloned.1.call-start = ((), (), s32[]{:S(2)}) async-start(), calls=%async_computation.62 | async-start | bytes 40960
  1588.8 598.3 %reduce-scatter.53.cloned.1.call-start = ((), (), s32[]{:S(2)}) async-start(), calls=%async_computation.47 | async-start | bytes 1179648 | tf_op jit(solution)/shard_map/reduce_scatter | solution.py:374
  1594.4 629.5 %reduce-scatter.75.cloned.1.call-start = ((), (), s32[]{:S(2)}) async-start(), calls=%async_computation.58 | async-start | bytes 491520
  1595.0 840.6 %reduce-scatter.63.cloned.1.call-start = ((), (), s32[]{:S(2)}) async-start(), calls=%async_computation.52 | async-start | bytes 8847360 | tf_op jit(solution)/shard_map/reduce_scatter | solution.py:388
  1630.7 929.5 %reduce-scatter.67.cloned.1.call-start = ((), (), s32[]{:S(2)}) async-start(), calls=%async_computation.54 | async-start | bytes 8847360 | tf_op jit(solution)/shard_map/reduce_scatter | solution.py:389
  1794.6 892.5 %reduce-scatter.71.cloned.1.call-start = ((), (), s32[]{:S(2)}) async-start(), calls=%async_computation.56 | async-start | bytes 8847360 | tf_op jit(solution)/shard_map/reduce_scatter | solution.py:390
  2175.2 544.5 %reduce-scatter.51.cloned.1.call-start = ((), (), s32[]{:S(2)}) async-start(), calls=%async_computation.46 | async-start | bytes 1474560 | tf_op jit(solution)/shard_map/reduce_scatter | solution.py:384
  2175.9 574.6 %reduce-scatter.59.cloned.1.call-start = ((), (), s32[]{:S(2)}) async-start(), calls=%async_computation.50 | async-start | bytes 1474560 | tf_op jit(solution)/shard_map/reduce_scatter | solution.py:386
  2176.7 594.9 %reduce-scatter.55.cloned.1.call-start = ((), (), s32[]{:S(2)}) async-start(), calls=%async_computation.48 | async-start | bytes 491520 | tf_op jit(solution)/shard_map/reduce_scatter | solution.py:385
  (70 other events, 5057.2 us)
Sparse Core Ops, SparseCore 0:
  34.0 80.1 all-gather.15
  116.3 95.1 all-gather.13
  290.5 39.8 all-gather.21
  352.2 99.0 reduce-scatter.36
  453.5 108.3 all-gather.25
  564.1 45.3 all-gather.23
  611.7 107.9 all-gather.27
  721.7 106.9 all-gather.29
  901.5 97.6 reduce-scatter.40
  1001.7 99.0 reduce-scatter.38
  1106.7 46.8 all-gather.33
  1260.9 31.8 reduce-scatter.44
  1321.1 98.4 reduce-scatter.46
  1467.8 162.8 reduce-scatter.60
  1633.1 161.4 reduce-scatter.64
  1797.0 161.4 reduce-scatter.68
  1960.1 46.7 all-gather.31
  2008.4 46.3 all-gather.35
  2057.2 34.2 reduce-scatter.48
  2093.6 34.7 reduce-scatter.56
  2189.1 34.7 reduce-scatter.74
  2226.9 208.6 reduce-scatter.62
  2438.6 121.5 reduce-scatter.66
  2563.1 124.0 reduce-scatter.70
  (12 shorter events, 246.0 us)
where the time goes:
time: 2790 us; the launch traced here: 2780 us
  waiting for transfers between devices  1940 us (70%)
  matrix products  400 us (14%)
  local copies, waits for them, and re-layouts  187 us (7%)
  blocking collectives  139 us (5%)
  other arithmetic  76.4 us (3%)
    reduce_scatter x1, waiting for transfers between devices, local(): lax.psum_scatter(up_held, 'ctx', scatter_dimension=0, tiled=True)  164 us
    reduce_scatter x1, waiting for transfers between devices, local(): lax.psum_scatter(down_held, 'ctx', scatter_dimension=1, tiled=True)  164 us
    all_to_all x1, waiting for transfers between devices, local(): lax.all_to_all(out_grad, 'fsdp', split_axis=0, concat_axis=0, tiled=True)  153 us
    dot_general x18, matrix products, contract_cols(): lax.dot_general(left_side, right_side, (((1,), (1,)), ((), ())), preferre...  135 us
    all_gather x1, blocking collectives, local(): lax.all_gather(norm_gains, ('fsdp', 'ctx'), axis=1, tiled=True)  129 us
    reduce_scatter x1, waiting for transfers between devices, local(): lax.psum_scatter(sectioned[6], 'fsdp', scatter_dimension=1, tiled=True)  127 us
    reduce_scatter x1, waiting for transfers between devices, local(): lax.psum_scatter(sectioned[5], 'fsdp', scatter_dimension=0, tiled=True)  125 us
    dot_general x14, matrix products, product(): return jnp.dot(left_side, right_side, preferred_element_type=jnp.float32)  105 us
  transfers between devices with their start and end apart: 41, of which 28 were waited for; matrix products, arithmetic and copies ran while one was open for 16% of the time, Pallas kernels for 0%

commit v1 on v0

v1 whole, which is shorter than its diff:
```python
import functools
import math

import jax
import jax.numpy as jnp
from jax import lax
from jax.experimental import pallas as pl
from jax.experimental.pallas import tpu as pltpu
from jax.sharding import PartitionSpec as P

EPS = 1e-06
ROPE_BASE = 10000.0
NEG_FILL = -1e30
LOW = jnp.bfloat16
WIDE = jnp.float32
DEAL_SHIFT = (0, 2, 1, 3)


def from_partner(value, axis, apart):
    pairs = [(source, source ^ apart) for source in range(lax.axis_size(axis))]
    return lax.ppermute(value, axis, pairs)


def product(left_side, right_side, kind=WIDE):
    return jnp.dot(left_side, right_side, preferred_element_type=WIDE).astype(kind)


def contract_rows(left_side, right_side, kind=WIDE):
    return lax.dot_general(
        left_side, right_side, (((0,), (0,)), ((), ())), preferred_element_type=WIDE
    ).astype(kind)


def contract_cols(left_side, right_side, kind=WIDE):
    return lax.dot_general(
        left_side, right_side, (((1,), (1,)), ((), ())), preferred_element_type=WIDE
    ).astype(kind)


def norm_backward(values, scale_inv, gain_row, upstream):
    scaled = gain_row * upstream
    inner_mean = jnp.mean(values * scaled, axis=-1, keepdims=True)
    grad_in = scale_inv * scaled - values * (scale_inv * scale_inv * scale_inv) * inner_mean
    gain_grad = jnp.sum(upstream * values * scale_inv, axis=0)
    return (grad_in, gain_grad)


def spread_rows(own):
    far = from_partner(own, "tp", 2)
    near = from_partner(own, "tp", 1)
    cross = from_partner(far, "tp", 1)
    return (own, near, far, cross)


def collect_rows(parts):
    wide = parts[2].astype(WIDE) + from_partner(parts[3], "tp", 1).astype(WIDE)
    far = from_partner(wide.astype(LOW), "tp", 2)
    near = from_partner(parts[1], "tp", 1)
    return parts[0].astype(WIDE) + near.astype(WIDE) + far.astype(WIDE)


def interleave(own, other, ctx_rank):
    first = jnp.where(ctx_rank == 0, own, other)
    second = jnp.where(ctx_rank == 0, other, own)
    return (first, second)


def gather_small(shard, ctx_rank):
    if lax.axis_size("ctx") != 2:
        return lax.all_gather(shard, ("fsdp", "ctx"), axis=0, tiled=True)
    both = jnp.stack(interleave(shard, from_partner(shard, "ctx", 1), ctx_rank), axis=0)
    full = lax.all_gather(both, "fsdp", axis=0, tiled=False)
    return full.reshape(-1, shard.shape[1])


def gather_large(shard, ctx_rank):
    if lax.axis_size("ctx") != 2:
        return lax.all_gather(shard, ("fsdp", "ctx"), axis=0, tiled=True)
    held = lax.all_gather(shard, "fsdp", axis=0, tiled=False)
    other = from_partner(held, "ctx", 1)
    return jnp.stack(interleave(held, other, ctx_rank), axis=1).reshape(-1, shard.shape[1])


def scatter_sum(grad, ctx_rank, kind):
    fsdp_count, ctx_count = lax.axis_size("fsdp"), lax.axis_size("ctx")
    rows, cols = grad.shape
    blocks = grad.reshape(fsdp_count, ctx_count, rows // (fsdp_count * ctx_count), cols)
    if ctx_count == 2:
        kept = lax.dynamic_index_in_dim(blocks, ctx_rank, 1, keepdims=False)
        sent = lax.dynamic_index_in_dim(blocks, 1 - ctx_rank, 1, keepdims=False)
        got = from_partner(sent, "ctx", 1)
        held = (kept.astype(WIDE) + got.astype(WIDE)).astype(kind)
    else:
        swapped = jnp.swapaxes(blocks, 0, 1).reshape(rows, cols)
        held = lax.psum_scatter(swapped, "ctx", scatter_dimension=0, tiled=True)
    held = held.reshape(rows // ctx_count, cols)
    return lax.psum_scatter(held, "fsdp", scatter_dimension=0, tiled=True)


def turn(values, cosine, sine_signed):
    return values * cosine + pltpu.roll(values, values.shape[-1] // 2, 1) * sine_signed


def turn_back(values, cosine, sine_signed):
    return values * cosine - pltpu.roll(values, values.shape[-1] // 2, 1) * sine_signed


def project_kernel(
    heads, head_dim, x0, x1, x2, x3, gain, weight, bias, cosine, sine, h_out, q_out, k_out, v_out
):
    slot = pl.program_id(0)

    def run(x_ref):
        x = x_ref[...].astype(WIDE)
        scale_inv = lax.rsqrt(jnp.mean(x * x, axis=-1, keepdims=True) + EPS)
        normed = (x * scale_inv * gain[...]).astype(LOW)
        h_out[0] = normed
        lin = jnp.dot(normed, weight[...], preferred_element_type=WIDE) + bias[...]
        cos, sin = cosine[0], sine[0]
        for h in range(heads + 1):
            part = turn(lin[:, h * head_dim : (h + 1) * head_dim], cos, sin).astype(LOW)
            if h < heads:
                q_out[0, :, h * head_dim : (h + 1) * head_dim] = part
            else:
                k_out[0] = part
        v_out[0] = lin[:, (heads + 1) * head_dim :].astype(LOW)

    for r, x_ref in enumerate((x0, x1, x2, x3)):
        pl.when(slot == r)(functools.partial(run, x_ref))


def project(rows, gain, weight, bias, cosine, sine, heads, head_dim):
    length, width = rows[0].shape
    count = len(rows)
    cols = (heads + 2) * head_dim
    whole = lambda *shape: pl.BlockSpec(shape, lambda s: (0,) * len(shape))
    by_slot = lambda *shape: pl.BlockSpec((1, *shape), lambda s: (s,) + (0,) * len(shape))
    return pl.pallas_call(
        functools.partial(project_kernel, heads, head_dim),
        grid=(count,),
        in_specs=[whole(length, width)] * count
        + [whole(1, width), whole(width, cols), whole(1, cols)]
        + [by_slot(length, head_dim)] * 2,
        out_specs=[
            by_slot(length, width),
            by_slot(length, heads * head_dim),
            by_slot(length, head_dim),
            by_slot(length, head_dim),
        ],
        out_shape=[
            jax.ShapeDtypeStruct((count, length, width), LOW),
            jax.ShapeDtypeStruct((count, length, heads * head_dim), LOW),
            jax.ShapeDtypeStruct((count, length, head_dim), LOW),
            jax.ShapeDtypeStruct((count, length, head_dim), LOW),
        ],
        compiler_params=pltpu.CompilerParams(vmem_limit_bytes=56 << 20),
        cost_estimate=pl.CostEstimate(
            flops=2 * count * length * width * cols,
            bytes_accessed=count * length * (2 * width + cols) * 2 + width * cols * 2,
            transcendentals=0,
        ),
    )(*rows, gain, weight, bias, cosine, sine)


def row_blocks(length):
    return [(i, min(256, length)) for i in range(0, length, min(256, length))]


def key_biases(length, offset, start, rows, past, keys):
    past_pos = lax.broadcasted_iota(jnp.int32, (1, past), 1)
    past_bias = jnp.where((past_pos < offset) & (past_pos < length), 0.0, NEG_FILL)
    query_pos = offset + start + lax.broadcasted_iota(jnp.int32, (rows, keys), 0)
    own_pos = offset + lax.broadcasted_iota(jnp.int32, (rows, keys), 1)
    own_bias = jnp.where((own_pos <= query_pos) & (own_pos < length), 0.0, NEG_FILL)
    return past_bias, own_bias


def dot_cols(left, right):
    return lax.dot_general(left, right, (((1,), (1,)), ((), ())), preferred_element_type=WIDE)


def dot_rows(left, right):
    return lax.dot_general(left, right, (((0,), (0,)), ((), ())), preferred_element_type=WIDE)


def attend_kernel(heads, head_dim, scale, info, q, k_past, v_past, k_own, v_own, out, lse):
    slot = pl.program_id(0)
    length, offset = info[slot], info[pl.num_programs(0)]
    past = k_past.shape[1]
    for start, rows in row_blocks(q.shape[1]):
        keys = start + rows
        past_bias, own_bias = key_biases(length, offset, start, rows, past, keys)
        here = slice(start, start + rows)
        for h in range(heads):
            cols = slice(h * head_dim, (h + 1) * head_dim)
            query = q[0, here, cols]
            s_past = dot_cols(query, k_past[0]) * scale + past_bias
            s_own = dot_cols(query, k_own[0, :keys]) * scale + own_bias
            top = jnp.maximum(
                jnp.max(s_past, axis=1, keepdims=True), jnp.max(s_own, axis=1, keepdims=True)
            )
            e_past, e_own = jnp.exp(s_past - top), jnp.exp(s_own - top)
            total = jnp.sum(e_past, axis=1, keepdims=True) + jnp.sum(e_own, axis=1, keepdims=True)
            inverse = 1.0 / total
            mixed = jnp.dot(
                (e_past * inverse).astype(LOW), v_past[0], preferred_element_type=WIDE
            ) + jnp.dot((e_own * inverse).astype(LOW), v_own[0, :keys], preferred_element_type=WIDE)
            out[0, here, cols] = mixed.astype(LOW)
            lse[0, here, h : h + 1] = top + jnp.log(total)


def attend_forward(info, q, k_past, v_past, k_own, v_own, heads, head_dim, scale):
    count, length, width = q.shape
    past = k_past.shape[1]
    by_slot = lambda *shape: pl.BlockSpec((1, *shape), lambda s, info: (s,) + (0,) * len(shape))
    keys = count * length * (past + length) * heads
    return pl.pallas_call(
        functools.partial(attend_kernel, heads, head_dim, scale),
        grid_spec=pltpu.PrefetchScalarGridSpec(
            num_scalar_prefetch=1,
            grid=(count,),
            in_specs=[
                by_slot(length, width),
                by_slot(past, head_dim),
                by_slot(past, head_dim),
                by_slot(length, head_dim),
                by_slot(length, head_dim),
            ],
            out_specs=[by_slot(length, width), by_slot(length, 128)],
        ),
        out_shape=[
            jax.ShapeDtypeStruct((count, length, width), LOW),
            jax.ShapeDtypeStruct((count, length, 128), WIDE),
        ],
        compiler_params=pltpu.CompilerParams(vmem_limit_bytes=56 << 20),
        cost_estimate=pl.CostEstimate(
            flops=4 * keys * head_dim, bytes_accessed=4 * count * length * width, transcendentals=keys
        ),
    )(info, q, k_past, v_past, k_own, v_own)


def attend_back_kernel(
    heads,
    head_dim,
    scale,
    info,
    q,
    k_past,
    v_past,
    k_own,
    v_own,
    grad,
    lse,
    cosine,
    sine,
    dq_out,
    mine_past,
    mine_own,
    other_past,
    other_own,
    dk_past,
    dk_own,
    dv_past,
    dv_own,
):
    slot = pl.program_id(0)
    length, offset = info[slot], info[pl.num_programs(0)]
    parity = info[pl.num_programs(0) + 1]
    past = k_past.shape[1]
    for total in (dk_past, dk_own, dv_past, dv_own):
        total[...] = jnp.zeros_like(total)
    for start, rows in row_blocks(q.shape[1]):
        keys = start + rows
        past_bias, own_bias = key_biases(length, offset, start, rows, past, keys)
        here = slice(start, start + rows)
        cos, sin = cosine[0, here], sine[0, here]
        for h in range(heads):
            cols = slice(h * head_dim, (h + 1) * head_dim)
            query, upstream = q[0, here, cols], grad[0, here, cols]
            log_total = lse[0, here, h : h + 1]
            p_past = jnp.exp(dot_cols(query, k_past[0]) * scale + past_bias - log_total)
            p_own = jnp.exp(dot_cols(query, k_own[0, :keys]) * scale + own_bias - log_total)
            g_past = dot_cols(upstream, v_past[0])
            g_own = dot_cols(upstream, v_own[0, :keys])
            row_dot = jnp.sum(p_past * g_past, axis=1, keepdims=True) + jnp.sum(
                p_own * g_own, axis=1, keepdims=True
            )
            s_past = (p_past * (g_past - row_dot)).astype(LOW)
            s_own = (p_own * (g_own - row_dot)).astype(LOW)
            dq = (
                jnp.dot(s_past, k_past[0], preferred_element_type=WIDE)
                + jnp.dot(s_own, k_own[0, :keys], preferred_element_type=WIDE)
            ) * scale
            dq_out[0, here, cols] = turn_back(dq, cos, sin).astype(LOW)
            dk_past[...] += dot_rows(s_past, query)
            dk_own[:keys] += dot_rows(s_own, query)
            dv_past[...] += dot_rows(p_past.astype(LOW), upstream)
            dv_own[:keys] += dot_rows(p_own.astype(LOW), upstream)

    @pl.when(parity == 0)
    def _():
        mine_past[0] = dk_past[...] * scale
        mine_own[0] = dk_own[...] * scale
        other_past[0] = dv_past[...]
        other_own[0] = dv_own[...]

    @pl.when(parity != 0)
    def _():
        mine_past[0] = dv_past[...]
        mine_own[0] = dv_own[...]
        other_past[0] = dk_past[...] * scale
        other_own[0] = dk_own[...] * scale


def attend_backward(
    info, q, k_past, v_past, k_own, v_own, grad, lse, cosine, sine, heads, head_dim, scale
):
    count, length, width = q.shape
    past = k_past.shape[1]
    by_slot = lambda *shape: pl.BlockSpec((1, *shape), lambda s, info: (s,) + (0,) * len(shape))
    keys = count * length * (past + length) * heads
    return pl.pallas_call(
        functools.partial(attend_back_kernel, heads, head_dim, scale),
        grid_spec=pltpu.PrefetchScalarGridSpec(
            num_scalar_prefetch=1,
            grid=(count,),
            in_specs=[
                by_slot(length, width),
                by_slot(past, head_dim),
                by_slot(past, head_dim),
                by_slot(length, head_dim),
                by_slot(length, head_dim),
                by_slot(length, width),
                by_slot(length, 128),
                by_slot(length, head_dim),
                by_slot(length, head_dim),
            ],
            out_specs=[
                by_slot(length, width),
                by_slot(past, head_dim),
                by_slot(length, head_dim),
                by_slot(past, head_dim),
                by_slot(length, head_dim),
            ],
            scratch_shapes=[
                pltpu.VMEM((past, head_dim), WIDE),
                pltpu.VMEM((length, head_dim), WIDE),
                pltpu.VMEM((past, head_dim), WIDE),
                pltpu.VMEM((length, head_dim), WIDE),
            ],
        ),
        out_shape=[
            jax.ShapeDtypeStruct((count, length, width), LOW),
            jax.ShapeDtypeStruct((count, past, head_dim), WIDE),
            jax.ShapeDtypeStruct((count, length, head_dim), WIDE),
            jax.ShapeDtypeStruct((count, past, head_dim), WIDE),
            jax.ShapeDtypeStruct((count, length, head_dim), WIDE),
        ],
        compiler_params=pltpu.CompilerParams(vmem_limit_bytes=56 << 20),
        cost_estimate=pl.CostEstimate(
            flops=10 * keys * head_dim, bytes_accessed=8 * count * length * width, transcendentals=keys
        ),
    )(info, q, k_past, v_past, k_own, v_own, grad, lse, cosine, sine)


def local(
    hidden_in,
    cotangent,
    seq_lengths,
    positions,
    permutation,
    query_weight,
    keyval_weight,
    output_weight,
    norm_gains,
    bias_query,
    bias_keyval,
    gate_weight,
    up_weight,
    down_weight,
):
    group_rank = lax.axis_index("fsdp")
    ctx_rank = lax.axis_index("ctx")
    tensor_rank = lax.axis_index("tp")
    fsdp_count = lax.axis_size("fsdp")
    ctx_count = lax.axis_size("ctx")
    tensor_count = lax.axis_size("tp")
    seq_grp, local_len, model_width = hidden_in.shape
    heads, head_dim = bias_query.shape
    keyval_heads = bias_keyval.shape[0] // 2
    assert seq_grp == tensor_count == fsdp_count == len(DEAL_SHIFT)
    token_count = seq_grp * local_len
    scale = 1.0 / math.sqrt(head_dim)
    offset = ctx_rank * local_len
    head_pair = tensor_rank // (tensor_count // keyval_heads)
    parity = tensor_rank % 2
    shifts = jnp.array(DEAL_SHIFT, jnp.int32)

    table = permutation.reshape(fsdp_count, seq_grp)
    far_group = lax.rem(group_rank + shifts[tensor_rank], fsdp_count)
    far_row = lax.dynamic_index_in_dim(table, far_group, 0, keepdims=False)
    leaving = jnp.sum(jnp.where(far_row // seq_grp == group_rank, far_row - group_rank * seq_grp, 0))
    own_row = lax.dynamic_index_in_dim(table, group_rank, 0, keepdims=False)
    slot_now, seq_now, home_now = [], [], []
    for r in range(seq_grp):
        shift = shifts[tensor_rank ^ r]
        source = lax.rem(group_rank - shift + fsdp_count, fsdp_count)
        hit = own_row // seq_grp == source
        slot_now.append(jnp.sum(jnp.where(hit, jnp.arange(seq_grp), 0)))
        seq_now.append(jnp.sum(jnp.where(hit, own_row, 0)))
        target = lax.rem(group_rank + shift, fsdp_count)
        target_row = lax.dynamic_index_in_dim(table, target, 0, keepdims=False)
        home_now.append(
            jnp.sum(jnp.where(target_row // seq_grp == group_rank, target_row - group_rank * seq_grp, 0))
        )
    there = [
        (f * tensor_count + t, (f + DEAL_SHIFT[t]) % fsdp_count * tensor_count + t)
        for f in range(fsdp_count)
        for t in range(tensor_count)
    ]
    back = [(target, source) for source, target in there]

    outgoing = lax.dynamic_index_in_dim(hidden_in, leaving, 0, keepdims=False)
    own_in = lax.ppermute(outgoing, ("fsdp", "tp"), there)
    head_width = 2 * head_dim
    small = jnp.concatenate(
        [
            query_weight,
            lax.dynamic_slice_in_dim(keyval_weight, head_pair * head_width, head_width, axis=1),
            output_weight.T,
            jnp.pad(norm_gains.T, ((0, 0), (0, 128 - norm_gains.shape[0]))),
        ],
        axis=1,
    )
    small_full = gather_small(small, ctx_rank)
    down_full = gather_large(down_weight.T, ctx_rank)
    gate_full = gather_large(gate_weight, ctx_rank)
    up_full = gather_large(up_weight, ctx_rank)
    query_cols = heads * head_dim
    project_full = small_full[:, : query_cols + head_width]
    output_full = small_full[:, query_cols + head_width : 2 * query_cols + head_width]
    gains_now = small_full[:, 2 * query_cols + head_width :][:, :2].astype(WIDE).T
    own_weight = lax.dynamic_slice_in_dim(
        project_full, query_cols + parity * head_dim, head_dim, axis=1
    )
    back_full = jnp.concatenate([project_full[:, :query_cols], own_weight], axis=1)

    lengths_now = jnp.stack([seq_lengths[s] for s in seq_now])
    info = jnp.concatenate([lengths_now, jnp.stack([offset, parity])]).astype(jnp.int32)
    positions_now = jnp.stack(
        [lax.dynamic_index_in_dim(positions, s, 0, keepdims=False) for s in seq_now]
    )
    lane = jnp.arange(head_dim)
    frequency = 1.0 / ROPE_BASE ** (
        (lane % (head_dim // 2)).astype(WIDE) * 2.0 / head_dim
    )
    angles = positions_now.astype(WIDE)[..., None] * frequency
    cosine = jnp.cos(angles)
    sine = jnp.sin(angles) * jnp.where(lane < head_dim // 2, -1.0, 1.0)
    grad_rows = jnp.concatenate(
        [lax.dynamic_index_in_dim(cotangent, s, 0, keepdims=False) for s in slot_now], axis=0
    )

    bias_head = lax.dynamic_slice_in_dim(bias_keyval, head_pair * 2, 2, axis=0)
    bias_row = jnp.concatenate([bias_query.reshape(1, -1), bias_head.reshape(1, -1)], axis=1).astype(WIDE)
    rows_in = spread_rows(own_in)
    normed_one, query_rot, key_own, value_own = project(
        rows_in, gains_now[0:1], project_full, bias_row, cosine, sine, heads, head_dim
    )
    if ctx_count == 2:
        key_past, value_past = lax.ppermute((key_own, value_own), "ctx", [(0, 1)])
    else:
        key_past = lax.all_gather(key_own, "ctx", axis=1, tiled=True)
        value_past = lax.all_gather(value_own, "ctx", axis=1, tiled=True)
    mixed, lse = attend_forward(
        info, query_rot, key_past, value_past, key_own, value_own, heads, head_dim, scale
    )
    in_share = own_in.astype(WIDE)

    def row_parts(far_part, near_part):
        far_part = far_part.reshape(2, local_len, model_width)
        near_part = near_part.reshape(2, local_len, model_width)
        return (near_part[0], near_part[1], far_part[0], far_part[1])

    def halves(value):
        half = token_count // 2
        return value[half:], value[:half]

    mixed_flat = mixed.reshape(token_count, query_cols)
    attn_parts = row_parts(*[contract_cols(m, output_full, LOW) for m in halves(mixed_flat)])
    middle_share = in_share + collect_rows(attn_parts)
    inv_two = lax.rsqrt(jnp.mean(middle_share * middle_share, axis=-1, keepdims=True) + EPS)
    normed_share = (middle_share * inv_two * gains_now[1]).astype(LOW)
    normed_two = jnp.concatenate(spread_rows(normed_share), axis=0)

    grad_hidden = product(grad_rows, down_full)
    gate_lin = product(normed_two, gate_full)
    up_lin = product(normed_two, up_full)
    gate_sigmoid = jax.nn.sigmoid(gate_lin)
    silu_gate = gate_lin * gate_sigmoid
    hidden_act = (silu_gate * up_lin).astype(LOW)
    grad_gate = (
        grad_hidden * up_lin * gate_sigmoid * (1.0 + gate_lin * (1.0 - gate_sigmoid))
    ).astype(LOW)
    grad_up = (grad_hidden * silu_gate).astype(LOW)
    back_parts = row_parts(
        *[
            (contract_cols(g, gate_full) + contract_cols(u, up_full)).astype(LOW)
            for g, u in zip(halves(grad_gate), halves(grad_up))
        ]
    )
    grad_two_share = collect_rows(back_parts)
    down_grad = scatter_sum(contract_rows(grad_rows, hidden_act, LOW), ctx_rank, LOW)
    gate_grad = scatter_sum(contract_rows(normed_two, grad_gate, LOW), ctx_rank, LOW)
    up_grad = scatter_sum(contract_rows(normed_two, grad_up, LOW), ctx_rank, LOW)
    mlp_parts = row_parts(*[contract_cols(a, down_full, LOW) for a in halves(hidden_act)])
    block_share = (middle_share + collect_rows(mlp_parts)).astype(LOW)

    grad_norm_two, gain_two = norm_backward(middle_share, inv_two, gains_now[1], grad_two_share)
    grad_middle = grad_rows[:local_len].astype(WIDE) + grad_norm_two
    grad_branch = jnp.concatenate(spread_rows(grad_middle.astype(LOW)), axis=0)
    grad_mixed = product(grad_branch, output_full, LOW)
    output_grad = contract_rows(grad_branch, mixed_flat, LOW)

    grad_query, mine_past, mine_own, other_past, other_own = attend_backward(
        info,
        query_rot,
        key_past,
        value_past,
        key_own,
        value_own,
        grad_mixed.reshape(seq_grp, local_len, query_cols),
        lse,
        cosine,
        sine,
        heads,
        head_dim,
        scale,
    )
    swap = lambda value: jnp.stack([value[r ^ 1] for r in range(seq_grp)])
    got_past, got_own = from_partner((other_past, other_own), "tp", 1)
    past_sum = mine_past + swap(got_past)
    own_sum = mine_own + swap(got_own)
    if ctx_count == 2:
        own_sum = own_sum + lax.ppermute(past_sum.astype(LOW), "ctx", [(1, 0)]).astype(WIDE)
    else:
        own_sum = own_sum + lax.psum_scatter(past_sum, "ctx", scatter_dimension=1, tiled=True)
    half_lanes = head_dim // 2
    turned = own_sum * cosine - jnp.roll(own_sum, half_lanes, axis=-1) * sine
    own_grad = jnp.where(parity == 0, turned, own_sum).astype(LOW).reshape(token_count, head_dim)
    line_grad = jnp.concatenate([grad_query.reshape(token_count, query_cols), own_grad], axis=1)
    normed_flat = normed_one.reshape(token_count, model_width)
    line_weight_grad = contract_rows(normed_flat, line_grad, LOW)
    bias_grad = jnp.sum(line_grad.astype(WIDE), axis=0)
    line_parts = row_parts(*[contract_cols(g, back_full, LOW) for g in halves(line_grad)])
    grad_one_share = collect_rows(line_parts)
    inv_one = lax.rsqrt(jnp.mean(in_share * in_share, axis=-1, keepdims=True) + EPS)
    grad_norm_one, gain_one = norm_backward(in_share, inv_one, gains_now[0], grad_one_share)
    input_share = (grad_middle + grad_norm_one).astype(LOW)

    def go_home(share):
        rows = spread_rows(lax.ppermute(share, ("fsdp", "tp"), back))
        out = jnp.zeros((seq_grp, local_len, model_width), LOW)
        for home, row in zip(home_now, rows):
            out = lax.dynamic_update_index_in_dim(out, row, home, 0)
        return out

    block_out = go_home(block_share)
    input_grad = go_home(input_share)

    attn_grad = scatter_sum(jnp.concatenate([line_weight_grad, output_grad], axis=1), ctx_rank, LOW)
    gain_grad = jnp.stack([gain_one, gain_two], axis=1)
    gain_grad = gain_grad + from_partner(gain_grad, "tp", 1)
    gain_grad = gain_grad + from_partner(gain_grad, "tp", 2)
    shards = fsdp_count * ctx_count
    bias_cols = bias_grad.reshape(heads + 1, shards, head_dim // shards)
    bias_cols = jnp.transpose(bias_cols, (1, 2, 0))
    bias_cols = jnp.pad(bias_cols, ((0, 0), (0, (model_width - head_dim) // shards), (0, 0)))
    tiny = jnp.concatenate([gain_grad, bias_cols.reshape(model_width, heads + 1)], axis=1)
    tiny = jnp.pad(tiny, ((0, 0), (0, 8 - tiny.shape[1])))
    tiny_grad = scatter_sum(tiny, ctx_rank, WIDE)
    share = head_dim // shards
    return (
        block_out,
        input_grad,
        attn_grad[:, :query_cols].astype(WIDE),
        attn_grad[:, query_cols : query_cols + head_dim].astype(WIDE),
        attn_grad[:, query_cols + head_dim :].astype(WIDE).T,
        tiny_grad[:, :2].T,
        tiny_grad[:share, 2 : 2 + heads].T,
        tiny_grad[:share, 2 + heads : 3 + heads].T,
        gate_grad.astype(WIDE),
        up_grad.astype(WIDE),
        down_grad.astype(WIDE).T,
    )


def solution(mesh):
    placed = (
        P("fsdp", "ctx", None),
        P("fsdp", "ctx", None),
        P(),
        P(None, "ctx"),
        P(),
        P(("fsdp", "ctx"), "tp"),
        P(("fsdp", "ctx"), None),
        P("tp", ("fsdp", "ctx")),
        P(None, ("fsdp", "ctx")),
        P("tp", None),
        P(),
        P(("fsdp", "ctx"), "tp"),
        P(("fsdp", "ctx"), "tp"),
        P("tp", ("fsdp", "ctx")),
    )
    return jax.shard_map(
        local,
        mesh=mesh,
        in_specs=placed,
        out_specs=(
            P("fsdp", "ctx", None),
            P("fsdp", "ctx", None),
            P(("fsdp", "ctx"), "tp"),
            P(("fsdp", "ctx"), "tp"),
            P("tp", ("fsdp", "ctx")),
            P(None, ("fsdp", "ctx")),
            P("tp", ("fsdp", "ctx")),
            P("tp", ("fsdp", "ctx")),
            P(("fsdp", "ctx"), "tp"),
            P(("fsdp", "ctx"), "tp"),
            P("tp", ("fsdp", "ctx")),
        ),
        check_vma=False,
    )
```

time: 2790 us -> 1170 us (0.42)
  waiting for transfers between devices: 1940 us -> 541 us
  matrix products: 400 us -> 238 us
  blocking collectives: 139 us -> 0 us
  local copies, waits for them, and re-layouts: 187 us -> 112 us
  starting transfers between devices: 20 us -> 81.5 us
  Pallas kernels: 0 us -> 54.9 us
  between operations: 15.4 us -> 43.7 us
    reduce_scatter x18 -> x4, waiting for transfers between devices: 1170 us -> 0.01 us  [scatter_sum(): return lax.psum_scatter(held, 'fsdp', scatter_dimension=0, tiled=True)]
    all_gather x12 -> x4, waiting for transfers between devices: 460 us -> 113 us  [the longest x3 113 us: gather_large(): held = lax.all_gather(shard, 'fsdp', axis=0, tiled=False)]
    ppermute x2 -> x40, waiting for transfers between devices: 0.01 us -> 282 us  [from_partner(): return lax.ppermute(value, axis, pairs)]
    all_to_all x3 -> x0, waiting for transfers between devices: 282 us -> none  [the longest x1 153 us: local(): lax.all_to_all(out_grad, 'fsdp', split_axis=0, concat_axis=0, tiled=True)]
    ppermute x0 -> x6, waiting for transfers between devices: none -> 144 us  [the longest x1 91.7 us: local(): own_in = lax.ppermute(outgoing, ('fsdp', 'tp'), there)]
    all_gather x1 -> x0, blocking collectives: 129 us -> none  [local(): lax.all_gather(norm_gains, ('fsdp', 'ctx'), axis=1, tiled=True)]
    dot_general x20 -> x4, matrix products: 168 us -> 92.3 us  [product(): jnp.dot(left_side, right_side, preferred_element_type=WIDE).astype(kind)]
    dot_general x18 -> x10, matrix products: 135 us -> 76.3 us  [contract_cols(): lax.dot_general(left_side, right_side, (((1,), (1,)), ((), ())), preferre...]
  transfers between devices with their start and end apart: 41 -> 55, of which waited for: 28 -> 22; matrix products, arithmetic and copies ran while one was open for 16% -> 27% of each run, Pallas kernels for 0% -> 5%
where the time goes in v1:
time: 1170 us; the launch traced here: 1160 us
  waiting for transfers between devices  541 us (46%)
  matrix products  238 us (20%)
  local copies, waits for them, and re-layouts  112 us (10%)
  other arithmetic  91.1 us (8%)
  starting transfers between devices  81.5 us (7%)
  Pallas kernels  54.9 us (5%)
  between operations  43.7 us (4%)
    ppermute x40, waiting for transfers between devices, from_partner(): return lax.ppermute(value, axis, pairs)  282 us
    all_gather x3, waiting for transfers between devices, gather_large(): held = lax.all_gather(shard, 'fsdp', axis=0, tiled=False)  113 us
    dot_general x4, matrix products, product(): jnp.dot(left_side, right_side, preferred_element_type=WIDE).astype(kind)  92.3 us
    ppermute x1, waiting for transfers between devices, local(): own_in = lax.ppermute(outgoing, ('fsdp', 'tp'), there)  91.7 us
    dot_general x10, matrix products, contract_cols(): lax.dot_general(left_side, right_side, (((1,), (1,)), ((), ())), preferre...  76.3 us
    dot_general x5, matrix products, contract_rows(): lax.dot_general(left_side, right_side, (((0,), (0,)), ((), ())), preferre...  69.4 us
    ppermute x2, waiting for transfers between devices, go_home(): rows = spread_rows(lax.ppermute(share, ('fsdp', 'tp'), back))  48.2 us
    ppermute x2, starting transfers between devices, go_home(): rows = spread_rows(lax.ppermute(share, ('fsdp', 'tp'), back))  36.9 us
  transfers between devices with their start and end apart: 55, of which 22 were waited for; matrix products, arithmetic and copies ran while one was open for 27% of the time, Pallas kernels for 5%

profile of v1, /device:TPU:1, one launch (start us, length us, event | category | flops | bytes accessed | tf_op | source)
XLA Modules:
  0.0 1162.0 jit_solution(5053573085845254321)
XLA Ops:
  36.7 91.7 %collective-permute-done.x0 = bf16[512,1536]{1,0:T(8,128)(2,1)S(1)} collective-permute-done((bf16[512,1536]{1,0:T(8,128)(2,1)S(1)}, bf16[512,1536]{1,0:T(8,128)(2,1)S(1)}, u32[]{:S(2)}, u32[]{:S(2)}) %collective-permute-start) | collective-permute-done | bytes 1572896 | tf_op jit(solution)/shard_map/ppermute | solution.py:424
  181.0 18.1 %all-gather.11.cloned.1.call-done = bf16[768,2240]{1,0:T(8,128)(2,1)} async-done(((bf16[192,2240]{1,0:T(8,128)(2,1)}), bf16[768,2240]{1,0:T(8,128)(2,1)}) %all-gather.11.cloned.1.call-update) | async-done | bytes 3440656 | tf_op jit(solution)/shard_map/all_gather | solution.py:79
  200.3 69.0 %all-gather.13.cloned.1.call-done = bf16[768,2240]{1,0:T(8,128)(2,1)} async-done(((bf16[192,2240]{1,0:T(8,128)(2,1)}), bf16[768,2240]{1,0:T(8,128)(2,1)}) %all-gather.13.cloned.1.call-update) | async-done | bytes 3440656 | tf_op jit(solution)/shard_map/all_gather | solution.py:79
  275.4 16.8 %shard_map.231 = (bf16[4,512,384]{2,1,0:T(8,128)(2,1)}, f32[4,512,128]{2,1,0:T(8,128)}) custom-call(s32[6]{0:T(128)} %concatenate.50.info, bf16[4,512,384]{2,1,0:T(8,128)(2,1)} %get-tuple-element.22.q, bf16[4,512,128]{2,1,0:T(8,128)(2,1)} %copy-done.51, bf16[4,512,128]{2,1,0:T(8,128)(2,1)} %copy-done.52, bf16[4,512,128]{2,1,0:T(8,128)(2,1)} %get-tuple-element.23.k_own, ...), custom_call_target="tpu_custom_call" | custom-call | flops 3221225472 | bytes 3145728 | tf_op jit(solution)/shard_map/pallas_call | solution.py:217
  313.3 26.0 %all-gather.15.cloned.1.call-done = bf16[768,2240]{1,0:T(8,128)(2,1)} async-done(((bf16[192,2240]{1,0:T(8,128)(2,1)}), bf16[768,2240]{1,0:T(8,128)(2,1)}) %all-gather.15.cloned.1.call-update) | async-done | bytes 3440656 | tf_op jit(solution)/shard_map/all_gather | solution.py:79
  370.7 14.8 %collective-permute-done.9 = bf16[512,1536]{1,0:T(8,128)(2,1)} collective-permute-done((bf16[512,1536]{1,0:T(8,128)(2,1)}, bf16[512,1536]{1,0:T(8,128)(2,1)}, u32[]{:S(2)}, u32[]{:S(2)}) %collective-permute-start.9) | collective-permute-done | bytes 1572896 | tf_op jit(solution)/shard_map/ppermute | solution.py:21
  392.5 36.4 %collective-permute-done.15 = bf16[4,192,2240]{2,1,0:T(8,128)(2,1)} collective-permute-done((bf16[4,192,2240]{2,1,0:T(8,128)(2,1)}, bf16[4,192,2240]{2,1,0:T(8,128)(2,1)}, u32[]{:S(2)}, u32[]{:S(2)}) %collective-permute-start.15) | collective-permute-done | bytes 3440672 | tf_op jit(solution)/shard_map/ppermute | solution.py:21
  436.4 22.6 %fusion.35 = f32[2048,2240]{0,1:T(8,128)} fusion(bf16[1536,2240]{1,0:T(8,128)(2,1)} %bitcast.182, bf16[512,1536]{1,0:T(8,128)(2,1)} %get-tuple-element.72, bf16[512,1536]{1,0:T(8,128)(2,1)} %get-tuple-element.73, bf16[512,1536]{1,0:T(8,128)(2,1)} %get-tuple-element.71, bf16[512,1536]{1,0:T(8,128)(2,1)S(1)} %copy-done.11), kind=kOutput, calls=%fused_computation.104 | convolution fusion | flops 14118027264 | bytes 31522816 | tf_op jit(solution)/shard_map/dot_general | solution.py:25
  459.0 23.1 %fusion.81 = f32[2048,2240]{0,1:T(8,128)} fusion(bf16[1536,2240]{1,0:T(8,128)(2,1)} %bitcast.185, bf16[512,1536]{1,0:T(8,128)(2,1)} %collective-permute-done.12, bf16[512,1536]{1,0:T(8,128)(2,1)} %collective-permute-done.11, bf16[512,1536]{1,0:T(8,128)(2,1)} %collective-permute-done.10, bf16[512,1536]{1,0:T(8,128)(2,1)} %copy-done.28), kind=kOutput, calls=%fused_computation.224 | convolution fusion | flops 14118027264 | bytes 31522816 | tf_op jit(solution)/shard_map/dot_general | solution.py:25
  482.1 38.8 %multiply_convert_fusion.1 = (bf16[2048,2240]{0,1:T(8,128)(2,1)}, bf16[2048,2240]{0,1:T(8,128)(2,1)}, bf16[2048,2240]{0,1:T(8,128)(2,1)}) fusion(f32[2048,2240]{0,1:T(8,128)} %fusion.35, f32[2048,2240]{0,1:T(8,128)} %fusion.81, bf16[1536,2240]{1,0:T(8,128)(2,1)} %bitcast.177, bf16[512,1536]{1,0:T(8,128)(2,1)} %collective-permute-done.12, ...), kind=kOutput, calls=%fused_computation.1 | convolution fusion | flops 14186840064 | bytes 77398016 | tf_op jit(solution)/shard_map/dot_general | solution.py:25
  542.0 18.5 %convolution_convert_fusion.1 = bf16[1536,2240]{0,1:T(8,128)(2,1)} fusion(bf16[2048,2240]{0,1:T(8,128)(2,1)S(1)} %copy-done.54, bf16[512,1536]{1,0:T(8,128)(2,1)} %collective-permute-done.12, bf16[512,1536]{1,0:T(8,128)(2,1)} %collective-permute-done.11, bf16[512,1536]{1,0:T(8,128)(2,1)} %collective-permute-done.10, bf16[512,1536]{1,0:T(8,128)(2,1)S(1)} %copy-done.29), kind=kOutput, calls=%fused_computation.6 | convolution fusion | flops 14121467904 | bytes 22347776 | tf_op jit(solution)/shard_map/dot_general | solution.py:29
  612.2 21.7 %convolution_convert_fusion.2 = bf16[1536,2240]{0,1:T(8,128)(2,1)} fusion(bf16[2048,2240]{0,1:T(8,128)(2,1)} %get-tuple-element.61, bf16[512,1536]{1,0:T(8,128)(2,1)} %collective-permute-done.12, bf16[512,1536]{1,0:T(8,128)(2,1)} %collective-permute-done.11, bf16[512,1536]{1,0:T(8,128)(2,1)} %collective-permute-done.10, bf16[512,1536]{1,0:T(8,128)(2,1)} %copy-done.28), kind=kOutput, calls=%fused_computation.7 | convolution fusion | flops 14121467904 | bytes 22347776 | tf_op jit(solution)/shard_map/dot_general | solution.py:29
  633.9 17.9 %collective-permute-done.44 = bf16[4,192,2240]{2,1,0:T(8,128)(2,1)S(1)} collective-permute-done((bf16[4,192,2240]{2,1,0:T(8,128)(2,1)S(1)}, bf16[4,192,2240]{2,1,0:T(8,128)(2,1)S(1)}, u32[]{:S(2)}, u32[]{:S(2)}) %collective-permute-start.44) | collective-permute-done | bytes 3440672 | tf_op jit(solution)/shard_map/ppermute | solution.py:21
  688.5 29.1 %collective-permute-done.25 = bf16[512,1536]{1,0:T(8,128)(2,1)S(1)} collective-permute-done((bf16[512,1536]{1,0:T(8,128)(2,1)S(1)}, bf16[512,1536]{1,0:T(8,128)(2,1)S(1)}, u32[]{:S(2)}, u32[]{:S(2)}) %collective-permute-start.25) | collective-permute-done | bytes 1572896 | tf_op jit(solution)/shard_map/ppermute | solution.py:21
  719.0 32.3 %collective-permute-done.18 = bf16[512,1536]{1,0:T(8,128)(2,1)S(1)} collective-permute-done((bf16[512,1536]{1,0:T(8,128)(2,1)}, bf16[512,1536]{1,0:T(8,128)(2,1)S(1)}, u32[]{:S(2)}, u32[]{:S(2)}) %collective-permute-start.18) | collective-permute-done | bytes 1572896 | tf_op jit(solution)/shard_map/ppermute | solution.py:21
  762.4 29.8 %collective-permute-done.27 = bf16[512,1536]{1,0:T(8,128)(2,1)} collective-permute-done((bf16[512,1536]{1,0:T(8,128)(2,1)}, bf16[512,1536]{1,0:T(8,128)(2,1)}, u32[]{:S(2)}, u32[]{:S(2)}) %collective-permute-start.27) | collective-permute-done | bytes 1572896 | tf_op jit(solution)/shard_map/ppermute | solution.py:21
  793.6 20.5 %convolution_convert_fusion = bf16[1536,2240]{0,1:T(8,128)(2,1)} fusion(bf16[2048,2240]{0,1:T(8,128)(2,1)} %get-tuple-element.63, bf16[512,1536]{1,0:T(8,128)(2,1)} %get-tuple-element.72, bf16[512,1536]{1,0:T(8,128)(2,1)} %get-tuple-element.73, bf16[512,1536]{1,0:T(8,128)(2,1)S(1)} %copy-done.30, bf16[512,1536]{1,0:T(8,128)(2,1)S(1)} %copy-done.13), kind=kOutput, calls=%fused_computation.5 | convolution fusion | flops 14121467904 | bytes 22347776 | tf_op jit(solution)/shard_map/dot_general | solution.py:29
  837.5 25.8 %shard_map.232 = (bf16[4,512,384]{2,1,0:T(8,128)(2,1)}, f32[4,512,128]{2,1,0:T(8,128)}, f32[4,512,128]{2,1,0:T(8,128)}, f32[4,512,128]{2,1,0:T(8,128)}, f32[4,512,128]{2,1,0:T(8,128)}) custom-call(s32[6]{0:T(128)} %concatenate.50.info, bf16[4,512,384]{2,1,0:T(8,128)(2,1)} %get-tuple-element.22.q, bf16[4,512,128]{2,1,0:T(8,128)(2,1)} %copy-done.51, ...), custom_call_target="tpu_custom_call" | custom-call | flops 8053063680 | bytes 6291456 | tf_op jit(solution)/shard_map/pallas_call | solution.py:322
  867.3 18.0 %collective-permute-start.19 = (bf16[512,1536]{1,0:T(8,128)(2,1)S(1)}, bf16[512,1536]{1,0:T(8,128)(2,1)}, u32[]{:S(2)}, u32[]{:S(2)}) collective-permute-start(bf16[512,1536]{1,0:T(8,128)(2,1)S(1)} %copy-done.31), channel_id=1, source_target_pairs={{0,0},{17,1},{10,2},{27,3},{8,8},{25,9},{18,10},{3,11},{16,16},{1,... | collective-permute-start | bytes 4718600 | tf_op jit(solution)/shard_map/ppermute | solution.py:562
  888.0 18.5 %collective-permute-done.45 = bf16[4,192,2240]{2,1,0:T(8,128)(2,1)} collective-permute-done((bf16[4,192,2240]{2,1,0:T(8,128)(2,1)}, bf16[4,192,2240]{2,1,0:T(8,128)(2,1)}, u32[]{:S(2)}, u32[]{:S(2)}) %collective-permute-start.45) | collective-permute-done | bytes 3440672 | tf_op jit(solution)/shard_map/ppermute | solution.py:21
  950.2 47.2 %collective-permute-done.34 = bf16[512,1536]{1,0:T(8,128)(2,1)} collective-permute-done((bf16[512,1536]{1,0:T(8,128)(2,1)}, bf16[512,1536]{1,0:T(8,128)(2,1)}, u32[]{:S(2)}, u32[]{:S(2)}) %collective-permute-start.34) | collective-permute-done | bytes 1572896 | tf_op jit(solution)/shard_map/ppermute | solution.py:21
  1015.8 20.5 %collective-permute-done.42 = f32[4,192,8]{1,0,2:T(4,128)S(1)} collective-permute-done((f32[4,192,8]{1,0,2:T(4,128)S(1)}, f32[4,192,8]{1,0,2:T(4,128)S(1)}, u32[]{:S(2)}, u32[]{:S(2)}) %collective-permute-start.42) | collective-permute-done | bytes 24608 | tf_op jit(solution)/shard_map/ppermute | solution.py:21
  1044.1 18.9 %collective-permute-start.35 = (bf16[512,1536]{1,0:T(8,128)(2,1)S(1)}, bf16[512,1536]{1,0:T(8,128)(2,1)S(1)}, u32[]{:S(2)}, u32[]{:S(2)}) collective-permute-start(bf16[512,1536]{1,0:T(8,128)(2,1)S(1)} %fusion.30), channel_id=1, source_target_pairs={{0,0},{17,1},{10,2},{27,3},{8,8},{25,9},{18,10},{3,11},{16,16},{1,... | collective-permute-start | bytes 4718600 | tf_op jit(solution)/shard_map/ppermute | solution.py:562
  1074.2 48.2 %collective-permute-done.35 = bf16[512,1536]{1,0:T(8,128)(2,1)S(1)} collective-permute-done((bf16[512,1536]{1,0:T(8,128)(2,1)S(1)}, bf16[512,1536]{1,0:T(8,128)(2,1)S(1)}, u32[]{:S(2)}, u32[]{:S(2)}) %collective-permute-start.35) | collective-permute-done | bytes 1572896 | tf_op jit(solution)/shard_map/ppermute | solution.py:562
  (358 shorter events, 394.2 us)
Async XLA Ops:
  7.2 150.5 %all-gather.9.cloned.1.call-start = ((), (), s32[]{:S(2)}) async-start(), calls=%async_computation.9 | async-start | bytes 4423680 | tf_op jit(solution)/shard_map/all_gather | solution.py:72
  23.4 175.7 %all-gather.11.cloned.1.call-start = ((), (), s32[]{:S(2)}) async-start(), calls=%async_computation.10 | async-start | bytes 4423680 | tf_op jit(solution)/shard_map/all_gather | solution.py:79
  24.2 245.1 %all-gather.13.cloned.1.call-start = ((), (), s32[]{:S(2)}) async-start(), calls=%async_computation.11 | async-start | bytes 4423680 | tf_op jit(solution)/shard_map/all_gather | solution.py:79
  24.9 314.4 %all-gather.15.cloned.1.call-start = ((), (), s32[]{:S(2)}) async-start(), calls=%async_computation.12 | async-start | bytes 4423680 | tf_op jit(solution)/shard_map/all_gather | solution.py:79
  32.6 95.8 %collective-permute-start = (bf16[512,1536]{1,0:T(8,128)(2,1)S(1)}, bf16[512,1536]{1,0:T(8,128)(2,1)S(1)}, u32[]{:S(2)}, u32[]{:S(2)}) collective-permute-start(bf16[512,1536]{1,0:T(8,128)(2,1)S(1)} %dynamic-slice_bitcast_fusion.7), channel_id=1, source_target_pairs={{0,0},{1,17},{2,10},{3,27},{8,8},{9,25},{10,18},{11,3},{16,16},{17... | collective-permute-start | bytes 4718600 | tf_op jit(solution)/shard_map/ppermute | solution.py:424
  128.6 996.5 %reduce-scatter.12.cloned.1.call-start = ((), (), s32[]{:S(2)}) async-start(), calls=%async_computation.7 | async-start | bytes 4423680 | tf_op jit(solution)/shard_map/reduce_scatter | solution.py:97
  176.1 98.4 %collective-permute-start.5 = (bf16[4,512,128]{2,1,0:T(8,128)(2,1)}, bf16[4,512,128]{2,1,0:T(8,128)(2,1)S(1)}, u32[]{:S(2)}, u32[]{:S(2)}) collective-permute-start(bf16[4,512,128]{2,1,0:T(8,128)(2,1)} %get-tuple-element.23.k_own), channel_id=1, source_target_pairs={{0,4},{1,5},{2,6},{3,7},{8,12},{9,13},{10,14},{11,15},{16,20},{17,... | collective-permute-start | bytes 1572872 | tf_op jit(solution)/shard_map/ppermute | solution.py:471
  179.1 95.3 %collective-permute-start.6 = (bf16[4,512,128]{2,1,0:T(8,128)(2,1)}, bf16[4,512,128]{2,1,0:T(8,128)(2,1)S(1)}, u32[]{:S(2)}, u32[]{:S(2)}) collective-permute-start(bf16[4,512,128]{2,1,0:T(8,128)(2,1)} %get-tuple-element.24.v_own), channel_id=1, source_target_pairs={{0,4},{1,5},{2,6},{3,7},{8,12},{9,13},{10,14},{11,15},{16,20},{17,... | collective-permute-start | bytes 1572872 | tf_op jit(solution)/shard_map/ppermute | solution.py:471
  199.1 152.1 %collective-permute-start.13 = (bf16[4,192,2240]{2,1,0:T(8,128)(2,1)}, bf16[4,192,2240]{2,1,0:T(8,128)(2,1)}, u32[]{:S(2)}, u32[]{:S(2)}) collective-permute-start(bf16[4,192,2240]{2,1,0:T(8,128)(2,1)} %bitcast.199), channel_id=1, source_target_pairs={{0,4},{4,0},{1,5},{5,1},{2,6},{6,2},{3,7},{7,3},{8,12},{12,8},{9,1... | collective-permute-start | bytes 10321928 | tf_op jit(solution)/shard_map/ppermute | solution.py:21
  269.3 83.8 %collective-permute-start.14 = (bf16[4,192,2240]{2,1,0:T(8,128)(2,1)}, bf16[4,192,2240]{2,1,0:T(8,128)(2,1)}, u32[]{:S(2)}, u32[]{:S(2)}) collective-permute-start(bf16[4,192,2240]{2,1,0:T(8,128)(2,1)} %bitcast.201), channel_id=1, source_target_pairs={{0,4},{4,0},{1,5},{5,1},{2,6},{6,2},{3,7},{7,3},{8,12},{12,8},{9,1... | collective-permute-start | bytes 10321928 | tf_op jit(solution)/shard_map/ppermute | solution.py:21
  339.3 89.6 %collective-permute-start.15 = (bf16[4,192,2240]{2,1,0:T(8,128)(2,1)}, bf16[4,192,2240]{2,1,0:T(8,128)(2,1)}, u32[]{:S(2)}, u32[]{:S(2)}) collective-permute-start(bf16[4,192,2240]{2,1,0:T(8,128)(2,1)} %bitcast.191), channel_id=1, source_target_pairs={{0,4},{4,0},{1,5},{5,1},{2,6},{6,2},{3,7},{7,3},{8,12},{12,8},{9,1... | collective-permute-start | bytes 10321928 | tf_op jit(solution)/shard_map/ppermute | solution.py:21
  573.0 78.8 %collective-permute-start.44 = (bf16[4,192,2240]{2,1,0:T(8,128)(2,1)S(1)}, bf16[4,192,2240]{2,1,0:T(8,128)(2,1)S(1)}, u32[]{:S(2)}, u32[]{:S(2)}) collective-permute-start(bf16[4,192,2240]{2,1,0:T(8,128)(2,1)S(1)} %dynamic-slice_bitcast_fusion.1), channel_id=1, source_target_pairs={{0,4},{4,0},{1,5},{5,1},{2,6},{6,2},{3,7},{7,3},{8,12},{12,8},{9,1... | collective-permute-start | bytes 10321928 | tf_op jit(solution)/shard_map/ppermute | solution.py:21
  588.5 95.9 %collective-permute-start.17 = (bf16[512,1536]{1,0:T(8,128)(2,1)}, bf16[512,1536]{1,0:T(8,128)(2,1)}, u32[]{:S(2)}, u32[]{:S(2)}) collective-permute-start(bf16[512,1536]{1,0:T(8,128)(2,1)} %slice.237), channel_id=1, source_target_pairs={{0,1},{1,0},{2,3},{3,2},{4,5},{5,4},{6,7},{7,6},{8,9},{9,8},{10,11... | collective-permute-start | bytes 4718600 | tf_op jit(solution)/shard_map/ppermute | solution.py:21
  611.5 66.9 %collective-permute-start.24 = (bf16[512,1536]{1,0:T(8,128)(2,1)}, bf16[512,1536]{1,0:T(8,128)(2,1)}, u32[]{:S(2)}, u32[]{:S(2)}) collective-permute-start(bf16[512,1536]{1,0:T(8,128)(2,1)} %slice.245), channel_id=1, source_target_pairs={{0,1},{1,0},{2,3},{3,2},{4,5},{5,4},{6,7},{7,6},{8,9},{9,8},{10,11... | collective-permute-start | bytes 4718600 | tf_op jit(solution)/shard_map/ppermute | solution.py:21
  654.6 473.0 %reduce-scatter.10.cloned.1.call-start = ((), (), s32[]{:S(2)}) async-start(), calls=%async_computation.6 | async-start | bytes 4423680 | tf_op jit(solution)/shard_map/reduce_scatter | solution.py:97
  682.0 77.7 %collective-permute-start.43 = (bf16[4,192,2240]{2,1,0:T(8,128)(2,1)S(1)}, bf16[4,192,2240]{2,1,0:T(8,128)(2,1)S(1)}, u32[]{:S(2)}, u32[]{:S(2)}) collective-permute-start(bf16[4,192,2240]{2,1,0:T(8,128)(2,1)S(1)} %dynamic-slice_bitcast_fusion.2), channel_id=1, source_target_pairs={{0,4},{4,0},{1,5},{5,1},{2,6},{6,2},{3,7},{7,3},{8,12},{12,8},{9,1... | collective-permute-start | bytes 10321928 | tf_op jit(solution)/shard_map/ppermute | solution.py:21
  757.0 72.7 %collective-permute-start.26 = (bf16[512,1536]{1,0:T(8,128)(2,1)}, bf16[512,1536]{1,0:T(8,128)(2,1)}, u32[]{:S(2)}, u32[]{:S(2)}) collective-permute-start(bf16[512,1536]{1,0:T(8,128)(2,1)} %get-tuple-element.55), channel_id=1, source_target_pairs={{0,1},{1,0},{2,3},{3,2},{4,5},{5,4},{6,7},{7,6},{8,9},{9,8},{10,11... | collective-permute-start | bytes 4718600 | tf_op jit(solution)/shard_map/ppermute | solution.py:21
  762.4 367.7 %reduce-scatter.14.cloned.1.call-start = ((), (), s32[]{:S(2)}) async-start(), calls=%async_computation.8 | async-start | bytes 4423680 | tf_op jit(solution)/shard_map/reduce_scatter | solution.py:97
  828.3 78.3 %collective-permute-start.45 = (bf16[4,192,2240]{2,1,0:T(8,128)(2,1)}, bf16[4,192,2240]{2,1,0:T(8,128)(2,1)}, u32[]{:S(2)}, u32[]{:S(2)}) collective-permute-start(bf16[4,192,2240]{2,1,0:T(8,128)(2,1)} %dynamic-slice_bitcast_fusion), channel_id=1, source_target_pairs={{0,4},{4,0},{1,5},{5,1},{2,6},{6,2},{3,7},{7,3},{8,12},{12,8},{9,1... | collective-permute-start | bytes 10321928 | tf_op jit(solution)/shard_map/ppermute | solution.py:21
  912.3 220.3 %reduce-scatter.16.cloned.1.call-start = ((), (), s32[]{:S(2)}) async-start(), calls=%async_computation.13 | async-start | bytes 491520
  927.8 87.9 %collective-permute-start.21 = (bf16[512,1536]{1,0:T(8,128)(2,1)}, bf16[512,1536]{1,0:T(8,128)(2,1)}, u32[]{:S(2)}, u32[]{:S(2)}) collective-permute-start(bf16[512,1536]{1,0:T(8,128)(2,1)} %collective-permute-done.19), channel_id=1, source_target_pairs={{0,2},{1,3},{2,0},{3,1},{4,6},{5,7},{6,4},{7,5},{8,10},{9,11},{10,... | collective-permute-start | bytes 4718600 | tf_op jit(solution)/shard_map/ppermute | solution.py:21
  1015.7 106.7 %collective-permute-start.22 = (bf16[512,1536]{1,0:T(8,128)(2,1)}, bf16[512,1536]{1,0:T(8,128)(2,1)}, u32[]{:S(2)}, u32[]{:S(2)}) collective-permute-start(bf16[512,1536]{1,0:T(8,128)(2,1)} %collective-permute-done.21), channel_id=1, source_target_pairs={{0,1},{1,0},{2,3},{3,2},{4,5},{5,4},{6,7},{7,6},{8,9},{9,8},{10,11... | collective-permute-start | bytes 4718600 | tf_op jit(solution)/shard_map/ppermute | solution.py:21
  1037.2 99.7 %reduce-scatter.8.cloned.1.call-start = ((), (), s32[]{:S(2)}) async-start(), calls=%async_computation.5 | async-start | bytes 1720320 | tf_op jit(solution)/shard_map/reduce_scatter | solution.py:97
  1044.1 78.4 %collective-permute-start.35 = (bf16[512,1536]{1,0:T(8,128)(2,1)S(1)}, bf16[512,1536]{1,0:T(8,128)(2,1)S(1)}, u32[]{:S(2)}, u32[]{:S(2)}) collective-permute-start(bf16[512,1536]{1,0:T(8,128)(2,1)S(1)} %fusion.30), channel_id=1, source_target_pairs={{0,0},{17,1},{10,2},{27,3},{8,8},{25,9},{18,10},{3,11},{16,16},{1,... | collective-permute-start | bytes 4718600 | tf_op jit(solution)/shard_map/ppermute | solution.py:562
  (94 other events, 2551.4 us)
Sparse Core Ops, SparseCore 0:
  23.5 102.7 all-gather.8
  127.9 71.1 all-gather.10
  200.6 68.5 all-gather.12
  270.7 68.5 all-gather.14
  654.7 81.6 reduce-scatter.11
  762.5 82.8 reduce-scatter.9
  912.4 82.0 reduce-scatter.13
  1037.3 34.5 reduce-scatter.15
  1074.9 50.0 reduce-scatter.7

commit v2 on v1

--- a/solution.py
+++ b/solution.py
@@ -45,56 +45,146 @@
     return (grad_in, gain_grad)
 
 
-def spread_rows(own):
-    far = from_partner(own, "tp", 2)
-    near = from_partner(own, "tp", 1)
-    cross = from_partner(far, "tp", 1)
-    return (own, near, far, cross)
-
-
-def collect_rows(parts):
-    wide = parts[2].astype(WIDE) + from_partner(parts[3], "tp", 1).astype(WIDE)
-    far = from_partner(wide.astype(LOW), "tp", 2)
-    near = from_partner(parts[1], "tp", 1)
-    return parts[0].astype(WIDE) + near.astype(WIDE) + far.astype(WIDE)
-
-
-def interleave(own, other, ctx_rank):
-    first = jnp.where(ctx_rank == 0, own, other)
-    second = jnp.where(ctx_rank == 0, other, own)
-    return (first, second)
-
-
-def gather_small(shard, ctx_rank):
-    if lax.axis_size("ctx") != 2:
-        return lax.all_gather(shard, ("fsdp", "ctx"), axis=0, tiled=True)
-    both = jnp.stack(interleave(shard, from_partner(shard, "ctx", 1), ctx_rank), axis=0)
-    full = lax.all_gather(both, "fsdp", axis=0, tiled=False)
-    return full.reshape(-1, shard.shape[1])
-
-
-def gather_large(shard, ctx_rank):
-    if lax.axis_size("ctx") != 2:
-        return lax.all_gather(shard, ("fsdp", "ctx"), axis=0, tiled=True)
-    held = lax.all_gather(shard, "fsdp", axis=0, tiled=False)
-    other = from_partner(held, "ctx", 1)
-    return jnp.stack(interleave(held, other, ctx_rank), axis=1).reshape(-1, shard.shape[1])
-
-
-def scatter_sum(grad, ctx_rank, kind):
+def after(value, *earlier):
+    return lax.optimization_barrier((value, *earlier))[0]
+
+
+def collect_far(far_part, cross_part):
+    wide = far_part.astype(WIDE) + from_partner(cross_part, "tp", 1).astype(WIDE)
+    return wide.astype(LOW)
+
+
+def units_split():
+    return lax.axis_size("ctx") == 2
+
+
+def all_rows(shard):
+    return lax.all_gather(shard, "fsdp", axis=0, tiled=True)
+
+
+def scatter_ctx(blocks, ctx_rank):
+    kept = lax.dynamic_index_in_dim(blocks, ctx_rank, 1, keepdims=False)
+    sent = lax.dynamic_index_in_dim(blocks, 1 - ctx_rank, 1, keepdims=False)
+    return kept, sent
+
+
+def scatter_sum(grad, ctx_rank, kind, *earlier):
     fsdp_count, ctx_count = lax.axis_size("fsdp"), lax.axis_size("ctx")
     rows, cols = grad.shape
     blocks = grad.reshape(fsdp_count, ctx_count, rows // (fsdp_count * ctx_count), cols)
     if ctx_count == 2:
-        kept = lax.dynamic_index_in_dim(blocks, ctx_rank, 1, keepdims=False)
-        sent = lax.dynamic_index_in_dim(blocks, 1 - ctx_rank, 1, keepdims=False)
+        kept, sent = scatter_ctx(blocks, ctx_rank)
         got = from_partner(sent, "ctx", 1)
-        held = (kept.astype(WIDE) + got.astype(WIDE)).astype(kind)
+        held = (after(kept, *earlier).astype(WIDE) + got.astype(WIDE)).astype(kind)
     else:
         swapped = jnp.swapaxes(blocks, 0, 1).reshape(rows, cols)
         held = lax.psum_scatter(swapped, "ctx", scatter_dimension=0, tiled=True)
     held = held.reshape(rows // ctx_count, cols)
     return lax.psum_scatter(held, "fsdp", scatter_dimension=0, tiled=True)
+
+
+def whole_spec(*shape, once=False):
+    mode = {"pipeline_mode": pl.Buffered(1)} if once else {}
+    return pl.BlockSpec(shape, lambda *_: (0,) * len(shape), **mode)
+
+
+def gate_kernel(count, *refs):
+    slot = pl.program_id(0)
+    weight, lin, stacked = refs[count:]
+
+    def run(x):
+        value = x[...]
+        stacked[...] = value
+        lin[...] = jnp.dot(value, weight[...], preferred_element_type=WIDE).astype(LOW)
+
+    for r in range(count):
+        pl.when(slot == r)(functools.partial(run, refs[r]))
+
+
+def gate_rows(rows, weight):
+    length, width = rows[0].shape
+    count, cols = len(rows), weight.shape[1]
+    return pl.pallas_call(
+        functools.partial(gate_kernel, count),
+        grid=(count,),
+        in_specs=[whole_spec(length, width, once=True)] * count
+        + [whole_spec(width, cols, once=True)],
+        out_specs=[
+            pl.BlockSpec((length, cols), lambda s: (s, 0)),
+            pl.BlockSpec((length, width), lambda s: (s, 0)),
+        ],
+        out_shape=[
+            jax.ShapeDtypeStruct((count * length, cols), LOW),
+            jax.ShapeDtypeStruct((count * length, width), LOW),
+        ],
+        compiler_params=pltpu.CompilerParams(vmem_limit_bytes=60 << 20),
+        cost_estimate=pl.CostEstimate(
+            flops=2 * count * length * width * cols,
+            bytes_accessed=2 * (count * length * (2 * width + cols) + width * cols),
+            transcendentals=0,
+        ),
+    )(*rows, weight)
+
+
+def units_kernel(h, up, gate, grad, hid, grad_gate, grad_up):
+    up_lin = jnp.dot(h[...], up[...], preferred_element_type=WIDE)
+    gate_lin = gate[...].astype(WIDE)
+    grad_hidden = grad[...].astype(WIDE)
+    sigmoid = 1.0 / (1.0 + jnp.exp(-gate_lin))
+    silu = gate_lin * sigmoid
+    hid[...] = (silu * up_lin).astype(LOW)
+    grad_gate[...] = (grad_hidden * up_lin * sigmoid * (1.0 + gate_lin * (1.0 - sigmoid))).astype(LOW)
+    grad_up[...] = (grad_hidden * silu).astype(LOW)
+
+
+def hidden_units(h, up, gate_lin, grad_hidden):
+    tokens, width = h.shape
+    cols = up.shape[1]
+    step = math.gcd(512, tokens)
+    by_row = lambda n: pl.BlockSpec((step, n), lambda i: (i, 0))
+    return pl.pallas_call(
+        units_kernel,
+        grid=(tokens // step,),
+        in_specs=[by_row(width), whole_spec(width, cols, once=True), by_row(cols), by_row(cols)],
+        out_specs=[by_row(cols)] * 3,
+        out_shape=[jax.ShapeDtypeStruct((tokens, cols), LOW)] * 3,
+        compiler_params=pltpu.CompilerParams(vmem_limit_bytes=60 << 20),
+        cost_estimate=pl.CostEstimate(
+            flops=2 * tokens * width * cols,
+            bytes_accessed=2 * (tokens * width + width * cols + 5 * tokens * cols),
+            transcendentals=tokens * cols,
+        ),
+    )(h, up, gate_lin, grad_hidden)
+
+
+def back_kernel(terms, *refs):
+    lefts, weights, out = refs[:terms], refs[terms:-1], refs[-1]
+    total = None
+    for left, weight in zip(lefts, weights):
+        term = dot_cols(left[...], weight[...])
+        total = term if total is None else total + term
+    out[0] = total.astype(LOW)
+
+
+def back_rows(lefts, weights, first_slot, slots, length):
+    width = weights[0].shape[0]
+    depth = sum(left.shape[1] for left in lefts)
+    return pl.pallas_call(
+        functools.partial(back_kernel, len(lefts)),
+        grid=(slots,),
+        in_specs=[
+            pl.BlockSpec((length, left.shape[1]), lambda s: (first_slot + s, 0)) for left in lefts
+        ]
+        + [whole_spec(*w.shape, once=True) for w in weights],
+        out_specs=pl.BlockSpec((1, length, width), lambda s: (s, 0, 0)),
+        out_shape=jax.ShapeDtypeStruct((slots, length, width), LOW),
+        compiler_params=pltpu.CompilerParams(vmem_limit_bytes=60 << 20),
+        cost_estimate=pl.CostEstimate(
+            flops=2 * slots * length * width * depth,
+            bytes_accessed=2 * (slots * length * (width + depth) + width * depth),
+            transcendentals=0,
+        ),
+    )(*lefts, *weights)
 
 
 def turn(values, cosine, sine_signed):
@@ -133,7 +223,7 @@
     length, width = rows[0].shape
     count = len(rows)
     cols = (heads + 2) * head_dim
-    whole = lambda *shape: pl.BlockSpec(shape, lambda s: (0,) * len(shape))
+    whole = whole_spec
     by_slot = lambda *shape: pl.BlockSpec((1, *shape), lambda s: (s,) + (0,) * len(shape))
     return pl.pallas_call(
         functools.partial(project_kernel, heads, head_dim),
@@ -183,9 +273,8 @@
     return lax.dot_general(left, right, (((0,), (0,)), ((), ())), preferred_element_type=WIDE)
 
 
-def attend_kernel(heads, head_dim, scale, info, q, k_past, v_past, k_own, v_own, out, lse):
-    slot = pl.program_id(0)
-    length, offset = info[slot], info[pl.num_programs(0)]
+def attend_kernel(heads, head_dim, scale, first, total_slots, info, q, k_past, v_past, k_own, v_own, out, lse):
+    length, offset = info[first + pl.program_id(0)], info[total_slots]
     past = k_past.shape[1]
     for start, rows in row_blocks(q.shape[1]):
         keys = start + rows
@@ -209,13 +298,14 @@
             lse[0, here, h : h + 1] = top + jnp.log(total)
 
 
-def attend_forward(info, q, k_past, v_past, k_own, v_own, heads, head_dim, scale):
-    count, length, width = q.shape
+def attend_forward(info, q, k_past, v_past, k_own, v_own, heads, head_dim, scale, first, count):
+    _, length, width = q.shape
     past = k_past.shape[1]
-    by_slot = lambda *shape: pl.BlockSpec((1, *shape), lambda s, info: (s,) + (0,) * len(shape))
+    by_slot = lambda *shape: pl.BlockSpec((1, *shape), lambda s, info: (first + s,) + (0,) * len(shape))
+    out_slot = lambda *shape: pl.BlockSpec((1, *shape), lambda s, info: (s,) + (0,) * len(shape))
     keys = count * length * (past + length) * heads
     return pl.pallas_call(
-        functools.partial(attend_kernel, heads, head_dim, scale),
+        functools.partial(attend_kernel, heads, head_dim, scale, first, q.shape[0]),
         grid_spec=pltpu.PrefetchScalarGridSpec(
             num_scalar_prefetch=1,
             grid=(count,),
@@ -226,7 +316,7 @@
                 by_slot(length, head_dim),
                 by_slot(length, head_dim),
             ],
-            out_specs=[by_slot(length, width), by_slot(length, 128)],
+            out_specs=[out_slot(length, width), out_slot(length, 128)],
         ),
         out_shape=[
             jax.ShapeDtypeStruct((count, length, width), LOW),
@@ -420,30 +510,54 @@
     ]
     back = [(target, source) for source, target in there]
 
+    split = units_split()
+    head_width = 2 * head_dim
+    query_cols = heads * head_dim
+    near_cols = query_cols + head_width + 128
+
     outgoing = lax.dynamic_index_in_dim(hidden_in, leaving, 0, keepdims=False)
     own_in = lax.ppermute(outgoing, ("fsdp", "tp"), there)
-    head_width = 2 * head_dim
     small = jnp.concatenate(
         [
             query_weight,
             lax.dynamic_slice_in_dim(keyval_weight, head_pair * head_width, head_width, axis=1),
+            jnp.pad(norm_gains.T, ((0, 0), (0, 128 - norm_gains.shape[0]))),
             output_weight.T,
-            jnp.pad(norm_gains.T, ((0, 0), (0, 128 - norm_gains.shape[0]))),
         ],
         axis=1,
     )
-    small_full = gather_small(small, ctx_rank)
-    down_full = gather_large(down_weight.T, ctx_rank)
-    gate_full = gather_large(gate_weight, ctx_rank)
-    up_full = gather_large(up_weight, ctx_rank)
-    query_cols = heads * head_dim
-    project_full = small_full[:, : query_cols + head_width]
-    output_full = small_full[:, query_cols + head_width : 2 * query_cols + head_width]
-    gains_now = small_full[:, 2 * query_cols + head_width :][:, :2].astype(WIDE).T
-    own_weight = lax.dynamic_slice_in_dim(
-        project_full, query_cols + parity * head_dim, head_dim, axis=1
-    )
-    back_full = jnp.concatenate([project_full[:, :query_cols], own_weight], axis=1)
+    units = gate_weight.shape[1]
+    units_pad = -(-units // 256) * 256
+    widen = lambda w: jnp.pad(w, ((0, 0), (0, units_pad - units)))
+    shards = [widen(w) for w in (down_weight.T, gate_weight, up_weight)]
+    if split:
+        half_units = units_pad // 2
+        cut = lambda w, c: lax.dynamic_slice_in_dim(w, c * half_units, half_units, axis=1)
+
+        def in_order(own, other):
+            return jnp.stack(
+                [jnp.where(ctx_rank == 0, own, other), jnp.where(ctx_rank == 0, other, own)]
+            )
+
+        def all_rows(both, *earlier):
+            full = lax.all_gather(after(both, *earlier), "fsdp", axis=0, tiled=False)
+            return full.reshape(-1, both.shape[-1])
+
+        small_both = in_order(small, from_partner(after(small, outgoing), "ctx", 1))
+        leaving_units = jnp.concatenate([cut(w, 1 - ctx_rank) for w in shards], axis=1)
+        arriving_units = from_partner(after(leaving_units, small), "ctx", 1)
+        unit_both = [
+            in_order(cut(w, ctx_rank), arriving_units[:, i * half_units : (i + 1) * half_units])
+            for i, w in enumerate(shards)
+        ]
+    else:
+        all_rows = lambda shard, *earlier: lax.all_gather(
+            shard, ("fsdp", "ctx"), axis=0, tiled=True
+        )
+        small_both, unit_both = small, shards
+    far_in = from_partner(own_in, "tp", 2)
+    near_in = from_partner(own_in, "tp", 1)
+    cross_in = from_partner(far_in, "tp", 1)
 
     lengths_now = jnp.stack([seq_lengths[s] for s in seq_now])
     info = jnp.concatenate([lengths_now, jnp.stack([offset, parity])]).astype(jnp.int32)
@@ -451,77 +565,142 @@
         [lax.dynamic_index_in_dim(positions, s, 0, keepdims=False) for s in seq_now]
     )
     lane = jnp.arange(head_dim)
-    frequency = 1.0 / ROPE_BASE ** (
-        (lane % (head_dim // 2)).astype(WIDE) * 2.0 / head_dim
-    )
+    frequency = 1.0 / ROPE_BASE ** ((lane % (head_dim // 2)).astype(WIDE) * 2.0 / head_dim)
     angles = positions_now.astype(WIDE)[..., None] * frequency
     cosine = jnp.cos(angles)
     sine = jnp.sin(angles) * jnp.where(lane < head_dim // 2, -1.0, 1.0)
-    grad_rows = jnp.concatenate(
-        [lax.dynamic_index_in_dim(cotangent, s, 0, keepdims=False) for s in slot_now], axis=0
-    )
-
+    grad_slots = [lax.dynamic_index_in_dim(cotangent, s, 0, keepdims=False) for s in slot_now]
+
+    near_full = all_rows(small_both[..., :near_cols], own_in)
+    output_full = all_rows(small_both[..., near_cols:], far_in)
+    down_full = all_rows(unit_both[0], cross_in)
+    project_full = near_full[:, : query_cols + head_width]
+    gains_now = near_full[:, query_cols + head_width :][:, :2].astype(WIDE).T
     bias_head = lax.dynamic_slice_in_dim(bias_keyval, head_pair * 2, 2, axis=0)
     bias_row = jnp.concatenate([bias_query.reshape(1, -1), bias_head.reshape(1, -1)], axis=1).astype(WIDE)
-    rows_in = spread_rows(own_in)
     normed_one, query_rot, key_own, value_own = project(
-        rows_in, gains_now[0:1], project_full, bias_row, cosine, sine, heads, head_dim
-    )
-    if ctx_count == 2:
+        (own_in, near_in, far_in, cross_in),
+        gains_now[0:1],
+        project_full,
+        bias_row,
+        cosine,
+        sine,
+        heads,
+        head_dim,
+    )
+    gate_full = all_rows(unit_both[1], query_rot)
+    if split:
         key_past, value_past = lax.ppermute((key_own, value_own), "ctx", [(0, 1)])
+        grad_pair = after(jnp.stack([grad_slots[0], grad_slots[2]]), value_past)
+        other_pair = from_partner(grad_pair, "ctx", 1)
+        cross_pair = from_partner(other_pair, "tp", 1)
+        others = [other_pair[0], cross_pair[0], other_pair[1], cross_pair[1]]
     else:
         key_past = lax.all_gather(key_own, "ctx", axis=1, tiled=True)
         value_past = lax.all_gather(value_own, "ctx", axis=1, tiled=True)
-    mixed, lse = attend_forward(
-        info, query_rot, key_past, value_past, key_own, value_own, heads, head_dim, scale
+        others = []
+    attend = lambda first, *held: attend_forward(
+        info, query_rot, *held, key_own, value_own, heads, head_dim, scale, first, 2
     )
     in_share = own_in.astype(WIDE)
 
-    def row_parts(far_part, near_part):
-        far_part = far_part.reshape(2, local_len, model_width)
-        near_part = near_part.reshape(2, local_len, model_width)
-        return (near_part[0], near_part[1], far_part[0], far_part[1])
-
-    def halves(value):
-        half = token_count // 2
-        return value[half:], value[:half]
-
-    mixed_flat = mixed.reshape(token_count, query_cols)
-    attn_parts = row_parts(*[contract_cols(m, output_full, LOW) for m in halves(mixed_flat)])
-    middle_share = in_share + collect_rows(attn_parts)
+    mixed_far, lse_far = attend(2, key_past, value_past)
+    attn_far = contract_cols(mixed_far.reshape(-1, query_cols), output_full, LOW)
+    attn_far = attn_far.reshape(2, local_len, model_width)
+    attn_wide = collect_far(attn_far[0], attn_far[1])
+    attn_got = from_partner(attn_wide, "tp", 2)
+    mixed_near, lse_near = attend(0, after(key_past, attn_wide), value_past)
+    attn_near = contract_cols(mixed_near.reshape(-1, query_cols), output_full, LOW)
+    attn_near = attn_near.reshape(2, local_len, model_width)
+    attn_core = from_partner(attn_near[1], "tp", 1)
+    up_full = all_rows(unit_both[2], attn_near)
+    middle_share = (
+        in_share
+        + attn_near[0].astype(WIDE)
+        + attn_core.astype(WIDE)
+        + attn_got.astype(WIDE)
+    )
     inv_two = lax.rsqrt(jnp.mean(middle_share * middle_share, axis=-1, keepdims=True) + EPS)
     normed_share = (middle_share * inv_two * gains_now[1]).astype(LOW)
-    normed_two = jnp.concatenate(spread_rows(normed_share), axis=0)
-
-    grad_hidden = product(grad_rows, down_full)
-    gate_lin = product(normed_two, gate_full)
-    up_lin = product(normed_two, up_full)
-    gate_sigmoid = jax.nn.sigmoid(gate_lin)
-    silu_gate = gate_lin * gate_sigmoid
-    hidden_act = (silu_gate * up_lin).astype(LOW)
-    grad_gate = (
-        grad_hidden * up_lin * gate_sigmoid * (1.0 + gate_lin * (1.0 - gate_sigmoid))
-    ).astype(LOW)
-    grad_up = (grad_hidden * silu_gate).astype(LOW)
-    back_parts = row_parts(
-        *[
-            (contract_cols(g, gate_full) + contract_cols(u, up_full)).astype(LOW)
-            for g, u in zip(halves(grad_gate), halves(grad_up))
-        ]
-    )
-    grad_two_share = collect_rows(back_parts)
-    down_grad = scatter_sum(contract_rows(grad_rows, hidden_act, LOW), ctx_rank, LOW)
-    gate_grad = scatter_sum(contract_rows(normed_two, grad_gate, LOW), ctx_rank, LOW)
-    up_grad = scatter_sum(contract_rows(normed_two, grad_up, LOW), ctx_rank, LOW)
-    mlp_parts = row_parts(*[contract_cols(a, down_full, LOW) for a in halves(hidden_act)])
-    block_share = (middle_share + collect_rows(mlp_parts)).astype(LOW)
-
+    half_len = local_len // 2
+
+    def spread_all(own, then):
+        far = from_partner(own, "tp", 2)
+        near = from_partner(own, "tp", 1)
+        if not split:
+            return (own, near, far, from_partner(far, "tp", 1)), then()
+        side = from_partner(own, "ctx", 1)
+        between = then()
+        diagonal = (
+            from_partner(far[:half_len], "ctx", 1),
+            from_partner(side[half_len:], "tp", 2),
+        )
+        diagonal = jnp.concatenate(diagonal, axis=0)
+        cores = [from_partner(v, "tp", 1) for v in (far, side, diagonal)]
+        return (own, near, far, cores[0], side, cores[1], diagonal, cores[2]), between
+
+    grad_rows = jnp.concatenate(grad_slots + others, axis=0)
+    normed_rows, grad_hidden = spread_all(
+        normed_share, lambda: product(after(grad_rows, normed_share), down_full, LOW)
+    )
+    gate_lin, normed_two = gate_rows(normed_rows, gate_full)
+    hidden_act, grad_gate, grad_up = hidden_units(normed_two, up_full, gate_lin, grad_hidden)
+
+    def collect_all(lefts, weights, *earlier):
+        lefts = list(lefts)
+        lefts[0] = after(lefts[0], *earlier)
+        if split:
+            last = back_rows(lefts, weights, 6, 2, local_len)
+            diagonal = collect_far(last[0], last[1])
+            to_far = from_partner(diagonal[:half_len], "tp", 2)
+            to_side = from_partner(diagonal[half_len:], "ctx", 1)
+            lefts[0] = after(lefts[0], diagonal)
+            middle = back_rows(lefts, weights, 2, 4, local_len)
+            core_far, core_side = (from_partner(middle[i], "tp", 1) for i in (1, 3))
+            far = middle[0].astype(WIDE) + core_far.astype(WIDE)
+            side = middle[2].astype(WIDE) + core_side.astype(WIDE)
+            side = jnp.concatenate(
+                [side[:half_len] + to_far.astype(WIDE), side[half_len:]], axis=0
+            ).astype(LOW)
+            far = jnp.concatenate(
+                [far[:half_len], far[half_len:] + to_side.astype(WIDE)], axis=0
+            ).astype(LOW)
+            got = [from_partner(far, "tp", 2), from_partner(side, "ctx", 1)]
+            lefts[0] = after(lefts[0], far, side)
+        else:
+            last = back_rows(lefts, weights, 2, 2, local_len)
+            got = [from_partner(collect_far(last[0], last[1]), "tp", 2)]
+        first = back_rows(lefts, weights, 0, 2, local_len)
+        got.append(from_partner(first[1], "tp", 1))
+
+        def finish():
+            return sum((v.astype(WIDE) for v in got), first[0].astype(WIDE))
+
+        return first, finish
+
+    first_back, finish_back = collect_all((grad_gate, grad_up), (gate_full, up_full))
+    down_grad = contract_rows(after(grad_rows, first_back), hidden_act, LOW)
+    gate_grad = contract_rows(normed_two, after(grad_gate, down_grad), LOW)
+    grad_two_share = finish_back()
     grad_norm_two, gain_two = norm_backward(middle_share, inv_two, gains_now[1], grad_two_share)
-    grad_middle = grad_rows[:local_len].astype(WIDE) + grad_norm_two
-    grad_branch = jnp.concatenate(spread_rows(grad_middle.astype(LOW)), axis=0)
+    grad_middle = grad_slots[0].astype(WIDE) + grad_norm_two
+    branch_own = grad_middle.astype(LOW)
+    branch_far = from_partner(branch_own, "tp", 2)
+    branch_near = from_partner(branch_own, "tp", 1)
+    branch_cross = from_partner(branch_far, "tp", 1)
+    grad_branch = jnp.concatenate([branch_own, branch_near, branch_far, branch_cross], axis=0)
+    up_grad = contract_rows(normed_two, after(grad_up, branch_own), LOW)
+
+    def scatter_units(grad):
+        if not split:
+            return scatter_sum(grad, ctx_rank, LOW)
+        return lax.psum_scatter(grad, "fsdp", scatter_dimension=0, tiled=True)
+
+    unit_sums = [scatter_units(g) for g in (down_grad, gate_grad, up_grad)]
+
     grad_mixed = product(grad_branch, output_full, LOW)
-    output_grad = contract_rows(grad_branch, mixed_flat, LOW)
-
+    mixed_flat = jnp.concatenate([mixed_near, mixed_far], axis=0).reshape(token_count, query_cols)
+    lse = jnp.concatenate([lse_near, lse_far], axis=0)
     grad_query, mine_past, mine_own, other_past, other_own = attend_backward(
         info,
         query_rot,
@@ -541,7 +720,7 @@
     got_past, got_own = from_partner((other_past, other_own), "tp", 1)
     past_sum = mine_past + swap(got_past)
     own_sum = mine_own + swap(got_own)
-    if ctx_count == 2:
+    if split:
         own_sum = own_sum + lax.ppermute(past_sum.astype(LOW), "ctx", [(1, 0)]).astype(WIDE)
     else:
         own_sum = own_sum + lax.psum_scatter(past_sum, "ctx", scatter_dimension=1, tiled=True)
@@ -549,49 +728,83 @@
     turned = own_sum * cosine - jnp.roll(own_sum, half_lanes, axis=-1) * sine
     own_grad = jnp.where(parity == 0, turned, own_sum).astype(LOW).reshape(token_count, head_dim)
     line_grad = jnp.concatenate([grad_query.reshape(token_count, query_cols), own_grad], axis=1)
-    normed_flat = normed_one.reshape(token_count, model_width)
-    line_weight_grad = contract_rows(normed_flat, line_grad, LOW)
-    bias_grad = jnp.sum(line_grad.astype(WIDE), axis=0)
-    line_parts = row_parts(*[contract_cols(g, back_full, LOW) for g in halves(line_grad)])
-    grad_one_share = collect_rows(line_parts)
+    own_weight = lax.dynamic_slice_in_dim(
+        project_full, query_cols + parity * head_dim, head_dim, axis=1
+    )
+    back_full = jnp.concatenate([project_full[:, :query_cols], own_weight], axis=1)
+    half = token_count // 2
+    line_far = contract_cols(line_grad[half:], back_full, LOW).reshape(2, local_len, model_width)
+    line_near = contract_cols(line_grad[:half], back_full, LOW).reshape(2, local_len, model_width)
+    line_wide = collect_far(line_far[0], line_far[1])
+    line_got = from_partner(line_wide, "tp", 2)
+    line_core = from_partner(line_near[1], "tp", 1)
+
+    first_mlp, finish_mlp = collect_all((hidden_act,), (down_full,), up_grad, branch_far)
+    block_share = (middle_share + finish_mlp()).astype(LOW)
+
+    grad_one_share = line_near[0].astype(WIDE) + line_core.astype(WIDE) + line_got.astype(WIDE)
     inv_one = lax.rsqrt(jnp.mean(in_share * in_share, axis=-1, keepdims=True) + EPS)
     grad_norm_one, gain_one = norm_backward(in_share, inv_one, gains_now[0], grad_one_share)
     input_share = (grad_middle + grad_norm_one).astype(LOW)
 
-    def go_home(share):
-        rows = spread_rows(lax.ppermute(share, ("fsdp", "tp"), back))
+    normed_flat = normed_one.reshape(token_count, model_width)
+    late = after(line_grad, line_wide, line_near)
+    attn_grad = jnp.concatenate(
+        [contract_rows(normed_flat, late, LOW), contract_rows(grad_branch, mixed_flat, LOW)], axis=1
+    )
+    bias_grad = jnp.sum(late.astype(WIDE), axis=0)
+    attn_end = scatter_sum(attn_grad, ctx_rank, LOW, input_share)
+
+    def leave(share):
+        return lax.ppermute(share, ("fsdp", "tp"), back)
+
+    def arrive(own, *earlier):
+        far = from_partner(after(own, *earlier), "tp", 2)
+        near = from_partner(own, "tp", 1)
+        cross = from_partner(far, "tp", 1)
         out = jnp.zeros((seq_grp, local_len, model_width), LOW)
-        for home, row in zip(home_now, rows):
+        for home, row in zip(home_now, (own, near, far, cross)):
             out = lax.dynamic_update_index_in_dim(out, row, home, 0)
         return out
 
-    block_out = go_home(block_share)
-    input_grad = go_home(input_share)
-
-    attn_grad = scatter_sum(jnp.concatenate([line_weight_grad, output_grad], axis=1), ctx_rank, LOW)
+    block_home = leave(block_share)
+    input_home = leave(input_share)
+    block_out = arrive(block_home, input_share)
+    input_grad = arrive(input_home)
+
     gain_grad = jnp.stack([gain_one, gain_two], axis=1)
     gain_grad = gain_grad + from_partner(gain_grad, "tp", 1)
     gain_grad = gain_grad + from_partner(gain_grad, "tp", 2)
-    shards = fsdp_count * ctx_count
-    bias_cols = bias_grad.reshape(heads + 1, shards, head_dim // shards)
-    bias_cols = jnp.transpose(bias_cols, (1, 2, 0))
-    bias_cols = jnp.pad(bias_cols, ((0, 0), (0, (model_width - head_dim) // shards), (0, 0)))
+    shard_count = fsdp_count * ctx_count
+    share = head_dim // shard_count
+    bias_cols = jnp.transpose(bias_grad.reshape(heads + 1, shard_count, share), (1, 2, 0))
+    bias_cols = jnp.pad(bias_cols, ((0, 0), (0, (model_width - head_dim) // shard_count), (0, 0)))
     tiny = jnp.concatenate([gain_grad, bias_cols.reshape(model_width, heads + 1)], axis=1)
-    tiny = jnp.pad(tiny, ((0, 0), (0, 8 - tiny.shape[1])))
-    tiny_grad = scatter_sum(tiny, ctx_rank, WIDE)
-    share = head_dim // shards
+    tiny_grad = scatter_sum(jnp.pad(tiny, ((0, 0), (0, 8 - tiny.shape[1]))), ctx_rank, WIDE)
+
+    def unit_end(total):
+        if split:
+            blocks = total.reshape(1, ctx_count, -1, half_units)
+            kept, sent = scatter_ctx(blocks, ctx_rank)
+            kept, got = kept[0], from_partner(sent[0], "ctx", 1)
+            first = jnp.where(ctx_rank == 0, kept, got)
+            second = jnp.where(ctx_rank == 0, got, kept)
+            total = jnp.concatenate([first, second], axis=1)
+        return total[:, :units].astype(WIDE)
+
+    down_end, gate_end, up_end = (unit_end(after(t, input_share)) for t in unit_sums)
     return (
         block_out,
         input_grad,
-        attn_grad[:, :query_cols].astype(WIDE),
-        attn_grad[:, query_cols : query_cols + head_dim].astype(WIDE),
-        attn_grad[:, query_cols + head_dim :].astype(WIDE).T,
+        attn_end[:, :query_cols].astype(WIDE),
+        attn_end[:, query_cols : query_cols + head_dim].astype(WIDE),
+        attn_end[:, query_cols + head_dim :].astype(WIDE).T,
         tiny_grad[:, :2].T,
         tiny_grad[:share, 2 : 2 + heads].T,
         tiny_grad[:share, 2 + heads : 3 + heads].T,
-        gate_grad.astype(WIDE),
-        up_grad.astype(WIDE),
-        down_grad.astype(WIDE).T,
+        gate_end,
+        up_end,
+        down_end.T,
     )
 
 

time: 1170 us -> 938 us (0.80)
  waiting for transfers between devices: 541 us -> 303 us
  Pallas kernels: 54.9 us -> 192 us
  matrix products: 238 us -> 119 us
    pallas_call x1 -> x10, Pallas kernels: 16.8 us -> 154 us  [the longest x6 77.8 us: back_rows(): pl.pallas_call(functools.partial(back_kernel, len(lefts)), grid=(slots,),...]
    all_gather x4 -> x5, waiting for transfers between devices: 113 us -> 0.03 us  [all_rows(): full = lax.all_gather(after(both, *earlier), 'fsdp', axis=0, tiled=False)]
    ppermute x1, waiting for transfers between devices: 91.7 us -> 21.8 us  [local(): own_in = lax.ppermute(outgoing, ('fsdp', 'tp'), there)]
    dot_general x10 -> x4, matrix products: 76.3 us -> 10.1 us  [contract_cols(): lax.dot_general(left_side, right_side, (((1,), (1,)), ((), ())), preferre...]
    dot_general x4 -> x2, matrix products: 92.3 us -> 29 us  [product(): jnp.dot(left_side, right_side, preferred_element_type=WIDE).astype(kind)]
    ppermute x40 -> x55, waiting for transfers between devices: 282 us -> 236 us  [from_partner(): return lax.ppermute(value, axis, pairs)]
    ppermute x2, waiting for transfers between devices: 48.2 us -> 10.8 us  [leave(): return lax.ppermute(share, ('fsdp', 'tp'), back)]
    ppermute x2, starting transfers between devices: 36.9 us -> 5.9 us  [leave(): return lax.ppermute(share, ('fsdp', 'tp'), back)]
  transfers between devices with their start and end apart: 55 -> 71, of which waited for: 22 -> 22; matrix products, arithmetic and copies ran while one was open for 27% -> 29% of each run, Pallas kernels for 5% -> 12%
where the time goes in v2:
time: 938 us; the launch traced here: 927 us
  waiting for transfers between devices  303 us (32%)
  Pallas kernels  192 us (20%)
  matrix products  119 us (13%)
  local copies, waits for them, and re-layouts  110 us (12%)
  other arithmetic  83.7 us (9%)
  starting transfers between devices  74.9 us (8%)
  between operations  44.3 us (5%)
    ppermute x55, waiting for transfers between devices, from_partner(): return lax.ppermute(value, axis, pairs)  236 us
    dot_general x5, matrix products, contract_rows(): lax.dot_general(left_side, right_side, (((0,), (0,)), ((), ())), preferre...  80.2 us
    pallas_call x6, Pallas kernels, back_rows(): pl.pallas_call(functools.partial(back_kernel, len(lefts)), grid=(slots,),...  77.8 us
    ppermute x55, starting transfers between devices, from_partner(): return lax.ppermute(value, axis, pairs)  57.1 us
    pallas_call x1, Pallas kernels, hidden_units(): pl.pallas_call(units_kernel, grid=(tokens // step,), in_specs=[by_row(wid...  30.6 us
    dot_general x2, matrix products, product(): jnp.dot(left_side, right_side, preferred_element_type=WIDE).astype(kind)  29 us
    pallas_call x1, Pallas kernels, gate_rows(): pl.pallas_call(functools.partial(gate_kernel, count), grid=(count,), in_s...  26 us
    pallas_call x1, Pallas kernels, attend_backward(): pl.pallas_call(functools.partial(attend_back_kernel, heads, head_dim, sca...  25.7 us
  transfers between devices with their start and end apart: 71, of which 22 were waited for; matrix products, arithmetic and copies ran while one was open for 29% of the time, Pallas kernels for 12%

profile of v2, /device:TPU:1, one launch (start us, length us, event | category | flops | bytes accessed | tf_op | source)
XLA Modules:
  0.0 926.9 jit_solution(9808737814277040431)
XLA Ops:
  35.5 21.8 %collective-permute-done.x0 = bf16[512,1536]{1,0:T(8,128)(2,1)S(1)} collective-permute-done((bf16[512,1536]{1,0:T(8,128)(2,1)}, bf16[512,1536]{1,0:T(8,128)(2,1)S(1)}, u32[]{:S(2)}, u32[]{:S(2)}) %collective-permute-start) | collective-permute-done | bytes 1572896 | tf_op jit(solution)/shard_map/ppermute | solution.py:519
  63.9 28.2 %collective-permute-done.2.x2 = bf16[512,1536]{1,0:T(8,128)(2,1)} collective-permute-done((bf16[512,1536]{1,0:T(8,128)(2,1)S(1)}, bf16[512,1536]{1,0:T(8,128)(2,1)}, u32[]{:S(2)}, u32[]{:S(2)}) %collective-permute-start.2) | collective-permute-done | bytes 1572896 | tf_op jit(solution)/shard_map/ppermute | solution.py:21
  123.9 12.3 %shard_map.230 = (bf16[4,512,1536]{2,1,0:T(8,128)(2,1)}, bf16[4,512,384]{2,1,0:T(8,128)(2,1)}, bf16[4,512,128]{2,1,0:T(8,128)(2,1)}, bf16[4,512,128]{2,1,0:T(8,128)(2,1)}) custom-call(bf16[512,1536]{1,0:T(8,128)(2,1)} %copy-done.5, bf16[512,1536]{1,0:T(8,128)(2,1)} %collective-permute-done.1.x1, bf16[512,1536]{1,0:T(8,128)(2,1)} %collective-permute-done.2.x2, ...), custom_call_target="tpu_custom_call" | custom-call | flops 4026531840 | bytes 17170432 | tf_op jit(solution)/shard_map/pallas_call | solution.py:228
  150.7 11.0 %collective-permute-done.5.k_past = bf16[4,512,128]{2,1,0:T(8,128)(2,1)S(1)} collective-permute-done((bf16[4,512,128]{2,1,0:T(8,128)(2,1)}, bf16[4,512,128]{2,1,0:T(8,128)(2,1)S(1)}, u32[]{:S(2)}, u32[]{:S(2)}) %collective-permute-start.5) | collective-permute-done | bytes 524320 | tf_op jit(solution)/shard_map/ppermute | solution.py:593
  162.6 9.8 %shard_map.231 = (bf16[2,512,384]{2,1,0:T(8,128)(2,1)}, f32[2,512,128]{2,1,0:T(8,128)}) custom-call(s32[6]{0:T(128)} %concatenate.84.info, bf16[4,512,384]{2,1,0:T(8,128)(2,1)} %get-tuple-element.54.q, bf16[4,512,128]{2,1,0:T(8,128)(2,1)} %copy-done.56, bf16[4,512,128]{2,1,0:T(8,128)(2,1)} %copy-done.55, bf16[4,512,128]{2,1,0:T(8,128)(2,1)} %get-tuple-element.55.k_own, ...), custom_call_target="tpu_custom_call" | custom-call | flops 1610612736 | bytes 1572864 | tf_op jit(solution)/shard_map/pallas_call | solution.py:307
  204.8 49.6 %collective-permute-done.19 = bf16[2,512,1536]{2,1,0:T(8,128)(2,1)} collective-permute-done((bf16[2,512,1536]{2,1,0:T(8,128)(2,1)S(1)}, bf16[2,512,1536]{2,1,0:T(8,128)(2,1)}, u32[]{:S(2)}, u32[]{:S(2)}) %collective-permute-start.19) | collective-permute-done | bytes 3145760 | tf_op jit(solution)/shard_map/ppermute | solution.py:21
  266.0 29.2 %collective-permute-done.11.refs_2_ = bf16[512,1536]{1,0:T(8,128)(2,1)} collective-permute-done((bf16[512,1536]{1,0:T(8,128)(2,1)}, bf16[512,1536]{1,0:T(8,128)(2,1)}, u32[]{:S(2)}, u32[]{:S(2)}) %collective-permute-start.11) | collective-permute-done | bytes 1572896 | tf_op jit(solution)/shard_map/ppermute | solution.py:21
  331.5 22.0 %convolution_convert_fusion.grad = bf16[4096,1152]{1,0:T(8,128)(2,1)} fusion(bf16[4096,1536]{1,0:T(8,128)(2,1)} %fusion.22, bf16[1536,1152]{1,0:T(8,128)(2,1)} %bitcast.247), kind=kOutput, calls=%fused_computation | convolution fusion | flops 14500233216 | bytes 25559040 | tf_op jit(solution)/shard_map/dot_general | solution.py:25
  353.6 26.0 %shard_map.233 = (bf16[4096,1152]{1,0:T(8,128)(2,1)}, bf16[4096,1536]{1,0:T(8,128)(2,1)}) custom-call(bf16[512,1536]{1,0:T(8,128)(2,1)} %multiply_convert_fusion.refs_0_, bf16[512,1536]{1,0:T(8,128)(2,1)} %collective-permute-done.10.refs_1_, bf16[512,1536]{1,0:T(8,128)(2,1)} %collective-permute-done.11.refs_2_, ...), custom_call_target="tpu_custom_call" | custom-call | flops 14495514624 | bytes 38141952 | tf_op jit(solution)/shard_map/pallas_call | solution.py:107
  379.6 30.6 %shard_map.234 = (bf16[4096,1152]{1,0:T(8,128)(2,1)}, bf16[4096,1152]{1,0:T(8,128)(2,1)}, bf16[4096,1152]{1,0:T(8,128)(2,1)}) custom-call(bf16[4096,1536]{1,0:T(8,128)(2,1)} %get-tuple-element.63.h, bf16[1536,1152]{1,0:T(8,128)(2,1)} %bitcast.243, bf16[4096,1152]{1,0:T(8,128)(2,1)} %get-tuple-element.64.gate, bf16[4096,1152]{1,0:T(8,128)(2,1)} %convolution_convert_fusion.grad), custom_call_target="tpu_custom_call" | custom-call | flops 14495514624 | bytes 63307776 | tf_op jit(solution)/shard_map/pallas_call | solution.py:145
  410.3 13.5 %shard_map.235 = bf16[2,512,1536]{2,1,0:T(8,128)(2,1)} custom-call(bf16[4096,1152]{1,0:T(8,128)(2,1)} %get-tuple-element.89.refs_0_, bf16[4096,1152]{1,0:T(8,128)(2,1)} %get-tuple-element.73.refs_1_, bf16[1536,1152]{1,0:T(8,128)(2,1)} %bitcast.240, bf16[1536,1152]{1,0:T(8,128)(2,1)} %bitcast.244), custom_call_target="tpu_custom_call" | custom-call | flops 7247757312 | bytes 14942208 | tf_op jit(solution)/shard_map/pallas_call | solution.py:172
  430.4 22.0 %shard_map.236 = bf16[4,512,1536]{2,1,0:T(8,128)(2,1)} custom-call(bf16[4096,1152]{1,0:T(8,128)(2,1)} %get-tuple-element.89.refs_0_, bf16[4096,1152]{1,0:T(8,128)(2,1)} %get-tuple-element.73.refs_1_, bf16[1536,1152]{1,0:T(8,128)(2,1)} %bitcast.241, bf16[1536,1152]{1,0:T(8,128)(2,1)} %bitcast.245), custom_call_target="tpu_custom_call" | custom-call | flops 14495514624 | bytes 22806528 | tf_op jit(solution)/shard_map/pallas_call | solution.py:172
  461.5 14.2 %collective-permute-done.25 = bf16[256,1536]{1,0:T(8,128)(2,1)S(1)} collective-permute-done((bf16[256,1536]{1,0:T(8,128)(2,1)S(1)}, bf16[256,1536]{1,0:T(8,128)(2,1)S(1)}, u32[]{:S(2)}, u32[]{:S(2)}) %collective-permute-start.25) | collective-permute-done | bytes 786464 | tf_op jit(solution)/shard_map/ppermute | solution.py:21
  478.7 13.7 %shard_map.237 = bf16[2,512,1536]{2,1,0:T(8,128)(2,1)} custom-call(bf16[4096,1152]{1,0:T(8,128)(2,1)} %get-tuple-element.89.refs_0_, bf16[4096,1152]{1,0:T(8,128)(2,1)} %get-tuple-element.73.refs_1_, bf16[1536,1152]{1,0:T(8,128)(2,1)} %bitcast.242, bf16[1536,1152]{1,0:T(8,128)(2,1)} %bitcast.246), custom_call_target="tpu_custom_call" | custom-call | flops 7247757312 | bytes 14942208 | tf_op jit(solution)/shard_map/pallas_call | solution.py:172
  492.3 23.0 %convolution_convert_fusion.2 = bf16[1536,1152]{1,0:T(8,128)(2,1)} fusion(bf16[4096,1536]{1,0:T(8,128)(2,1)} %fusion.22, bf16[4096,1152]{1,0:T(8,128)(2,1)} %get-tuple-element.76.refs_0_), kind=kOutput, calls=%fused_computation.2 | convolution fusion | flops 14497284096 | bytes 25559040 | tf_op jit(solution)/shard_map/dot_general | solution.py:29
  521.1 33.3 %collective-permute-done.27 = bf16[512,1536]{1,0:T(8,128)(2,1)S(1)} collective-permute-done((bf16[512,1536]{1,0:T(8,128)(2,1)}, bf16[512,1536]{1,0:T(8,128)(2,1)S(1)}, u32[]{:S(2)}, u32[]{:S(2)}) %collective-permute-start.27) | collective-permute-done | bytes 1572896 | tf_op jit(solution)/shard_map/ppermute | solution.py:21
  559.6 20.6 %convolution_convert_fusion.3 = bf16[1536,1152]{1,0:T(8,128)(2,1)} fusion(bf16[4096,1536]{1,0:T(8,128)(2,1)} %get-tuple-element.63.h, bf16[4096,1152]{1,0:T(8,128)(2,1)S(1)} %bitcast.238), kind=kOutput, calls=%fused_computation.3 | convolution fusion | flops 14497284096 | bytes 25559040 | tf_op jit(solution)/shard_map/dot_general | solution.py:29
  594.7 21.2 %collective-permute-done.29 = bf16[512,1536]{1,0:T(8,128)(2,1)} collective-permute-done((bf16[512,1536]{1,0:T(8,128)(2,1)}, bf16[512,1536]{1,0:T(8,128)(2,1)}, u32[]{:S(2)}, u32[]{:S(2)}) %collective-permute-start.29) | collective-permute-done | bytes 1572896 | tf_op jit(solution)/shard_map/ppermute | solution.py:21
  617.5 23.1 %convolution_convert_fusion.1 = bf16[1536,1152]{1,0:T(8,128)(2,1)} fusion(bf16[4096,1536]{1,0:T(8,128)(2,1)} %get-tuple-element.63.h, bf16[4096,1152]{1,0:T(8,128)(2,1)} %get-tuple-element.89.refs_0_), kind=kOutput, calls=%fused_computation.1 | convolution fusion | flops 14497284096 | bytes 25559040 | tf_op jit(solution)/shard_map/dot_general | solution.py:29
  657.6 25.7 %shard_map.241 = (bf16[4,512,384]{2,1,0:T(8,128)(2,1)}, f32[4,512,128]{2,1,0:T(8,128)}, f32[4,512,128]{2,1,0:T(8,128)}, f32[4,512,128]{2,1,0:T(8,128)}, f32[4,512,128]{2,1,0:T(8,128)}) custom-call(s32[6]{0:T(128)} %concatenate.84.info, bf16[4,512,384]{2,1,0:T(8,128)(2,1)} %get-tuple-element.54.q, bf16[4,512,128]{2,1,0:T(8,128)(2,1)} %copy-done.56, ...), custom_call_target="tpu_custom_call" | custom-call | flops 8053063680 | bytes 6291456 | tf_op jit(solution)/shard_map/pallas_call | solution.py:412
  687.0 12.5 %shard_map.239 = bf16[4,512,1536]{2,1,0:T(8,128)(2,1)} custom-call(bf16[4096,1152]{1,0:T(8,128)(2,1)} %get-tuple-element.76.refs_0_, bf16[1536,1152]{1,0:T(8,128)(2,1)} %bitcast.249), custom_call_target="tpu_custom_call" | custom-call | flops 7247757312 | bytes 14548992 | tf_op jit(solution)/shard_map/pallas_call | solution.py:172
  786.3 18.9 %collective-permute-done.47 = bf16[512,1536]{1,0:T(8,128)(2,1)} collective-permute-done((bf16[512,1536]{1,0:T(8,128)(2,1)}, bf16[512,1536]{1,0:T(8,128)(2,1)}, u32[]{:S(2)}, u32[]{:S(2)}) %collective-permute-start.47) | collective-permute-done | bytes 1572896 | tf_op jit(solution)/shard_map/ppermute | solution.py:21
  828.7 10.8 %collective-permute-done.38 = bf16[512,1536]{1,0:T(8,128)(2,1)} collective-permute-done((bf16[512,1536]{1,0:T(8,128)(2,1)}, bf16[512,1536]{1,0:T(8,128)(2,1)}, u32[]{:S(2)}, u32[]{:S(2)}) %collective-permute-start.38) | collective-permute-done | bytes 1572896 | tf_op jit(solution)/shard_map/ppermute | solution.py:759
  900.8 11.7 %collective-permute-done.52 = bf16[512,1536]{1,0:T(8,128)(2,1)S(1)} collective-permute-done((bf16[512,1536]{1,0:T(8,128)(2,1)}, bf16[512,1536]{1,0:T(8,128)(2,1)S(1)}, u32[]{:S(2)}, u32[]{:S(2)}) %collective-permute-start.52) | collective-permute-done | bytes 1572896 | tf_op jit(solution)/shard_map/ppermute | solution.py:21
  (427 shorter events, 378.0 us)
Async XLA Ops:
  7.2 110.5 %all-gather.11.cloned.1.call-start = ((), (), s32[]{:S(2)}) async-start(), calls=%async_computation.9 | async-start | bytes 2949120 | tf_op jit(solution)/shard_map/all_gather | solution.py:543
  57.4 115.0 %all-gather.13.cloned.1.call-start = ((), (), s32[]{:S(2)}) async-start(), calls=%async_computation.10 | async-start | bytes 1474560 | tf_op jit(solution)/shard_map/all_gather | solution.py:543
  92.2 239.3 %all-gather.19.cloned.1.call-start = ((), (), s32[]{:S(2)}) async-start(), calls=%async_computation.13 | async-start | bytes 4423680 | tf_op jit(solution)/shard_map/all_gather | solution.py:543
  99.3 254.2 %all-gather.15.cloned.1.call-start = ((), (), s32[]{:S(2)}) async-start(), calls=%async_computation.11 | async-start | bytes 4423680 | tf_op jit(solution)/shard_map/all_gather | solution.py:543
  184.2 70.2 %collective-permute-start.19 = (bf16[2,512,1536]{2,1,0:T(8,128)(2,1)S(1)}, bf16[2,512,1536]{2,1,0:T(8,128)(2,1)}, u32[]{:S(2)}, u32[]{:S(2)}) collective-permute-start(bf16[2,512,1536]{2,1,0:T(8,128)(2,1)S(1)} %pad_maximum_fusion.2), channel_id=1, source_target_pairs={{0,4},{4,0},{1,5},{5,1},{2,6},{6,2},{3,7},{7,3},{8,12},{12,8},{9,1... | collective-permute-start | bytes 9437192 | tf_op jit(solution)/shard_map/ppermute | solution.py:21
  187.4 192.2 %all-gather.17.cloned.1.call-start = ((), (), s32[]{:S(2)}) async-start(), calls=%async_computation.12 | async-start | bytes 4423680 | tf_op jit(solution)/shard_map/all_gather | solution.py:543
  202.9 52.7 %collective-permute-start.8 = (bf16[512,1536]{1,0:T(8,128)(2,1)S(1)}, bf16[512,1536]{1,0:T(8,128)(2,1)S(1)}, u32[]{:S(2)}, u32[]{:S(2)}) collective-permute-start(bf16[512,1536]{1,0:T(8,128)(2,1)S(1)} %slice.319), channel_id=1, source_target_pairs={{0,1},{1,0},{2,3},{3,2},{4,5},{5,4},{6,7},{7,6},{8,9},{9,8},{10,11... | collective-permute-start | bytes 4718600 | tf_op jit(solution)/shard_map/ppermute | solution.py:21
  203.8 51.7 %collective-permute-start.9 = (bf16[512,1536]{1,0:T(8,128)(2,1)S(1)}, bf16[512,1536]{1,0:T(8,128)(2,1)S(1)}, u32[]{:S(2)}, u32[]{:S(2)}) collective-permute-start(bf16[512,1536]{1,0:T(8,128)(2,1)S(1)} %add_convert_fusion.1), channel_id=1, source_target_pairs={{0,2},{1,3},{2,0},{3,1},{4,6},{5,7},{6,4},{7,5},{8,10},{9,11},{10,... | collective-permute-start | bytes 4718600 | tf_op jit(solution)/shard_map/ppermute | solution.py:21
  254.4 68.9 %collective-permute-start.20 = (bf16[2,512,1536]{2,1,0:T(8,128)(2,1)}, bf16[2,512,1536]{2,1,0:T(8,128)(2,1)}, u32[]{:S(2)}, u32[]{:S(2)}) collective-permute-start(bf16[2,512,1536]{2,1,0:T(8,128)(2,1)} %collective-permute-done.19), channel_id=1, source_target_pairs={{0,1},{1,0},{2,3},{3,2},{4,5},{5,4},{6,7},{7,6},{8,9},{9,8},{10,11... | collective-permute-start | bytes 9437192 | tf_op jit(solution)/shard_map/ppermute | solution.py:21
  299.8 514.9 %reduce-scatter.14.cloned.1.call-start = ((), (), s32[]{:S(2)}) async-start(), calls=%async_computation.8 | async-start | bytes 4423680 | tf_op jit(solution)/shard_map/reduce_scatter | solution.py:697
  300.1 53.5 %collective-permute-start.10 = (bf16[512,1536]{1,0:T(8,128)(2,1)}, bf16[512,1536]{1,0:T(8,128)(2,1)}, u32[]{:S(2)}, u32[]{:S(2)}) collective-permute-start(bf16[512,1536]{1,0:T(8,128)(2,1)} %multiply_convert_fusion.refs_0_), channel_id=1, source_target_pairs={{0,1},{1,0},{2,3},{3,2},{4,5},{5,4},{6,7},{7,6},{8,9},{9,8},{10,11... | collective-permute-start | bytes 4718600 | tf_op jit(solution)/shard_map/ppermute | solution.py:21
  306.1 47.5 %collective-permute-start.12 = (bf16[512,1536]{1,0:T(8,128)(2,1)}, bf16[512,1536]{1,0:T(8,128)(2,1)}, u32[]{:S(2)}, u32[]{:S(2)}) collective-permute-start(bf16[512,1536]{1,0:T(8,128)(2,1)} %collective-permute-done.11.refs_2_), channel_id=1, source_target_pairs={{0,1},{1,0},{2,3},{3,2},{4,5},{5,4},{6,7},{7,6},{8,9},{9,8},{10,11... | collective-permute-start | bytes 4718600 | tf_op jit(solution)/shard_map/ppermute | solution.py:21
  515.3 304.5 %reduce-scatter.12.cloned.1.call-start = ((), (), s32[]{:S(2)}) async-start(), calls=%async_computation.7 | async-start | bytes 4423680 | tf_op jit(solution)/shard_map/reduce_scatter | solution.py:697
  580.3 245.5 %reduce-scatter.10.cloned.1.call-start = ((), (), s32[]{:S(2)}) async-start(), calls=%async_computation.6 | async-start | bytes 4423680 | tf_op jit(solution)/shard_map/reduce_scatter | solution.py:697
  593.6 57.0 %collective-permute-start.40 = (bf16[512,1536]{1,0:T(8,128)(2,1)}, bf16[512,1536]{1,0:T(8,128)(2,1)}, u32[]{:S(2)}, u32[]{:S(2)}) collective-permute-start(bf16[512,1536]{1,0:T(8,128)(2,1)} %get-tuple-element.115), channel_id=1, source_target_pairs={{0,1},{1,0},{2,3},{3,2},{4,5},{5,4},{6,7},{7,6},{8,9},{9,8},{10,11... | collective-permute-start | bytes 4718600 | tf_op jit(solution)/shard_map/ppermute | solution.py:21
  640.6 218.9 %reduce-scatter.16.cloned.1.call-start = ((), (), s32[]{:S(2)}) async-start(), calls=%async_computation.14 | async-start | bytes 491520
  733.5 45.2 %collective-permute-start.36 = (bf16[512,1536]{1,0:T(8,128)(2,1)}, bf16[512,1536]{1,0:T(8,128)(2,1)}, u32[]{:S(2)}, u32[]{:S(2)}) collective-permute-start(bf16[512,1536]{1,0:T(8,128)(2,1)} %pad_maximum_fusion.7), channel_id=1, source_target_pairs={{0,4},{4,0},{1,5},{5,1},{2,6},{6,2},{3,7},{7,3},{8,12},{12,8},{9,1... | collective-permute-start | bytes 4718600 | tf_op jit(solution)/shard_map/ppermute | solution.py:21
  739.7 46.6 %collective-permute-start.45 = (bf16[512,1536]{1,0:T(8,128)(2,1)}, bf16[512,1536]{1,0:T(8,128)(2,1)}, u32[]{:S(2)}, u32[]{:S(2)}) collective-permute-start(bf16[512,1536]{1,0:T(8,128)(2,1)} %slice.372), channel_id=1, source_target_pairs={{0,1},{1,0},{2,3},{3,2},{4,5},{5,4},{6,7},{7,6},{8,9},{9,8},{10,11... | collective-permute-start | bytes 4718600 | tf_op jit(solution)/shard_map/ppermute | solution.py:21
  757.9 47.2 %collective-permute-start.47 = (bf16[512,1536]{1,0:T(8,128)(2,1)}, bf16[512,1536]{1,0:T(8,128)(2,1)}, u32[]{:S(2)}, u32[]{:S(2)}) collective-permute-start(bf16[512,1536]{1,0:T(8,128)(2,1)} %add_convert_fusion), channel_id=1, source_target_pairs={{0,2},{1,3},{2,0},{3,1},{4,6},{5,7},{6,4},{7,5},{8,10},{9,11},{10,... | collective-permute-start | bytes 4718600 | tf_op jit(solution)/shard_map/ppermute | solution.py:21
  778.6 63.4 %collective-permute-start.54 = (bf16[4,192,896]{2,1,0:T(8,128)(2,1)}, bf16[4,192,896]{2,1,0:T(8,128)(2,1)}, u32[]{:S(2)}, u32[]{:S(2)}) collective-permute-start(bf16[4,192,896]{2,1,0:T(8,128)(2,1)} %get-tuple-element.134), channel_id=1, source_target_pairs={{0,4},{4,0},{1,5},{5,1},{2,6},{6,2},{3,7},{7,3},{8,12},{12,8},{9,1... | collective-permute-start | bytes 4128776 | tf_op jit(solution)/shard_map/ppermute | solution.py:21
  783.4 56.1 %collective-permute-start.38 = (bf16[512,1536]{1,0:T(8,128)(2,1)}, bf16[512,1536]{1,0:T(8,128)(2,1)}, u32[]{:S(2)}, u32[]{:S(2)}) collective-permute-start(bf16[512,1536]{1,0:T(8,128)(2,1)} %fusion.13), channel_id=1, source_target_pairs={{0,0},{17,1},{10,2},{27,3},{8,8},{25,9},{18,10},{3,11},{16,16},{1,... | collective-permute-start | bytes 4718600 | tf_op jit(solution)/shard_map/ppermute | solution.py:759
  811.7 64.3 %collective-permute-start.50 = (bf16[512,1536]{1,0:T(8,128)(2,1)S(1)}, bf16[512,1536]{1,0:T(8,128)(2,1)}, u32[]{:S(2)}, u32[]{:S(2)}) collective-permute-start(bf16[512,1536]{1,0:T(8,128)(2,1)S(1)} %fusion.6), channel_id=1, source_target_pairs={{0,0},{17,1},{10,2},{27,3},{8,8},{25,9},{18,10},{3,11},{16,16},{1,... | collective-permute-start | bytes 4718600 | tf_op jit(solution)/shard_map/ppermute | solution.py:759
  819.0 44.9 %collective-permute-start.60 = (bf16[192,1152]{1,0:T(8,128)(2,1)}, bf16[192,1152]{1,0:T(8,128)(2,1)}, u32[]{:S(2)}, u32[]{:S(2)}) collective-permute-start(bf16[192,1152]{1,0:T(8,128)(2,1)} %dynamic-slice_bitcast_fusion.3), channel_id=1, source_target_pairs={{0,4},{4,0},{1,5},{5,1},{2,6},{6,2},{3,7},{7,3},{8,12},{12,8},{9,1... | collective-permute-start | bytes 1327112 | tf_op jit(solution)/shard_map/ppermute | solution.py:21
  842.0 55.6 %reduce-scatter.8.cloned.1.call-start = ((), (), s32[]{:S(2)}) async-start(), calls=%async_computation.5 | async-start | bytes 1720320 | tf_op jit(solution)/shard_map/reduce_scatter | solution.py:83
  (112 other events, 1923.5 us)
Sparse Core Ops, SparseCore 0:
  57.5 51.9 all-gather.10
  111.7 28.7 all-gather.12
  142.1 69.6 all-gather.18
  213.2 68.5 all-gather.14
  299.9 70.6 all-gather.16
  515.4 66.7 reduce-scatter.13
  584.6 66.6 reduce-scatter.11
  653.6 66.6 reduce-scatter.9
  842.1 17.4 reduce-scatter.15
  861.8 35.6 reduce-scatter.7

commit v3 on v2

--- a/solution.py
+++ b/solution.py
@@ -41,7 +41,7 @@
     scaled = gain_row * upstream
     inner_mean = jnp.mean(values * scaled, axis=-1, keepdims=True)
     grad_in = scale_inv * scaled - values * (scale_inv * scale_inv * scale_inv) * inner_mean
-    gain_grad = jnp.sum(upstream * values * scale_inv, axis=0)
+    gain_grad = jnp.sum(upstream * values * scale_inv, axis=0, keepdims=True)
     return (grad_in, gain_grad)
 
 
@@ -83,32 +83,46 @@
     return lax.psum_scatter(held, "fsdp", scatter_dimension=0, tiled=True)
 
 
+def estimate(flops, moved, transcendentals=0):
+    return pl.CostEstimate(flops=flops, bytes_accessed=moved, transcendentals=transcendentals)
+
+
+def part_spec(rows, cols, part):
+    return pl.BlockSpec((rows, cols), lambda *_: (0, part), pipeline_mode=pl.Buffered(1))
+
+
 def whole_spec(*shape, once=False):
     mode = {"pipeline_mode": pl.Buffered(1)} if once else {}
     return pl.BlockSpec(shape, lambda *_: (0,) * len(shape), **mode)
 
 
-def gate_kernel(count, *refs):
+def rows_kernel(groups, *refs):
     slot = pl.program_id(0)
-    weight, lin, stacked = refs[count:]
-
-    def run(x):
-        value = x[...]
-        stacked[...] = value
-        lin[...] = jnp.dot(value, weight[...], preferred_element_type=WIDE).astype(LOW)
-
-    for r in range(count):
-        pl.when(slot == r)(functools.partial(run, refs[r]))
-
-
-def gate_rows(rows, weight):
-    length, width = rows[0].shape
-    count, cols = len(rows), weight.shape[1]
+    weight, lin, stacked = refs[-3:]
+
+    def run(pieces):
+        start = 0
+        for piece in pieces:
+            stacked[start : start + piece.shape[0]] = piece[...]
+            start += piece.shape[0]
+        lin[...] = jnp.dot(stacked[...], weight[...], preferred_element_type=WIDE).astype(LOW)
+
+    first = 0
+    for r, pieces in enumerate(groups):
+        pl.when(slot == r)(functools.partial(run, refs[first : first + pieces]))
+        first += pieces
+
+
+def stack_rows(slots, weight, part, parts):
+    groups = [len(s) for s in slots]
+    rows = [piece for s in slots for piece in s]
+    width, length = rows[0].shape[1], sum(piece.shape[0] for piece in slots[0])
+    count, cols = len(slots), weight.shape[1] // parts
     return pl.pallas_call(
-        functools.partial(gate_kernel, count),
+        functools.partial(rows_kernel, groups),
         grid=(count,),
-        in_specs=[whole_spec(length, width, once=True)] * count
-        + [whole_spec(width, cols, once=True)],
+        in_specs=[whole_spec(*piece.shape, once=True) for piece in rows]
+        + [part_spec(width, cols, part)],
         out_specs=[
             pl.BlockSpec((length, cols), lambda s: (s, 0)),
             pl.BlockSpec((length, width), lambda s: (s, 0)),
@@ -118,10 +132,8 @@
             jax.ShapeDtypeStruct((count * length, width), LOW),
         ],
         compiler_params=pltpu.CompilerParams(vmem_limit_bytes=60 << 20),
-        cost_estimate=pl.CostEstimate(
-            flops=2 * count * length * width * cols,
-            bytes_accessed=2 * (count * length * (2 * width + cols) + width * cols),
-            transcendentals=0,
+        cost_estimate=estimate(
+            2 * count * length * width * cols, 2 * (count * length * (2 * width + cols) + width * cols)
         ),
     )(*rows, weight)
 
@@ -137,37 +149,39 @@
     grad_up[...] = (grad_hidden * silu).astype(LOW)
 
 
-def hidden_units(h, up, gate_lin, grad_hidden):
+def hidden_units(h, up, part, parts, gate_lin, grad_hidden):
     tokens, width = h.shape
-    cols = up.shape[1]
+    cols = up.shape[1] // parts
     step = math.gcd(512, tokens)
     by_row = lambda n: pl.BlockSpec((step, n), lambda i: (i, 0))
     return pl.pallas_call(
         units_kernel,
         grid=(tokens // step,),
-        in_specs=[by_row(width), whole_spec(width, cols, once=True), by_row(cols), by_row(cols)],
+        in_specs=[by_row(width), part_spec(width, cols, part), by_row(cols), by_row(cols)],
         out_specs=[by_row(cols)] * 3,
         out_shape=[jax.ShapeDtypeStruct((tokens, cols), LOW)] * 3,
         compiler_params=pltpu.CompilerParams(vmem_limit_bytes=60 << 20),
-        cost_estimate=pl.CostEstimate(
-            flops=2 * tokens * width * cols,
-            bytes_accessed=2 * (tokens * width + width * cols + 5 * tokens * cols),
-            transcendentals=tokens * cols,
+        cost_estimate=estimate(
+            2 * tokens * width * cols, 2 * (tokens * width + width * cols + 5 * tokens * cols)
         ),
     )(h, up, gate_lin, grad_hidden)
 
 
 def back_kernel(terms, *refs):
-    lefts, weights, out = refs[:terms], refs[terms:-1], refs[-1]
+    lefts, weights, outs = refs[:terms], refs[terms : 2 * terms], refs[2 * terms :]
     total = None
     for left, weight in zip(lefts, weights):
         term = dot_cols(left[...], weight[...])
         total = term if total is None else total + term
-    out[0] = total.astype(LOW)
+    for i, out in enumerate(outs):
+
+        @pl.when(pl.program_id(0) == i)
+        def _():
+            out[...] = total.astype(LOW)
 
 
 def back_rows(lefts, weights, first_slot, slots, length):
-    width = weights[0].shape[0]
+    width = weights[0][0].shape[0]
     depth = sum(left.shape[1] for left in lefts)
     return pl.pallas_call(
         functools.partial(back_kernel, len(lefts)),
@@ -175,16 +189,423 @@
         in_specs=[
             pl.BlockSpec((length, left.shape[1]), lambda s: (first_slot + s, 0)) for left in lefts
         ]
-        + [whole_spec(*w.shape, once=True) for w in weights],
-        out_specs=pl.BlockSpec((1, length, width), lambda s: (s, 0, 0)),
-        out_shape=jax.ShapeDtypeStruct((slots, length, width), LOW),
+        + [part_spec(width, w.shape[1] // parts, part) for w, part, parts in weights],
+        out_specs=[whole_spec(length, width)] * slots,
+        out_shape=[jax.ShapeDtypeStruct((length, width), LOW)] * slots,
         compiler_params=pltpu.CompilerParams(vmem_limit_bytes=60 << 20),
-        cost_estimate=pl.CostEstimate(
-            flops=2 * slots * length * width * depth,
-            bytes_accessed=2 * (slots * length * (width + depth) + width * depth),
-            transcendentals=0,
+        cost_estimate=estimate(
+            2 * slots * length * width * depth,
+            2 * (slots * length * (width + depth) + width * depth),
         ),
-    )(*lefts, *weights)
+    )(*lefts, *[w for w, _, _ in weights])
+
+
+MESH_ID = pl.DeviceIdType.MESH
+
+
+def meet(partners):
+    barrier = pltpu.get_barrier_semaphore()
+    for partner in partners:
+        pl.semaphore_signal(barrier, inc=1, device_id=partner, device_id_type=MESH_ID)
+    pl.semaphore_wait(barrier, len(partners))
+
+
+def partners_of():
+    tensor_rank, ctx_rank = lax.axis_index("tp"), lax.axis_index("ctx")
+    return {"tp": tensor_rank ^ 1}, {"tp": tensor_rank ^ 2}, {"ctx": ctx_rank ^ 1}
+
+
+def collect_kernel(
+    slots, gate, up, weight_gate, weight_up, left, right, total, grad, parts, core_in, across_in,
+    last_in, held, send, recv, load
+):
+    step = pl.program_id(0)
+    steps = pl.num_programs(0)
+    core, far, side = partners_of()
+    half = total.shape[0] // 2
+
+    def remote(source, target, index, partner):
+        return pltpu.make_async_remote_copy(
+            source, target, send.at[index], recv.at[index], device_id=partner, device_id_type=MESH_ID
+        )
+
+    cores = [remote(parts.at[7 - 2 * k], core_in.at[k], k, core) for k in range(4)]
+    across = [
+        remote(parts.at[6, pl.ds(0, half)], across_in.at[0], 4, far),
+        remote(parts.at[6, pl.ds(half, half)], across_in.at[1], 5, side),
+    ]
+    lasts = [
+        remote(parts.at[2], last_in.at[0], 6, far),
+        remote(parts.at[4, pl.ds(half, half)], last_in.at[1, pl.ds(half, half)], 7, side),
+        remote(parts.at[4, pl.ds(0, half)], last_in.at[1, pl.ds(0, half)], 8, side),
+    ]
+    loading = pltpu.make_async_copy(right, held, load)
+
+    @pl.when(step == 0)
+    def _():
+        loading.start()
+        meet((core, far, side))
+
+    @pl.when(step < slots)
+    def _():
+        part = dot_cols(gate[...], weight_gate[...]) + dot_cols(up[...], weight_up[...])
+        parts[slots - 1 - step] = part.astype(LOW)
+
+        @pl.when(step == slots - 1)
+        def _():
+            total[...] = part
+
+    for k in range(4):
+        pl.when(step == 2 * k)(cores[k].start)
+
+    def add(slot, rows, value):
+        parts[slot, rows] = (parts[slot, rows].astype(WIDE) + value.astype(WIDE)).astype(LOW)
+
+    whole, low, high = slice(None), pl.ds(0, half), pl.ds(half, half)
+
+    @pl.when(step == 1)
+    def _():
+        cores[0].wait_recv()
+        add(6, whole, core_in[0])
+        for copy in across:
+            copy.start()
+
+    @pl.when(step == 3)
+    def _():
+        cores[1].wait_recv()
+        add(4, whole, core_in[1])
+        lasts[1].start()
+
+    @pl.when(step == 5)
+    def _():
+        cores[2].wait_recv()
+        add(2, whole, core_in[2])
+        across[1].wait_recv()
+        add(2, high, across_in[1])
+        lasts[0].start()
+        across[0].wait_recv()
+        add(4, low, across_in[0])
+        lasts[2].start()
+
+    @pl.when(step >= slots)
+    def _():
+        pl.when(step == slots)(loading.wait)
+        grad[...] = dot_rows(left[...], held[...]).astype(LOW)
+
+    @pl.when(step == steps - 1)
+    def _():
+        cores[3].wait_recv()
+        for copy in lasts:
+            copy.wait_recv()
+        total[...] += (
+            core_in[3].astype(WIDE) + last_in[0].astype(WIDE) + last_in[1].astype(WIDE)
+        )
+        for copy in (*cores, *across, *lasts):
+            copy.wait_send()
+
+
+def collect_back(grad_gate, grad_up, weight, left, right, length):
+    tokens, cols = grad_gate.shape
+    width = weight.shape[0]
+    slots, tile = tokens // length, 256
+    tiles = width // tile
+    row = pl.BlockSpec((length, cols), lambda i: (jnp.maximum(slots - 1 - i, 0), 0))
+    column = lambda i: jnp.clip(i - slots, 0, tiles - 1)
+    return pl.pallas_call(
+        functools.partial(collect_kernel, slots),
+        grid=(slots + tiles,),
+        in_specs=[
+            row,
+            row,
+            part_spec(width, cols, 0),
+            part_spec(width, cols, 1),
+            pl.BlockSpec((tokens, tile), lambda i: (0, column(i))),
+            pl.BlockSpec(memory_space=pl.ANY),
+        ],
+        out_specs=[
+            pl.BlockSpec((length, width), lambda i: (0, 0)),
+            pl.BlockSpec((tile, cols), lambda i: (column(i), 0)),
+        ],
+        out_shape=[
+            jax.ShapeDtypeStruct((length, width), WIDE),
+            jax.ShapeDtypeStruct((width, cols), LOW),
+        ],
+        scratch_shapes=[
+            pltpu.VMEM((slots, length, width), LOW),
+            pltpu.VMEM((4, length, width), LOW),
+            pltpu.VMEM((2, length // 2, width), LOW),
+            pltpu.VMEM((2, length, width), LOW),
+            pltpu.VMEM((tokens, cols), LOW),
+            pltpu.SemaphoreType.DMA((9,)),
+            pltpu.SemaphoreType.DMA((9,)),
+            pltpu.SemaphoreType.DMA,
+        ],
+        compiler_params=pltpu.CompilerParams(
+            vmem_limit_bytes=63 << 20, collective_id=1, has_side_effects=True
+        ),
+        cost_estimate=estimate(6 * tokens * width * cols, 10 * tokens * cols),
+    )(grad_gate, grad_up, weight, weight, left, right)
+
+
+def remote_copy(send, recv):
+    def make(source, target, index, partner):
+        return pltpu.make_async_remote_copy(
+            source, target, send.at[index], recv.at[index], device_id=partner, device_id_type=MESH_ID
+        )
+
+    return make
+
+
+def branch_kernel(
+    slots, tiles, total, middle, own_grad, gain, hid, weight, turned, gate, grad_middle, gain_grad,
+    gate_out, branch, mlp_own, mlp_far, mlp_side, mlp_first, mlp_second, own, parts, core_in, held,
+    send, recv, load
+):
+    step = pl.program_id(0)
+    core, far, _ = partners_of()
+    half = own.shape[0] // 2
+    remote = remote_copy(send, recv)
+    to_far = remote(own, branch.at[2], 0, far)
+    to_near = remote(own, branch.at[1], 1, core)
+    to_cross = remote(branch.at[2], branch.at[3], 2, core)
+    keep = pltpu.make_async_copy(own, branch.at[0], load.at[0])
+    loading = pltpu.make_async_copy(gate, held, load.at[1])
+    cores = [remote(parts.at[7 - 2 * k], core_in.at[k], 3 + k, core) for k in range(4)]
+    store = lambda source, target, i: pltpu.make_async_copy(source, target, load.at[i])
+    stores = [
+        [
+            store(parts.at[6, pl.ds(0, half)], mlp_first, 2),
+            store(parts.at[6, pl.ds(half, half)], mlp_second, 3),
+        ],
+        [store(parts.at[4], mlp_side, 4)],
+        [store(parts.at[2], mlp_far, 5)],
+        [store(parts.at[0], mlp_own, 6)],
+    ]
+
+    @pl.when(step == 0)
+    def _():
+        loading.start()
+        meet((core, far))
+        values, upstream = middle[...], total[...]
+        inverse = lax.rsqrt(jnp.mean(values * values, axis=-1, keepdims=True) + EPS)
+        grad_in, gain_grad[...] = norm_backward(values, inverse, gain[...], upstream)
+        grad_in = own_grad[...].astype(WIDE) + grad_in
+        grad_middle[...] = grad_in
+        own[...] = grad_in.astype(LOW)
+        for copy in (to_far, to_near, keep):
+            copy.start()
+
+    @pl.when(step < slots)
+    def _():
+        parts[slots - 1 - step] = dot_cols(hid[...], weight[...]).astype(LOW)
+
+    for k in range(4):
+        pl.when(step == 2 * k)(cores[k].start)
+
+        def finish(k=k):
+            slot = 6 - 2 * k
+            cores[k].wait_recv()
+            parts[slot] = (parts[slot].astype(WIDE) + core_in[k].astype(WIDE)).astype(LOW)
+            for copy in stores[k]:
+                copy.start()
+
+        pl.when(step == 2 * k + 1)(finish)
+
+    @pl.when(step >= slots)
+    def _():
+        pl.when(step == slots)(loading.wait)
+        gate_out[...] = dot_rows(turned[...], held[...]).astype(LOW)
+
+    @pl.when(step == slots + tiles - 2)
+    def _():
+        to_far.wait_recv()
+        to_cross.start()
+
+    @pl.when(step == slots + tiles - 1)
+    def _():
+        to_near.wait_recv()
+        to_cross.wait_recv()
+        keep.wait()
+        for group in stores:
+            for copy in group:
+                copy.wait()
+        for copy in (to_far, to_near, to_cross, *cores):
+            copy.wait_send()
+
+
+ANYWHERE = pl.BlockSpec(memory_space=pl.ANY)
+
+
+def spread_branch(total, middle, own_grad, gain, hid, weight, rows, grad_gate):
+    length, width = total.shape
+    tokens, cols = grad_gate.shape
+    slots, tile = tokens // length, 256
+    tiles = width // tile
+    once = whole_spec(length, width, once=True)
+    column = lambda i: jnp.clip(i - slots, 0, tiles - 1)
+    part = jax.ShapeDtypeStruct((length, width), LOW)
+    piece = jax.ShapeDtypeStruct((length // 2, width), LOW)
+    return pl.pallas_call(
+        functools.partial(branch_kernel, slots, tiles),
+        grid=(slots + tiles,),
+        in_specs=[
+            once,
+            once,
+            once,
+            whole_spec(1, width),
+            pl.BlockSpec((length, cols), lambda i: (jnp.maximum(slots - 1 - i, 0), 0)),
+            part_spec(width, cols, 0),
+            pl.BlockSpec((tokens, tile), lambda i: (0, column(i))),
+            ANYWHERE,
+        ],
+        out_specs=[
+            whole_spec(length, width, once=True),
+            whole_spec(1, width),
+            pl.BlockSpec((tile, cols), lambda i: (column(i), 0)),
+        ]
+        + [ANYWHERE] * 6,
+        out_shape=[
+            jax.ShapeDtypeStruct((length, width), WIDE),
+            jax.ShapeDtypeStruct((1, width), WIDE),
+            jax.ShapeDtypeStruct((width, cols), LOW),
+            jax.ShapeDtypeStruct((4, length, width), LOW),
+            part,
+            part,
+            part,
+            piece,
+            piece,
+        ],
+        scratch_shapes=[
+            pltpu.VMEM((length, width), LOW),
+            pltpu.VMEM((slots, length, width), LOW),
+            pltpu.VMEM((4, length, width), LOW),
+            pltpu.VMEM((tokens, cols), LOW),
+            pltpu.SemaphoreType.DMA((7,)),
+            pltpu.SemaphoreType.DMA((7,)),
+            pltpu.SemaphoreType.DMA((7,)),
+        ],
+        compiler_params=pltpu.CompilerParams(
+            vmem_limit_bytes=63 << 20, collective_id=2, has_side_effects=True
+        ),
+        cost_estimate=estimate(4 * tokens * width * cols, 10 * tokens * cols),
+    )(total, middle, own_grad, gain, hid, weight, rows, grad_gate)
+
+
+def line_kernel(
+    slots, tiles, line, weight, own_in, grad_middle, gain, turned, up, rows_one, branch, line_all,
+    mixed, share, gain_grad, up_out, attn_out, bias_out, parts, core_in, far_in, total, held, send,
+    recv, load
+):
+    step = pl.program_id(0)
+    core, far, _ = partners_of()
+    remote = remote_copy(send, recv)
+    cores = [remote(parts.at[3 - 2 * k], core_in.at[k], k, core) for k in range(2)]
+    to_far = remote(parts.at[2], far_in, 2, far)
+    loading = pltpu.make_async_copy(up, held, load)
+
+    @pl.when(step == 0)
+    def _():
+        loading.start()
+        meet((core, far))
+
+    @pl.when(step < slots)
+    def _():
+        part = dot_cols(line[...], weight[...])
+        parts[slots - 1 - step] = part.astype(LOW)
+
+        @pl.when(step == slots - 1)
+        def _():
+            total[...] = part
+
+    for k in range(2):
+        pl.when(step == 2 * k)(cores[k].start)
+
+    @pl.when(step == 1)
+    def _():
+        cores[0].wait_recv()
+        parts[2] = (parts[2].astype(WIDE) + core_in[0].astype(WIDE)).astype(LOW)
+        to_far.start()
+
+    @pl.when(step == slots - 1)
+    def _():
+        bias_out[...] = jnp.sum(line_all[...].astype(WIDE), axis=0, keepdims=True)
+
+    @pl.when(step >= slots)
+    def _():
+        pl.when(step == slots)(loading.wait)
+        up_out[...] = dot_rows(turned[...], held[...]).astype(LOW)
+        cols = line_all.shape[1]
+        attn_out[:, :cols] = dot_rows(rows_one[...], line_all[...]).astype(LOW)
+        attn_out[:, cols:] = dot_rows(branch[...], mixed[...]).astype(LOW)
+
+    @pl.when(step == slots + tiles - 1)
+    def _():
+        cores[1].wait_recv()
+        to_far.wait_recv()
+        upstream = total[...] + core_in[1].astype(WIDE) + far_in[...].astype(WIDE)
+        values = own_in[...].astype(WIDE)
+        inverse = lax.rsqrt(jnp.mean(values * values, axis=-1, keepdims=True) + EPS)
+        grad_in, gain_grad[...] = norm_backward(values, inverse, gain[...], upstream)
+        share[...] = (grad_middle[...] + grad_in).astype(LOW)
+        for copy in (*cores, to_far):
+            copy.wait_send()
+
+
+def finish_rows(line, weight, own_in, grad_middle, gain, rows_two, grad_up, rows_one, branch, mixed):
+    length, width = own_in.shape
+    tokens, cols = grad_up.shape
+    near_tokens, line_cols = line.shape
+    slots, tile = near_tokens // length, 256
+    tiles = width // tile
+    once = whole_spec(length, width, once=True)
+    column = lambda i: jnp.clip(i - slots, 0, tiles - 1)
+    by_column = lambda n: pl.BlockSpec((n, tile), lambda i: (0, column(i)))
+    attn_cols = line_cols + mixed.shape[1]
+    return pl.pallas_call(
+        functools.partial(line_kernel, slots, tiles),
+        grid=(slots + tiles,),
+        in_specs=[
+            pl.BlockSpec((length, line_cols), lambda i: (jnp.maximum(slots - 1 - i, 0), 0)),
+            whole_spec(width, line_cols, once=True),
+            once,
+            once,
+            whole_spec(1, width),
+            by_column(tokens),
+            ANYWHERE,
+            by_column(near_tokens),
+            by_column(near_tokens),
+            whole_spec(near_tokens, line_cols, once=True),
+            whole_spec(*mixed.shape, once=True),
+        ],
+        out_specs=[
+            whole_spec(length, width),
+            whole_spec(1, width),
+            pl.BlockSpec((tile, cols), lambda i: (column(i), 0)),
+            pl.BlockSpec((tile, attn_cols), lambda i: (column(i), 0)),
+            whole_spec(1, line_cols),
+        ],
+        out_shape=[
+            jax.ShapeDtypeStruct((length, width), LOW),
+            jax.ShapeDtypeStruct((1, width), WIDE),
+            jax.ShapeDtypeStruct((width, cols), LOW),
+            jax.ShapeDtypeStruct((width, attn_cols), LOW),
+            jax.ShapeDtypeStruct((1, line_cols), WIDE),
+        ],
+        scratch_shapes=[
+            pltpu.VMEM((slots, length, width), LOW),
+            pltpu.VMEM((2, length, width), LOW),
+            pltpu.VMEM((length, width), LOW),
+            pltpu.VMEM((length, width), WIDE),
+            pltpu.VMEM((tokens, cols), LOW),
+            pltpu.SemaphoreType.DMA((3,)),
+            pltpu.SemaphoreType.DMA((3,)),
+            pltpu.SemaphoreType.DMA,
+        ],
+        compiler_params=pltpu.CompilerParams(
+            vmem_limit_bytes=63 << 20, collective_id=3, has_side_effects=True
+        ),
+        cost_estimate=estimate(2 * tokens * width * cols, 10 * tokens * cols),
+    )(line, weight, own_in, grad_middle, gain, rows_two, grad_up, rows_one, branch, line, mixed)
 
 
 def turn(values, cosine, sine_signed):
@@ -196,14 +617,19 @@
 
 
 def project_kernel(
-    heads, head_dim, x0, x1, x2, x3, gain, weight, bias, cosine, sine, h_out, q_out, k_out, v_out
+    heads, head_dim, x0, x1, x2, x3, gains, weight, bias, cosine, sine, h_out, q_out, k_out, v_out, gain
 ):
     slot = pl.program_id(0)
+
+    @pl.when(slot == 0)
+    def _():
+        gain[...] = gains[...].astype(WIDE).T[:8]
+
 
     def run(x_ref):
         x = x_ref[...].astype(WIDE)
         scale_inv = lax.rsqrt(jnp.mean(x * x, axis=-1, keepdims=True) + EPS)
-        normed = (x * scale_inv * gain[...]).astype(LOW)
+        normed = (x * scale_inv * gain[0:1]).astype(LOW)
         h_out[0] = normed
         lin = jnp.dot(normed, weight[...], preferred_element_type=WIDE) + bias[...]
         cos, sin = cosine[0], sine[0]
@@ -219,7 +645,7 @@
         pl.when(slot == r)(functools.partial(run, x_ref))
 
 
-def project(rows, gain, weight, bias, cosine, sine, heads, head_dim):
+def project(rows, held, bias, cosine, sine, heads, head_dim):
     length, width = rows[0].shape
     count = len(rows)
     cols = (heads + 2) * head_dim
@@ -229,7 +655,7 @@
         functools.partial(project_kernel, heads, head_dim),
         grid=(count,),
         in_specs=[whole(length, width)] * count
-        + [whole(1, width), whole(width, cols), whole(1, cols)]
+        + [part_spec(width, 128, cols // 128), part_spec(width, cols, 0), whole(1, cols)]
         + [by_slot(length, head_dim)] * 2,
         out_specs=[
             by_slot(length, width),
@@ -243,13 +669,14 @@
             jax.ShapeDtypeStruct((count, length, head_dim), LOW),
             jax.ShapeDtypeStruct((count, length, head_dim), LOW),
         ],
+        scratch_shapes=[pltpu.VMEM((8, width), WIDE)],
         compiler_params=pltpu.CompilerParams(vmem_limit_bytes=56 << 20),
         cost_estimate=pl.CostEstimate(
             flops=2 * count * length * width * cols,
             bytes_accessed=count * length * (2 * width + cols) * 2 + width * cols * 2,
             transcendentals=0,
         ),
-    )(*rows, gain, weight, bias, cosine, sine)
+    )(*rows, held, held, bias, cosine, sine)
 
 
 def row_blocks(length):
@@ -273,7 +700,9 @@
     return lax.dot_general(left, right, (((0,), (0,)), ((), ())), preferred_element_type=WIDE)
 
 
-def attend_kernel(heads, head_dim, scale, first, total_slots, info, q, k_past, v_past, k_own, v_own, out, lse):
+def attend_kernel(
+    heads, head_dim, scale, first, total_slots, info, q, k_past, v_past, k_own, v_own, weight, out, lse, *parts
+):
     length, offset = info[first + pl.program_id(0)], info[total_slots]
     past = k_past.shape[1]
     for start, rows in row_blocks(q.shape[1]):
@@ -296,9 +725,15 @@
             ) + jnp.dot((e_own * inverse).astype(LOW), v_own[0, :keys], preferred_element_type=WIDE)
             out[0, here, cols] = mixed.astype(LOW)
             lse[0, here, h : h + 1] = top + jnp.log(total)
-
-
-def attend_forward(info, q, k_past, v_past, k_own, v_own, heads, head_dim, scale, first, count):
+        rows_out = dot_cols(out[0, here], weight[...]).astype(LOW)
+        for i, part in enumerate(parts):
+
+            @pl.when(pl.program_id(0) == i)
+            def _():
+                part[here] = rows_out
+
+
+def attend_forward(info, q, k_past, v_past, k_own, v_own, weight, heads, head_dim, scale, first, count):
     _, length, width = q.shape
     past = k_past.shape[1]
     by_slot = lambda *shape: pl.BlockSpec((1, *shape), lambda s, info: (first + s,) + (0,) * len(shape))
@@ -315,18 +750,19 @@
                 by_slot(past, head_dim),
                 by_slot(length, head_dim),
                 by_slot(length, head_dim),
+                whole_spec(*weight.shape, once=True),
             ],
-            out_specs=[out_slot(length, width), out_slot(length, 128)],
+            out_specs=[out_slot(length, width), out_slot(length, 128)]
+            + [whole_spec(length, weight.shape[0])] * count,
         ),
         out_shape=[
             jax.ShapeDtypeStruct((count, length, width), LOW),
             jax.ShapeDtypeStruct((count, length, 128), WIDE),
-        ],
+        ]
+        + [jax.ShapeDtypeStruct((length, weight.shape[0]), LOW)] * count,
         compiler_params=pltpu.CompilerParams(vmem_limit_bytes=56 << 20),
-        cost_estimate=pl.CostEstimate(
-            flops=4 * keys * head_dim, bytes_accessed=4 * count * length * width, transcendentals=keys
-        ),
-    )(info, q, k_past, v_past, k_own, v_own)
+        cost_estimate=estimate(4 * keys * head_dim, 4 * count * length * width, keys),
+    )(info, q, k_past, v_past, k_own, v_own, weight)
 
 
 def attend_back_kernel(
@@ -447,9 +883,7 @@
             jax.ShapeDtypeStruct((count, length, head_dim), WIDE),
         ],
         compiler_params=pltpu.CompilerParams(vmem_limit_bytes=56 << 20),
-        cost_estimate=pl.CostEstimate(
-            flops=10 * keys * head_dim, bytes_accessed=8 * count * length * width, transcendentals=keys
-        ),
+        cost_estimate=estimate(10 * keys * head_dim, 8 * count * length * width, keys),
     )(info, q, k_past, v_past, k_own, v_own, grad, lse, cosine, sine)
 
 
@@ -546,15 +980,13 @@
         small_both = in_order(small, from_partner(after(small, outgoing), "ctx", 1))
         leaving_units = jnp.concatenate([cut(w, 1 - ctx_rank) for w in shards], axis=1)
         arriving_units = from_partner(after(leaving_units, small), "ctx", 1)
-        unit_both = [
-            in_order(cut(w, ctx_rank), arriving_units[:, i * half_units : (i + 1) * half_units])
-            for i, w in enumerate(shards)
-        ]
+        own_units = jnp.concatenate([cut(w, ctx_rank) for w in shards], axis=1)
+        unit_both = in_order(own_units, arriving_units)
     else:
         all_rows = lambda shard, *earlier: lax.all_gather(
             shard, ("fsdp", "ctx"), axis=0, tiled=True
         )
-        small_both, unit_both = small, shards
+        small_both, unit_both, half_units = small, jnp.concatenate(shards, axis=1), units_pad
     far_in = from_partner(own_in, "tp", 2)
     near_in = from_partner(own_in, "tp", 1)
     cross_in = from_partner(far_in, "tp", 1)
@@ -571,49 +1003,41 @@
     sine = jnp.sin(angles) * jnp.where(lane < head_dim // 2, -1.0, 1.0)
     grad_slots = [lax.dynamic_index_in_dim(cotangent, s, 0, keepdims=False) for s in slot_now]
 
-    near_full = all_rows(small_both[..., :near_cols], own_in)
-    output_full = all_rows(small_both[..., near_cols:], far_in)
-    down_full = all_rows(unit_both[0], cross_in)
+    near_full = all_rows(small_both, own_in)
+    down_full = all_rows(unit_both[..., :half_units], cross_in)
+    gate_up_full = all_rows(unit_both[..., half_units:], cross_in)
     project_full = near_full[:, : query_cols + head_width]
-    gains_now = near_full[:, query_cols + head_width :][:, :2].astype(WIDE).T
+    output_full = near_full[:, near_cols:]
     bias_head = lax.dynamic_slice_in_dim(bias_keyval, head_pair * 2, 2, axis=0)
     bias_row = jnp.concatenate([bias_query.reshape(1, -1), bias_head.reshape(1, -1)], axis=1).astype(WIDE)
     normed_one, query_rot, key_own, value_own = project(
         (own_in, near_in, far_in, cross_in),
-        gains_now[0:1],
-        project_full,
+        near_full,
         bias_row,
         cosine,
         sine,
         heads,
         head_dim,
     )
-    gate_full = all_rows(unit_both[1], query_rot)
+    gains_now = near_full[:, query_cols + head_width : near_cols][:, :2].astype(WIDE).T
     if split:
         key_past, value_past = lax.ppermute((key_own, value_own), "ctx", [(0, 1)])
         grad_pair = after(jnp.stack([grad_slots[0], grad_slots[2]]), value_past)
         other_pair = from_partner(grad_pair, "ctx", 1)
-        cross_pair = from_partner(other_pair, "tp", 1)
-        others = [other_pair[0], cross_pair[0], other_pair[1], cross_pair[1]]
+        cross_pair = functools.partial(from_partner, axis="tp", apart=1)
     else:
         key_past = lax.all_gather(key_own, "ctx", axis=1, tiled=True)
         value_past = lax.all_gather(value_own, "ctx", axis=1, tiled=True)
-        others = []
     attend = lambda first, *held: attend_forward(
-        info, query_rot, *held, key_own, value_own, heads, head_dim, scale, first, 2
+        info, query_rot, *held, key_own, value_own, output_full, heads, head_dim, scale, first, 2
     )
     in_share = own_in.astype(WIDE)
 
-    mixed_far, lse_far = attend(2, key_past, value_past)
-    attn_far = contract_cols(mixed_far.reshape(-1, query_cols), output_full, LOW)
-    attn_far = attn_far.reshape(2, local_len, model_width)
+    mixed_far, lse_far, *attn_far = attend(2, key_past, value_past)
     attn_wide = collect_far(attn_far[0], attn_far[1])
     attn_got = from_partner(attn_wide, "tp", 2)
-    mixed_near, lse_near = attend(0, after(key_past, attn_wide), value_past)
-    attn_near = contract_cols(mixed_near.reshape(-1, query_cols), output_full, LOW)
-    attn_near = attn_near.reshape(2, local_len, model_width)
+    mixed_near, lse_near, *attn_near = attend(0, after(key_past, attn_wide), value_past)
     attn_core = from_partner(attn_near[1], "tp", 1)
-    up_full = all_rows(unit_both[2], attn_near)
     middle_share = (
         in_share
         + attn_near[0].astype(WIDE)
@@ -624,79 +1048,81 @@
     normed_share = (middle_share * inv_two * gains_now[1]).astype(LOW)
     half_len = local_len // 2
 
-    def spread_all(own, then):
+    others = []
+    if split:
+        cross_pair = cross_pair(after(other_pair, normed_share))
+        others = [other_pair[0], cross_pair[0], other_pair[1], cross_pair[1]]
+
+    grad_hidden, grad_rows = stack_rows(
+        [(after(grad_slots[0], normed_share),)] + [(g,) for g in grad_slots[1:] + others], down_full, 0, 1
+    )
+
+    def spread_all(own):
         far = from_partner(own, "tp", 2)
         near = from_partner(own, "tp", 1)
         if not split:
-            return (own, near, far, from_partner(far, "tp", 1)), then()
+            return (own, near, far, from_partner(far, "tp", 1))
         side = from_partner(own, "ctx", 1)
-        between = then()
-        diagonal = (
-            from_partner(far[:half_len], "ctx", 1),
-            from_partner(side[half_len:], "tp", 2),
-        )
-        diagonal = jnp.concatenate(diagonal, axis=0)
-        cores = [from_partner(v, "tp", 1) for v in (far, side, diagonal)]
-        return (own, near, far, cores[0], side, cores[1], diagonal, cores[2]), between
-
-    grad_rows = jnp.concatenate(grad_slots + others, axis=0)
-    normed_rows, grad_hidden = spread_all(
-        normed_share, lambda: product(after(grad_rows, normed_share), down_full, LOW)
+        held = after(far, grad_hidden), after(side, grad_hidden)
+        across = from_partner(held[0][:half_len], "ctx", 1), from_partner(held[1][half_len:], "tp", 2)
+        cores = [from_partner(v, "tp", 1) for v in (*held, *across)]
+        return (own, near, far, cores[0], side, cores[1], *across, *cores[2:])
+
+    def in_slots(rows):
+        if not split:
+            return [(row,) for row in rows]
+        return [(row,) for row in rows[:6]] + [rows[6:8], rows[8:]]
+
+    gate_lin, normed_two = stack_rows(in_slots(spread_all(normed_share)), gate_up_full, 0, 2)
+    hidden_act, grad_gate, grad_up = hidden_units(
+        normed_two, gate_up_full, 1, 2, gate_lin, grad_hidden
     )
-    gate_lin, normed_two = gate_rows(normed_rows, gate_full)
-    hidden_act, grad_gate, grad_up = hidden_units(normed_two, up_full, gate_lin, grad_hidden)
 
     def collect_all(lefts, weights, *earlier):
         lefts = list(lefts)
         lefts[0] = after(lefts[0], *earlier)
-        if split:
-            last = back_rows(lefts, weights, 6, 2, local_len)
-            diagonal = collect_far(last[0], last[1])
-            to_far = from_partner(diagonal[:half_len], "tp", 2)
-            to_side = from_partner(diagonal[half_len:], "ctx", 1)
-            lefts[0] = after(lefts[0], diagonal)
-            middle = back_rows(lefts, weights, 2, 4, local_len)
-            core_far, core_side = (from_partner(middle[i], "tp", 1) for i in (1, 3))
-            far = middle[0].astype(WIDE) + core_far.astype(WIDE)
-            side = middle[2].astype(WIDE) + core_side.astype(WIDE)
-            side = jnp.concatenate(
-                [side[:half_len] + to_far.astype(WIDE), side[half_len:]], axis=0
-            ).astype(LOW)
-            far = jnp.concatenate(
-                [far[:half_len], far[half_len:] + to_side.astype(WIDE)], axis=0
-            ).astype(LOW)
-            got = [from_partner(far, "tp", 2), from_partner(side, "ctx", 1)]
-            lefts[0] = after(lefts[0], far, side)
-        else:
-            last = back_rows(lefts, weights, 2, 2, local_len)
-            got = [from_partner(collect_far(last[0], last[1]), "tp", 2)]
+        last = back_rows(lefts, weights, 2, 2, local_len)
+        got = [from_partner(collect_far(last[0], last[1]), "tp", 2)]
         first = back_rows(lefts, weights, 0, 2, local_len)
         got.append(from_partner(first[1], "tp", 1))
 
         def finish():
             return sum((v.astype(WIDE) for v in got), first[0].astype(WIDE))
 
-        return first, finish
-
-    first_back, finish_back = collect_all((grad_gate, grad_up), (gate_full, up_full))
-    down_grad = contract_rows(after(grad_rows, first_back), hidden_act, LOW)
-    gate_grad = contract_rows(normed_two, after(grad_gate, down_grad), LOW)
-    grad_two_share = finish_back()
-    grad_norm_two, gain_two = norm_backward(middle_share, inv_two, gains_now[1], grad_two_share)
-    grad_middle = grad_slots[0].astype(WIDE) + grad_norm_two
-    branch_own = grad_middle.astype(LOW)
-    branch_far = from_partner(branch_own, "tp", 2)
-    branch_near = from_partner(branch_own, "tp", 1)
-    branch_cross = from_partner(branch_far, "tp", 1)
-    grad_branch = jnp.concatenate([branch_own, branch_near, branch_far, branch_cross], axis=0)
-    up_grad = contract_rows(normed_two, after(grad_up, branch_own), LOW)
-
-    def scatter_units(grad):
-        if not split:
-            return scatter_sum(grad, ctx_rank, LOW)
-        return lax.psum_scatter(grad, "fsdp", scatter_dimension=0, tiled=True)
-
-    unit_sums = [scatter_units(g) for g in (down_grad, gate_grad, up_grad)]
+        return first[0], finish
+
+    if split:
+        grad_two_share, down_grad = collect_back(
+            grad_gate, grad_up, gate_up_full, grad_rows, hidden_act, local_len
+        )
+        grad_middle, gain_two, gate_grad, grad_branch, *mlp = spread_branch(
+            grad_two_share,
+            middle_share,
+            grad_slots[0],
+            gains_now[1:2],
+            hidden_act,
+            down_full,
+            normed_two,
+            grad_gate,
+        )
+        grad_branch = grad_branch.reshape(token_count, model_width)
+    else:
+        first_back, finish_back = collect_all(
+            (grad_gate, grad_up), ((gate_up_full, 0, 2), (gate_up_full, 1, 2))
+        )
+        down_grad = contract_rows(after(grad_rows, first_back), hidden_act, LOW)
+        gate_grad = contract_rows(normed_two, after(grad_gate, down_grad), LOW)
+        grad_two_share = finish_back()
+        grad_norm_two, gain_two = norm_backward(
+            middle_share, inv_two, gains_now[1], grad_two_share
+        )
+        grad_middle = grad_slots[0].astype(WIDE) + grad_norm_two
+        branch_own = grad_middle.astype(LOW)
+        branch_far = from_partner(branch_own, "tp", 2)
+        branch_near = from_partner(branch_own, "tp", 1)
+        branch_cross = from_partner(branch_far, "tp", 1)
+        grad_branch = jnp.concatenate([branch_own, branch_near, branch_far, branch_cross], axis=0)
+        up_grad = contract_rows(normed_two, after(grad_up, branch_own), LOW)
 
     grad_mixed = product(grad_branch, output_full, LOW)
     mixed_flat = jnp.concatenate([mixed_near, mixed_far], axis=0).reshape(token_count, query_cols)
@@ -732,28 +1158,63 @@
         project_full, query_cols + parity * head_dim, head_dim, axis=1
     )
     back_full = jnp.concatenate([project_full[:, :query_cols], own_weight], axis=1)
-    half = token_count // 2
-    line_far = contract_cols(line_grad[half:], back_full, LOW).reshape(2, local_len, model_width)
-    line_near = contract_cols(line_grad[:half], back_full, LOW).reshape(2, local_len, model_width)
-    line_wide = collect_far(line_far[0], line_far[1])
-    line_got = from_partner(line_wide, "tp", 2)
-    line_core = from_partner(line_near[1], "tp", 1)
-
-    first_mlp, finish_mlp = collect_all((hidden_act,), (down_full,), up_grad, branch_far)
-    block_share = (middle_share + finish_mlp()).astype(LOW)
-
-    grad_one_share = line_near[0].astype(WIDE) + line_core.astype(WIDE) + line_got.astype(WIDE)
-    inv_one = lax.rsqrt(jnp.mean(in_share * in_share, axis=-1, keepdims=True) + EPS)
-    grad_norm_one, gain_one = norm_backward(in_share, inv_one, gains_now[0], grad_one_share)
-    input_share = (grad_middle + grad_norm_one).astype(LOW)
-
     normed_flat = normed_one.reshape(token_count, model_width)
-    late = after(line_grad, line_wide, line_near)
-    attn_grad = jnp.concatenate(
-        [contract_rows(normed_flat, late, LOW), contract_rows(grad_branch, mixed_flat, LOW)], axis=1
-    )
-    bias_grad = jnp.sum(late.astype(WIDE), axis=0)
-    attn_end = scatter_sum(attn_grad, ctx_rank, LOW, input_share)
+    if split:
+        mlp_own, mlp_far, mlp_side, mlp_first, mlp_second = mlp
+        got_first = from_partner(mlp_first, "tp", 2).astype(WIDE)
+        got_second = from_partner(mlp_second, "ctx", 1).astype(WIDE)
+        add_half = lambda rows, low, high: jnp.concatenate(
+            [
+                rows[:half_len] if low is None else (rows[:half_len].astype(WIDE) + low).astype(LOW),
+                rows[half_len:] if high is None else (rows[half_len:].astype(WIDE) + high).astype(LOW),
+            ],
+            axis=0,
+        )
+        mlp_sum = (
+            mlp_own.astype(WIDE)
+            + from_partner(add_half(mlp_far, None, got_second), "tp", 2).astype(WIDE)
+            + from_partner(add_half(mlp_side, got_first, None), "ctx", 1).astype(WIDE)
+        )
+        block_share = (middle_share + mlp_sum).astype(LOW)
+        input_share, gain_one, up_grad, attn_grad, bias_grad = finish_rows(
+            line_grad,
+            back_full,
+            own_in,
+            grad_middle,
+            gains_now[0:1],
+            normed_two,
+            grad_up,
+            normed_flat,
+            grad_branch,
+            mixed_flat,
+        )
+    else:
+        half = token_count // 2
+        line_far = contract_cols(line_grad[half:], back_full, LOW).reshape(2, local_len, model_width)
+        line_near = contract_cols(line_grad[:half], back_full, LOW).reshape(2, local_len, model_width)
+        line_wide = collect_far(line_far[0], line_far[1])
+        line_got = from_partner(line_wide, "tp", 2)
+        line_core = from_partner(line_near[1], "tp", 1)
+        first_mlp, finish_mlp = collect_all((hidden_act,), ((down_full, 0, 1),), up_grad, branch_far)
+        block_share = (middle_share + finish_mlp()).astype(LOW)
+        grad_one_share = line_near[0].astype(WIDE) + line_core.astype(WIDE) + line_got.astype(WIDE)
+        inv_one = lax.rsqrt(jnp.mean(in_share * in_share, axis=-1, keepdims=True) + EPS)
+        grad_norm_one, gain_one = norm_backward(in_share, inv_one, gains_now[0], grad_one_share)
+        input_share = (grad_middle + grad_norm_one).astype(LOW)
+        attn_grad = jnp.concatenate(
+            [contract_rows(normed_flat, line_grad, LOW), contract_rows(grad_branch, mixed_flat, LOW)],
+            axis=1,
+        )
+        bias_grad = jnp.sum(line_grad.astype(WIDE), axis=0)
+
+    def scatter_units(grad):
+        if not split:
+            return scatter_sum(grad, ctx_rank, LOW)
+        return lax.psum_scatter(grad, "fsdp", scatter_dimension=0, tiled=True)
+
+    unit_sums = [scatter_units(g) for g in (down_grad, gate_grad, up_grad)]
+
+    attn_end = scatter_sum(attn_grad, ctx_rank, LOW, *unit_sums)
 
     def leave(share):
         return lax.ppermute(share, ("fsdp", "tp"), back)
@@ -772,7 +1233,7 @@
     block_out = arrive(block_home, input_share)
     input_grad = arrive(input_home)
 
-    gain_grad = jnp.stack([gain_one, gain_two], axis=1)
+    gain_grad = jnp.concatenate([gain_one, gain_two], axis=0).T
     gain_grad = gain_grad + from_partner(gain_grad, "tp", 1)
     gain_grad = gain_grad + from_partner(gain_grad, "tp", 2)
     shard_count = fsdp_count * ctx_count
@@ -780,7 +1241,21 @@
     bias_cols = jnp.transpose(bias_grad.reshape(heads + 1, shard_count, share), (1, 2, 0))
     bias_cols = jnp.pad(bias_cols, ((0, 0), (0, (model_width - head_dim) // shard_count), (0, 0)))
     tiny = jnp.concatenate([gain_grad, bias_cols.reshape(model_width, heads + 1)], axis=1)
-    tiny_grad = scatter_sum(jnp.pad(tiny, ((0, 0), (0, 8 - tiny.shape[1]))), ctx_rank, WIDE)
+    tiny = jnp.pad(tiny, ((0, 0), (0, 8 - tiny.shape[1])))
+    tiny = tiny.reshape(fsdp_count, ctx_count, model_width // shard_count, 8)
+    if split:
+        kept, sent = scatter_ctx(tiny, ctx_rank)
+        tiny = kept + from_partner(sent, "ctx", 1)
+    else:
+        tiny = lax.psum_scatter(tiny, "ctx", scatter_dimension=1, tiled=True)
+    tiny = tiny.reshape(fsdp_count, -1, 8)
+    pick = lambda shift: lax.dynamic_index_in_dim(
+        tiny, lax.rem(group_rank + shift, fsdp_count), 0, keepdims=False
+    )
+    tiny_grad = pick(0)
+    for shift in range(1, fsdp_count):
+        pairs = [(f, (f + shift) % fsdp_count) for f in range(fsdp_count)]
+        tiny_grad = tiny_grad + lax.ppermute(pick(shift), "fsdp", pairs)
 
     def unit_end(total):
         if split:

time: 938 us -> 887 us (0.946)
  Pallas kernels: 192 us -> 337 us
  matrix products: 119 us -> 7.74 us
  local copies, waits for them, and re-layouts: 110 us -> 62.1 us
  other arithmetic: 83.7 us -> 58.5 us
  starting transfers between devices: 74.9 us -> 57.4 us
    pallas_call x7 -> x5, Pallas kernels: 104 us -> 241 us  [the longest x1 69.9 us: collect_back(): pl.pallas_call(functools.partial(collect_kernel, slots), grid=(slots + ti...]
    dot_general x9 -> x0, matrix products: 90.3 us -> none  [the longest x5 80.2 us: contract_rows(): lax.dot_general(left_side, right_side, (((0,), (0,)), ((), ())), preferre...]
    ppermute x0 -> x3, waiting for transfers between devices: none -> 59.1 us  [local(): tiny_grad = tiny_grad + lax.ppermute(pick(shift), 'fsdp', pairs)]
    ppermute x55 -> x38, waiting for transfers between devices: 236 us -> 186 us  [from_partner(): return lax.ppermute(value, axis, pairs)]
    dot_general x2 -> x1, matrix products: 29 us -> 7.74 us  [product(): jnp.dot(left_side, right_side, preferred_element_type=WIDE).astype(kind)]
    ppermute x55 -> x38, starting transfers between devices: 57.1 us -> 36.1 us  [from_partner(): return lax.ppermute(value, axis, pairs)]
    unnamed x148 -> x102, local copies, waits for them, and re-layouts: 23.5 us -> 7.57 us
    slice x14 -> x4, local copies, waits for them, and re-layouts: 10.8 us -> 1.34 us  [the longest x1 1.18 us: spread_all(): held[0][:half_len]]
  transfers between devices with their start and end apart: 71 -> 54, of which waited for: 22 -> 23; matrix products, arithmetic and copies ran while one was open for 29% -> 13% of each run, Pallas kernels for 12% -> 24%
where the time goes in v3:
time: 887 us; the launch traced here: 876 us
  Pallas kernels  337 us (38%)
  waiting for transfers between devices  309 us (35%)
  local copies, waits for them, and re-layouts  62.1 us (7%)
  other arithmetic  58.5 us (7%)
  starting transfers between devices  57.4 us (6%)
  between operations  43.7 us (5%)
    ppermute x38, waiting for transfers between devices, from_partner(): return lax.ppermute(value, axis, pairs)  186 us
    pallas_call x1, Pallas kernels, collect_back(): pl.pallas_call(functools.partial(collect_kernel, slots), grid=(slots + ti...  69.9 us
    pallas_call x1, Pallas kernels, finish_rows(): pl.pallas_call(functools.partial(line_kernel, slots, tiles), grid=(slots...  63.3 us
    ppermute x3, waiting for transfers between devices, local(): tiny_grad = tiny_grad + lax.ppermute(pick(shift), 'fsdp', pairs)  59.1 us
    pallas_call x1, Pallas kernels, spread_branch(): pl.pallas_call(functools.partial(branch_kernel, slots, tiles), grid=(slot...  55.8 us
    pallas_call x2, Pallas kernels, stack_rows(): pl.pallas_call(functools.partial(rows_kernel, groups), grid=(count,), in_...  51.8 us
    ppermute x38, starting transfers between devices, from_partner(): return lax.ppermute(value, axis, pairs)  36.1 us
    pallas_call x1, Pallas kernels, hidden_units(): pl.pallas_call(units_kernel, grid=(tokens // step,), in_specs=[by_row(wid...  30.6 us
  transfers between devices with their start and end apart: 54, of which 23 were waited for; matrix products, arithmetic and copies ran while one was open for 13% of the time, Pallas kernels for 24%

profile of v3, /device:TPU:1, one launch (start us, length us, event | category | flops | bytes accessed | tf_op | source)
XLA Modules:
  0.0 876.0 jit_solution(12716659345265011497)
XLA Ops:
  24.6 8.1 collective-permute-done.4
  35.0 21.0 %collective-permute-done.x0.own_in = bf16[512,1536]{1,0:T(8,128)(2,1)S(1)} collective-permute-done((bf16[512,1536]{1,0:T(8,128)(2,1)S(1)}, bf16[512,1536]{1,0:T(8,128)(2,1)S(1)}, u32[]{:S(2)}, u32[]{:S(2)}) %collective-permute-start) | collective-permute-done | bytes 1572896 | tf_op jit(solution)/shard_map/ppermute | solution.py:953
  60.9 32.2 %collective-permute-done.2.x2 = bf16[512,1536]{1,0:T(8,128)(2,1)} collective-permute-done((bf16[512,1536]{1,0:T(8,128)(2,1)S(1)}, bf16[512,1536]{1,0:T(8,128)(2,1)}, u32[]{:S(2)}, u32[]{:S(2)}) %collective-permute-start.2) | collective-permute-done | bytes 1572896 | tf_op jit(solution)/shard_map/ppermute | solution.py:21
  127.7 12.5 %shard_map.230 = (bf16[4,512,1536]{2,1,0:T(8,128)(2,1)}, bf16[4,512,384]{2,1,0:T(8,128)(2,1)}, bf16[4,512,128]{2,1,0:T(8,128)(2,1)}, bf16[4,512,128]{2,1,0:T(8,128)(2,1)}) custom-call(bf16[512,1536]{1,0:T(8,128)(2,1)} %copy-done.5, bf16[512,1536]{1,0:T(8,128)(2,1)} %collective-permute-done.1.x1, bf16[512,1536]{1,0:T(8,128)(2,1)} %collective-permute-done.2.x2, ...), custom_call_target="tpu_custom_call" | custom-call | flops 4026531840 | bytes 17170432 | tf_op jit(solution)/shard_map/pallas_call | solution.py:654
  154.1 11.2 %collective-permute-done.5.k_past = bf16[4,512,128]{2,1,0:T(8,128)(2,1)S(1)} collective-permute-done((bf16[4,512,128]{2,1,0:T(8,128)(2,1)}, bf16[4,512,128]{2,1,0:T(8,128)(2,1)S(1)}, u32[]{:S(2)}, u32[]{:S(2)}) %collective-permute-start.5) | collective-permute-done | bytes 524320 | tf_op jit(solution)/shard_map/ppermute | solution.py:1024
  166.2 13.7 %shard_map.231 = (bf16[2,512,384]{2,1,0:T(8,128)(2,1)}, f32[2,512,128]{2,1,0:T(8,128)}, bf16[512,1536]{1,0:T(8,128)(2,1)}, bf16[512,1536]{1,0:T(8,128)(2,1)}) custom-call(s32[6]{0:T(128)} %concatenate.68.info, bf16[4,512,384]{2,1,0:T(8,128)(2,1)} %get-tuple-element.69.q, bf16[4,512,128]{2,1,0:T(8,128)(2,1)} %copy-done.46, bf16[4,512,128]{2,1,0:T(8,128)(2,1)} %copy-done.45, ...), custom_call_target="tpu_custom_call" | custom-call | flops 1610612736 | bytes 1572864 | tf_op jit(solution)/shard_map/pallas_call | solution.py:742
  206.1 14.0 %shard_map.232 = (bf16[2,512,384]{2,1,0:T(8,128)(2,1)}, f32[2,512,128]{2,1,0:T(8,128)}, bf16[512,1536]{1,0:T(8,128)(2,1)}, bf16[512,1536]{1,0:T(8,128)(2,1)}) custom-call(s32[6]{0:T(128)} %concatenate.68.info, bf16[4,512,384]{2,1,0:T(8,128)(2,1)} %get-tuple-element.69.q, bf16[4,512,128]{2,1,0:T(8,128)(2,1)} %copy-done.46, bf16[4,512,128]{2,1,0:T(8,128)(2,1)} %copy-done.45, ...), custom_call_target="tpu_custom_call" | custom-call | flops 1610612736 | bytes 1572864 | tf_op jit(solution)/shard_map/pallas_call | solution.py:742
  223.9 32.6 %collective-permute-done.9 = bf16[512,1536]{1,0:T(8,128)(2,1)} collective-permute-done((bf16[512,1536]{1,0:T(8,128)(2,1)}, bf16[512,1536]{1,0:T(8,128)(2,1)}, u32[]{:S(2)}, u32[]{:S(2)}) %collective-permute-start.9) | collective-permute-done | bytes 1572896 | tf_op jit(solution)/shard_map/ppermute | solution.py:21
  261.5 10.4 %collective-permute-done.12 = bf16[2,512,1536]{2,1,0:T(8,128)(2,1)} collective-permute-done((bf16[2,512,1536]{2,1,0:T(8,128)(2,1)}, bf16[2,512,1536]{2,1,0:T(8,128)(2,1)}, u32[]{:S(2)}, u32[]{:S(2)}) %collective-permute-start.12) | collective-permute-done | bytes 3145760 | tf_op jit(solution)/shard_map/ppermute | solution.py:21
  281.3 25.9 %shard_map.233 = (bf16[4096,1152]{1,0:T(8,128)(2,1)}, bf16[4096,1536]{1,0:T(8,128)(2,1)}) custom-call(bf16[512,1536]{1,0:T(8,128)(2,1)} %bitcast.162, bf16[512,1536]{1,0:T(8,128)(2,1)} %get-tuple-element.144.refs_1_, bf16[512,1536]{1,0:T(8,128)(2,1)} %bitcast.164, bf16[512,1536]{1,0:T(8,128)(2,1)} %get-tuple-element.143.refs_3_, ...), custom_call_target="tpu_custom_call" | custom-call | flops 14495514624 | bytes 38141952 | tf_op jit(solution)/shard_map/pallas_call | solution.py:121
  314.0 14.6 %collective-permute-done.19.refs_7_ = bf16[256,1536]{1,0:T(8,128)(2,1)S(1)} collective-permute-done((bf16[256,1536]{1,0:T(8,128)(2,1)S(1)}, bf16[256,1536]{1,0:T(8,128)(2,1)S(1)}, u32[]{:S(2)}, u32[]{:S(2)}) %collective-permute-start.19) | collective-permute-done | bytes 786464 | tf_op jit(solution)/shard_map/ppermute | solution.py:21
  334.7 25.9 %shard_map.234 = (bf16[4096,1152]{1,0:T(8,128)(2,1)}, bf16[4096,1536]{1,0:T(8,128)(2,1)}) custom-call(bf16[512,1536]{1,0:T(8,128)(2,1)} %copy-done.12, bf16[512,1536]{1,0:T(8,128)(2,1)} %collective-permute-done.10.refs_1_, bf16[512,1536]{1,0:T(8,128)(2,1)} %collective-permute-done.11.refs_2_, bf16[512,1536]{1,0:T(8,128)(2,1)} %collective-permute-done.15.refs_3_, ...), custom_call_target="tpu_custom_call" | custom-call | flops 14495514624 | bytes 38141952 | tf_op jit(solution)/shard_map/pallas_call | solution.py:121
  360.6 30.6 %shard_map.235 = (bf16[4096,1152]{1,0:T(8,128)(2,1)}, bf16[4096,1152]{1,0:T(8,128)(2,1)}, bf16[4096,1152]{1,0:T(8,128)(2,1)}) custom-call(bf16[4096,1536]{1,0:T(8,128)(2,1)} %get-tuple-element.86.h.turned, bf16[1536,2304]{1,0:T(8,128)(2,1)} %bitcast.188, bf16[4096,1152]{1,0:T(8,128)(2,1)} %get-tuple-element.87.gate, bf16[4096,1152]{1,0:T(8,128)(2,1)} %get-tuple-element.82.grad), custom_call_target="tpu_custom_call" | custom-call | flops 14495514624 | bytes 63307776 | tf_op jit(solution)/shard_map/pallas_call | solution.py:157
  391.1 69.9 %shard_map.236 = (f32[512,1536]{1,0:T(8,128)}, bf16[1536,1152]{1,0:T(8,128)(2,1)}) custom-call(bf16[4096,1152]{1,0:T(8,128)(2,1)} %get-tuple-element.88.gate, bf16[4096,1152]{1,0:T(8,128)(2,1)} %get-tuple-element.89.up, bf16[1536,2304]{1,0:T(8,128)(2,1)} %bitcast.189, bf16[1536,2304]{1,0:T(8,128)(2,1)} %bitcast.190, ...), custom_call_target="tpu_custom_call" | custom-call | flops 43486543872 | bytes 47185920 | tf_op jit(solution)/shard_map/pallas_call | solution.py:314
  464.1 55.8 %shard_map.237 = (f32[512,1536]{1,0:T(8,128)}, f32[1,1536]{1,0:T(1,128)}, bf16[1536,1152]{1,0:T(8,128)(2,1)}, bf16[4,512,1536]{2,1,0:T(8,128)(2,1)}, bf16[512,15...) custom-call(f32[512,1536]{1,0:T(8,128)} %get-tuple-element.92.total,, ...), custom_call_target="tpu_custom_call" | custom-call | flops 28991029248 | bytes 47185920 | tf_op jit(solution)/shard_map/pallas_call | solution.py:448
  520.6 7.7 convolution_convert_fusion
  528.4 25.7 %shard_map.238 = (bf16[4,512,384]{2,1,0:T(8,128)(2,1)}, f32[4,512,128]{2,1,0:T(8,128)}, f32[4,512,128]{2,1,0:T(8,128)}, f32[4,512,128]{2,1,0:T(8,128)}, f32[4,512,128]{2,1,0:T(8,128)}) custom-call(s32[6]{0:T(128)} %concatenate.68.info, bf16[4,512,384]{2,1,0:T(8,128)(2,1)} %get-tuple-element.69.q, bf16[4,512,128]{2,1,0:T(8,128)(2,1)} %copy-done.46, ...), custom_call_target="tpu_custom_call" | custom-call | flops 8053063680 | bytes 6291456 | tf_op jit(solution)/shard_map/pallas_call | solution.py:848
  563.5 14.0 %collective-permute-done.24 = bf16[256,1536]{1,0:T(8,128)(2,1)S(1)} collective-permute-done((bf16[256,1536]{1,0:T(8,128)(2,1)S(1)}, bf16[256,1536]{1,0:T(8,128)(2,1)S(1)}, u32[]{:S(2)}, u32[]{:S(2)}) %collective-permute-start.24) | collective-permute-done | bytes 786464 | tf_op jit(solution)/shard_map/ppermute | solution.py:21
  586.2 63.3 %shard_map.239 = (bf16[512,1536]{1,0:T(8,128)(2,1)}, f32[1,1536]{1,0:T(1,128)}, bf16[1536,1152]{1,0:T(8,128)(2,1)}, bf16[1536,896]{1,0:T(8,128)(2,1)}, f32[1,512]{1,0:T(1,128)}) custom-call(bf16[2048,512]{1,0:T(8,128)(2,1)} %pad_maximum_fusion.1.line.line_all, bf16[1536,512]{1,0:T(8,128)(2,1)} %pad_maximum_fusion.5.weight, bf16[512,1536]{1,0:T(8,128)(2,1)} %copy-done.5, ...), custom_call_target="tpu_custom_call" | custom-call | flops 14495514624 | bytes 47185920 | tf_op jit(solution)/shard_map/pallas_call | solution.py:564
  666.0 24.6 %collective-permute-done.40 = f32[4,192,8]{1,2,0:T(8,128)S(1)} collective-permute-done((f32[4,192,8]{1,2,0:T(8,128)S(1)}, f32[4,192,8]{1,2,0:T(8,128)S(1)}, u32[]{:S(2)}, u32[]{:S(2)}) %collective-permute-start.40) | collective-permute-done | bytes 24608 | tf_op jit(solution)/shard_map/ppermute | solution.py:21
  703.2 59.1 %collective-permute-done.42 = f32[192,8]{0,1:T(8,128)S(1)} collective-permute-done((f32[192,8]{0,1:T(8,128)S(1)}, f32[192,8]{0,1:T(8,128)S(1)}, u32[]{:S(2)}, u32[]{:S(2)}) %collective-permute-start.42) | collective-permute-done | bytes 6176 | tf_op jit(solution)/shard_map/ppermute | solution.py:1258
  770.0 15.5 %collective-permute-done.26 = bf16[512,1536]{1,0:T(8,128)(2,1)S(1)} collective-permute-done((bf16[512,1536]{1,0:T(8,128)(2,1)S(1)}, bf16[512,1536]{1,0:T(8,128)(2,1)S(1)}, u32[]{:S(2)}, u32[]{:S(2)}) %collective-permute-start.26) | collective-permute-done | bytes 1572896 | tf_op jit(solution)/shard_map/ppermute | solution.py:1220
  795.6 24.6 %collective-permute-done.31 = bf16[512,1536]{1,0:T(8,128)(2,1)S(1)} collective-permute-done((bf16[512,1536]{1,0:T(8,128)(2,1)S(1)}, bf16[512,1536]{1,0:T(8,128)(2,1)S(1)}, u32[]{:S(2)}, u32[]{:S(2)}) %collective-permute-start.31) | collective-permute-done | bytes 1572896 | tf_op jit(solution)/shard_map/ppermute | solution.py:21
  841.0 8.4 collective-permute-done.44
  (298 shorter events, 211.1 us)
Async XLA Ops:
  7.2 120.5 %all-gather.7.cloned.1.call-start = ((), (), s32[]{:S(2)}) async-start(), calls=%async_computation.8 | async-start | bytes 4423680 | tf_op jit(solution)/shard_map/all_gather | solution.py:977
  16.3 39.7 %collective-permute-start = (bf16[512,1536]{1,0:T(8,128)(2,1)S(1)}, bf16[512,1536]{1,0:T(8,128)(2,1)S(1)}, u32[]{:S(2)}, u32[]{:S(2)}) collective-permute-start(bf16[512,1536]{1,0:T(8,128)(2,1)S(1)} %dynamic-slice_bitcast_fusion.2), channel_id=1, source_target_pairs={{0,0},{1,17},{2,10},{3,27},{8,8},{9,25},{10,18},{11,3},{16,16},{17... | collective-permute-start | bytes 4718600 | tf_op jit(solution)/shard_map/ppermute | solution.py:953
  56.0 225.3 %all-gather.9.cloned.1.call-start = ((), (), s32[]{:S(2)}) async-start(), calls=%async_computation.9 | async-start | bytes 4423680 | tf_op jit(solution)/shard_map/all_gather | solution.py:977
  58.4 34.7 %collective-permute-start.2 = (bf16[512,1536]{1,0:T(8,128)(2,1)S(1)}, bf16[512,1536]{1,0:T(8,128)(2,1)}, u32[]{:S(2)}, u32[]{:S(2)}) collective-permute-start(bf16[512,1536]{1,0:T(8,128)(2,1)S(1)} %collective-permute-done.x0.own_in), channel_id=1, source_target_pairs={{0,2},{1,3},{2,0},{3,1},{4,6},{5,7},{6,4},{7,5},{8,10},{9,11},{10,... | collective-permute-start | bytes 4718600 | tf_op jit(solution)/shard_map/ppermute | solution.py:21
  59.6 35.7 %collective-permute-start.14 = (bf16[192,3456]{1,0:T(8,128)(2,1)S(1)}, bf16[192,3456]{1,0:T(8,128)(2,1)S(1)}, u32[]{:S(2)}, u32[]{:S(2)}) collective-permute-start(bf16[192,3456]{1,0:T(8,128)(2,1)S(1)} %pad_maximum_fusion.8), channel_id=1, source_target_pairs={{0,4},{4,0},{1,5},{5,1},{2,6},{6,2},{3,7},{7,3},{8,12},{12,8},{9,1... | collective-permute-start | bytes 3981320 | tf_op jit(solution)/shard_map/ppermute | solution.py:21
  98.7 235.9 %all-gather.11.cloned.1.call-start = ((), (), s32[]{:S(2)}) async-start(), calls=%async_computation.10 | async-start | bytes 8847360 | tf_op jit(solution)/shard_map/all_gather | solution.py:977
  196.2 629.9 %reduce-scatter.5.cloned.1.call-start = ((), (), s32[]{:S(2)}) async-start(), calls=%async_computation.4 | async-start | bytes 4423680 | tf_op jit(solution)/shard_map/reduce_scatter | solution.py:1213
  201.0 70.9 %collective-permute-start.12 = (bf16[2,512,1536]{2,1,0:T(8,128)(2,1)}, bf16[2,512,1536]{2,1,0:T(8,128)(2,1)}, u32[]{:S(2)}, u32[]{:S(2)}) collective-permute-start(bf16[2,512,1536]{2,1,0:T(8,128)(2,1)} %pad_maximum_fusion), channel_id=1, source_target_pairs={{0,4},{4,0},{1,5},{5,1},{2,6},{6,2},{3,7},{7,3},{8,12},{12,8},{9,1... | collective-permute-start | bytes 9437192 | tf_op jit(solution)/shard_map/ppermute | solution.py:21
  220.4 36.1 %collective-permute-start.9 = (bf16[512,1536]{1,0:T(8,128)(2,1)}, bf16[512,1536]{1,0:T(8,128)(2,1)}, u32[]{:S(2)}, u32[]{:S(2)}) collective-permute-start(bf16[512,1536]{1,0:T(8,128)(2,1)} %add_convert_fusion.1), channel_id=1, source_target_pairs={{0,2},{1,3},{2,0},{3,1},{4,6},{5,7},{6,4},{7,5},{8,10},{9,11},{10,... | collective-permute-start | bytes 4718600 | tf_op jit(solution)/shard_map/ppermute | solution.py:21
  272.5 36.1 %collective-permute-start.16 = (bf16[512,1536]{1,0:T(8,128)(2,1)S(1)}, bf16[512,1536]{1,0:T(8,128)(2,1)S(1)}, u32[]{:S(2)}, u32[]{:S(2)}) collective-permute-start(bf16[512,1536]{1,0:T(8,128)(2,1)S(1)} %multiply_convert_fusion.refs_0_), channel_id=1, source_target_pairs={{0,4},{4,0},{1,5},{5,1},{2,6},{6,2},{3,7},{7,3},{8,12},{12,8},{9,1... | collective-permute-start | bytes 4718600 | tf_op jit(solution)/shard_map/ppermute | solution.py:21
  273.9 36.7 %collective-permute-start.11 = (bf16[512,1536]{1,0:T(8,128)(2,1)S(1)}, bf16[512,1536]{1,0:T(8,128)(2,1)}, u32[]{:S(2)}, u32[]{:S(2)}) collective-permute-start(bf16[512,1536]{1,0:T(8,128)(2,1)S(1)} %multiply_convert_fusion.refs_0_), channel_id=1, source_target_pairs={{0,2},{1,3},{2,0},{3,1},{4,6},{5,7},{6,4},{7,5},{8,10},{9,11},{10,... | collective-permute-start | bytes 4718600 | tf_op jit(solution)/shard_map/ppermute | solution.py:21
  275.1 56.7 %collective-permute-start.10 = (bf16[512,1536]{1,0:T(8,128)(2,1)S(1)}, bf16[512,1536]{1,0:T(8,128)(2,1)}, u32[]{:S(2)}, u32[]{:S(2)}) collective-permute-start(bf16[512,1536]{1,0:T(8,128)(2,1)S(1)} %multiply_convert_fusion.refs_0_), channel_id=1, source_target_pairs={{0,1},{1,0},{2,3},{3,2},{4,5},{5,4},{6,7},{7,6},{8,9},{9,8},{10,11... | collective-permute-start | bytes 4718600 | tf_op jit(solution)/shard_map/ppermute | solution.py:21
  461.0 367.6 %reduce-scatter.7.cloned.1.call-start = ((), (), s32[]{:S(2)}) async-start(), calls=%async_computation.5 | async-start | bytes 4423680 | tf_op jit(solution)/shard_map/reduce_scatter | solution.py:1213
  519.9 39.3 %collective-permute-start.22 = (bf16[256,1536]{1,0:T(8,128)(2,1)}, bf16[256,1536]{1,0:T(8,128)(2,1)S(1)}, u32[]{:S(2)}, u32[]{:S(2)}) collective-permute-start(bf16[256,1536]{1,0:T(8,128)(2,1)} %get-tuple-element.95), channel_id=1, source_target_pairs={{0,4},{4,0},{1,5},{5,1},{2,6},{6,2},{3,7},{7,3},{8,12},{12,8},{9,1... | collective-permute-start | bytes 2359304 | tf_op jit(solution)/shard_map/ppermute | solution.py:21
  528.4 305.4 %reduce-scatter.9.cloned.1.call-start = ((), (), s32[]{:S(2)}) async-start(), calls=%async_computation.6 | async-start | bytes 4423680 | tf_op jit(solution)/shard_map/reduce_scatter | solution.py:1213
  560.7 131.0 %collective-permute-start.23 = (bf16[512,1536]{1,0:T(8,128)(2,1)}, bf16[512,1536]{1,0:T(8,128)(2,1)}, u32[]{:S(2)}, u32[]{:S(2)}) collective-permute-start(bf16[512,1536]{1,0:T(8,128)(2,1)} %pad_maximum_fusion.3), channel_id=1, source_target_pairs={{0,2},{1,3},{2,0},{3,1},{4,6},{5,7},{6,4},{7,5},{8,10},{9,11},{10,... | collective-permute-start | bytes 4718600 | tf_op jit(solution)/shard_map/ppermute | solution.py:21
  653.6 40.4 %collective-permute-start.25 = (bf16[512,1536]{1,0:T(8,128)(2,1)}, bf16[512,1536]{1,0:T(8,128)(2,1)}, u32[]{:S(2)}, u32[]{:S(2)}) collective-permute-start(bf16[512,1536]{1,0:T(8,128)(2,1)} %pad_maximum_fusion.4), channel_id=1, source_target_pairs={{0,4},{4,0},{1,5},{5,1},{2,6},{6,2},{3,7},{7,3},{8,12},{12,8},{9,1... | collective-permute-start | bytes 4718600 | tf_op jit(solution)/shard_map/ppermute | solution.py:21
  656.1 106.2 %collective-permute-start.33 = (bf16[512,1536]{1,0:T(8,128)(2,1)}, bf16[512,1536]{1,0:T(8,128)(2,1)}, u32[]{:S(2)}, u32[]{:S(2)}) collective-permute-start(bf16[512,1536]{1,0:T(8,128)(2,1)} %get-tuple-element.110), channel_id=1, source_target_pairs={{0,0},{17,1},{10,2},{27,3},{8,8},{25,9},{18,10},{3,11},{16,16},{1,... | collective-permute-start | bytes 4718600 | tf_op jit(solution)/shard_map/ppermute | solution.py:1220
  666.0 199.6 %reduce-scatter.11.cloned.1.call-start = ((), (), s32[]{:S(2)}) async-start(), calls=%async_computation.7 | async-start | bytes 1720320 | tf_op jit(solution)/shard_map/reduce_scatter | solution.py:83
  690.7 71.6 %collective-permute-start.42 = (f32[192,8]{0,1:T(8,128)S(1)}, f32[192,8]{0,1:T(8,128)S(1)}, u32[]{:S(2)}, u32[]{:S(2)}) collective-permute-start(f32[192,8]{0,1:T(8,128)S(1)} %get-tuple-element.187), channel_id=1, source_target_pairs={{0,16},{8,24},{16,0},{24,8},{1,17},{9,25},{17,1},{25,9},{2,18},{10... | collective-permute-start | bytes 18440 | tf_op jit(solution)/shard_map/ppermute | solution.py:1258
  691.7 70.6 %collective-permute-start.43 = (f32[192,8]{0,1:T(8,128)S(1)}, f32[192,8]{0,1:T(8,128)S(1)}, u32[]{:S(2)}, u32[]{:S(2)}) collective-permute-start(f32[192,8]{0,1:T(8,128)S(1)} %get-tuple-element.186), channel_id=1, source_target_pairs={{0,24},{8,0},{16,8},{24,16},{1,25},{9,1},{17,9},{25,17},{2,26},{10... | collective-permute-start | bytes 18440 | tf_op jit(solution)/shard_map/ppermute | solution.py:1258
  697.3 88.1 %collective-permute-start.26 = (bf16[512,1536]{1,0:T(8,128)(2,1)S(1)}, bf16[512,1536]{1,0:T(8,128)(2,1)S(1)}, u32[]{:S(2)}, u32[]{:S(2)}) collective-permute-start(bf16[512,1536]{1,0:T(8,128)(2,1)S(1)} %add_convert_fusion), channel_id=1, source_target_pairs={{0,0},{17,1},{10,2},{27,3},{8,8},{25,9},{18,10},{3,11},{16,16},{1,... | collective-permute-start | bytes 4718600 | tf_op jit(solution)/shard_map/ppermute | solution.py:1220
  702.3 131.5 %collective-permute-start.37 = (bf16[4,192,896]{2,1,0:T(8,128)(2,1)}, bf16[4,192,896]{2,1,0:T(8,128)(2,1)}, u32[]{:S(2)}, u32[]{:S(2)}) collective-permute-start(bf16[4,192,896]{2,1,0:T(8,128)(2,1)} %get-tuple-element.154), channel_id=1, source_target_pairs={{0,4},{4,0},{1,5},{5,1},{2,6},{6,2},{3,7},{7,3},{8,12},{12,8},{9,1... | collective-permute-start | bytes 4128776 | tf_op jit(solution)/shard_map/ppermute | solution.py:21
  785.5 36.8 %collective-permute-start.27 = (bf16[512,1536]{1,0:T(8,128)(2,1)S(1)}, bf16[512,1536]{1,0:T(8,128)(2,1)S(1)}, u32[]{:S(2)}, u32[]{:S(2)}) collective-permute-start(bf16[512,1536]{1,0:T(8,128)(2,1)S(1)} %collective-permute-done.26), channel_id=1, source_target_pairs={{0,1},{1,0},{2,3},{3,2},{4,5},{5,4},{6,7},{7,6},{8,9},{9,8},{10,11... | collective-permute-start | bytes 4718600 | tf_op jit(solution)/shard_map/ppermute | solution.py:21
  (78 other events, 992.0 us)
Sparse Core Ops, SparseCore 0:
  56.1 71.4 all-gather.6
  129.2 68.5 all-gather.8
  200.0 127.0 all-gather.10
  461.2 65.9 reduce-scatter.4
  529.3 66.6 reduce-scatter.6
  666.1 97.7 reduce-scatter.8
  836.7 28.8 reduce-scatter.10

commit v4 on v3

--- a/solution.py
+++ b/solution.py
@@ -492,21 +492,39 @@
 
 
 def line_kernel(
-    slots, tiles, line, weight, own_in, grad_middle, gain, turned, up, rows_one, branch, line_all,
-    mixed, share, gain_grad, up_out, attn_out, bias_out, parts, core_in, far_in, total, held, send,
-    recv, load
+    slots, tiles, line, weight, own_in, grad_middle, gain, rows_one, branch, line_all, mixed, block, share,
+    gain_grad, attn_out, bias_out, home, parts, core_in, far_in, total, send, recv, load
 ):
     step = pl.program_id(0)
     core, far, _ = partners_of()
+    tensor_rank, group = lax.axis_index("tp"), lax.axis_index("fsdp")
+    shift = (tensor_rank % 2) * 2 + tensor_rank // 2
+    target = {"fsdp": (group + slots - shift) % slots}
+    source = {"fsdp": (group + shift) % slots}
+    stays = shift == 0
     remote = remote_copy(send, recv)
     cores = [remote(parts.at[3 - 2 * k], core_in.at[k], k, core) for k in range(2)]
     to_far = remote(parts.at[2], far_in, 2, far)
-    loading = pltpu.make_async_copy(up, held, load)
+    leave = remote(block, home, 3, target)
+    keep = pltpu.make_async_copy(block, home, load)
 
     @pl.when(step == 0)
     def _():
-        loading.start()
-        meet((core, far))
+        barrier = pltpu.get_barrier_semaphore()
+        for partner in (core, far):
+            pl.semaphore_signal(barrier, inc=1, device_id=partner, device_id_type=MESH_ID)
+
+        @pl.when(stays)
+        def _():
+            pl.semaphore_wait(barrier, 2)
+            keep.start()
+
+        @pl.when(jnp.logical_not(stays))
+        def _():
+            for partner in (target, source):
+                pl.semaphore_signal(barrier, inc=1, device_id=partner, device_id_type=MESH_ID)
+            pl.semaphore_wait(barrier, 4)
+            leave.start()
 
     @pl.when(step < slots)
     def _():
@@ -532,8 +550,6 @@
 
     @pl.when(step >= slots)
     def _():
-        pl.when(step == slots)(loading.wait)
-        up_out[...] = dot_rows(turned[...], held[...]).astype(LOW)
         cols = line_all.shape[1]
         attn_out[:, :cols] = dot_rows(rows_one[...], line_all[...]).astype(LOW)
         attn_out[:, cols:] = dot_rows(branch[...], mixed[...]).astype(LOW)
@@ -549,11 +565,16 @@
         share[...] = (grad_middle[...] + grad_in).astype(LOW)
         for copy in (*cores, to_far):
             copy.wait_send()
-
-
-def finish_rows(line, weight, own_in, grad_middle, gain, rows_two, grad_up, rows_one, branch, mixed):
+        pl.when(stays)(keep.wait)
+
+        @pl.when(jnp.logical_not(stays))
+        def _():
+            leave.wait_recv()
+            leave.wait_send()
+
+
+def finish_rows(line, weight, own_in, grad_middle, gain, rows_one, branch, mixed, block):
     length, width = own_in.shape
-    tokens, cols = grad_up.shape
     near_tokens, line_cols = line.shape
     slots, tile = near_tokens // length, 256
     tiles = width // tile
@@ -570,42 +591,67 @@
             once,
             once,
             whole_spec(1, width),
-            by_column(tokens),
-            ANYWHERE,
             by_column(near_tokens),
             by_column(near_tokens),
             whole_spec(near_tokens, line_cols, once=True),
             whole_spec(*mixed.shape, once=True),
+            ANYWHERE,
         ],
         out_specs=[
             whole_spec(length, width),
             whole_spec(1, width),
-            pl.BlockSpec((tile, cols), lambda i: (column(i), 0)),
             pl.BlockSpec((tile, attn_cols), lambda i: (column(i), 0)),
             whole_spec(1, line_cols),
+            ANYWHERE,
         ],
         out_shape=[
             jax.ShapeDtypeStruct((length, width), LOW),
             jax.ShapeDtypeStruct((1, width), WIDE),
-            jax.ShapeDtypeStruct((width, cols), LOW),
             jax.ShapeDtypeStruct((width, attn_cols), LOW),
             jax.ShapeDtypeStruct((1, line_cols), WIDE),
+            jax.ShapeDtypeStruct((length, width), LOW),
         ],
         scratch_shapes=[
             pltpu.VMEM((slots, length, width), LOW),
             pltpu.VMEM((2, length, width), LOW),
             pltpu.VMEM((length, width), LOW),
             pltpu.VMEM((length, width), WIDE),
-            pltpu.VMEM((tokens, cols), LOW),
-            pltpu.SemaphoreType.DMA((3,)),
-            pltpu.SemaphoreType.DMA((3,)),
+            pltpu.SemaphoreType.DMA((4,)),
+            pltpu.SemaphoreType.DMA((4,)),
             pltpu.SemaphoreType.DMA,
         ],
         compiler_params=pltpu.CompilerParams(
             vmem_limit_bytes=63 << 20, collective_id=3, has_side_effects=True
         ),
-        cost_estimate=estimate(2 * tokens * width * cols, 10 * tokens * cols),
-    )(line, weight, own_in, grad_middle, gain, rows_two, grad_up, rows_one, branch, line, mixed)
+        cost_estimate=estimate(2 * near_tokens * width * attn_cols, 10 * near_tokens * width),
+    )(line, weight, own_in, grad_middle, gain, rows_one, branch, line, mixed, block)
+
+
+def place_kernel(count, info, *refs):
+    out = refs[count]
+    for r in range(count):
+
+        @pl.when(pl.program_id(0) == r)
+        def _():
+            out[0] = refs[r][...]
+
+
+def place_rows(rows, order):
+    length, width = rows[0].shape
+    count = len(rows)
+    held = pl.BlockSpec((length, width), lambda s, info: (0, 0), pipeline_mode=pl.Buffered(1))
+    return pl.pallas_call(
+        functools.partial(place_kernel, count),
+        grid_spec=pltpu.PrefetchScalarGridSpec(
+            num_scalar_prefetch=1,
+            grid=(count,),
+            in_specs=[held] * count,
+            out_specs=pl.BlockSpec((1, length, width), lambda s, info: (info[s], 0, 0)),
+        ),
+        out_shape=jax.ShapeDtypeStruct((count, length, width), LOW),
+        compiler_params=pltpu.CompilerParams(vmem_limit_bytes=32 << 20),
+        cost_estimate=estimate(0, 4 * count * length * width),
+    )(order, *rows)
 
 
 def turn(values, cosine, sine_signed):
@@ -765,6 +811,40 @@
     )(info, q, k_past, v_past, k_own, v_own, weight)
 
 
+def attend_back_rows(
+    heads, head_dim, scale, length, offset, q, k_past, v_past, k_own, v_own, grad, lse, cosine, sine, put,
+    dk_past, dk_own, dv_past, dv_own
+):
+    past = k_past.shape[1]
+    for start, rows in row_blocks(q.shape[1]):
+        keys = start + rows
+        past_bias, own_bias = key_biases(length, offset, start, rows, past, keys)
+        here = slice(start, start + rows)
+        cos, sin = cosine[0, here], sine[0, here]
+        for h in range(heads):
+            cols = slice(h * head_dim, (h + 1) * head_dim)
+            query, upstream = q[0, here, cols], grad[0, here, cols]
+            log_total = lse[0, here, h : h + 1]
+            p_past = jnp.exp(dot_cols(query, k_past[0]) * scale + past_bias - log_total)
+            p_own = jnp.exp(dot_cols(query, k_own[0, :keys]) * scale + own_bias - log_total)
+            g_past = dot_cols(upstream, v_past[0])
+            g_own = dot_cols(upstream, v_own[0, :keys])
+            row_dot = jnp.sum(p_past * g_past, axis=1, keepdims=True) + jnp.sum(
+                p_own * g_own, axis=1, keepdims=True
+            )
+            s_past = (p_past * (g_past - row_dot)).astype(LOW)
+            s_own = (p_own * (g_own - row_dot)).astype(LOW)
+            dq = (
+                jnp.dot(s_past, k_past[0], preferred_element_type=WIDE)
+                + jnp.dot(s_own, k_own[0, :keys], preferred_element_type=WIDE)
+            ) * scale
+            put(here, cols, turn_back(dq, cos, sin).astype(LOW))
+            dk_past[...] += dot_rows(s_past, query)
+            dk_own[:keys] += dot_rows(s_own, query)
+            dv_past[...] += dot_rows(p_past.astype(LOW), upstream)
+            dv_own[:keys] += dot_rows(p_own.astype(LOW), upstream)
+
+
 def attend_back_kernel(
     heads,
     head_dim,
@@ -792,36 +872,13 @@
     slot = pl.program_id(0)
     length, offset = info[slot], info[pl.num_programs(0)]
     parity = info[pl.num_programs(0) + 1]
-    past = k_past.shape[1]
     for total in (dk_past, dk_own, dv_past, dv_own):
         total[...] = jnp.zeros_like(total)
-    for start, rows in row_blocks(q.shape[1]):
-        keys = start + rows
-        past_bias, own_bias = key_biases(length, offset, start, rows, past, keys)
-        here = slice(start, start + rows)
-        cos, sin = cosine[0, here], sine[0, here]
-        for h in range(heads):
-            cols = slice(h * head_dim, (h + 1) * head_dim)
-            query, upstream = q[0, here, cols], grad[0, here, cols]
-            log_total = lse[0, here, h : h + 1]
-            p_past = jnp.exp(dot_cols(query, k_past[0]) * scale + past_bias - log_total)
-            p_own = jnp.exp(dot_cols(query, k_own[0, :keys]) * scale + own_bias - log_total)
-            g_past = dot_cols(upstream, v_past[0])
-            g_own = dot_cols(upstream, v_own[0, :keys])
-            row_dot = jnp.sum(p_past * g_past, axis=1, keepdims=True) + jnp.sum(
-                p_own * g_own, axis=1, keepdims=True
-            )
-            s_past = (p_past * (g_past - row_dot)).astype(LOW)
-            s_own = (p_own * (g_own - row_dot)).astype(LOW)
-            dq = (
-                jnp.dot(s_past, k_past[0], preferred_element_type=WIDE)
-                + jnp.dot(s_own, k_own[0, :keys], preferred_element_type=WIDE)
-            ) * scale
-            dq_out[0, here, cols] = turn_back(dq, cos, sin).astype(LOW)
-            dk_past[...] += dot_rows(s_past, query)
-            dk_own[:keys] += dot_rows(s_own, query)
-            dv_past[...] += dot_rows(p_past.astype(LOW), upstream)
-            dv_own[:keys] += dot_rows(p_own.astype(LOW), upstream)
+    attend_back_rows(
+        heads, head_dim, scale, length, offset, q, k_past, v_past, k_own, v_own, grad, lse, cosine, sine,
+        lambda here, cols, value: dq_out.__setitem__((0, here, cols), value),
+        dk_past, dk_own, dv_past, dv_own,
+    )
 
     @pl.when(parity == 0)
     def _():
@@ -887,6 +944,148 @@
     )(info, q, k_past, v_past, k_own, v_own, grad, lse, cosine, sine)
 
 
+def exchange_kernel(
+    heads, head_dim, scale, slots, tiles, info, q, k_past, v_past, k_own, v_own, grad, lse, cosine, sine,
+    cosine_all, sine_all, turned, up, line, up_out, mine_past, mine_own, other_past, other_own, got_past,
+    got_own, side_out, side_in, dk_past, dk_own, dv_past, dv_own, held, send, recv, load
+):
+    step = pl.program_id(0)
+    tensor_rank = lax.axis_index("tp")
+    core, _, side = partners_of()
+    parity = lax.rem(tensor_rank, 2)
+    offset = lax.axis_index("ctx") * q.shape[1]
+    remote = remote_copy(send, recv)
+    pasts = [remote(other_past.at[r], got_past.at[r ^ 1], r, core) for r in range(slots)]
+    owns = [remote(other_own.at[r], got_own.at[r ^ 1], slots + r, core) for r in range(slots)]
+    sides = [remote(side_out.at[r], side_in.at[r], 2 * slots + r, side) for r in range(slots)]
+    loading = pltpu.make_async_copy(up, held, load)
+
+    @pl.when(step == 0)
+    def _():
+        loading.start()
+        meet((core, side))
+
+    @pl.when(step < slots)
+    def _():
+        length = info[jnp.minimum(step, slots - 1)]
+        for total in (dk_past, dk_own, dv_past, dv_own):
+            total[...] = jnp.zeros_like(total)
+        attend_back_rows(
+            heads, head_dim, scale, length, offset, q, k_past, v_past, k_own, v_own, grad, lse, cosine,
+            sine, lambda here, cols, value: line.__setitem__((step, here, cols), value),
+            dk_past, dk_own, dv_past, dv_own,
+        )
+
+        @pl.when(parity == 0)
+        def _():
+            mine_past[step] = dk_past[...] * scale
+            mine_own[step] = dk_own[...] * scale
+            other_past[step] = dv_past[...]
+            other_own[step] = dv_own[...]
+
+        @pl.when(parity != 0)
+        def _():
+            mine_past[step] = dv_past[...]
+            mine_own[step] = dv_own[...]
+            other_past[step] = dk_past[...] * scale
+            other_own[step] = dk_own[...] * scale
+
+    for r in range(slots):
+
+        def start(r=r):
+            pasts[r].start()
+            owns[r].start()
+
+        pl.when(step == r)(start)
+
+    for pair in range(0, slots, 2):
+
+        def merge(pair=pair):
+            for r in (pair, pair + 1):
+                pasts[r ^ 1].wait_recv()
+                side_out[r] = (mine_past[r] + got_past[r]).astype(LOW)
+                sides[r].start()
+
+        pl.when(step == pair + 1)(merge)
+
+    @pl.when(step >= slots)
+    def _():
+        pl.when(step == slots)(loading.wait)
+        up_out[...] = dot_rows(turned[...], held[...]).astype(LOW)
+
+    @pl.when(step == slots + tiles - 1)
+    def _():
+        for r in range(slots):
+            owns[r ^ 1].wait_recv()
+            sides[r].wait_recv()
+            total = mine_own[r] + got_own[r] + side_in[r].astype(WIDE)
+            back = turn_back(total, cosine_all[r], sine_all[r])
+            line[r, :, heads * head_dim :] = jnp.where(parity == 0, back, total).astype(LOW)
+        for copy in (*pasts, *owns, *sides):
+            copy.wait_send()
+
+
+def attend_exchange(
+    info, q, k_past, v_past, k_own, v_own, grad, lse, cosine, sine, heads, head_dim, scale, rows, grad_up
+):
+    count, length, width = q.shape
+    past = k_past.shape[1]
+    tokens, cols = grad_up.shape
+    model_width = rows.shape[1]
+    tile = 256
+    tiles = model_width // tile
+    slot = lambda i: jnp.minimum(i, count - 1)
+    by_slot = lambda *shape: pl.BlockSpec((1, *shape), lambda i, info: (slot(i),) + (0,) * len(shape))
+    column = lambda i: jnp.clip(i - count, 0, tiles - 1)
+    held = lambda *shape: pl.BlockSpec(
+        shape, lambda i, info: (0,) * len(shape), pipeline_mode=pl.Buffered(1)
+    )
+    line_cols = width + head_dim
+    return pl.pallas_call(
+        functools.partial(exchange_kernel, heads, head_dim, scale, count, tiles),
+        grid_spec=pltpu.PrefetchScalarGridSpec(
+            num_scalar_prefetch=1,
+            grid=(count + tiles,),
+            in_specs=[
+                by_slot(length, width),
+                by_slot(past, head_dim),
+                by_slot(past, head_dim),
+                by_slot(length, head_dim),
+                by_slot(length, head_dim),
+                by_slot(length, width),
+                by_slot(length, 128),
+                by_slot(length, head_dim),
+                by_slot(length, head_dim),
+                held(count, length, head_dim),
+                held(count, length, head_dim),
+                pl.BlockSpec((tokens, tile), lambda i, info: (0, column(i))),
+                ANYWHERE,
+            ],
+            out_specs=[
+                pl.BlockSpec((count, length, line_cols), lambda i, info: (0, 0, 0)),
+                pl.BlockSpec((tile, cols), lambda i, info: (column(i), 0)),
+            ],
+            scratch_shapes=[pltpu.VMEM((count, length, head_dim), WIDE)] * 6
+            + [pltpu.VMEM((count, length, head_dim), LOW)] * 2
+            + [pltpu.VMEM((length, head_dim), WIDE)] * 4
+            + [
+                pltpu.VMEM((tokens, cols), LOW),
+                pltpu.SemaphoreType.DMA((3 * count,)),
+                pltpu.SemaphoreType.DMA((3 * count,)),
+                pltpu.SemaphoreType.DMA,
+            ],
+        ),
+        out_shape=[
+            jax.ShapeDtypeStruct((count, length, line_cols), LOW),
+            jax.ShapeDtypeStruct((model_width, cols), LOW),
+        ],
+        compiler_params=pltpu.CompilerParams(
+            vmem_limit_bytes=63 << 20, collective_id=4, has_side_effects=True
+        ),
+        cost_estimate=estimate(2 * tokens * model_width * cols, 10 * tokens * cols),
+    )(info, q, k_past, v_past, k_own, v_own, grad, lse, cosine, sine, cosine, sine, rows, grad_up)
+
+
 def local(
     hidden_in,
     cotangent,
@@ -1022,8 +1221,7 @@
     gains_now = near_full[:, query_cols + head_width : near_cols][:, :2].astype(WIDE).T
     if split:
         key_past, value_past = lax.ppermute((key_own, value_own), "ctx", [(0, 1)])
-        grad_pair = after(jnp.stack([grad_slots[0], grad_slots[2]]), value_past)
-        other_pair = from_partner(grad_pair, "ctx", 1)
+        other_pair = [from_partner(after(grad_slots[r], value_past), "ctx", 1) for r in (0, 2)]
         cross_pair = functools.partial(from_partner, axis="tp", apart=1)
     else:
         key_past = lax.all_gather(key_own, "ctx", axis=1, tiled=True)
@@ -1050,7 +1248,7 @@
 
     others = []
     if split:
-        cross_pair = cross_pair(after(other_pair, normed_share))
+        cross_pair = [cross_pair(after(v, normed_share)) for v in other_pair]
         others = [other_pair[0], cross_pair[0], other_pair[1], cross_pair[1]]
 
     grad_hidden, grad_rows = stack_rows(
@@ -1127,7 +1325,7 @@
     grad_mixed = product(grad_branch, output_full, LOW)
     mixed_flat = jnp.concatenate([mixed_near, mixed_far], axis=0).reshape(token_count, query_cols)
     lse = jnp.concatenate([lse_near, lse_far], axis=0)
-    grad_query, mine_past, mine_own, other_past, other_own = attend_backward(
+    attend_args = (
         info,
         query_rot,
         key_past,
@@ -1142,18 +1340,20 @@
         head_dim,
         scale,
     )
-    swap = lambda value: jnp.stack([value[r ^ 1] for r in range(seq_grp)])
-    got_past, got_own = from_partner((other_past, other_own), "tp", 1)
-    past_sum = mine_past + swap(got_past)
-    own_sum = mine_own + swap(got_own)
     if split:
-        own_sum = own_sum + lax.ppermute(past_sum.astype(LOW), "ctx", [(1, 0)]).astype(WIDE)
+        line_grad, up_grad = attend_exchange(*attend_args, normed_two, grad_up)
+        line_grad = line_grad.reshape(token_count, -1)
     else:
+        grad_query, mine_past, mine_own, other_past, other_own = attend_backward(*attend_args)
+        swap = lambda value: jnp.stack([value[r ^ 1] for r in range(seq_grp)])
+        got_past, got_own = from_partner((other_past, other_own), "tp", 1)
+        past_sum = mine_past + swap(got_past)
+        own_sum = mine_own + swap(got_own)
         own_sum = own_sum + lax.psum_scatter(past_sum, "ctx", scatter_dimension=1, tiled=True)
-    half_lanes = head_dim // 2
-    turned = own_sum * cosine - jnp.roll(own_sum, half_lanes, axis=-1) * sine
-    own_grad = jnp.where(parity == 0, turned, own_sum).astype(LOW).reshape(token_count, head_dim)
-    line_grad = jnp.concatenate([grad_query.reshape(token_count, query_cols), own_grad], axis=1)
+        half_lanes = head_dim // 2
+        turned = own_sum * cosine - jnp.roll(own_sum, half_lanes, axis=-1) * sine
+        own_grad = jnp.where(parity == 0, turned, own_sum).astype(LOW).reshape(token_count, head_dim)
+        line_grad = jnp.concatenate([grad_query.reshape(token_count, query_cols), own_grad], axis=1)
     own_weight = lax.dynamic_slice_in_dim(
         project_full, query_cols + parity * head_dim, head_dim, axis=1
     )
@@ -1176,17 +1376,16 @@
             + from_partner(add_half(mlp_side, got_first, None), "ctx", 1).astype(WIDE)
         )
         block_share = (middle_share + mlp_sum).astype(LOW)
-        input_share, gain_one, up_grad, attn_grad, bias_grad = finish_rows(
+        input_share, gain_one, attn_grad, bias_grad, block_home = finish_rows(
             line_grad,
             back_full,
             own_in,
             grad_middle,
             gains_now[0:1],
-            normed_two,
-            grad_up,
             normed_flat,
             grad_branch,
             mixed_flat,
+            block_share,
         )
     else:
         half = token_count // 2
@@ -1216,21 +1415,20 @@
 
     attn_end = scatter_sum(attn_grad, ctx_rank, LOW, *unit_sums)
 
+    home_order = jnp.stack(home_now).astype(jnp.int32)
+
     def leave(share):
         return lax.ppermute(share, ("fsdp", "tp"), back)
 
-    def arrive(own, *earlier):
-        far = from_partner(after(own, *earlier), "tp", 2)
+    def arrive(own):
+        far = from_partner(own, "tp", 2)
         near = from_partner(own, "tp", 1)
-        cross = from_partner(far, "tp", 1)
-        out = jnp.zeros((seq_grp, local_len, model_width), LOW)
-        for home, row in zip(home_now, (own, near, far, cross)):
-            out = lax.dynamic_update_index_in_dim(out, row, home, 0)
-        return out
-
-    block_home = leave(block_share)
+        return place_rows((own, near, far, from_partner(far, "tp", 1)), home_order)
+
     input_home = leave(input_share)
-    block_out = arrive(block_home, input_share)
+    if not split:
+        block_home = leave(block_share)
+    block_out = arrive(block_home)
     input_grad = arrive(input_home)
 
     gain_grad = jnp.concatenate([gain_one, gain_two], axis=0).T

time: 887 us -> 857 us (0.966)
  Pallas kernels: 337 us -> 386 us
  waiting for transfers between devices: 309 us -> 267 us
  local copies, waits for them, and re-layouts: 62.1 us -> 40 us
    ppermute x3, waiting for transfers between devices: 59.1 us -> 3.34 us  [local(): tiny_grad = tiny_grad + lax.ppermute(pick(shift), 'fsdp', pairs)]
    pallas_call x1 -> x3, Pallas kernels: 25.7 us -> 63.4 us  [the longest x1 51.5 us: attend_exchange(): pl.pallas_call(functools.partial(exchange_kernel, heads, head_dim, scale,...]
    pallas_call x1, Pallas kernels: 63.3 us -> 76.5 us  [finish_rows(): pl.pallas_call(functools.partial(line_kernel, slots, tiles), grid=(slots...]
    dynamic_update_slice x8 -> x0, local copies, waits for them, and re-layouts: 12.8 us -> none  [arrive(): out = lax.dynamic_update_index_in_dim(out, row, home, 0)]
    ppermute x2 -> x1, waiting for transfers between devices: 15.5 us -> 27.3 us  [leave(): return lax.ppermute(share, ('fsdp', 'tp'), back)]
  transfers between devices with their start and end apart: 54 -> 52, of which waited for: 23 -> 26; matrix products, arithmetic and copies ran while one was open for 13% -> 10% of each run, Pallas kernels for 24% -> 31%
where the time goes in v4:
time: 857 us; the launch traced here: 847 us
  Pallas kernels  386 us (45%)
  waiting for transfers between devices  267 us (31%)
  starting transfers between devices  57.2 us (7%)
  other arithmetic  50.6 us (6%)
  local copies, waits for them, and re-layouts  40 us (5%)
  between operations  37.7 us (4%)
    ppermute x38, waiting for transfers between devices, from_partner(): return lax.ppermute(value, axis, pairs)  191 us
    pallas_call x1, Pallas kernels, finish_rows(): pl.pallas_call(functools.partial(line_kernel, slots, tiles), grid=(slots...  76.5 us
    pallas_call x1, Pallas kernels, collect_back(): pl.pallas_call(functools.partial(collect_kernel, slots), grid=(slots + ti...  70.6 us
    pallas_call x1, Pallas kernels, spread_branch(): pl.pallas_call(functools.partial(branch_kernel, slots, tiles), grid=(slot...  53.9 us
    pallas_call x2, Pallas kernels, stack_rows(): pl.pallas_call(functools.partial(rows_kernel, groups), grid=(count,), in_...  51.8 us
    pallas_call x1, Pallas kernels, attend_exchange(): pl.pallas_call(functools.partial(exchange_kernel, heads, head_dim, scale,...  51.5 us
    ppermute x38, starting transfers between devices, from_partner(): return lax.ppermute(value, axis, pairs)  40.3 us
    pallas_call x1, Pallas kernels, hidden_units(): pl.pallas_call(units_kernel, grid=(tokens // step,), in_specs=[by_row(wid...  30.6 us
  transfers between devices with their start and end apart: 52, of which 26 were waited for; matrix products, arithmetic and copies ran while one was open for 10% of the time, Pallas kernels for 31%

profile of v4, /device:TPU:1, one launch (start us, length us, event | category | flops | bytes accessed | tf_op | source)
XLA Modules:
  0.0 846.5 jit_solution(13367927101083134290)
XLA Ops:
  24.5 8.1 collective-permute-done.4
  35.0 21.0 %collective-permute-done.x0.own_in = bf16[512,1536]{1,0:T(8,128)(2,1)S(1)} collective-permute-done((bf16[512,1536]{1,0:T(8,128)(2,1)S(1)}, bf16[512,1536]{1,0:T(8,128)(2,1)S(1)}, u32[]{:S(2)}, u32[]{:S(2)}) %collective-permute-start) | collective-permute-done | bytes 1572896 | tf_op jit(solution)/shard_map/ppermute | solution.py:1152
  60.8 32.2 %collective-permute-done.2.x2 = bf16[512,1536]{1,0:T(8,128)(2,1)} collective-permute-done((bf16[512,1536]{1,0:T(8,128)(2,1)S(1)}, bf16[512,1536]{1,0:T(8,128)(2,1)}, u32[]{:S(2)}, u32[]{:S(2)}) %collective-permute-start.2) | collective-permute-done | bytes 1572896 | tf_op jit(solution)/shard_map/ppermute | solution.py:21
  127.6 12.5 %shard_map.230 = (bf16[4,512,1536]{2,1,0:T(8,128)(2,1)}, bf16[4,512,384]{2,1,0:T(8,128)(2,1)}, bf16[4,512,128]{2,1,0:T(8,128)(2,1)}, bf16[4,512,128]{2,1,0:T(8,128)(2,1)}) custom-call(bf16[512,1536]{1,0:T(8,128)(2,1)} %copy-done.6, bf16[512,1536]{1,0:T(8,128)(2,1)} %collective-permute-done.1.x1, bf16[512,1536]{1,0:T(8,128)(2,1)} %collective-permute-done.2.x2, ...), custom_call_target="tpu_custom_call" | custom-call | flops 4026531840 | bytes 17170432 | tf_op jit(solution)/shard_map/pallas_call | solution.py:700
  146.7 7.4 collective-permute-done.5.k_past
  154.1 11.2 %collective-permute-done.6.v_past = bf16[4,512,128]{2,1,0:T(8,128)(2,1)S(1)} collective-permute-done((bf16[4,512,128]{2,1,0:T(8,128)(2,1)}, bf16[4,512,128]{2,1,0:T(8,128)(2,1)S(1)}, u32[]{:S(2)}, u32[]{:S(2)}) %collective-permute-start.6) | collective-permute-done | bytes 524320 | tf_op jit(solution)/shard_map/ppermute | solution.py:1223
  166.1 13.6 %shard_map.231 = (bf16[2,512,384]{2,1,0:T(8,128)(2,1)}, f32[2,512,128]{2,1,0:T(8,128)}, bf16[512,1536]{1,0:T(8,128)(2,1)}, bf16[512,1536]{1,0:T(8,128)(2,1)}) custom-call(s32[6]{0:T(128)} %concatenate.61.info, bf16[4,512,384]{2,1,0:T(8,128)(2,1)} %get-tuple-element.67.q, bf16[4,512,128]{2,1,0:T(8,128)(2,1)} %copy-done.35, bf16[4,512,128]{2,1,0:T(8,128)(2,1)} %copy-done.36, ...), custom_call_target="tpu_custom_call" | custom-call | flops 1610612736 | bytes 1572864 | tf_op jit(solution)/shard_map/pallas_call | solution.py:788
  188.7 13.6 %shard_map.232 = (bf16[2,512,384]{2,1,0:T(8,128)(2,1)}, f32[2,512,128]{2,1,0:T(8,128)}, bf16[512,1536]{1,0:T(8,128)(2,1)}, bf16[512,1536]{1,0:T(8,128)(2,1)}) custom-call(s32[6]{0:T(128)} %concatenate.61.info, bf16[4,512,384]{2,1,0:T(8,128)(2,1)} %get-tuple-element.67.q, bf16[4,512,128]{2,1,0:T(8,128)(2,1)} %copy-done.35, bf16[4,512,128]{2,1,0:T(8,128)(2,1)} %copy-done.36, ...), custom_call_target="tpu_custom_call" | custom-call | flops 1610612736 | bytes 1572864 | tf_op jit(solution)/shard_map/pallas_call | solution.py:788
  228.6 25.2 %collective-permute-done.12.refs_4_ = bf16[512,1536]{1,0:T(8,128)(2,1)} collective-permute-done((bf16[512,1536]{1,0:T(8,128)(2,1)}, bf16[512,1536]{1,0:T(8,128)(2,1)}, u32[]{:S(2)}, u32[]{:S(2)}) %collective-permute-start.12) | collective-permute-done | bytes 1572896 | tf_op jit(solution)/shard_map/ppermute | solution.py:21
  254.6 32.9 %collective-permute-done.14.refs_6_ = bf16[512,1536]{1,0:T(8,128)(2,1)} collective-permute-done((bf16[512,1536]{1,0:T(8,128)(2,1)}, bf16[512,1536]{1,0:T(8,128)(2,1)}, u32[]{:S(2)}, u32[]{:S(2)}) %collective-permute-start.14) | collective-permute-done | bytes 1572896 | tf_op jit(solution)/shard_map/ppermute | solution.py:21
  291.5 25.6 %shard_map.233 = (bf16[4096,1152]{1,0:T(8,128)(2,1)}, bf16[4096,1536]{1,0:T(8,128)(2,1)}) custom-call(bf16[512,1536]{1,0:T(8,128)(2,1)} %get-tuple-element.76.refs_0_.own_grad, bf16[512,1536]{1,0:T(8,128)(2,1)} %get-tuple-element.140.refs_1_, bf16[512,1536]{1,0:T(8,128)(2,1)} %get-tuple-element.78.refs_2_, bf16[512,1536]{1,0:T(8,128)(2,1)} %get-tuple-element.139.refs_3_, ...), custom_call_target="tpu_custom_call" | custom-call | flops 14495514624 | bytes 38141952 | tf_op jit(solution)/shard_map/pallas_call | solution.py:121
  317.1 7.1 collective-permute-done.11.refs_2_
  329.2 15.3 %collective-permute-done.20.refs_6_ = bf16[256,1536]{1,0:T(8,128)(2,1)S(1)} collective-permute-done((bf16[256,1536]{1,0:T(8,128)(2,1)S(1)}, bf16[256,1536]{1,0:T(8,128)(2,1)S(1)}, u32[]{:S(2)}, u32[]{:S(2)}) %collective-permute-start.20) | collective-permute-done | bytes 786464 | tf_op jit(solution)/shard_map/ppermute | solution.py:21
  351.4 26.2 %shard_map.234 = (bf16[4096,1152]{1,0:T(8,128)(2,1)}, bf16[4096,1536]{1,0:T(8,128)(2,1)}) custom-call(bf16[512,1536]{1,0:T(8,128)(2,1)} %copy-done.16, bf16[512,1536]{1,0:T(8,128)(2,1)} %collective-permute-done.10.refs_1_, bf16[512,1536]{1,0:T(8,128)(2,1)} %copy-done.25, bf16[512,1536]{1,0:T(8,128)(2,1)} %copy-done.30, ...), custom_call_target="tpu_custom_call" | custom-call | flops 14495514624 | bytes 38141952 | tf_op jit(solution)/shard_map/pallas_call | solution.py:121
  377.6 30.6 %shard_map.235 = (bf16[4096,1152]{1,0:T(8,128)(2,1)}, bf16[4096,1152]{1,0:T(8,128)(2,1)}, bf16[4096,1152]{1,0:T(8,128)(2,1)}) custom-call(bf16[4096,1536]{1,0:T(8,128)(2,1)} %get-tuple-element.86.h.turned, bf16[1536,2304]{1,0:T(8,128)(2,1)} %bitcast.169, bf16[4096,1152]{1,0:T(8,128)(2,1)} %get-tuple-element.87.gate, bf16[4096,1152]{1,0:T(8,128)(2,1)} %get-tuple-element.82.grad), custom_call_target="tpu_custom_call" | custom-call | flops 14495514624 | bytes 63307776 | tf_op jit(solution)/shard_map/pallas_call | solution.py:157
  408.2 70.6 %shard_map.236 = (f32[512,1536]{1,0:T(8,128)}, bf16[1536,1152]{1,0:T(8,128)(2,1)}) custom-call(bf16[4096,1152]{1,0:T(8,128)(2,1)} %get-tuple-element.88.gate, bf16[4096,1152]{1,0:T(8,128)(2,1)} %get-tuple-element.89.up, bf16[1536,2304]{1,0:T(8,128)(2,1)} %bitcast.170, bf16[1536,2304]{1,0:T(8,128)(2,1)} %bitcast.171, ...), custom_call_target="tpu_custom_call" | custom-call | flops 43486543872 | bytes 47185920 | tf_op jit(solution)/shard_map/pallas_call | solution.py:314
  478.8 53.9 %shard_map.237 = (f32[512,1536]{1,0:T(8,128)}, f32[1,1536]{1,0:T(1,128)}, bf16[1536,1152]{1,0:T(8,128)(2,1)}, bf16[4,512,1536]{2,1,0:T(8,128)(2,1)}, bf16[512,15...) custom-call(f32[512,1536]{1,0:T(8,128)} %get-tuple-element.92.total,, ...), custom_call_target="tpu_custom_call" | custom-call | flops 28991029248 | bytes 47185920 | tf_op jit(solution)/shard_map/pallas_call | solution.py:448
  537.5 7.8 convolution_convert_fusion
  545.3 51.5 %shard_map.238 = (bf16[4,512,512]{2,1,0:T(8,128)(2,1)}, bf16[1536,1152]{1,0:T(8,128)(2,1)}) custom-call(s32[6]{0:T(128)} %concatenate.61.info, bf16[4,512,384]{2,1,0:T(8,128)(2,1)} %get-tuple-element.67.q, bf16[4,512,128]{2,1,0:T(8,128)(2,1)} %copy-done.35, bf16[4,512,128]{2,1,0:T(8,128)(2,1)} %copy-done.36, bf16[4,512,128]{2,1,0:T(8,128)(2,1)} %get-tuple-element.68.k_own, ...), custom_call_target="tpu_custom_call" | custom-call | flops 14495514624 | bytes 47185920 | tf_op jit(solution)/shard_map/pallas_call | solution.py:1044
  608.4 26.6 %collective-permute-done.27 = bf16[512,1536]{1,0:T(8,128)(2,1)S(1)} collective-permute-done((bf16[512,1536]{1,0:T(8,128)(2,1)}, bf16[512,1536]{1,0:T(8,128)(2,1)S(1)}, u32[]{:S(2)}, u32[]{:S(2)}) %collective-permute-start.27) | collective-permute-done | bytes 1572896 | tf_op jit(solution)/shard_map/ppermute | solution.py:21
  640.5 76.5 %shard_map.239 = (bf16[512,1536]{1,0:T(8,128)(2,1)}, f32[1,1536]{1,0:T(1,128)}, bf16[1536,896]{1,0:T(8,128)(2,1)}, f32[1,512]{1,0:T(1,128)}, bf16[512,1536]{1,0:T(8,128)(2,1)}) custom-call(bf16[2048,512]{1,0:T(8,128)(2,1)} %bitcast.143, bf16[1536,512]{1,0:T(8,128)(2,1)} %pad_maximum_fusion.1.weight, bf16[512,1536]{1,0:T(8,128)(2,1)} %copy-done.6, ...), custom_call_target="tpu_custom_call" | custom-call | flops 5637144576 | bytes 31457280 | tf_op jit(solution)/shard_map/pallas_call | solution.py:585
  727.7 27.3 %collective-permute-done.31.refs_0_ = bf16[512,1536]{1,0:T(8,128)(2,1)S(1)} collective-permute-done((bf16[512,1536]{1,0:T(8,128)(2,1)}, bf16[512,1536]{1,0:T(8,128)(2,1)S(1)}, u32[]{:S(2)}, u32[]{:S(2)}) %collective-permute-start.31) | collective-permute-done | bytes 1572896 | tf_op jit(solution)/shard_map/ppermute | solution.py:1421
  778.6 12.6 %collective-permute-done.33.refs_2_ = bf16[512,1536]{1,0:T(8,128)(2,1)} collective-permute-done((bf16[512,1536]{1,0:T(8,128)(2,1)S(1)}, bf16[512,1536]{1,0:T(8,128)(2,1)}, u32[]{:S(2)}, u32[]{:S(2)}) %collective-permute-start.33) | collective-permute-done | bytes 1572896 | tf_op jit(solution)/shard_map/ppermute | solution.py:21
  816.0 9.4 %collective-permute-done.43 = bf16[192,1152]{1,0:T(8,128)(2,1)S(1)} collective-permute-done((bf16[192,1152]{1,0:T(8,128)(2,1)S(1)}, bf16[192,1152]{1,0:T(8,128)(2,1)S(1)}, u32[]{:S(2)}, u32[]{:S(2)}) %collective-permute-start.43) | collective-permute-done | bytes 442400 | tf_op jit(solution)/shard_map/ppermute | solution.py:21
  (257 shorter events, 190.2 us)
Async XLA Ops:
  7.2 120.4 %all-gather.7.cloned.1.call-start = ((), (), s32[]{:S(2)}) async-start(), calls=%async_computation.8 | async-start | bytes 4423680 | tf_op jit(solution)/shard_map/all_gather | solution.py:1176
  16.2 39.7 %collective-permute-start = (bf16[512,1536]{1,0:T(8,128)(2,1)S(1)}, bf16[512,1536]{1,0:T(8,128)(2,1)S(1)}, u32[]{:S(2)}, u32[]{:S(2)}) collective-permute-start(bf16[512,1536]{1,0:T(8,128)(2,1)S(1)} %dynamic-slice_bitcast_fusion.4), channel_id=1, source_target_pairs={{0,0},{1,17},{2,10},{3,27},{8,8},{9,25},{10,18},{11,3},{16,16},{17... | collective-permute-start | bytes 4718600 | tf_op jit(solution)/shard_map/ppermute | solution.py:1152
  55.9 234.6 %all-gather.9.cloned.1.call-start = ((), (), s32[]{:S(2)}) async-start(), calls=%async_computation.9 | async-start | bytes 4423680 | tf_op jit(solution)/shard_map/all_gather | solution.py:1176
  59.5 35.7 %collective-permute-start.16 = (bf16[192,3456]{1,0:T(8,128)(2,1)S(1)}, bf16[192,3456]{1,0:T(8,128)(2,1)S(1)}, u32[]{:S(2)}, u32[]{:S(2)}) collective-permute-start(bf16[192,3456]{1,0:T(8,128)(2,1)S(1)} %pad_maximum_fusion.6), channel_id=1, source_target_pairs={{0,4},{4,0},{1,5},{5,1},{2,6},{6,2},{3,7},{7,3},{8,12},{12,8},{9,1... | collective-permute-start | bytes 3981320 | tf_op jit(solution)/shard_map/ppermute | solution.py:21
  98.7 252.7 %all-gather.11.cloned.1.call-start = ((), (), s32[]{:S(2)}) async-start(), calls=%async_computation.10 | async-start | bytes 8847360 | tf_op jit(solution)/shard_map/all_gather | solution.py:1176
  122.6 676.2 %reduce-scatter.5.cloned.1.call-start = ((), (), s32[]{:S(2)}) async-start(), calls=%async_computation.4 | async-start | bytes 4423680 | tf_op jit(solution)/shard_map/reduce_scatter | solution.py:1412
  187.6 35.9 %collective-permute-start.9 = (bf16[512,1536]{1,0:T(8,128)(2,1)}, bf16[512,1536]{1,0:T(8,128)(2,1)}, u32[]{:S(2)}, u32[]{:S(2)}) collective-permute-start(bf16[512,1536]{1,0:T(8,128)(2,1)} %add_convert_fusion.1), channel_id=1, source_target_pairs={{0,2},{1,3},{2,0},{3,1},{4,6},{5,7},{6,4},{7,5},{8,10},{9,11},{10,... | collective-permute-start | bytes 4718600 | tf_op jit(solution)/shard_map/ppermute | solution.py:21
  216.7 37.0 %collective-permute-start.12 = (bf16[512,1536]{1,0:T(8,128)(2,1)}, bf16[512,1536]{1,0:T(8,128)(2,1)}, u32[]{:S(2)}, u32[]{:S(2)}) collective-permute-start(bf16[512,1536]{1,0:T(8,128)(2,1)} %get-tuple-element.76.refs_0_.own_grad), channel_id=1, source_target_pairs={{0,4},{4,0},{1,5},{5,1},{2,6},{6,2},{3,7},{7,3},{8,12},{12,8},{9,1... | collective-permute-start | bytes 4718600 | tf_op jit(solution)/shard_map/ppermute | solution.py:21
  218.7 68.7 %collective-permute-start.14 = (bf16[512,1536]{1,0:T(8,128)(2,1)}, bf16[512,1536]{1,0:T(8,128)(2,1)}, u32[]{:S(2)}, u32[]{:S(2)}) collective-permute-start(bf16[512,1536]{1,0:T(8,128)(2,1)} %get-tuple-element.78.refs_2_), channel_id=1, source_target_pairs={{0,4},{4,0},{1,5},{5,1},{2,6},{6,2},{3,7},{7,3},{8,12},{12,8},{9,1... | collective-permute-start | bytes 4718600 | tf_op jit(solution)/shard_map/ppermute | solution.py:21
  253.8 36.8 %collective-permute-start.13 = (bf16[512,1536]{1,0:T(8,128)(2,1)}, bf16[512,1536]{1,0:T(8,128)(2,1)}, u32[]{:S(2)}, u32[]{:S(2)}) collective-permute-start(bf16[512,1536]{1,0:T(8,128)(2,1)} %collective-permute-done.12.refs_4_), channel_id=1, source_target_pairs={{0,1},{1,0},{2,3},{3,2},{4,5},{5,4},{6,7},{7,6},{8,9},{9,8},{10,11... | collective-permute-start | bytes 4718600 | tf_op jit(solution)/shard_map/ppermute | solution.py:21
  288.1 36.1 %collective-permute-start.11 = (bf16[512,1536]{1,0:T(8,128)(2,1)S(1)}, bf16[512,1536]{1,0:T(8,128)(2,1)S(1)}, u32[]{:S(2)}, u32[]{:S(2)}) collective-permute-start(bf16[512,1536]{1,0:T(8,128)(2,1)S(1)} %multiply_convert_fusion.refs_0_), channel_id=1, source_target_pairs={{0,2},{1,3},{2,0},{3,1},{4,6},{5,7},{6,4},{7,5},{8,10},{9,11},{10,... | collective-permute-start | bytes 4718600 | tf_op jit(solution)/shard_map/ppermute | solution.py:21
  288.5 36.4 %collective-permute-start.18 = (bf16[512,1536]{1,0:T(8,128)(2,1)S(1)}, bf16[512,1536]{1,0:T(8,128)(2,1)}, u32[]{:S(2)}, u32[]{:S(2)}) collective-permute-start(bf16[512,1536]{1,0:T(8,128)(2,1)S(1)} %multiply_convert_fusion.refs_0_), channel_id=1, source_target_pairs={{0,4},{4,0},{1,5},{5,1},{2,6},{6,2},{3,7},{7,3},{8,12},{12,8},{9,1... | collective-permute-start | bytes 4718600 | tf_op jit(solution)/shard_map/ppermute | solution.py:21
  290.0 58.1 %collective-permute-start.10 = (bf16[512,1536]{1,0:T(8,128)(2,1)S(1)}, bf16[512,1536]{1,0:T(8,128)(2,1)}, u32[]{:S(2)}, u32[]{:S(2)}) collective-permute-start(bf16[512,1536]{1,0:T(8,128)(2,1)S(1)} %multiply_convert_fusion.refs_0_), channel_id=1, source_target_pairs={{0,1},{1,0},{2,3},{3,2},{4,5},{5,4},{6,7},{7,6},{8,9},{9,8},{10,11... | collective-permute-start | bytes 4718600 | tf_op jit(solution)/shard_map/ppermute | solution.py:21
  478.7 320.1 %reduce-scatter.7.cloned.1.call-start = ((), (), s32[]{:S(2)}) async-start(), calls=%async_computation.5 | async-start | bytes 4423680 | tf_op jit(solution)/shard_map/reduce_scatter | solution.py:1412
  532.8 266.1 %reduce-scatter.9.cloned.1.call-start = ((), (), s32[]{:S(2)}) async-start(), calls=%async_computation.6 | async-start | bytes 4423680 | tf_op jit(solution)/shard_map/reduce_scatter | solution.py:1412
  535.9 60.9 %collective-permute-start.26 = (bf16[256,1536]{1,0:T(8,128)(2,1)}, bf16[256,1536]{1,0:T(8,128)(2,1)}, u32[]{:S(2)}, u32[]{:S(2)}) collective-permute-start(bf16[256,1536]{1,0:T(8,128)(2,1)} %get-tuple-element.105), channel_id=1, source_target_pairs={{0,2},{1,3},{2,0},{3,1},{4,6},{5,7},{6,4},{7,5},{8,10},{9,11},{10,... | collective-permute-start | bytes 2359304 | tf_op jit(solution)/shard_map/ppermute | solution.py:21
  537.5 63.0 %collective-permute-start.24 = (bf16[256,1536]{1,0:T(8,128)(2,1)}, bf16[256,1536]{1,0:T(8,128)(2,1)}, u32[]{:S(2)}, u32[]{:S(2)}) collective-permute-start(bf16[256,1536]{1,0:T(8,128)(2,1)} %get-tuple-element.103), channel_id=1, source_target_pairs={{0,4},{4,0},{1,5},{5,1},{2,6},{6,2},{3,7},{7,3},{8,12},{12,8},{9,1... | collective-permute-start | bytes 2359304 | tf_op jit(solution)/shard_map/ppermute | solution.py:21
  596.8 239.4 %reduce-scatter.11.cloned.1.call-start = ((), (), s32[]{:S(2)}) async-start(), calls=%async_computation.7 | async-start | bytes 1720320 | tf_op jit(solution)/shard_map/reduce_scatter | solution.py:83
  603.2 35.2 %collective-permute-start.25 = (bf16[512,1536]{1,0:T(8,128)(2,1)}, bf16[512,1536]{1,0:T(8,128)(2,1)S(1)}, u32[]{:S(2)}, u32[]{:S(2)}) collective-permute-start(bf16[512,1536]{1,0:T(8,128)(2,1)} %pad_maximum_fusion.3), channel_id=1, source_target_pairs={{0,2},{1,3},{2,0},{3,1},{4,6},{5,7},{6,4},{7,5},{8,10},{9,11},{10,... | collective-permute-start | bytes 4718600 | tf_op jit(solution)/shard_map/ppermute | solution.py:21
  717.1 37.9 %collective-permute-start.31 = (bf16[512,1536]{1,0:T(8,128)(2,1)}, bf16[512,1536]{1,0:T(8,128)(2,1)S(1)}, u32[]{:S(2)}, u32[]{:S(2)}) collective-permute-start(bf16[512,1536]{1,0:T(8,128)(2,1)} %get-tuple-element.107), channel_id=1, source_target_pairs={{0,0},{17,1},{10,2},{27,3},{8,8},{25,9},{18,10},{3,11},{16,16},{1,... | collective-permute-start | bytes 4718600 | tf_op jit(solution)/shard_map/ppermute | solution.py:1421
  719.0 39.5 %collective-permute-start.29 = (bf16[512,1536]{1,0:T(8,128)(2,1)}, bf16[512,1536]{1,0:T(8,128)(2,1)}, u32[]{:S(2)}, u32[]{:S(2)}) collective-permute-start(bf16[512,1536]{1,0:T(8,128)(2,1)} %get-tuple-element.106.refs_0_), channel_id=1, source_target_pairs={{0,2},{1,3},{2,0},{3,1},{4,6},{5,7},{6,4},{7,5},{8,10},{9,11},{10,... | collective-permute-start | bytes 4718600 | tf_op jit(solution)/shard_map/ppermute | solution.py:21
  725.2 67.6 %collective-permute-start.28 = (bf16[512,1536]{1,0:T(8,128)(2,1)}, bf16[512,1536]{1,0:T(8,128)(2,1)}, u32[]{:S(2)}, u32[]{:S(2)}) collective-permute-start(bf16[512,1536]{1,0:T(8,128)(2,1)} %get-tuple-element.106.refs_0_), channel_id=1, source_target_pairs={{0,1},{1,0},{2,3},{3,2},{4,5},{5,4},{6,7},{7,6},{8,9},{9,8},{10,11... | collective-permute-start | bytes 4718600 | tf_op jit(solution)/shard_map/ppermute | solution.py:21
  755.0 36.2 %collective-permute-start.33 = (bf16[512,1536]{1,0:T(8,128)(2,1)S(1)}, bf16[512,1536]{1,0:T(8,128)(2,1)}, u32[]{:S(2)}, u32[]{:S(2)}) collective-permute-start(bf16[512,1536]{1,0:T(8,128)(2,1)S(1)} %collective-permute-done.31.refs_0_), channel_id=1, source_target_pairs={{0,2},{1,3},{2,0},{3,1},{4,6},{5,7},{6,4},{7,5},{8,10},{9,11},{10,... | collective-permute-start | bytes 4718600 | tf_op jit(solution)/shard_map/ppermute | solution.py:21
  763.4 35.4 %collective-permute-start.35 = (bf16[4,192,896]{2,1,0:T(8,128)(2,1)}, bf16[4,192,896]{2,1,0:T(8,128)(2,1)}, u32[]{:S(2)}, u32[]{:S(2)}) collective-permute-start(bf16[4,192,896]{2,1,0:T(8,128)(2,1)} %get-tuple-element.146), channel_id=1, source_target_pairs={{0,4},{4,0},{1,5},{5,1},{2,6},{6,2},{3,7},{7,3},{8,12},{12,8},{9,1... | collective-permute-start | bytes 4128776 | tf_op jit(solution)/shard_map/ppermute | solution.py:21
  (66 other events, 937.7 us)
Sparse Core Ops, SparseCore 0:
  56.1 71.4 all-gather.6
  129.2 68.5 all-gather.8
  199.9 127.0 all-gather.10
  478.9 65.6 reduce-scatter.4
  546.7 66.6 reduce-scatter.6
  615.6 81.9 reduce-scatter.8
  802.2 31.3 reduce-scatter.10

commit v5 on v4

--- a/solution.py
+++ b/solution.py
@@ -200,6 +200,112 @@
     )(*lefts, *[w for w, _, _ in weights])
 
 
+def chosen_kernel(near, count, info, cotangent, *refs):
+    slot = pl.program_id(0)
+    others, (weight, lin, stacked) = refs[:count], refs[count:]
+
+    @pl.when(slot < near)
+    def _():
+        stacked[...] = cotangent[0]
+
+    for k, other in enumerate(others):
+
+        @pl.when((slot >= near) & (info[slot] == k))
+        def _():
+            stacked[...] = other[...]
+
+    lin[...] = jnp.dot(stacked[...], weight[...], preferred_element_type=WIDE).astype(LOW)
+
+
+def chosen_rows(info, cotangent, others, weight, part, parts):
+    near, length, width = cotangent.shape
+    slots, cols = near + len(others), weight.shape[1] // parts
+    held = lambda rows, n, at: pl.BlockSpec(
+        (rows, n), lambda s, info: (0, at), pipeline_mode=pl.Buffered(1)
+    )
+    return pl.pallas_call(
+        functools.partial(chosen_kernel, near, len(others)),
+        grid_spec=pltpu.PrefetchScalarGridSpec(
+            num_scalar_prefetch=1,
+            grid=(slots,),
+            in_specs=[
+                pl.BlockSpec((1, length, width), lambda s, info: (info[jnp.minimum(s, near - 1)], 0, 0))
+            ]
+            + [held(length, width, 0)] * len(others)
+            + [held(width, cols, part)],
+            out_specs=[
+                pl.BlockSpec((length, cols), lambda s, info: (s, 0)),
+                pl.BlockSpec((length, width), lambda s, info: (s, 0)),
+            ],
+        ),
+        out_shape=[
+            jax.ShapeDtypeStruct((slots * length, cols), LOW),
+            jax.ShapeDtypeStruct((slots * length, width), LOW),
+        ],
+        compiler_params=pltpu.CompilerParams(vmem_limit_bytes=60 << 20),
+        cost_estimate=estimate(
+            2 * slots * length * width * cols, 2 * (slots * length * (2 * width + cols) + width * cols)
+        ),
+    )(info, cotangent, *others, weight)
+
+
+def full_units_kernel(h, g, down, gate, up, hid, grad_gate, grad_up):
+    gate_lin = jnp.dot(h[...], gate[...], preferred_element_type=WIDE)
+    up_lin = jnp.dot(h[...], up[...], preferred_element_type=WIDE)
+    grad_hidden = jnp.dot(g[...], down[...], preferred_element_type=WIDE)
+    sigmoid = 1.0 / (1.0 + jnp.exp(-gate_lin))
+    silu = gate_lin * sigmoid
+    hid[...] = (silu * up_lin).astype(LOW)
+    grad_gate[...] = (grad_hidden * up_lin * sigmoid * (1.0 + gate_lin * (1.0 - sigmoid))).astype(LOW)
+    grad_up[...] = (grad_hidden * silu).astype(LOW)
+
+
+def full_units(h, g, weight):
+    tokens, width = h.shape
+    cols = weight.shape[1] // 3
+    step = math.gcd(512, tokens)
+    by_row = lambda n: pl.BlockSpec((step, n), lambda i: (i, 0))
+    return pl.pallas_call(
+        full_units_kernel,
+        grid=(tokens // step,),
+        in_specs=[by_row(width)] * 2 + [part_spec(width, cols, i) for i in range(3)],
+        out_specs=[by_row(cols)] * 3,
+        out_shape=[jax.ShapeDtypeStruct((tokens, cols), LOW)] * 3,
+        compiler_params=pltpu.CompilerParams(vmem_limit_bytes=60 << 20),
+        cost_estimate=estimate(
+            6 * tokens * width * cols, 2 * (2 * tokens * width + 3 * width * cols + 3 * tokens * cols)
+        ),
+    )(h, g, weight, weight, weight)
+
+
+def first_grads_kernel(g, h, hid, gate, up, out):
+    part = pl.program_id(0)
+    for i, (left, right) in enumerate(((g, hid), (h, gate), (h, up))):
+
+        @pl.when(part == i)
+        def _():
+            out[...] = dot_rows(left[...], right[...]).astype(LOW)
+
+
+def first_grads(grad_rows, rows, hid, grad_gate, grad_up):
+    tokens, width = rows.shape
+    cols, tile = hid.shape[1], 256
+    tiles = width // tile
+    return pl.pallas_call(
+        first_grads_kernel,
+        grid=(3, tiles),
+        in_specs=[
+            pl.BlockSpec((tokens, tile), lambda p, i: (0, jnp.where(p == 0, i, tiles - 1))),
+            pl.BlockSpec((tokens, tile), lambda p, i: (0, jnp.where(p == 0, 0, i))),
+        ]
+        + [whole_spec(tokens, cols, once=True)] * 3,
+        out_specs=pl.BlockSpec((tile, cols), lambda p, i: (i, p)),
+        out_shape=jax.ShapeDtypeStruct((width, 3 * cols), LOW),
+        compiler_params=pltpu.CompilerParams(vmem_limit_bytes=60 << 20),
+        cost_estimate=estimate(6 * tokens * width * cols, 6 * tokens * cols + 6 * width * cols),
+    )(grad_rows, rows, hid, grad_gate, grad_up)
+
+
 MESH_ID = pl.DeviceIdType.MESH
 
 
@@ -216,81 +322,94 @@
 
 
 def collect_kernel(
-    slots, gate, up, weight_gate, weight_up, left, right, total, grad, parts, core_in, across_in,
-    last_in, held, send, recv, load
+    slots, tiles, gate_a, up_a, gate_b, up_b, w_gate_a, w_up_a, w_gate_b, w_up_b, left, right, hid, up, total,
+    down_out, up_out, parts, sent, core_in, across_in, last_in, held, send, recv, load
 ):
     step = pl.program_id(0)
     steps = pl.num_programs(0)
     core, far, side = partners_of()
     half = total.shape[0] // 2
-
-    def remote(source, target, index, partner):
-        return pltpu.make_async_remote_copy(
-            source, target, send.at[index], recv.at[index], device_id=partner, device_id_type=MESH_ID
-        )
-
-    cores = [remote(parts.at[7 - 2 * k], core_in.at[k], k, core) for k in range(4)]
+    remote = remote_copy(send, recv)
+    cores = [remote(sent.at[k % 2], core_in.at[k], k, core) for k in range(4)]
     across = [
-        remote(parts.at[6, pl.ds(0, half)], across_in.at[0], 4, far),
-        remote(parts.at[6, pl.ds(half, half)], across_in.at[1], 5, side),
+        remote(parts.at[3, pl.ds(0, half)], across_in.at[0], 4, far),
+        remote(parts.at[3, pl.ds(half, half)], across_in.at[1], 5, side),
     ]
     lasts = [
-        remote(parts.at[2], last_in.at[0], 6, far),
-        remote(parts.at[4, pl.ds(half, half)], last_in.at[1, pl.ds(half, half)], 7, side),
-        remote(parts.at[4, pl.ds(0, half)], last_in.at[1, pl.ds(0, half)], 8, side),
+        remote(parts.at[1], last_in.at[0], 6, far),
+        remote(parts.at[2, pl.ds(half, half)], last_in.at[1, pl.ds(half, half)], 7, side),
+        remote(parts.at[2, pl.ds(0, half)], last_in.at[1, pl.ds(0, half)], 8, side),
     ]
-    loading = pltpu.make_async_copy(right, held, load)
+    loading = [
+        pltpu.make_async_copy(source, held.at[i], load.at[i]) for i, source in enumerate((hid, up))
+    ]
 
     @pl.when(step == 0)
     def _():
-        loading.start()
+        for copy in loading:
+            copy.start()
         meet((core, far, side))
 
+    for k in (2, 3):
+        pl.when(step == 2 * k)(cores[k - 2].wait_send)
+
     @pl.when(step < slots)
     def _():
-        part = dot_cols(gate[...], weight_gate[...]) + dot_cols(up[...], weight_up[...])
-        parts[slots - 1 - step] = part.astype(LOW)
+        part = (
+            dot_cols(gate_a[...], w_gate_a[...])
+            + dot_cols(up_a[...], w_up_a[...])
+            + dot_cols(gate_b[...], w_gate_b[...])
+            + dot_cols(up_b[...], w_up_b[...])
+        )
 
         @pl.when(step == slots - 1)
         def _():
             total[...] = part
 
-    for k in range(4):
-        pl.when(step == 2 * k)(cores[k].start)
+        for k in range(4):
+
+            @pl.when(step == 2 * k)
+            def _():
+                sent[k % 2] = part.astype(LOW)
+                cores[k].start()
+
+            if k < 3:
+
+                @pl.when(step == 2 * k + 1)
+                def _():
+                    cores[k].wait_recv()
+                    parts[3 - k] = (part + core_in[k].astype(WIDE)).astype(LOW)
 
     def add(slot, rows, value):
         parts[slot, rows] = (parts[slot, rows].astype(WIDE) + value.astype(WIDE)).astype(LOW)
 
-    whole, low, high = slice(None), pl.ds(0, half), pl.ds(half, half)
+    low, high = pl.ds(0, half), pl.ds(half, half)
 
     @pl.when(step == 1)
     def _():
-        cores[0].wait_recv()
-        add(6, whole, core_in[0])
         for copy in across:
             copy.start()
 
-    @pl.when(step == 3)
-    def _():
-        cores[1].wait_recv()
-        add(4, whole, core_in[1])
-        lasts[1].start()
+    pl.when(step == 3)(lasts[1].start)
 
     @pl.when(step == 5)
     def _():
-        cores[2].wait_recv()
-        add(2, whole, core_in[2])
         across[1].wait_recv()
-        add(2, high, across_in[1])
+        add(1, high, across_in[1])
         lasts[0].start()
         across[0].wait_recv()
-        add(4, low, across_in[0])
+        add(2, low, across_in[0])
         lasts[2].start()
 
-    @pl.when(step >= slots)
-    def _():
-        pl.when(step == slots)(loading.wait)
-        grad[...] = dot_rows(left[...], held[...]).astype(LOW)
+    @pl.when((step >= slots) & (step < slots + tiles))
+    def _():
+        pl.when(step == slots)(loading[0].wait)
+        down_out[...] = dot_rows(left[...], held[0]).astype(LOW)
+
+    @pl.when(step >= slots + tiles)
+    def _():
+        pl.when(step == slots + tiles)(loading[1].wait)
+        up_out[...] = dot_rows(right[...], held[1]).astype(LOW)
 
     @pl.when(step == steps - 1)
     def _():
@@ -300,51 +419,57 @@
         total[...] += (
             core_in[3].astype(WIDE) + last_in[0].astype(WIDE) + last_in[1].astype(WIDE)
         )
-        for copy in (*cores, *across, *lasts):
+        for copy in (*cores[2:], *across, *lasts):
             copy.wait_send()
 
 
-def collect_back(grad_gate, grad_up, weight, left, right, length):
-    tokens, cols = grad_gate.shape
-    width = weight.shape[0]
+def collect_back(first, second, weight_a, weight_b, grad_rows, rows, hid, length):
+    tokens, cols_a = first[0].shape
+    cols = second[0].shape[1]
+    width = weight_a.shape[0]
     slots, tile = tokens // length, 256
     tiles = width // tile
-    row = pl.BlockSpec((length, cols), lambda i: (jnp.maximum(slots - 1 - i, 0), 0))
-    column = lambda i: jnp.clip(i - slots, 0, tiles - 1)
+    row = lambda n: pl.BlockSpec((length, n), lambda i: (jnp.maximum(slots - 1 - i, 0), 0))
+    column = lambda i, start: jnp.clip(i - start, 0, tiles - 1)
+    down_at, up_at = (lambda i: column(i, slots)), (lambda i: column(i, slots + tiles))
     return pl.pallas_call(
-        functools.partial(collect_kernel, slots),
-        grid=(slots + tiles,),
-        in_specs=[
-            row,
-            row,
-            part_spec(width, cols, 0),
-            part_spec(width, cols, 1),
-            pl.BlockSpec((tokens, tile), lambda i: (0, column(i))),
-            pl.BlockSpec(memory_space=pl.ANY),
+        functools.partial(collect_kernel, slots, tiles),
+        grid=(slots + 2 * tiles,),
+        in_specs=[row(cols_a), row(cols_a), row(cols), row(cols)]
+        + [part_spec(width, cols_a, 1), part_spec(width, cols_a, 2)]
+        + [part_spec(width, cols, 1), part_spec(width, cols, 2)]
+        + [
+            pl.BlockSpec((tokens, tile), lambda i: (0, down_at(i))),
+            pl.BlockSpec((tokens, tile), lambda i: (0, up_at(i))),
+            ANYWHERE,
+            ANYWHERE,
         ],
         out_specs=[
-            pl.BlockSpec((length, width), lambda i: (0, 0)),
-            pl.BlockSpec((tile, cols), lambda i: (column(i), 0)),
+            whole_spec(length, width, once=True),
+            pl.BlockSpec((tile, cols), lambda i: (down_at(i), 0)),
+            pl.BlockSpec((tile, cols), lambda i: (up_at(i), 0)),
         ],
         out_shape=[
             jax.ShapeDtypeStruct((length, width), WIDE),
             jax.ShapeDtypeStruct((width, cols), LOW),
+            jax.ShapeDtypeStruct((width, cols), LOW),
         ],
         scratch_shapes=[
-            pltpu.VMEM((slots, length, width), LOW),
+            pltpu.VMEM((4, length, width), LOW),
+            pltpu.VMEM((2, length, width), LOW),
             pltpu.VMEM((4, length, width), LOW),
             pltpu.VMEM((2, length // 2, width), LOW),
             pltpu.VMEM((2, length, width), LOW),
-            pltpu.VMEM((tokens, cols), LOW),
+            pltpu.VMEM((2, tokens, cols), LOW),
             pltpu.SemaphoreType.DMA((9,)),
             pltpu.SemaphoreType.DMA((9,)),
-            pltpu.SemaphoreType.DMA,
+            pltpu.SemaphoreType.DMA((2,)),
         ],
         compiler_params=pltpu.CompilerParams(
             vmem_limit_bytes=63 << 20, collective_id=1, has_side_effects=True
         ),
         cost_estimate=estimate(6 * tokens * width * cols, 10 * tokens * cols),
-    )(grad_gate, grad_up, weight, weight, left, right)
+    )(*first, *second, weight_a, weight_a, weight_b, weight_b, grad_rows, rows, hid, second[1])
 
 
 def remote_copy(send, recv):
@@ -357,7 +482,7 @@
 
 
 def branch_kernel(
-    slots, tiles, total, middle, own_grad, gain, hid, weight, turned, gate, grad_middle, gain_grad,
+    slots, tiles, total, middle, own_grad, gain, hid_a, hid_b, w_a, w_b, turned, gate, grad_middle, gain_grad,
     gate_out, branch, mlp_own, mlp_far, mlp_side, mlp_first, mlp_second, own, parts, core_in, held,
     send, recv, load
 ):
@@ -397,7 +522,8 @@
 
     @pl.when(step < slots)
     def _():
-        parts[slots - 1 - step] = dot_cols(hid[...], weight[...]).astype(LOW)
+        part = dot_cols(hid_a[...], w_a[...]) + dot_cols(hid_b[...], w_b[...])
+        parts[slots - 1 - step] = part.astype(LOW)
 
     for k in range(4):
         pl.when(step == 2 * k)(cores[k].start)
@@ -436,7 +562,7 @@
 ANYWHERE = pl.BlockSpec(memory_space=pl.ANY)
 
 
-def spread_branch(total, middle, own_grad, gain, hid, weight, rows, grad_gate):
+def spread_branch(total, middle, own_grad, gain, hid_a, hid_b, weight_a, weight_b, rows, grad_gate):
     length, width = total.shape
     tokens, cols = grad_gate.shape
     slots, tile = tokens // length, 256
@@ -453,7 +579,9 @@
             once,
             once,
             whole_spec(1, width),
+            pl.BlockSpec((length, hid_a.shape[1]), lambda i: (jnp.maximum(slots - 1 - i, 0), 0)),
             pl.BlockSpec((length, cols), lambda i: (jnp.maximum(slots - 1 - i, 0), 0)),
+            part_spec(width, hid_a.shape[1], 0),
             part_spec(width, cols, 0),
             pl.BlockSpec((tokens, tile), lambda i: (0, column(i))),
             ANYWHERE,
@@ -488,11 +616,11 @@
             vmem_limit_bytes=63 << 20, collective_id=2, has_side_effects=True
         ),
         cost_estimate=estimate(4 * tokens * width * cols, 10 * tokens * cols),
-    )(total, middle, own_grad, gain, hid, weight, rows, grad_gate)
+    )(total, middle, own_grad, gain, hid_a, hid_b, weight_a, weight_b, rows, grad_gate)
 
 
 def line_kernel(
-    slots, tiles, line, weight, own_in, grad_middle, gain, rows_one, branch, line_all, mixed, block, share,
+    slots, tiles, line, weight, own_in, grad_middle, gain, rows_one, line_all, block, share,
     gain_grad, attn_out, bias_out, home, parts, core_in, far_in, total, send, recv, load
 ):
     step = pl.program_id(0)
@@ -550,9 +678,7 @@
 
     @pl.when(step >= slots)
     def _():
-        cols = line_all.shape[1]
-        attn_out[:, :cols] = dot_rows(rows_one[...], line_all[...]).astype(LOW)
-        attn_out[:, cols:] = dot_rows(branch[...], mixed[...]).astype(LOW)
+        attn_out[...] = dot_rows(rows_one[...], line_all[...]).astype(LOW)
 
     @pl.when(step == slots + tiles - 1)
     def _():
@@ -573,7 +699,7 @@
             leave.wait_send()
 
 
-def finish_rows(line, weight, own_in, grad_middle, gain, rows_one, branch, mixed, block):
+def finish_rows(line, weight, own_in, grad_middle, gain, rows_one, block):
     length, width = own_in.shape
     near_tokens, line_cols = line.shape
     slots, tile = near_tokens // length, 256
@@ -581,7 +707,7 @@
     once = whole_spec(length, width, once=True)
     column = lambda i: jnp.clip(i - slots, 0, tiles - 1)
     by_column = lambda n: pl.BlockSpec((n, tile), lambda i: (0, column(i)))
-    attn_cols = line_cols + mixed.shape[1]
+    attn_cols = line_cols
     return pl.pallas_call(
         functools.partial(line_kernel, slots, tiles),
         grid=(slots + tiles,),
@@ -592,9 +718,7 @@
             once,
             whole_spec(1, width),
             by_column(near_tokens),
-            by_column(near_tokens),
             whole_spec(near_tokens, line_cols, once=True),
-            whole_spec(*mixed.shape, once=True),
             ANYWHERE,
         ],
         out_specs=[
@@ -624,7 +748,7 @@
             vmem_limit_bytes=63 << 20, collective_id=3, has_side_effects=True
         ),
         cost_estimate=estimate(2 * near_tokens * width * attn_cols, 10 * near_tokens * width),
-    )(line, weight, own_in, grad_middle, gain, rows_one, branch, line, mixed, block)
+    )(line, weight, own_in, grad_middle, gain, rows_one, line, block)
 
 
 def place_kernel(count, info, *refs):
@@ -946,24 +1070,40 @@
 
 def exchange_kernel(
     heads, head_dim, scale, slots, tiles, info, q, k_past, v_past, k_own, v_own, grad, lse, cosine, sine,
-    cosine_all, sine_all, turned, up, line, up_out, mine_past, mine_own, other_past, other_own, got_past,
-    got_own, side_out, side_in, dk_past, dk_own, dv_past, dv_own, held, send, recv, load
+    cosine_all, sine_all, branch, mixed, first, second, mlp_far, mlp_side, mlp_own, middle, line, out_grad,
+    block, mine_past, mine_own, other_past, other_own, got_past, got_own, side_out, side_in, dk_past, dk_own,
+    dv_past, dv_own, across_in, rows, last_in, send, recv, load
 ):
     step = pl.program_id(0)
     tensor_rank = lax.axis_index("tp")
-    core, _, side = partners_of()
+    core, far, side = partners_of()
     parity = lax.rem(tensor_rank, 2)
     offset = lax.axis_index("ctx") * q.shape[1]
     remote = remote_copy(send, recv)
     pasts = [remote(other_past.at[r], got_past.at[r ^ 1], r, core) for r in range(slots)]
     owns = [remote(other_own.at[r], got_own.at[r ^ 1], slots + r, core) for r in range(slots)]
     sides = [remote(side_out.at[r], side_in.at[r], 2 * slots + r, side) for r in range(slots)]
-    loading = pltpu.make_async_copy(up, held, load)
+    across = [
+        remote(first, across_in.at[0], 3 * slots, far),
+        remote(second, across_in.at[1], 3 * slots + 1, side),
+    ]
+    lasts = [
+        remote(rows.at[0], last_in.at[0], 3 * slots + 2, far),
+        remote(rows.at[1], last_in.at[1], 3 * slots + 3, side),
+    ]
+    loading = [
+        pltpu.make_async_copy(source, rows.at[i], load.at[i])
+        for i, source in enumerate((mlp_far, mlp_side, mlp_own))
+    ]
+    half = across_in.shape[1]
 
     @pl.when(step == 0)
     def _():
-        loading.start()
-        meet((core, side))
+        for copy in loading:
+            copy.start()
+        meet((core, far, side))
+        for copy in across:
+            copy.start()
 
     @pl.when(step < slots)
     def _():
@@ -1008,10 +1148,19 @@
 
         pl.when(step == pair + 1)(merge)
 
+    @pl.when(step == slots - 1)
+    def _():
+        for copy in loading:
+            copy.wait()
+        for copy in across:
+            copy.wait_recv()
+        for i, here in ((0, pl.ds(half, half)), (1, pl.ds(0, half))):
+            rows[i, here] = (rows[i, here].astype(WIDE) + across_in[1 - i].astype(WIDE)).astype(LOW)
+            lasts[i].start()
+
     @pl.when(step >= slots)
     def _():
-        pl.when(step == slots)(loading.wait)
-        up_out[...] = dot_rows(turned[...], held[...]).astype(LOW)
+        out_grad[...] = dot_rows(branch[...], mixed[...]).astype(LOW)
 
     @pl.when(step == slots + tiles - 1)
     def _():
@@ -1021,17 +1170,21 @@
             total = mine_own[r] + got_own[r] + side_in[r].astype(WIDE)
             back = turn_back(total, cosine_all[r], sine_all[r])
             line[r, :, heads * head_dim :] = jnp.where(parity == 0, back, total).astype(LOW)
-        for copy in (*pasts, *owns, *sides):
+        for copy in lasts:
+            copy.wait_recv()
+        block[...] = (
+            middle[...] + rows[2].astype(WIDE) + last_in[0].astype(WIDE) + last_in[1].astype(WIDE)
+        ).astype(LOW)
+        for copy in (*pasts, *owns, *sides, *across, *lasts):
             copy.wait_send()
 
 
 def attend_exchange(
-    info, q, k_past, v_past, k_own, v_own, grad, lse, cosine, sine, heads, head_dim, scale, rows, grad_up
+    info, q, k_past, v_past, k_own, v_own, grad, lse, cosine, sine, heads, head_dim, scale, branch, mixed, mlp, middle
 ):
     count, length, width = q.shape
     past = k_past.shape[1]
-    tokens, cols = grad_up.shape
-    model_width = rows.shape[1]
+    tokens, model_width = branch.shape
     tile = 256
     tiles = model_width // tile
     slot = lambda i: jnp.minimum(i, count - 1)
@@ -1059,31 +1212,37 @@
                 held(count, length, head_dim),
                 held(count, length, head_dim),
                 pl.BlockSpec((tokens, tile), lambda i, info: (0, column(i))),
-                ANYWHERE,
-            ],
+                held(*mixed.shape),
+            ]
+            + [ANYWHERE] * 5
+            + [held(length, model_width)],
             out_specs=[
-                pl.BlockSpec((count, length, line_cols), lambda i, info: (0, 0, 0)),
-                pl.BlockSpec((tile, cols), lambda i, info: (column(i), 0)),
+                held(count, length, line_cols),
+                pl.BlockSpec((tile, width), lambda i, info: (column(i), 0)),
+                held(length, model_width),
             ],
             scratch_shapes=[pltpu.VMEM((count, length, head_dim), WIDE)] * 6
             + [pltpu.VMEM((count, length, head_dim), LOW)] * 2
             + [pltpu.VMEM((length, head_dim), WIDE)] * 4
             + [
-                pltpu.VMEM((tokens, cols), LOW),
-                pltpu.SemaphoreType.DMA((3 * count,)),
-                pltpu.SemaphoreType.DMA((3 * count,)),
-                pltpu.SemaphoreType.DMA,
+                pltpu.VMEM((2, length // 2, model_width), LOW),
+                pltpu.VMEM((3, length, model_width), LOW),
+                pltpu.VMEM((2, length, model_width), LOW),
+                pltpu.SemaphoreType.DMA((3 * count + 4,)),
+                pltpu.SemaphoreType.DMA((3 * count + 4,)),
+                pltpu.SemaphoreType.DMA((3,)),
             ],
         ),
         out_shape=[
             jax.ShapeDtypeStruct((count, length, line_cols), LOW),
-            jax.ShapeDtypeStruct((model_width, cols), LOW),
+            jax.ShapeDtypeStruct((model_width, width), LOW),
+            jax.ShapeDtypeStruct((length, model_width), LOW),
         ],
         compiler_params=pltpu.CompilerParams(
             vmem_limit_bytes=63 << 20, collective_id=4, has_side_effects=True
         ),
-        cost_estimate=estimate(2 * tokens * model_width * cols, 10 * tokens * cols),
-    )(info, q, k_past, v_past, k_own, v_own, grad, lse, cosine, sine, cosine, sine, rows, grad_up)
+        cost_estimate=estimate(2 * tokens * model_width * width, 10 * tokens * width),
+    )(info, q, k_past, v_past, k_own, v_own, grad, lse, cosine, sine, cosine, sine, branch, mixed, *mlp, middle)
 
 
 def local(
@@ -1177,10 +1336,21 @@
             return full.reshape(-1, both.shape[-1])
 
         small_both = in_order(small, from_partner(after(small, outgoing), "ctx", 1))
-        leaving_units = jnp.concatenate([cut(w, 1 - ctx_rank) for w in shards], axis=1)
-        arriving_units = from_partner(after(leaving_units, small), "ctx", 1)
-        own_units = jnp.concatenate([cut(w, ctx_rank) for w in shards], axis=1)
-        unit_both = in_order(own_units, arriving_units)
+        first_units = half_units // 2 // 256 * 256
+        first_cols = 3 * first_units
+
+        def in_parts(c):
+            halves = [cut(w, c) for w in shards]
+            return jnp.concatenate(
+                [w[:, :first_units] for w in halves] + [w[:, first_units:] for w in halves], axis=1
+            )
+
+        arriving_units = from_partner(after(in_parts(1 - ctx_rank), small), "ctx", 1)
+        unit_both = in_order(in_parts(ctx_rank), arriving_units)
+        slot_pick = lax.dynamic_index_in_dim(cotangent, tensor_rank, 0, keepdims=False)
+        other_own = from_partner(after(slot_pick, arriving_units), "ctx", 1)
+        other_far = from_partner(other_own, "tp", 2)
+        other_near = from_partner(other_own, "tp", 1)
     else:
         all_rows = lambda shard, *earlier: lax.all_gather(
             shard, ("fsdp", "ctx"), axis=0, tiled=True
@@ -1203,8 +1373,12 @@
     grad_slots = [lax.dynamic_index_in_dim(cotangent, s, 0, keepdims=False) for s in slot_now]
 
     near_full = all_rows(small_both, own_in)
-    down_full = all_rows(unit_both[..., :half_units], cross_in)
-    gate_up_full = all_rows(unit_both[..., half_units:], cross_in)
+    if split:
+        units_a = all_rows(unit_both[..., :first_cols], cross_in)
+        units_b = all_rows(unit_both[..., first_cols:], cross_in)
+    else:
+        down_full = all_rows(unit_both[..., :half_units], cross_in)
+        gate_up_full = all_rows(unit_both[..., half_units:], cross_in)
     project_full = near_full[:, : query_cols + head_width]
     output_full = near_full[:, near_cols:]
     bias_head = lax.dynamic_slice_in_dim(bias_keyval, head_pair * 2, 2, axis=0)
@@ -1213,7 +1387,7 @@
         (own_in, near_in, far_in, cross_in),
         near_full,
         bias_row,
-        cosine,
+        after(cosine, other_own, unit_both) if split else cosine,
         sine,
         heads,
         head_dim,
@@ -1221,8 +1395,9 @@
     gains_now = near_full[:, query_cols + head_width : near_cols][:, :2].astype(WIDE).T
     if split:
         key_past, value_past = lax.ppermute((key_own, value_own), "ctx", [(0, 1)])
-        other_pair = [from_partner(after(grad_slots[r], value_past), "ctx", 1) for r in (0, 2)]
-        cross_pair = functools.partial(from_partner, axis="tp", apart=1)
+        other_cross = from_partner(after(other_far, query_rot), "tp", 1)
+        other_rows = (other_own, other_near, other_far, other_cross)
+        key_past = after(key_past, *other_rows)
     else:
         key_past = lax.all_gather(key_own, "ctx", axis=1, tiled=True)
         value_past = lax.all_gather(value_own, "ctx", axis=1, tiled=True)
@@ -1246,14 +1421,18 @@
     normed_share = (middle_share * inv_two * gains_now[1]).astype(LOW)
     half_len = local_len // 2
 
-    others = []
     if split:
-        cross_pair = [cross_pair(after(v, normed_share)) for v in other_pair]
-        others = [other_pair[0], cross_pair[0], other_pair[1], cross_pair[1]]
-
-    grad_hidden, grad_rows = stack_rows(
-        [(after(grad_slots[0], normed_share),)] + [(g,) for g in grad_slots[1:] + others], down_full, 0, 1
-    )
+        picks = [s ^ tensor_rank for s in slot_now]
+        grad_hidden, grad_rows = chosen_rows(
+            jnp.stack(slot_now + picks).astype(jnp.int32),
+            after(cotangent, normed_share),
+            other_rows,
+            units_a,
+            0,
+            3,
+        )
+    else:
+        grad_hidden, grad_rows = stack_rows([(g,) for g in grad_slots], down_full, 0, 1)
 
     def spread_all(own):
         far = from_partner(own, "tp", 2)
@@ -1271,10 +1450,17 @@
             return [(row,) for row in rows]
         return [(row,) for row in rows[:6]] + [rows[6:8], rows[8:]]
 
-    gate_lin, normed_two = stack_rows(in_slots(spread_all(normed_share)), gate_up_full, 0, 2)
-    hidden_act, grad_gate, grad_up = hidden_units(
-        normed_two, gate_up_full, 1, 2, gate_lin, grad_hidden
-    )
+    normed_slots = in_slots(spread_all(normed_share))
+    if split:
+        gate_lin, normed_two = stack_rows(normed_slots, units_a, 1, 3)
+        hidden_a, gate_a, up_a = hidden_units(normed_two, units_a, 2, 3, gate_lin, grad_hidden)
+        grad_a = first_grads(grad_rows, normed_two, hidden_a, gate_a, up_a)
+        hidden_b, gate_b, up_b = full_units(after(normed_two, grad_a), grad_rows, units_b)
+    else:
+        gate_lin, normed_two = stack_rows(normed_slots, gate_up_full, 0, 2)
+        hidden_act, grad_gate, grad_up = hidden_units(
+            normed_two, gate_up_full, 1, 2, gate_lin, grad_hidden
+        )
 
     def collect_all(lefts, weights, *earlier):
         lefts = list(lefts)
@@ -1290,19 +1476,29 @@
         return first[0], finish
 
     if split:
-        grad_two_share, down_grad = collect_back(
-            grad_gate, grad_up, gate_up_full, grad_rows, hidden_act, local_len
+        grad_two_share, down_b, up_grad_b = collect_back(
+            (gate_a, up_a),
+            (gate_b, up_b),
+            units_a,
+            units_b,
+            grad_rows,
+            normed_two,
+            hidden_b,
+            local_len,
         )
-        grad_middle, gain_two, gate_grad, grad_branch, *mlp = spread_branch(
+        grad_middle, gain_two, gate_grad_b, grad_branch, *mlp = spread_branch(
             grad_two_share,
             middle_share,
             grad_slots[0],
             gains_now[1:2],
-            hidden_act,
-            down_full,
+            hidden_a,
+            hidden_b,
+            units_a,
+            units_b,
             normed_two,
-            grad_gate,
+            gate_b,
         )
+        mlp_own, mlp_far, mlp_side, mlp_first, mlp_second = mlp
         grad_branch = grad_branch.reshape(token_count, model_width)
     else:
         first_back, finish_back = collect_all(
@@ -1341,7 +1537,13 @@
         scale,
     )
     if split:
-        line_grad, up_grad = attend_exchange(*attend_args, normed_two, grad_up)
+        line_grad, output_grad, block_share = attend_exchange(
+            *attend_args,
+            grad_branch,
+            mixed_flat,
+            (mlp_first, mlp_second, mlp_far, mlp_side, mlp_own),
+            middle_share,
+        )
         line_grad = line_grad.reshape(token_count, -1)
     else:
         grad_query, mine_past, mine_own, other_past, other_own = attend_backward(*attend_args)
@@ -1360,22 +1562,6 @@
     back_full = jnp.concatenate([project_full[:, :query_cols], own_weight], axis=1)
     normed_flat = normed_one.reshape(token_count, model_width)
     if split:
-        mlp_own, mlp_far, mlp_side, mlp_first, mlp_second = mlp
-        got_first = from_partner(mlp_first, "tp", 2).astype(WIDE)
-        got_second = from_partner(mlp_second, "ctx", 1).astype(WIDE)
-        add_half = lambda rows, low, high: jnp.concatenate(
-            [
-                rows[:half_len] if low is None else (rows[:half_len].astype(WIDE) + low).astype(LOW),
-                rows[half_len:] if high is None else (rows[half_len:].astype(WIDE) + high).astype(LOW),
-            ],
-            axis=0,
-        )
-        mlp_sum = (
-            mlp_own.astype(WIDE)
-            + from_partner(add_half(mlp_far, None, got_second), "tp", 2).astype(WIDE)
-            + from_partner(add_half(mlp_side, got_first, None), "ctx", 1).astype(WIDE)
-        )
-        block_share = (middle_share + mlp_sum).astype(LOW)
         input_share, gain_one, attn_grad, bias_grad, block_home = finish_rows(
             line_grad,
             back_full,
@@ -1383,10 +1569,9 @@
             grad_middle,
             gains_now[0:1],
             normed_flat,
-            grad_branch,
-            mixed_flat,
             block_share,
         )
+        attn_grad = jnp.concatenate([attn_grad, output_grad], axis=1)
     else:
         half = token_count // 2
         line_far = contract_cols(line_grad[half:], back_full, LOW).reshape(2, local_len, model_width)
@@ -1411,7 +1596,8 @@
             return scatter_sum(grad, ctx_rank, LOW)
         return lax.psum_scatter(grad, "fsdp", scatter_dimension=0, tiled=True)
 
-    unit_sums = [scatter_units(g) for g in (down_grad, gate_grad, up_grad)]
+    unit_grads = (grad_a, down_b, up_grad_b, gate_grad_b) if split else (down_grad, gate_grad, up_grad)
+    unit_sums = [scatter_units(g) for g in unit_grads]
 
     attn_end = scatter_sum(attn_grad, ctx_rank, LOW, *unit_sums)
 
@@ -1455,17 +1641,25 @@
         pairs = [(f, (f + shift) % fsdp_count) for f in range(fsdp_count)]
         tiny_grad = tiny_grad + lax.ppermute(pick(shift), "fsdp", pairs)
 
-    def unit_end(total):
-        if split:
-            blocks = total.reshape(1, ctx_count, -1, half_units)
-            kept, sent = scatter_ctx(blocks, ctx_rank)
-            kept, got = kept[0], from_partner(sent[0], "ctx", 1)
-            first = jnp.where(ctx_rank == 0, kept, got)
-            second = jnp.where(ctx_rank == 0, got, kept)
-            total = jnp.concatenate([first, second], axis=1)
-        return total[:, :units].astype(WIDE)
-
-    down_end, gate_end, up_end = (unit_end(after(t, input_share)) for t in unit_sums)
+    if split:
+
+        def unit_end(total, *earlier):
+            kept, sent = scatter_ctx(total.reshape(1, ctx_count, -1, total.shape[1]), ctx_rank)
+            return kept[0], from_partner(after(sent[0], *earlier), "ctx", 1)
+
+        own_a, got_a = unit_end(unit_sums[0], line_grad)
+        ends = [unit_end(t, line_grad) for t in unit_sums[1:]]
+
+        def joined(part, end):
+            cols = slice(part * first_units, (part + 1) * first_units)
+            own = jnp.concatenate([own_a[:, cols], end[0]], axis=1)
+            got = jnp.concatenate([got_a[:, cols], end[1]], axis=1)
+            first, second = jnp.where(ctx_rank == 0, own, got), jnp.where(ctx_rank == 0, got, own)
+            return jnp.concatenate([first, second], axis=1)[:, :units].astype(WIDE)
+
+        down_end, gate_end, up_end = joined(0, ends[0]), joined(1, ends[2]), joined(2, ends[1])
+    else:
+        down_end, gate_end, up_end = (t[:, :units].astype(WIDE) for t in unit_sums)
     return (
         block_out,
         input_grad,

time: 857 us -> 926 us (1.081)
  Pallas kernels: 386 us -> 439 us
  waiting for transfers between devices: 267 us -> 291 us
    pallas_call x1 -> x4, Pallas kernels: 70.6 us -> 157 us  [the longest x1 71.2 us: collect_back(): pl.pallas_call(functools.partial(collect_kernel, slots, tiles), grid=(slo...]
    ppermute x1, waiting for transfers between devices: 27.3 us -> 96.6 us  [leave(): return lax.ppermute(share, ('fsdp', 'tp'), back)]
    ppermute x38 -> x35, waiting for transfers between devices: 191 us -> 144 us  [from_partner(): return lax.ppermute(value, axis, pairs)]
    pallas_call x2 -> x1, Pallas kernels: 51.8 us -> 15.5 us  [stack_rows(): pl.pallas_call(functools.partial(rows_kernel, groups), grid=(count,), in_...]
    pallas_call x1, Pallas kernels: 51.5 us -> 74.4 us  [attend_exchange(): pl.pallas_call(functools.partial(exchange_kernel, heads, head_dim, scale,...]
    pallas_call x1, Pallas kernels: 30.6 us -> 17.8 us  [hidden_units(): pl.pallas_call(units_kernel, grid=(tokens // step,), in_specs=[by_row(wid...]
    ppermute x38 -> x35, starting transfers between devices: 40.3 us -> 40.8 us  [from_partner(): return lax.ppermute(value, axis, pairs)]
  transfers between devices with their start and end apart: 52 -> 50, of which waited for: 26 -> 21; matrix products, arithmetic and copies ran while one was open for 10% -> 8% of each run, Pallas kernels for 31% -> 31%
where the time goes in v5:
time: 926 us; the launch traced here: 912 us
  Pallas kernels  439 us (47%)
  waiting for transfers between devices  291 us (31%)
  starting transfers between devices  53.2 us (6%)
  local copies, waits for them, and re-layouts  44 us (5%)
  other arithmetic  43.7 us (5%)
  between operations  34.8 us (4%)
    ppermute x35, waiting for transfers between devices, from_partner(): return lax.ppermute(value, axis, pairs)  144 us
    ppermute x1, waiting for transfers between devices, leave(): return lax.ppermute(share, ('fsdp', 'tp'), back)  96.6 us
    pallas_call x1, Pallas kernels, attend_exchange(): pl.pallas_call(functools.partial(exchange_kernel, heads, head_dim, scale,...  74.4 us
    pallas_call x1, Pallas kernels, finish_rows(): pl.pallas_call(functools.partial(line_kernel, slots, tiles), grid=(slots...  72.3 us
    pallas_call x1, Pallas kernels, collect_back(): pl.pallas_call(functools.partial(collect_kernel, slots, tiles), grid=(slo...  71.2 us
    pallas_call x1, Pallas kernels, spread_branch(): pl.pallas_call(functools.partial(branch_kernel, slots, tiles), grid=(slot...  50.4 us
    ppermute x35, starting transfers between devices, from_partner(): return lax.ppermute(value, axis, pairs)  40.8 us
    pallas_call x1, Pallas kernels, full_units(): pl.pallas_call(full_units_kernel, grid=(tokens // step,), in_specs=[by_ro...  37 us
  transfers between devices with their start and end apart: 50, of which 21 were waited for; matrix products, arithmetic and copies ran while one was open for 8% of the time, Pallas kernels for 31%

profile of v5, /device:TPU:1, one launch (start us, length us, event | category | flops | bytes accessed | tf_op | source)
XLA Modules:
  0.0 911.6 jit_solution(10575716763350325221)
XLA Ops:
  24.0 9.1 collective-permute-done.4
  34.3 23.0 %collective-permute-done.x0.own_in = bf16[512,1536]{1,0:T(8,128)(2,1)S(1)} collective-permute-done((bf16[512,1536]{1,0:T(8,128)(2,1)}, bf16[512,1536]{1,0:T(8,128)(2,1)S(1)}, u32[]{:S(2)}, u32[]{:S(2)}) %collective-permute-start) | collective-permute-done | bytes 1572896 | tf_op jit(solution)/shard_map/ppermute | solution.py:1311
  70.8 22.0 %collective-permute-done.2.x2 = bf16[512,1536]{1,0:T(8,128)(2,1)} collective-permute-done((bf16[512,1536]{1,0:T(8,128)(2,1)S(1)}, bf16[512,1536]{1,0:T(8,128)(2,1)}, u32[]{:S(2)}, u32[]{:S(2)}) %collective-permute-start.2) | collective-permute-done | bytes 1572896 | tf_op jit(solution)/shard_map/ppermute | solution.py:21
  104.4 30.8 %collective-permute-done.6.refs_0_ = bf16[512,1536]{1,0:T(8,128)(2,1)} collective-permute-done((bf16[512,1536]{1,0:T(8,128)(2,1)}, bf16[512,1536]{1,0:T(8,128)(2,1)}, u32[]{:S(2)}, u32[]{:S(2)}) %collective-permute-start.6) | collective-permute-done | bytes 1572896 | tf_op jit(solution)/shard_map/ppermute | solution.py:21
  152.1 12.4 %shard_map.230 = (bf16[4,512,1536]{2,1,0:T(8,128)(2,1)}, bf16[4,512,384]{2,1,0:T(8,128)(2,1)}, bf16[4,512,128]{2,1,0:T(8,128)(2,1)}, bf16[4,512,128]{2,1,0:T(8,128)(2,1)}) custom-call(bf16[512,1536]{1,0:T(8,128)(2,1)} %copy-done.4, bf16[512,1536]{1,0:T(8,128)(2,1)} %collective-permute-done.1.x1, bf16[512,1536]{1,0:T(8,128)(2,1)} %collective-permute-done.2.x2, ...), custom_call_target="tpu_custom_call" | custom-call | flops 4026531840 | bytes 17170432 | tf_op jit(solution)/shard_map/pallas_call | solution.py:824
  184.1 6.8 collective-permute-done.7.k_past
  190.9 11.2 %collective-permute-done.11.v_past = bf16[4,512,128]{2,1,0:T(8,128)(2,1)S(1)} collective-permute-done((bf16[4,512,128]{2,1,0:T(8,128)(2,1)}, bf16[4,512,128]{2,1,0:T(8,128)(2,1)S(1)}, u32[]{:S(2)}, u32[]{:S(2)}) %collective-permute-start.11) | collective-permute-done | bytes 524320 | tf_op jit(solution)/shard_map/ppermute | solution.py:1397
  203.0 13.6 %shard_map.231 = (bf16[2,512,384]{2,1,0:T(8,128)(2,1)}, f32[2,512,128]{2,1,0:T(8,128)}, bf16[512,1536]{1,0:T(8,128)(2,1)}, bf16[512,1536]{1,0:T(8,128)(2,1)}) custom-call(s32[6]{0:T(128)} %concatenate.76.info, bf16[4,512,384]{2,1,0:T(8,128)(2,1)} %get-tuple-element.77.q, bf16[4,512,128]{2,1,0:T(8,128)(2,1)} %copy-done.20, bf16[4,512,128]{2,1,0:T(8,128)(2,1)} %copy-done.21, ...), custom_call_target="tpu_custom_call" | custom-call | flops 1610612736 | bytes 1572864 | tf_op jit(solution)/shard_map/pallas_call | solution.py:912
  224.5 13.6 %shard_map.232 = (bf16[2,512,384]{2,1,0:T(8,128)(2,1)}, f32[2,512,128]{2,1,0:T(8,128)}, bf16[512,1536]{1,0:T(8,128)(2,1)}, bf16[512,1536]{1,0:T(8,128)(2,1)}) custom-call(s32[6]{0:T(128)} %concatenate.76.info, bf16[4,512,384]{2,1,0:T(8,128)(2,1)} %get-tuple-element.77.q, bf16[4,512,128]{2,1,0:T(8,128)(2,1)} %copy-done.20, bf16[4,512,128]{2,1,0:T(8,128)(2,1)} %copy-done.21, ...), custom_call_target="tpu_custom_call" | custom-call | flops 1610612736 | bytes 1572864 | tf_op jit(solution)/shard_map/pallas_call | solution.py:912
  242.5 17.0 %collective-permute-done.14 = bf16[512,1536]{1,0:T(8,128)(2,1)} collective-permute-done((bf16[512,1536]{1,0:T(8,128)(2,1)}, bf16[512,1536]{1,0:T(8,128)(2,1)}, u32[]{:S(2)}, u32[]{:S(2)}) %collective-permute-start.14) | collective-permute-done | bytes 1572896 | tf_op jit(solution)/shard_map/ppermute | solution.py:21
  275.0 15.6 %shard_map.233 = (bf16[4096,512]{1,0:T(8,128)(2,1)}, bf16[4096,1536]{1,0:T(8,128)(2,1)}) custom-call(s32[8]{0:T(128)} %stack.95.info, bf16[4,512,1536]{2,1,0:T(8,128)(2,1)} %cotangent, bf16[512,1536]{1,0:T(8,128)(2,1)} %collective-permute-done.6.refs_0_, bf16[512,1536]{1,0:T(8,128)(2,1)} %collective-permute-done.8.refs_1_, ...), custom_call_target="tpu_custom_call" | custom-call | flops 6442450944 | bytes 30932992 | tf_op jit(solution)/shard_map/pallas_call | solution.py:226
  290.6 9.7 %collective-permute-done.18.refs_4_ = bf16[512,1536]{1,0:T(8,128)(2,1)S(1)} collective-permute-done((bf16[512,1536]{1,0:T(8,128)(2,1)S(1)}, bf16[512,1536]{1,0:T(8,128)(2,1)S(1)}, u32[]{:S(2)}, u32[]{:S(2)}) %collective-permute-start.18) | collective-permute-done | bytes 1572896 | tf_op jit(solution)/shard_map/ppermute | solution.py:21
  306.4 11.6 %collective-permute-done.21.refs_7_ = bf16[256,1536]{1,0:T(8,128)(2,1)S(1)} collective-permute-done((bf16[256,1536]{1,0:T(8,128)(2,1)S(1)}, bf16[256,1536]{1,0:T(8,128)(2,1)S(1)}, u32[]{:S(2)}, u32[]{:S(2)}) %collective-permute-start.21) | collective-permute-done | bytes 786464 | tf_op jit(solution)/shard_map/ppermute | solution.py:21
  326.2 15.5 %shard_map.234 = (bf16[4096,512]{1,0:T(8,128)(2,1)}, bf16[4096,1536]{1,0:T(8,128)(2,1)}) custom-call(bf16[512,1536]{1,0:T(8,128)(2,1)} %copy-done.14, bf16[512,1536]{1,0:T(8,128)(2,1)} %collective-permute-done.15.refs_1_, bf16[512,1536]{1,0:T(8,128)(2,1)} %collective-permute-done.16.refs_2_, bf16[512,1536]{1,0:T(8,128)(2,1)} %collective-permute-done.17.refs_3_, ...), custom_call_target="tpu_custom_call" | custom-call | flops 6442450944 | bytes 30932992 | tf_op jit(solution)/shard_map/pallas_call | solution.py:121
  341.7 17.8 %shard_map.235 = (bf16[4096,512]{1,0:T(8,128)(2,1)}, bf16[4096,512]{1,0:T(8,128)(2,1)}, bf16[4096,512]{1,0:T(8,128)(2,1)}) custom-call(bf16[4096,1536]{1,0:T(8,128)(2,1)} %get-tuple-element.98.h.right.turned, bf16[1536,1536]{1,0:T(8,128)(2,1)} %bitcast.161, bf16[4096,512]{1,0:T(8,128)(2,1)} %get-tuple-element.93.gate, bf16[4096,512]{1,0:T(8,128)(2,1)} %get-tuple-element.89.grad), custom_call_target="tpu_custom_call" | custom-call | flops 6442450944 | bytes 35127296 | tf_op jit(solution)/shard_map/pallas_call | solution.py:157
  359.5 33.5 %shard_map.236 = bf16[1536,1536]{1,0:T(8,128)(2,1)} custom-call(bf16[4096,1536]{1,0:T(8,128)(2,1)} %get-tuple-element.96.g.left, bf16[4096,1536]{1,0:T(8,128)(2,1)} %get-tuple-element.98.h.right.turned, bf16[4096,512]{1,0:T(8,128)(2,1)} %get-tuple-element.97.hid.hid_a, bf16[4096,512]{1,0:T(8,128)(2,1)} %get-tuple-element.94.gate.gate_a, ...), custom_call_target="tpu_custom_call" | custom-call | flops 19327352832 | bytes 17301504 | tf_op jit(solution)/shard_map/pallas_call | solution.py:294
  393.0 37.0 %shard_map.237 = (bf16[4096,640]{1,0:T(8,128)(2,1)}, bf16[4096,640]{1,0:T(8,128)(2,1)}, bf16[4096,640]{1,0:T(8,128)(2,1)}) custom-call(bf16[4096,1536]{1,0:T(8,128)(2,1)} %get-tuple-element.98.h.right.turned, bf16[4096,1536]{1,0:T(8,128)(2,1)} %get-tuple-element.96.g.left, bf16[1536,1920]{1,0:T(8,128)(2,1)} %bitcast.182, bf16[1536,1920]{1,0:T(8,128)(2,1)} %bitcast.183, ...), custom_call_target="tpu_custom_call" | custom-call | flops 24159191040 | bytes 46792704 | tf_op jit(solution)/shard_map/pallas_call | solution.py:268
  430.0 71.2 %shard_map.238 = (f32[512,1536]{1,0:T(8,128)}, bf16[1536,640]{1,0:T(8,128)(2,1)}, bf16[1536,640]{1,0:T(8,128)(2,1)}) custom-call(bf16[4096,512]{1,0:T(8,128)(2,1)} %get-tuple-element.94.gate.gate_a, bf16[4096,512]{1,0:T(8,128)(2,1)} %get-tuple-element.95.up.up_a, bf16[4096,640]{1,0:T(8,128)(2,1)} %get-tuple-element.100.gate_b.gate, ...), custom_call_target="tpu_custom_call" | custom-call | flops 24159191040 | bytes 26214400 | tf_op jit(solution)/shard_map/pallas_call | solution.py:435
  501.2 50.4 %shard_map.239 = (f32[512,1536]{1,0:T(8,128)}, f32[1,1536]{1,0:T(1,128)}, bf16[1536,640]{1,0:T(8,128)(2,1)}, bf16[4,512,1536]{2,1,0:T(8,128)(2,1)}, bf16[512,153...) custom-call(f32[512,1536]{1,0:T(8,128)} %get-tuple-element.103.total, ...), custom_call_target="tpu_custom_call" | custom-call | flops 16106127360 | bytes 26214400 | tf_op jit(solution)/shard_map/pallas_call | solution.py:574
  566.4 74.4 %shard_map.240 = (bf16[4,512,512]{2,1,0:T(8,128)(2,1)}, bf16[1536,384]{1,0:T(8,128)(2,1)}, bf16[512,1536]{1,0:T(8,128)(2,1)}) custom-call(s32[6]{0:T(128)} %concatenate.76.info, bf16[4,512,384]{2,1,0:T(8,128)(2,1)} %get-tuple-element.77.q, bf16[4,512,128]{2,1,0:T(8,128)(2,1)} %copy-done.20, bf16[4,512,128]{2,1,0:T(8,128)(2,1)} %copy-done.21, ...), custom_call_target="tpu_custom_call" | custom-call | flops 2415919104 | bytes 7864320 | tf_op jit(solution)/shard_map/pallas_call | solution.py:1197
  640.8 72.3 %shard_map.241 = (bf16[512,1536]{1,0:T(8,128)(2,1)}, f32[1,1536]{1,0:T(1,128)}, bf16[1536,512]{1,0:T(8,128)(2,1)}, f32[1,512]{1,0:T(1,128)}, bf16[512,1536]{1,0:T(8,128)(2,1)}) custom-call(bf16[2048,512]{1,0:T(8,128)(2,1)} %bitcast.150, bf16[1536,512]{1,0:T(8,128)(2,1)} %pad_maximum_fusion.3.weight, bf16[512,1536]{1,0:T(8,128)(2,1)} %copy-done.4, ...), custom_call_target="tpu_custom_call" | custom-call | flops 3221225472 | bytes 31457280 | tf_op jit(solution)/shard_map/pallas_call | solution.py:711
  726.1 96.6 %collective-permute-done.27.refs_0_ = bf16[512,1536]{1,0:T(8,128)(2,1)S(1)} collective-permute-done((bf16[512,1536]{1,0:T(8,128)(2,1)}, bf16[512,1536]{1,0:T(8,128)(2,1)S(1)}, u32[]{:S(2)}, u32[]{:S(2)}) %collective-permute-start.27) | collective-permute-done | bytes 1572896 | tf_op jit(solution)/shard_map/ppermute | solution.py:1607
  842.9 9.1 collective-permute-done.29.refs_2_
  880.8 15.8 %collective-permute-done.39 = bf16[192,640]{1,0:T(8,128)(2,1)S(1)} collective-permute-done((bf16[192,640]{1,0:T(8,128)(2,1)S(1)}, bf16[192,640]{1,0:T(8,128)(2,1)S(1)}, u32[]{:S(2)}, u32[]{:S(2)}) %collective-permute-start.39) | collective-permute-done | bytes 245792 | tf_op jit(solution)/shard_map/ppermute | solution.py:21
  (266 shorter events, 186.9 us)
Async XLA Ops:
  7.2 144.9 %all-gather.7.cloned.1.call-start = ((), (), s32[]{:S(2)}) async-start(), calls=%async_computation.10 | async-start | bytes 4423680 | tf_op jit(solution)/shard_map/all_gather | solution.py:1335
  17.3 39.9 %collective-permute-start = (bf16[512,1536]{1,0:T(8,128)(2,1)}, bf16[512,1536]{1,0:T(8,128)(2,1)S(1)}, u32[]{:S(2)}, u32[]{:S(2)}) collective-permute-start(bf16[512,1536]{1,0:T(8,128)(2,1)} %dynamic-slice_bitcast_fusion.2), channel_id=1, source_target_pairs={{0,0},{1,17},{2,10},{3,27},{8,8},{9,25},{10,18},{11,3},{16,16},{17... | collective-permute-start | bytes 4718600 | tf_op jit(solution)/shard_map/ppermute | solution.py:1311
  57.3 217.7 %all-gather.9.cloned.1.call-start = ((), (), s32[]{:S(2)}) async-start(), calls=%async_computation.11 | async-start | bytes 5898240 | tf_op jit(solution)/shard_map/all_gather | solution.py:1335
  58.1 34.7 %collective-permute-start.2 = (bf16[512,1536]{1,0:T(8,128)(2,1)S(1)}, bf16[512,1536]{1,0:T(8,128)(2,1)}, u32[]{:S(2)}, u32[]{:S(2)}) collective-permute-start(bf16[512,1536]{1,0:T(8,128)(2,1)S(1)} %collective-permute-done.x0.own_in), channel_id=1, source_target_pairs={{0,2},{1,3},{2,0},{3,1},{4,6},{5,7},{6,4},{7,5},{8,10},{9,11},{10,... | collective-permute-start | bytes 4718600 | tf_op jit(solution)/shard_map/ppermute | solution.py:21
  64.1 34.7 %collective-permute-start.5 = (bf16[192,3456]{1,0:T(8,128)(2,1)}, bf16[192,3456]{1,0:T(8,128)(2,1)S(1)}, u32[]{:S(2)}, u32[]{:S(2)}) collective-permute-start(bf16[192,3456]{1,0:T(8,128)(2,1)} %get-tuple-element.74), channel_id=1, source_target_pairs={{0,4},{4,0},{1,5},{5,1},{2,6},{6,2},{3,7},{7,3},{8,12},{12,8},{9,1... | collective-permute-start | bytes 3981320 | tf_op jit(solution)/shard_map/ppermute | solution.py:21
  98.8 36.4 %collective-permute-start.6 = (bf16[512,1536]{1,0:T(8,128)(2,1)}, bf16[512,1536]{1,0:T(8,128)(2,1)}, u32[]{:S(2)}, u32[]{:S(2)}) collective-permute-start(bf16[512,1536]{1,0:T(8,128)(2,1)} %get-tuple-element.75), channel_id=1, source_target_pairs={{0,4},{4,0},{1,5},{5,1},{2,6},{6,2},{3,7},{7,3},{8,12},{12,8},{9,1... | collective-permute-start | bytes 4718600 | tf_op jit(solution)/shard_map/ppermute | solution.py:21
  104.0 289.0 %all-gather.11.cloned.1.call-start = ((), (), s32[]{:S(2)}) async-start(), calls=%async_computation.12 | async-start | bytes 7372800 | tf_op jit(solution)/shard_map/all_gather | solution.py:1335
  104.0 48.0 %collective-permute-start.1 = (bf16[512,1536]{1,0:T(8,128)(2,1)S(1)}, bf16[512,1536]{1,0:T(8,128)(2,1)}, u32[]{:S(2)}, u32[]{:S(2)}) collective-permute-start(bf16[512,1536]{1,0:T(8,128)(2,1)S(1)} %collective-permute-done.x0.own_in), channel_id=1, source_target_pairs={{0,1},{1,0},{2,3},{3,2},{4,5},{5,4},{6,7},{7,6},{8,9},{9,8},{10,11... | collective-permute-start | bytes 4718600 | tf_op jit(solution)/shard_map/ppermute | solution.py:21
  135.2 35.5 %collective-permute-start.9 = (bf16[512,1536]{1,0:T(8,128)(2,1)}, bf16[512,1536]{1,0:T(8,128)(2,1)}, u32[]{:S(2)}, u32[]{:S(2)}) collective-permute-start(bf16[512,1536]{1,0:T(8,128)(2,1)} %collective-permute-done.6.refs_0_), channel_id=1, source_target_pairs={{0,2},{1,3},{2,0},{3,1},{4,6},{5,7},{6,4},{7,5},{8,10},{9,11},{10,... | collective-permute-start | bytes 4718600 | tf_op jit(solution)/shard_map/ppermute | solution.py:21
  151.0 33.1 %collective-permute-start.8 = (bf16[512,1536]{1,0:T(8,128)(2,1)}, bf16[512,1536]{1,0:T(8,128)(2,1)}, u32[]{:S(2)}, u32[]{:S(2)}) collective-permute-start(bf16[512,1536]{1,0:T(8,128)(2,1)} %collective-permute-done.6.refs_0_), channel_id=1, source_target_pairs={{0,1},{1,0},{2,3},{3,2},{4,5},{5,4},{6,7},{7,6},{8,9},{9,8},{10,11... | collective-permute-start | bytes 4718600 | tf_op jit(solution)/shard_map/ppermute | solution.py:21
  223.6 35.9 %collective-permute-start.14 = (bf16[512,1536]{1,0:T(8,128)(2,1)}, bf16[512,1536]{1,0:T(8,128)(2,1)}, u32[]{:S(2)}, u32[]{:S(2)}) collective-permute-start(bf16[512,1536]{1,0:T(8,128)(2,1)} %add_convert_fusion), channel_id=1, source_target_pairs={{0,2},{1,3},{2,0},{3,1},{4,6},{5,7},{6,4},{7,5},{8,10},{9,11},{10,... | collective-permute-start | bytes 4718600 | tf_op jit(solution)/shard_map/ppermute | solution.py:21
  240.2 620.9 %reduce-scatter.12.cloned.1.call-start = ((), (), s32[]{:S(2)}) async-start(), calls=%async_computation.8 | async-start | bytes 2457600 | tf_op jit(solution)/shard_map/reduce_scatter | solution.py:1597
  264.5 35.7 %collective-permute-start.18 = (bf16[512,1536]{1,0:T(8,128)(2,1)S(1)}, bf16[512,1536]{1,0:T(8,128)(2,1)S(1)}, u32[]{:S(2)}, u32[]{:S(2)}) collective-permute-start(bf16[512,1536]{1,0:T(8,128)(2,1)S(1)} %multiply_convert_fusion.refs_0_), channel_id=1, source_target_pairs={{0,4},{4,0},{1,5},{5,1},{2,6},{6,2},{3,7},{7,3},{8,12},{12,8},{9,1... | collective-permute-start | bytes 4718600 | tf_op jit(solution)/shard_map/ppermute | solution.py:21
  266.6 34.5 %collective-permute-start.16 = (bf16[512,1536]{1,0:T(8,128)(2,1)S(1)}, bf16[512,1536]{1,0:T(8,128)(2,1)}, u32[]{:S(2)}, u32[]{:S(2)}) collective-permute-start(bf16[512,1536]{1,0:T(8,128)(2,1)S(1)} %multiply_convert_fusion.refs_0_), channel_id=1, source_target_pairs={{0,2},{1,3},{2,0},{3,1},{4,6},{5,7},{6,4},{7,5},{8,10},{9,11},{10,... | collective-permute-start | bytes 4718600 | tf_op jit(solution)/shard_map/ppermute | solution.py:21
  273.2 50.2 %collective-permute-start.15 = (bf16[512,1536]{1,0:T(8,128)(2,1)S(1)}, bf16[512,1536]{1,0:T(8,128)(2,1)}, u32[]{:S(2)}, u32[]{:S(2)}) collective-permute-start(bf16[512,1536]{1,0:T(8,128)(2,1)S(1)} %multiply_convert_fusion.refs_0_), channel_id=1, source_target_pairs={{0,1},{1,0},{2,3},{3,2},{4,5},{5,4},{6,7},{7,6},{8,9},{9,8},{10,11... | collective-permute-start | bytes 4718600 | tf_op jit(solution)/shard_map/ppermute | solution.py:21
  551.7 309.4 %reduce-scatter.8.cloned.1.call-start = ((), (), s32[]{:S(2)}) async-start(), calls=%async_computation.6 | async-start | bytes 2457600 | tf_op jit(solution)/shard_map/reduce_scatter | solution.py:1597
  552.3 308.8 %reduce-scatter.10.cloned.1.call-start = ((), (), s32[]{:S(2)}) async-start(), calls=%async_computation.7 | async-start | bytes 2457600 | tf_op jit(solution)/shard_map/reduce_scatter | solution.py:1597
  552.9 308.2 %reduce-scatter.6.cloned.1.call-start = ((), (), s32[]{:S(2)}) async-start(), calls=%async_computation.5 | async-start | bytes 5898240 | tf_op jit(solution)/shard_map/reduce_scatter | solution.py:1597
  553.6 347.5 %reduce-scatter.14.cloned.1.call-start = ((), (), s32[]{:S(2)}) async-start(), calls=%async_computation.9 | async-start | bytes 1720320 | tf_op jit(solution)/shard_map/reduce_scatter | solution.py:83
  713.2 109.6 %collective-permute-start.27 = (bf16[512,1536]{1,0:T(8,128)(2,1)}, bf16[512,1536]{1,0:T(8,128)(2,1)S(1)}, u32[]{:S(2)}, u32[]{:S(2)}) collective-permute-start(bf16[512,1536]{1,0:T(8,128)(2,1)} %get-tuple-element.119), channel_id=1, source_target_pairs={{0,0},{17,1},{10,2},{27,3},{8,8},{25,9},{18,10},{3,11},{16,16},{1,... | collective-permute-start | bytes 4718600 | tf_op jit(solution)/shard_map/ppermute | solution.py:1607
  715.1 107.8 %collective-permute-start.25 = (bf16[512,1536]{1,0:T(8,128)(2,1)}, bf16[512,1536]{1,0:T(8,128)(2,1)}, u32[]{:S(2)}, u32[]{:S(2)}) collective-permute-start(bf16[512,1536]{1,0:T(8,128)(2,1)} %get-tuple-element.118.refs_0_), channel_id=1, source_target_pairs={{0,2},{1,3},{2,0},{3,1},{4,6},{5,7},{6,4},{7,5},{8,10},{9,11},{10,... | collective-permute-start | bytes 4718600 | tf_op jit(solution)/shard_map/ppermute | solution.py:21
  719.6 134.1 %collective-permute-start.24 = (bf16[512,1536]{1,0:T(8,128)(2,1)}, bf16[512,1536]{1,0:T(8,128)(2,1)}, u32[]{:S(2)}, u32[]{:S(2)}) collective-permute-start(bf16[512,1536]{1,0:T(8,128)(2,1)} %get-tuple-element.118.refs_0_), channel_id=1, source_target_pairs={{0,1},{1,0},{2,3},{3,2},{4,5},{5,4},{6,7},{7,6},{8,9},{9,8},{10,11... | collective-permute-start | bytes 4718600 | tf_op jit(solution)/shard_map/ppermute | solution.py:21
  721.1 101.6 %collective-permute-start.33 = (f32[1536,2]{0,1:T(2,128)S(1)}, f32[1536,2]{0,1:T(2,128)S(1)}, u32[]{:S(2)}, u32[]{:S(2)}) collective-permute-start(f32[1536,2]{0,1:T(2,128)S(1)} %fusion.51), channel_id=1, source_target_pairs={{0,2},{1,3},{2,0},{3,1},{4,6},{5,7},{6,4},{7,5},{8,10},{9,11},{10,... | collective-permute-start | bytes 36872 | tf_op jit(solution)/shard_map/ppermute | solution.py:21
  827.9 33.2 %collective-permute-start.31 = (bf16[4,192,896]{2,1,0:T(8,128)(2,1)}, bf16[4,192,896]{2,1,0:T(8,128)(2,1)}, u32[]{:S(2)}, u32[]{:S(2)}) collective-permute-start(bf16[4,192,896]{2,1,0:T(8,128)(2,1)} %get-tuple-element.158), channel_id=1, source_target_pairs={{0,4},{4,0},{1,5},{5,1},{2,6},{6,2},{3,7},{7,3},{8,12},{12,8},{9,1... | collective-permute-start | bytes 4128776 | tf_op jit(solution)/shard_map/ppermute | solution.py:21
  (68 other events, 1032.4 us)
Sparse Core Ops, SparseCore 0:
  57.4 71.4 all-gather.6
  130.5 88.1 all-gather.8
  240.3 110.1 all-gather.10
  551.8 41.2 reduce-scatter.11
  595.3 40.6 reduce-scatter.7
  638.1 54.4 reduce-scatter.9
  695.0 123.0 reduce-scatter.5
  864.4 35.3 reduce-scatter.13

commit v6 on v5

--- a/solution.py
+++ b/solution.py
@@ -483,12 +483,12 @@
 
 def branch_kernel(
     slots, tiles, total, middle, own_grad, gain, hid_a, hid_b, w_a, w_b, turned, gate, grad_middle, gain_grad,
-    gate_out, branch, mlp_own, mlp_far, mlp_side, mlp_first, mlp_second, own, parts, core_in, held,
-    send, recv, load
+    gate_out, branch, mlp_own, mlp_far, mlp_side, own, parts, core_in, across_in, held, send, recv, load
 ):
     step = pl.program_id(0)
-    core, far, _ = partners_of()
+    core, far, side = partners_of()
     half = own.shape[0] // 2
+    low, high = pl.ds(0, half), pl.ds(half, half)
     remote = remote_copy(send, recv)
     to_far = remote(own, branch.at[2], 0, far)
     to_near = remote(own, branch.at[1], 1, core)
@@ -496,21 +496,20 @@
     keep = pltpu.make_async_copy(own, branch.at[0], load.at[0])
     loading = pltpu.make_async_copy(gate, held, load.at[1])
     cores = [remote(parts.at[7 - 2 * k], core_in.at[k], 3 + k, core) for k in range(4)]
-    store = lambda source, target, i: pltpu.make_async_copy(source, target, load.at[i])
+    across = [
+        remote(parts.at[6, low], across_in.at[0], 7, far),
+        remote(parts.at[6, high], across_in.at[1], 8, side),
+    ]
     stores = [
-        [
-            store(parts.at[6, pl.ds(0, half)], mlp_first, 2),
-            store(parts.at[6, pl.ds(half, half)], mlp_second, 3),
-        ],
-        [store(parts.at[4], mlp_side, 4)],
-        [store(parts.at[2], mlp_far, 5)],
-        [store(parts.at[0], mlp_own, 6)],
+        pltpu.make_async_copy(parts.at[4], mlp_side, load.at[2]),
+        pltpu.make_async_copy(parts.at[2], mlp_far, load.at[3]),
+        pltpu.make_async_copy(parts.at[0], mlp_own, load.at[4]),
     ]
 
     @pl.when(step == 0)
     def _():
         loading.start()
-        meet((core, far))
+        meet((core, far, side))
         values, upstream = middle[...], total[...]
         inverse = lax.rsqrt(jnp.mean(values * values, axis=-1, keepdims=True) + EPS)
         grad_in, gain_grad[...] = norm_backward(values, inverse, gain[...], upstream)
@@ -532,8 +531,11 @@
             slot = 6 - 2 * k
             cores[k].wait_recv()
             parts[slot] = (parts[slot].astype(WIDE) + core_in[k].astype(WIDE)).astype(LOW)
-            for copy in stores[k]:
-                copy.start()
+            if k == 0:
+                for copy in across:
+                    copy.start()
+            if k == 3:
+                stores[2].start()
 
         pl.when(step == 2 * k + 1)(finish)
 
@@ -551,11 +553,16 @@
     def _():
         to_near.wait_recv()
         to_cross.wait_recv()
+        for i, (slot, here) in enumerate(((4, low), (2, high))):
+            across[i].wait_recv()
+            parts[slot, here] = (
+                parts[slot, here].astype(WIDE) + across_in[i].astype(WIDE)
+            ).astype(LOW)
+            stores[i].start()
         keep.wait()
-        for group in stores:
-            for copy in group:
-                copy.wait()
-        for copy in (to_far, to_near, to_cross, *cores):
+        for copy in stores:
+            copy.wait()
+        for copy in (to_far, to_near, to_cross, *cores, *across):
             copy.wait_send()
 
 
@@ -570,7 +577,6 @@
     once = whole_spec(length, width, once=True)
     column = lambda i: jnp.clip(i - slots, 0, tiles - 1)
     part = jax.ShapeDtypeStruct((length, width), LOW)
-    piece = jax.ShapeDtypeStruct((length // 2, width), LOW)
     return pl.pallas_call(
         functools.partial(branch_kernel, slots, tiles),
         grid=(slots + tiles,),
@@ -591,7 +597,7 @@
             whole_spec(1, width),
             pl.BlockSpec((tile, cols), lambda i: (column(i), 0)),
         ]
-        + [ANYWHERE] * 6,
+        + [ANYWHERE] * 4,
         out_shape=[
             jax.ShapeDtypeStruct((length, width), WIDE),
             jax.ShapeDtypeStruct((1, width), WIDE),
@@ -600,17 +606,16 @@
             part,
             part,
             part,
-            piece,
-            piece,
         ],
         scratch_shapes=[
             pltpu.VMEM((length, width), LOW),
             pltpu.VMEM((slots, length, width), LOW),
             pltpu.VMEM((4, length, width), LOW),
+            pltpu.VMEM((2, length // 2, width), LOW),
             pltpu.VMEM((tokens, cols), LOW),
-            pltpu.SemaphoreType.DMA((7,)),
-            pltpu.SemaphoreType.DMA((7,)),
-            pltpu.SemaphoreType.DMA((7,)),
+            pltpu.SemaphoreType.DMA((9,)),
+            pltpu.SemaphoreType.DMA((9,)),
+            pltpu.SemaphoreType.DMA((5,)),
         ],
         compiler_params=pltpu.CompilerParams(
             vmem_limit_bytes=63 << 20, collective_id=2, has_side_effects=True
@@ -1070,9 +1075,9 @@
 
 def exchange_kernel(
     heads, head_dim, scale, slots, tiles, info, q, k_past, v_past, k_own, v_own, grad, lse, cosine, sine,
-    cosine_all, sine_all, branch, mixed, first, second, mlp_far, mlp_side, mlp_own, middle, line, out_grad,
-    block, mine_past, mine_own, other_past, other_own, got_past, got_own, side_out, side_in, dk_past, dk_own,
-    dv_past, dv_own, across_in, rows, last_in, send, recv, load
+    cosine_all, sine_all, branch, mixed, mlp_far, mlp_side, mlp_own, middle, line, out_grad, block, mine_past,
+    mine_own, other_past, other_own, got_past, got_own, side_out, side_in, dk_past, dk_own, dv_past, dv_own,
+    own_rows, last_in, send, recv, load
 ):
     step = pl.program_id(0)
     tensor_rank = lax.axis_index("tp")
@@ -1083,26 +1088,17 @@
     pasts = [remote(other_past.at[r], got_past.at[r ^ 1], r, core) for r in range(slots)]
     owns = [remote(other_own.at[r], got_own.at[r ^ 1], slots + r, core) for r in range(slots)]
     sides = [remote(side_out.at[r], side_in.at[r], 2 * slots + r, side) for r in range(slots)]
-    across = [
-        remote(first, across_in.at[0], 3 * slots, far),
-        remote(second, across_in.at[1], 3 * slots + 1, side),
+    lasts = [
+        remote(mlp_far, last_in.at[0], 3 * slots, far),
+        remote(mlp_side, last_in.at[1], 3 * slots + 1, side),
     ]
-    lasts = [
-        remote(rows.at[0], last_in.at[0], 3 * slots + 2, far),
-        remote(rows.at[1], last_in.at[1], 3 * slots + 3, side),
-    ]
-    loading = [
-        pltpu.make_async_copy(source, rows.at[i], load.at[i])
-        for i, source in enumerate((mlp_far, mlp_side, mlp_own))
-    ]
-    half = across_in.shape[1]
+    loading = pltpu.make_async_copy(mlp_own, own_rows, load)
 
     @pl.when(step == 0)
     def _():
-        for copy in loading:
-            copy.start()
+        loading.start()
         meet((core, far, side))
-        for copy in across:
+        for copy in lasts:
             copy.start()
 
     @pl.when(step < slots)
@@ -1148,16 +1144,6 @@
 
         pl.when(step == pair + 1)(merge)
 
-    @pl.when(step == slots - 1)
-    def _():
-        for copy in loading:
-            copy.wait()
-        for copy in across:
-            copy.wait_recv()
-        for i, here in ((0, pl.ds(half, half)), (1, pl.ds(0, half))):
-            rows[i, here] = (rows[i, here].astype(WIDE) + across_in[1 - i].astype(WIDE)).astype(LOW)
-            lasts[i].start()
-
     @pl.when(step >= slots)
     def _():
         out_grad[...] = dot_rows(branch[...], mixed[...]).astype(LOW)
@@ -1170,12 +1156,13 @@
             total = mine_own[r] + got_own[r] + side_in[r].astype(WIDE)
             back = turn_back(total, cosine_all[r], sine_all[r])
             line[r, :, heads * head_dim :] = jnp.where(parity == 0, back, total).astype(LOW)
+        loading.wait()
         for copy in lasts:
             copy.wait_recv()
         block[...] = (
-            middle[...] + rows[2].astype(WIDE) + last_in[0].astype(WIDE) + last_in[1].astype(WIDE)
+            middle[...] + own_rows[...].astype(WIDE) + last_in[0].astype(WIDE) + last_in[1].astype(WIDE)
         ).astype(LOW)
-        for copy in (*pasts, *owns, *sides, *across, *lasts):
+        for copy in (*pasts, *owns, *sides, *lasts):
             copy.wait_send()
 
 
@@ -1214,7 +1201,7 @@
                 pl.BlockSpec((tokens, tile), lambda i, info: (0, column(i))),
                 held(*mixed.shape),
             ]
-            + [ANYWHERE] * 5
+            + [ANYWHERE] * 3
             + [held(length, model_width)],
             out_specs=[
                 held(count, length, line_cols),
@@ -1225,12 +1212,11 @@
             + [pltpu.VMEM((count, length, head_dim), LOW)] * 2
             + [pltpu.VMEM((length, head_dim), WIDE)] * 4
             + [
-                pltpu.VMEM((2, length // 2, model_width), LOW),
-                pltpu.VMEM((3, length, model_width), LOW),
+                pltpu.VMEM((length, model_width), LOW),
                 pltpu.VMEM((2, length, model_width), LOW),
-                pltpu.SemaphoreType.DMA((3 * count + 4,)),
-                pltpu.SemaphoreType.DMA((3 * count + 4,)),
-                pltpu.SemaphoreType.DMA((3,)),
+                pltpu.SemaphoreType.DMA((3 * count + 2,)),
+                pltpu.SemaphoreType.DMA((3 * count + 2,)),
+                pltpu.SemaphoreType.DMA,
             ],
         ),
         out_shape=[
@@ -1318,48 +1304,6 @@
         ],
         axis=1,
     )
-    units = gate_weight.shape[1]
-    units_pad = -(-units // 256) * 256
-    widen = lambda w: jnp.pad(w, ((0, 0), (0, units_pad - units)))
-    shards = [widen(w) for w in (down_weight.T, gate_weight, up_weight)]
-    if split:
-        half_units = units_pad // 2
-        cut = lambda w, c: lax.dynamic_slice_in_dim(w, c * half_units, half_units, axis=1)
-
-        def in_order(own, other):
-            return jnp.stack(
-                [jnp.where(ctx_rank == 0, own, other), jnp.where(ctx_rank == 0, other, own)]
-            )
-
-        def all_rows(both, *earlier):
-            full = lax.all_gather(after(both, *earlier), "fsdp", axis=0, tiled=False)
-            return full.reshape(-1, both.shape[-1])
-
-        small_both = in_order(small, from_partner(after(small, outgoing), "ctx", 1))
-        first_units = half_units // 2 // 256 * 256
-        first_cols = 3 * first_units
-
-        def in_parts(c):
-            halves = [cut(w, c) for w in shards]
-            return jnp.concatenate(
-                [w[:, :first_units] for w in halves] + [w[:, first_units:] for w in halves], axis=1
-            )
-
-        arriving_units = from_partner(after(in_parts(1 - ctx_rank), small), "ctx", 1)
-        unit_both = in_order(in_parts(ctx_rank), arriving_units)
-        slot_pick = lax.dynamic_index_in_dim(cotangent, tensor_rank, 0, keepdims=False)
-        other_own = from_partner(after(slot_pick, arriving_units), "ctx", 1)
-        other_far = from_partner(other_own, "tp", 2)
-        other_near = from_partner(other_own, "tp", 1)
-    else:
-        all_rows = lambda shard, *earlier: lax.all_gather(
-            shard, ("fsdp", "ctx"), axis=0, tiled=True
-        )
-        small_both, unit_both, half_units = small, jnp.concatenate(shards, axis=1), units_pad
-    far_in = from_partner(own_in, "tp", 2)
-    near_in = from_partner(own_in, "tp", 1)
-    cross_in = from_partner(far_in, "tp", 1)
-
     lengths_now = jnp.stack([seq_lengths[s] for s in seq_now])
     info = jnp.concatenate([lengths_now, jnp.stack([offset, parity])]).astype(jnp.int32)
     positions_now = jnp.stack(
@@ -1370,12 +1314,55 @@
     angles = positions_now.astype(WIDE)[..., None] * frequency
     cosine = jnp.cos(angles)
     sine = jnp.sin(angles) * jnp.where(lane < head_dim // 2, -1.0, 1.0)
+    pick_info = jnp.stack(slot_now + [s ^ tensor_rank for s in slot_now]).astype(jnp.int32)
+    units = gate_weight.shape[1]
+    units_pad = -(-units // 256) * 256
+    widen = lambda w: jnp.pad(w, ((0, 0), (0, units_pad - units)))
+    shards = [widen(w) for w in (down_weight.T, gate_weight, up_weight)]
+    if split:
+        half_units = units_pad // 2
+        cut = lambda w, c: lax.dynamic_slice_in_dim(w, c * half_units, half_units, axis=1)
+
+        def in_order(own, other):
+            return jnp.stack(
+                [jnp.where(ctx_rank == 0, own, other), jnp.where(ctx_rank == 0, other, own)]
+            )
+
+        def all_rows(both, *earlier):
+            full = lax.all_gather(after(both, *earlier), "fsdp", axis=0, tiled=False)
+            return full.reshape(-1, both.shape[-1])
+
+        first_units = half_units // 2 // 256 * 256
+        first_cols = 3 * first_units
+
+        def in_parts(c):
+            halves = [cut(w, c) for w in shards]
+            return jnp.concatenate(
+                [w[:, :first_units] for w in halves] + [w[:, first_units:] for w in halves], axis=1
+            )
+
+        leaving_units, own_units = in_parts(1 - ctx_rank), in_parts(ctx_rank)
+        slot_pick = lax.dynamic_index_in_dim(cotangent, tensor_rank, 0, keepdims=False)
+        small = after(small, outgoing, cosine, sine, info, pick_info, leaving_units, own_units, slot_pick)
+        small_both = in_order(small, from_partner(small, "ctx", 1))
+        arriving_units = from_partner(after(leaving_units, small_both), "ctx", 1)
+        other_own = from_partner(after(slot_pick, arriving_units), "ctx", 1)
+        both_a = in_order(own_units[:, :first_cols], arriving_units[:, :first_cols])
+        both_b = in_order(own_units[:, first_cols:], arriving_units[:, first_cols:])
+    else:
+        all_rows = lambda shard, *earlier: lax.all_gather(
+            shard, ("fsdp", "ctx"), axis=0, tiled=True
+        )
+        small_both, unit_both, half_units = small, jnp.concatenate(shards, axis=1), units_pad
+    far_in = from_partner(own_in, "tp", 2)
+    near_in = from_partner(own_in, "tp", 1)
+    cross_in = from_partner(far_in, "tp", 1)
     grad_slots = [lax.dynamic_index_in_dim(cotangent, s, 0, keepdims=False) for s in slot_now]
 
     near_full = all_rows(small_both, own_in)
     if split:
-        units_a = all_rows(unit_both[..., :first_cols], cross_in)
-        units_b = all_rows(unit_both[..., first_cols:], cross_in)
+        units_a = all_rows(both_a, cross_in)
+        units_b = all_rows(both_b, cross_in)
     else:
         down_full = all_rows(unit_both[..., :half_units], cross_in)
         gate_up_full = all_rows(unit_both[..., half_units:], cross_in)
@@ -1387,7 +1374,7 @@
         (own_in, near_in, far_in, cross_in),
         near_full,
         bias_row,
-        after(cosine, other_own, unit_both) if split else cosine,
+        after(cosine, other_own, both_a, both_b, info, pick_info) if split else cosine,
         sine,
         heads,
         head_dim,
@@ -1395,9 +1382,11 @@
     gains_now = near_full[:, query_cols + head_width : near_cols][:, :2].astype(WIDE).T
     if split:
         key_past, value_past = lax.ppermute((key_own, value_own), "ctx", [(0, 1)])
-        other_cross = from_partner(after(other_far, query_rot), "tp", 1)
+        other_far = from_partner(other_own, "tp", 2)
+        other_near = from_partner(after(other_own, key_past), "tp", 1)
+        other_cross = from_partner(after(other_far, key_past), "tp", 1)
         other_rows = (other_own, other_near, other_far, other_cross)
-        key_past = after(key_past, *other_rows)
+        key_past = after(key_past, other_far)
     else:
         key_past = lax.all_gather(key_own, "ctx", axis=1, tiled=True)
         value_past = lax.all_gather(value_own, "ctx", axis=1, tiled=True)
@@ -1422,9 +1411,8 @@
     half_len = local_len // 2
 
     if split:
-        picks = [s ^ tensor_rank for s in slot_now]
         grad_hidden, grad_rows = chosen_rows(
-            jnp.stack(slot_now + picks).astype(jnp.int32),
+            pick_info,
             after(cotangent, normed_share),
             other_rows,
             units_a,
@@ -1498,7 +1486,7 @@
             normed_two,
             gate_b,
         )
-        mlp_own, mlp_far, mlp_side, mlp_first, mlp_second = mlp
+        mlp_own, mlp_far, mlp_side = mlp
         grad_branch = grad_branch.reshape(token_count, model_width)
     else:
         first_back, finish_back = collect_all(
@@ -1541,7 +1529,7 @@
             *attend_args,
             grad_branch,
             mixed_flat,
-            (mlp_first, mlp_second, mlp_far, mlp_side, mlp_own),
+            (mlp_far, mlp_side, mlp_own),
             middle_share,
         )
         line_grad = line_grad.reshape(token_count, -1)
@@ -1597,7 +1585,12 @@
         return lax.psum_scatter(grad, "fsdp", scatter_dimension=0, tiled=True)
 
     unit_grads = (grad_a, down_b, up_grad_b, gate_grad_b) if split else (down_grad, gate_grad, up_grad)
-    unit_sums = [scatter_units(g) for g in unit_grads]
+    unit_sums = [scatter_units(unit_grads[0])]
+    if split:
+        unit_sums += [scatter_units(after(g, unit_sums[0])) for g in unit_grads[1:3]]
+        unit_sums += [scatter_units(after(unit_grads[3], *unit_sums))]
+    else:
+        unit_sums += [scatter_units(g) for g in unit_grads[1:]]
 
     attn_end = scatter_sum(attn_grad, ctx_rank, LOW, *unit_sums)
 

time: 926 us -> 892 us (0.963)
  Pallas kernels: 439 us -> 414 us
    ppermute x35, waiting for transfers between devices: 144 us -> 210 us  [from_partner(): return lax.ppermute(value, axis, pairs)]
    ppermute x1, waiting for transfers between devices: 96.6 us -> 62.1 us  [leave(): return lax.ppermute(share, ('fsdp', 'tp'), back)]
    ppermute x1, waiting for transfers between devices: 23 us -> 0.01 us  [local(): own_in = lax.ppermute(outgoing, ('fsdp', 'tp'), there)]
    pallas_call x1, Pallas kernels: 72.3 us -> 51.6 us  [finish_rows(): pl.pallas_call(functools.partial(line_kernel, slots, tiles), grid=(slots...]
    pallas_call x1, Pallas kernels: 74.4 us -> 54.4 us  [attend_exchange(): pl.pallas_call(functools.partial(exchange_kernel, heads, head_dim, scale,...]
    pallas_call x1, Pallas kernels: 50.4 us -> 65.6 us  [spread_branch(): pl.pallas_call(functools.partial(branch_kernel, slots, tiles), grid=(slot...]
    ppermute x2, waiting for transfers between devices: 18 us -> 7.38 us  [local(): key_past, value_past = lax.ppermute((key_own, value_own), 'ctx', [(0, 1)])]
  transfers between devices with their start and end apart: 50 -> 50, of which waited for: 21 -> 22; matrix products, arithmetic and copies ran while one was open for 8% -> 8% of each run, Pallas kernels for 31% -> 47%
where the time goes in v6:
time: 892 us; the launch traced here: 881 us
  Pallas kernels  414 us (46%)
  waiting for transfers between devices  285 us (32%)
  starting transfers between devices  57.3 us (6%)
  other arithmetic  41.7 us (5%)
  local copies, waits for them, and re-layouts  40.8 us (5%)
  between operations  34.7 us (4%)
    ppermute x35, waiting for transfers between devices, from_partner(): return lax.ppermute(value, axis, pairs)  210 us
    pallas_call x1, Pallas kernels, collect_back(): pl.pallas_call(functools.partial(collect_kernel, slots, tiles), grid=(slo...  71.1 us
    pallas_call x1, Pallas kernels, spread_branch(): pl.pallas_call(functools.partial(branch_kernel, slots, tiles), grid=(slot...  65.6 us
    ppermute x1, waiting for transfers between devices, leave(): return lax.ppermute(share, ('fsdp', 'tp'), back)  62.1 us
    pallas_call x1, Pallas kernels, attend_exchange(): pl.pallas_call(functools.partial(exchange_kernel, heads, head_dim, scale,...  54.4 us
    pallas_call x1, Pallas kernels, finish_rows(): pl.pallas_call(functools.partial(line_kernel, slots, tiles), grid=(slots...  51.6 us
    ppermute x35, starting transfers between devices, from_partner(): return lax.ppermute(value, axis, pairs)  41 us
    pallas_call x1, Pallas kernels, full_units(): pl.pallas_call(full_units_kernel, grid=(tokens // step,), in_specs=[by_ro...  37 us
  transfers between devices with their start and end apart: 50, of which 22 were waited for; matrix products, arithmetic and copies ran while one was open for 8% of the time, Pallas kernels for 47%

profile of v6, /device:TPU:1, one launch (start us, length us, event | category | flops | bytes accessed | tf_op | source)
XLA Modules:
  0.0 881.4 jit_solution(12087680566697976549)
XLA Ops:
  63.2 9.2 %collective-permute-done.4 = bf16[192,1152]{1,0:T(8,128)(2,1)S(1)} collective-permute-done((bf16[192,1152]{1,0:T(8,128)(2,1)S(1)}, bf16[192,1152]{1,0:T(8,128)(2,1)S(1)}, u32[]{:S(2)}, u32[]{:S(2)}) %collective-permute-start.4) | collective-permute-done | bytes 442400 | tf_op jit(solution)/shard_map/ppermute | solution.py:21
  78.0 33.6 %collective-permute-done.2.x2 = bf16[512,1536]{1,0:T(8,128)(2,1)S(1)} collective-permute-done((bf16[512,1536]{1,0:T(8,128)(2,1)S(1)}, bf16[512,1536]{1,0:T(8,128)(2,1)S(1)}, u32[]{:S(2)}, u32[]{:S(2)}) %collective-permute-start.2) | collective-permute-done | bytes 1572896 | tf_op jit(solution)/shard_map/ppermute | solution.py:21
  118.0 33.9 %collective-permute-done.6.refs_0_ = bf16[512,1536]{1,0:T(8,128)(2,1)} collective-permute-done((bf16[512,1536]{1,0:T(8,128)(2,1)}, bf16[512,1536]{1,0:T(8,128)(2,1)}, u32[]{:S(2)}, u32[]{:S(2)}) %collective-permute-start.6) | collective-permute-done | bytes 1572896 | tf_op jit(solution)/shard_map/ppermute | solution.py:21
  157.4 12.5 %shard_map.230 = (bf16[4,512,1536]{2,1,0:T(8,128)(2,1)}, bf16[4,512,384]{2,1,0:T(8,128)(2,1)}, bf16[4,512,128]{2,1,0:T(8,128)(2,1)}, bf16[4,512,128]{2,1,0:T(8,128)(2,1)}) custom-call(bf16[512,1536]{1,0:T(8,128)(2,1)} %copy-done.5, bf16[512,1536]{1,0:T(8,128)(2,1)} %copy-done.14, bf16[512,1536]{1,0:T(8,128)(2,1)} %copy-done.13, ...), custom_call_target="tpu_custom_call" | custom-call | flops 4026531840 | bytes 17170432 | tf_op jit(solution)/shard_map/pallas_call | solution.py:829
  176.3 10.8 %collective-permute-done.8.refs_2_ = bf16[512,1536]{1,0:T(8,128)(2,1)} collective-permute-done((bf16[512,1536]{1,0:T(8,128)(2,1)}, bf16[512,1536]{1,0:T(8,128)(2,1)}, u32[]{:S(2)}, u32[]{:S(2)}) %collective-permute-start.8) | collective-permute-done | bytes 1572896 | tf_op jit(solution)/shard_map/ppermute | solution.py:21
  195.3 13.6 %shard_map.231 = (bf16[2,512,384]{2,1,0:T(8,128)(2,1)}, f32[2,512,128]{2,1,0:T(8,128)}, bf16[512,1536]{1,0:T(8,128)(2,1)}, bf16[512,1536]{1,0:T(8,128)(2,1)}) custom-call(s32[6]{0:T(128)} %concatenate.80.info, bf16[4,512,384]{2,1,0:T(8,128)(2,1)} %get-tuple-element.79.q, bf16[4,512,128]{2,1,0:T(8,128)(2,1)} %copy-done.22, bf16[4,512,128]{2,1,0:T(8,128)(2,1)} %copy-done.23, ...), custom_call_target="tpu_custom_call" | custom-call | flops 1610612736 | bytes 1572864 | tf_op jit(solution)/shard_map/pallas_call | solution.py:917
  217.5 13.6 %shard_map.232 = (bf16[2,512,384]{2,1,0:T(8,128)(2,1)}, f32[2,512,128]{2,1,0:T(8,128)}, bf16[512,1536]{1,0:T(8,128)(2,1)}, bf16[512,1536]{1,0:T(8,128)(2,1)}) custom-call(s32[6]{0:T(128)} %concatenate.80.info, bf16[4,512,384]{2,1,0:T(8,128)(2,1)} %get-tuple-element.79.q, bf16[4,512,128]{2,1,0:T(8,128)(2,1)} %copy-done.22, bf16[4,512,128]{2,1,0:T(8,128)(2,1)} %copy-done.23, ...), custom_call_target="tpu_custom_call" | custom-call | flops 1610612736 | bytes 1572864 | tf_op jit(solution)/shard_map/pallas_call | solution.py:917
  234.6 18.8 %collective-permute-done.12 = bf16[512,1536]{1,0:T(8,128)(2,1)} collective-permute-done((bf16[512,1536]{1,0:T(8,128)(2,1)}, bf16[512,1536]{1,0:T(8,128)(2,1)}, u32[]{:S(2)}, u32[]{:S(2)}) %collective-permute-start.12) | collective-permute-done | bytes 1572896 | tf_op jit(solution)/shard_map/ppermute | solution.py:21
  262.3 15.6 %shard_map.233 = (bf16[4096,512]{1,0:T(8,128)(2,1)}, bf16[4096,1536]{1,0:T(8,128)(2,1)}) custom-call(s32[8]{0:T(128)} %stack.98.info, bf16[4,512,1536]{2,1,0:T(8,128)(2,1)} %cotangent, bf16[512,1536]{1,0:T(8,128)(2,1)} %collective-permute-done.6.refs_0_, bf16[512,1536]{1,0:T(8,128)(2,1)} %collective-permute-done.15.refs_1_, ...), custom_call_target="tpu_custom_call" | custom-call | flops 6442450944 | bytes 30932992 | tf_op jit(solution)/shard_map/pallas_call | solution.py:226
  277.9 16.1 %collective-permute-done.18.refs_4_ = bf16[512,1536]{1,0:T(8,128)(2,1)S(1)} collective-permute-done((bf16[512,1536]{1,0:T(8,128)(2,1)S(1)}, bf16[512,1536]{1,0:T(8,128)(2,1)S(1)}, u32[]{:S(2)}, u32[]{:S(2)}) %collective-permute-start.18) | collective-permute-done | bytes 1572896 | tf_op jit(solution)/shard_map/ppermute | solution.py:21
  299.4 12.4 %collective-permute-done.21.refs_7_ = bf16[256,1536]{1,0:T(8,128)(2,1)S(1)} collective-permute-done((bf16[256,1536]{1,0:T(8,128)(2,1)S(1)}, bf16[256,1536]{1,0:T(8,128)(2,1)S(1)}, u32[]{:S(2)}, u32[]{:S(2)}) %collective-permute-start.21) | collective-permute-done | bytes 786464 | tf_op jit(solution)/shard_map/ppermute | solution.py:21
  319.2 15.5 %shard_map.234 = (bf16[4096,512]{1,0:T(8,128)(2,1)}, bf16[4096,1536]{1,0:T(8,128)(2,1)}) custom-call(bf16[512,1536]{1,0:T(8,128)(2,1)} %copy-done.15, bf16[512,1536]{1,0:T(8,128)(2,1)} %collective-permute-done.13.refs_1_, bf16[512,1536]{1,0:T(8,128)(2,1)} %collective-permute-done.14.refs_2_, bf16[512,1536]{1,0:T(8,128)(2,1)} %collective-permute-done.17.refs_3_, ...), custom_call_target="tpu_custom_call" | custom-call | flops 6442450944 | bytes 30932992 | tf_op jit(solution)/shard_map/pallas_call | solution.py:121
  334.7 17.8 %shard_map.235 = (bf16[4096,512]{1,0:T(8,128)(2,1)}, bf16[4096,512]{1,0:T(8,128)(2,1)}, bf16[4096,512]{1,0:T(8,128)(2,1)}) custom-call(bf16[4096,1536]{1,0:T(8,128)(2,1)} %get-tuple-element.101.h.right.turned, bf16[1536,1536]{1,0:T(8,128)(2,1)} %bitcast.163, bf16[4096,512]{1,0:T(8,128)(2,1)} %get-tuple-element.96.gate, bf16[4096,512]{1,0:T(8,128)(2,1)} %get-tuple-element.92.grad), custom_call_target="tpu_custom_call" | custom-call | flops 6442450944 | bytes 35127296 | tf_op jit(solution)/shard_map/pallas_call | solution.py:157
  352.4 33.5 %shard_map.236 = bf16[1536,1536]{1,0:T(8,128)(2,1)} custom-call(bf16[4096,1536]{1,0:T(8,128)(2,1)} %get-tuple-element.99.g.left, bf16[4096,1536]{1,0:T(8,128)(2,1)} %get-tuple-element.101.h.right.turned, bf16[4096,512]{1,0:T(8,128)(2,1)} %get-tuple-element.100.hid.hid_a, bf16[4096,512]{1,0:T(8,128)(2,1)} %get-tuple-element.97.gate.gate_a, ...), custom_call_target="tpu_custom_call" | custom-call | flops 19327352832 | bytes 17301504 | tf_op jit(solution)/shard_map/pallas_call | solution.py:294
  386.5 37.0 %shard_map.237 = (bf16[4096,640]{1,0:T(8,128)(2,1)}, bf16[4096,640]{1,0:T(8,128)(2,1)}, bf16[4096,640]{1,0:T(8,128)(2,1)}) custom-call(bf16[4096,1536]{1,0:T(8,128)(2,1)} %get-tuple-element.101.h.right.turned, bf16[4096,1536]{1,0:T(8,128)(2,1)} %get-tuple-element.99.g.left, bf16[1536,1920]{1,0:T(8,128)(2,1)} %bitcast.182, bf16[1536,1920]{1,0:T(8,128)(2,1)} %bitcast.183, ...), custom_call_target="tpu_custom_call" | custom-call | flops 24159191040 | bytes 46792704 | tf_op jit(solution)/shard_map/pallas_call | solution.py:268
  423.5 71.1 %shard_map.238 = (f32[512,1536]{1,0:T(8,128)}, bf16[1536,640]{1,0:T(8,128)(2,1)}, bf16[1536,640]{1,0:T(8,128)(2,1)}) custom-call(bf16[4096,512]{1,0:T(8,128)(2,1)} %get-tuple-element.97.gate.gate_a, bf16[4096,512]{1,0:T(8,128)(2,1)} %get-tuple-element.98.up.up_a, bf16[4096,640]{1,0:T(8,128)(2,1)} %get-tuple-element.103.gate_b.gate, ...), custom_call_target="tpu_custom_call" | custom-call | flops 24159191040 | bytes 26214400 | tf_op jit(solution)/shard_map/pallas_call | solution.py:435
  502.3 65.6 %shard_map.239 = (f32[512,1536]{1,0:T(8,128)}, f32[1,1536]{1,0:T(1,128)}, bf16[1536,640]{1,0:T(8,128)(2,1)}, bf16[4,512,1536]{2,1,0:T(8,128)(2,1)}, bf16[512,153...) custom-call(f32[512,1536]{1,0:T(8,128)} %get-tuple-element.106.total, f32[512,1536]{1,0:T(8,128)} %copy-done.4, ...), custom_call_target="tpu_custom_call" | custom-call | flops 16106127360 | bytes 26214400 | tf_op jit(solution)/shard_map/pallas_call | solution.py:580
  567.9 7.7 convolution_convert_fusion
  575.6 54.4 %shard_map.240 = (bf16[4,512,512]{2,1,0:T(8,128)(2,1)}, bf16[1536,384]{1,0:T(8,128)(2,1)}, bf16[512,1536]{1,0:T(8,128)(2,1)}) custom-call(s32[6]{0:T(128)} %concatenate.80.info, bf16[4,512,384]{2,1,0:T(8,128)(2,1)} %get-tuple-element.79.q, bf16[4,512,128]{2,1,0:T(8,128)(2,1)} %copy-done.22, bf16[4,512,128]{2,1,0:T(8,128)(2,1)} %copy-done.23, ...), custom_call_target="tpu_custom_call" | custom-call | flops 2415919104 | bytes 7864320 | tf_op jit(solution)/shard_map/pallas_call | solution.py:1184
  630.0 51.6 %shard_map.241 = (bf16[512,1536]{1,0:T(8,128)(2,1)}, f32[1,1536]{1,0:T(1,128)}, bf16[1536,512]{1,0:T(8,128)(2,1)}, f32[1,512]{1,0:T(1,128)}, bf16[512,1536]{1,0:T(8,128)(2,1)}) custom-call(bf16[2048,512]{1,0:T(8,128)(2,1)} %bitcast.154, bf16[1536,512]{1,0:T(8,128)(2,1)} %pad_maximum_fusion.2.weight, bf16[512,1536]{1,0:T(8,128)(2,1)} %copy-done.5, ...), custom_call_target="tpu_custom_call" | custom-call | flops 3221225472 | bytes 31457280 | tf_op jit(solution)/shard_map/pallas_call | solution.py:716
  690.2 62.1 %collective-permute-done.27.refs_0_ = bf16[512,1536]{1,0:T(8,128)(2,1)S(1)} collective-permute-done((bf16[512,1536]{1,0:T(8,128)(2,1)}, bf16[512,1536]{1,0:T(8,128)(2,1)S(1)}, u32[]{:S(2)}, u32[]{:S(2)}) %collective-permute-start.27) | collective-permute-done | bytes 1572896 | tf_op jit(solution)/shard_map/ppermute | solution.py:1600
  755.2 32.8 %collective-permute-done.33 = f32[1536,2]{0,1:T(2,128)S(1)} collective-permute-done((f32[1536,2]{0,1:T(2,128)S(1)}, f32[1536,2]{0,1:T(2,128)S(1)}, u32[]{:S(2)}, u32[]{:S(2)}) %collective-permute-start.33) | collective-permute-done | bytes 12320 | tf_op jit(solution)/shard_map/ppermute | solution.py:21
  821.7 13.0 %collective-permute-done.31 = bf16[4,192,896]{2,1,0:T(8,128)(2,1)} collective-permute-done((bf16[4,192,896]{2,1,0:T(8,128)(2,1)}, bf16[4,192,896]{2,1,0:T(8,128)(2,1)}, u32[]{:S(2)}, u32[]{:S(2)}) %collective-permute-start.31) | collective-permute-done | bytes 1376288 | tf_op jit(solution)/shard_map/ppermute | solution.py:21
  839.5 7.7 collective-permute-done.38
  (272 shorter events, 186.7 us)
Async XLA Ops:
  7.2 149.0 %all-gather.7.cloned.1.call-start = ((), (), s32[]{:S(2)}) async-start(), calls=%async_computation.10 | async-start | bytes 4423680 | tf_op jit(solution)/shard_map/all_gather | solution.py:1332
  17.5 56.1 %collective-permute-start = (bf16[512,1536]{1,0:T(8,128)(2,1)}, bf16[512,1536]{1,0:T(8,128)(2,1)S(1)}, u32[]{:S(2)}, u32[]{:S(2)}) collective-permute-start(bf16[512,1536]{1,0:T(8,128)(2,1)} %dynamic-slice_bitcast_fusion.2), channel_id=1, source_target_pairs={{0,0},{1,17},{2,10},{3,27},{8,8},{9,25},{10,18},{11,3},{16,16},{17... | collective-permute-start | bytes 4718600 | tf_op jit(solution)/shard_map/ppermute | solution.py:1297
  73.6 188.7 %all-gather.9.cloned.1.call-start = ((), (), s32[]{:S(2)}) async-start(), calls=%async_computation.11 | async-start | bytes 5898240 | tf_op jit(solution)/shard_map/all_gather | solution.py:1332
  73.6 38.0 %collective-permute-start.2 = (bf16[512,1536]{1,0:T(8,128)(2,1)S(1)}, bf16[512,1536]{1,0:T(8,128)(2,1)S(1)}, u32[]{:S(2)}, u32[]{:S(2)}) collective-permute-start(bf16[512,1536]{1,0:T(8,128)(2,1)S(1)} %collective-permute-done.x0.own_in), channel_id=1, source_target_pairs={{0,2},{1,3},{2,0},{3,1},{4,6},{5,7},{6,4},{7,5},{8,10},{9,11},{10,... | collective-permute-start | bytes 4718600 | tf_op jit(solution)/shard_map/ppermute | solution.py:21
  76.8 35.4 %collective-permute-start.5 = (bf16[192,3456]{1,0:T(8,128)(2,1)}, bf16[192,3456]{1,0:T(8,128)(2,1)S(1)}, u32[]{:S(2)}, u32[]{:S(2)}) collective-permute-start(bf16[192,3456]{1,0:T(8,128)(2,1)} %get-tuple-element.76), channel_id=1, source_target_pairs={{0,4},{4,0},{1,5},{5,1},{2,6},{6,2},{3,7},{7,3},{8,12},{12,8},{9,1... | collective-permute-start | bytes 3981320 | tf_op jit(solution)/shard_map/ppermute | solution.py:21
  115.6 270.9 %all-gather.11.cloned.1.call-start = ((), (), s32[]{:S(2)}) async-start(), calls=%async_computation.12 | async-start | bytes 7372800 | tf_op jit(solution)/shard_map/all_gather | solution.py:1332
  115.6 36.2 %collective-permute-start.6 = (bf16[512,1536]{1,0:T(8,128)(2,1)}, bf16[512,1536]{1,0:T(8,128)(2,1)}, u32[]{:S(2)}, u32[]{:S(2)}) collective-permute-start(bf16[512,1536]{1,0:T(8,128)(2,1)} %get-tuple-element.77), channel_id=1, source_target_pairs={{0,4},{4,0},{1,5},{5,1},{2,6},{6,2},{3,7},{7,3},{8,12},{12,8},{9,1... | collective-permute-start | bytes 4718600 | tf_op jit(solution)/shard_map/ppermute | solution.py:21
  116.9 39.3 %collective-permute-start.1 = (bf16[512,1536]{1,0:T(8,128)(2,1)S(1)}, bf16[512,1536]{1,0:T(8,128)(2,1)S(1)}, u32[]{:S(2)}, u32[]{:S(2)}) collective-permute-start(bf16[512,1536]{1,0:T(8,128)(2,1)S(1)} %collective-permute-done.x0.own_in), channel_id=1, source_target_pairs={{0,1},{1,0},{2,3},{3,2},{4,5},{5,4},{6,7},{7,6},{8,9},{9,8},{10,11... | collective-permute-start | bytes 4718600 | tf_op jit(solution)/shard_map/ppermute | solution.py:21
  151.9 35.2 %collective-permute-start.8 = (bf16[512,1536]{1,0:T(8,128)(2,1)}, bf16[512,1536]{1,0:T(8,128)(2,1)}, u32[]{:S(2)}, u32[]{:S(2)}) collective-permute-start(bf16[512,1536]{1,0:T(8,128)(2,1)} %collective-permute-done.6.refs_0_), channel_id=1, source_target_pairs={{0,2},{1,3},{2,0},{3,1},{4,6},{5,7},{6,4},{7,5},{8,10},{9,11},{10,... | collective-permute-start | bytes 4718600 | tf_op jit(solution)/shard_map/ppermute | solution.py:21
  217.4 35.9 %collective-permute-start.12 = (bf16[512,1536]{1,0:T(8,128)(2,1)}, bf16[512,1536]{1,0:T(8,128)(2,1)}, u32[]{:S(2)}, u32[]{:S(2)}) collective-permute-start(bf16[512,1536]{1,0:T(8,128)(2,1)} %add_convert_fusion), channel_id=1, source_target_pairs={{0,2},{1,3},{2,0},{3,1},{4,6},{5,7},{6,4},{7,5},{8,10},{9,11},{10,... | collective-permute-start | bytes 4718600 | tf_op jit(solution)/shard_map/ppermute | solution.py:21
  231.9 262.8 %reduce-scatter.6.cloned.1.call-start = ((), (), s32[]{:S(2)}) async-start(), calls=%async_computation.5 | async-start | bytes 5898240 | tf_op jit(solution)/shard_map/reduce_scatter | solution.py:1585
  258.4 35.7 %collective-permute-start.18 = (bf16[512,1536]{1,0:T(8,128)(2,1)S(1)}, bf16[512,1536]{1,0:T(8,128)(2,1)S(1)}, u32[]{:S(2)}, u32[]{:S(2)}) collective-permute-start(bf16[512,1536]{1,0:T(8,128)(2,1)S(1)} %multiply_convert_fusion.refs_0_), channel_id=1, source_target_pairs={{0,4},{4,0},{1,5},{5,1},{2,6},{6,2},{3,7},{7,3},{8,12},{12,8},{9,1... | collective-permute-start | bytes 4718600 | tf_op jit(solution)/shard_map/ppermute | solution.py:21
  260.5 34.5 %collective-permute-start.14 = (bf16[512,1536]{1,0:T(8,128)(2,1)S(1)}, bf16[512,1536]{1,0:T(8,128)(2,1)}, u32[]{:S(2)}, u32[]{:S(2)}) collective-permute-start(bf16[512,1536]{1,0:T(8,128)(2,1)S(1)} %multiply_convert_fusion.refs_0_), channel_id=1, source_target_pairs={{0,2},{1,3},{2,0},{3,1},{4,6},{5,7},{6,4},{7,5},{8,10},{9,11},{10,... | collective-permute-start | bytes 4718600 | tf_op jit(solution)/shard_map/ppermute | solution.py:21
  260.5 55.8 %collective-permute-start.13 = (bf16[512,1536]{1,0:T(8,128)(2,1)S(1)}, bf16[512,1536]{1,0:T(8,128)(2,1)}, u32[]{:S(2)}, u32[]{:S(2)}) collective-permute-start(bf16[512,1536]{1,0:T(8,128)(2,1)S(1)} %multiply_convert_fusion.refs_0_), channel_id=1, source_target_pairs={{0,1},{1,0},{2,3},{3,2},{4,5},{5,4},{6,7},{7,6},{8,9},{9,8},{10,11... | collective-permute-start | bytes 4718600 | tf_op jit(solution)/shard_map/ppermute | solution.py:21
  386.0 297.8 %reduce-scatter.10.cloned.1.call-start = ((), (), s32[]{:S(2)}) async-start(), calls=%async_computation.7 | async-start | bytes 2457600 | tf_op jit(solution)/shard_map/reduce_scatter | solution.py:1585
  494.7 189.1 %reduce-scatter.8.cloned.1.call-start = ((), (), s32[]{:S(2)}) async-start(), calls=%async_computation.6 | async-start | bytes 2457600 | tf_op jit(solution)/shard_map/reduce_scatter | solution.py:1585
  500.1 321.6 %reduce-scatter.12.cloned.1.call-start = ((), (), s32[]{:S(2)}) async-start(), calls=%async_computation.8 | async-start | bytes 2457600 | tf_op jit(solution)/shard_map/reduce_scatter | solution.py:1585
  681.7 70.7 %collective-permute-start.27 = (bf16[512,1536]{1,0:T(8,128)(2,1)}, bf16[512,1536]{1,0:T(8,128)(2,1)S(1)}, u32[]{:S(2)}, u32[]{:S(2)}) collective-permute-start(bf16[512,1536]{1,0:T(8,128)(2,1)} %get-tuple-element.120), channel_id=1, source_target_pairs={{0,0},{17,1},{10,2},{27,3},{8,8},{25,9},{18,10},{3,11},{16,16},{1,... | collective-permute-start | bytes 4718600 | tf_op jit(solution)/shard_map/ppermute | solution.py:1600
  683.8 187.0 %reduce-scatter.14.cloned.1.call-start = ((), (), s32[]{:S(2)}) async-start(), calls=%async_computation.9 | async-start | bytes 1720320 | tf_op jit(solution)/shard_map/reduce_scatter | solution.py:83
  683.9 68.5 %collective-permute-start.32 = (f32[1536,2]{0,1:T(2,128)S(1)}, f32[1536,2]{0,1:T(2,128)S(1)}, u32[]{:S(2)}, u32[]{:S(2)}) collective-permute-start(f32[1536,2]{0,1:T(2,128)S(1)} %maximum_bitcast_fusion), channel_id=1, source_target_pairs={{0,1},{1,0},{2,3},{3,2},{4,5},{5,4},{6,7},{7,6},{8,9},{9,8},{10,11... | collective-permute-start | bytes 36872 | tf_op jit(solution)/shard_map/ppermute | solution.py:21
  690.2 107.7 %collective-permute-start.25 = (bf16[512,1536]{1,0:T(8,128)(2,1)S(1)}, bf16[512,1536]{1,0:T(8,128)(2,1)}, u32[]{:S(2)}, u32[]{:S(2)}) collective-permute-start(bf16[512,1536]{1,0:T(8,128)(2,1)S(1)} %copy-done.2), channel_id=1, source_target_pairs={{0,2},{1,3},{2,0},{3,1},{4,6},{5,7},{6,4},{7,5},{8,10},{9,11},{10,... | collective-permute-start | bytes 4718600 | tf_op jit(solution)/shard_map/ppermute | solution.py:21
  752.3 45.6 %collective-permute-start.29 = (bf16[512,1536]{1,0:T(8,128)(2,1)S(1)}, bf16[512,1536]{1,0:T(8,128)(2,1)}, u32[]{:S(2)}, u32[]{:S(2)}) collective-permute-start(bf16[512,1536]{1,0:T(8,128)(2,1)S(1)} %collective-permute-done.27.refs_0_), channel_id=1, source_target_pairs={{0,2},{1,3},{2,0},{3,1},{4,6},{5,7},{6,4},{7,5},{8,10},{9,11},{10,... | collective-permute-start | bytes 4718600 | tf_op jit(solution)/shard_map/ppermute | solution.py:21
  752.4 35.7 %collective-permute-start.33 = (f32[1536,2]{0,1:T(2,128)S(1)}, f32[1536,2]{0,1:T(2,128)S(1)}, u32[]{:S(2)}, u32[]{:S(2)}) collective-permute-start(f32[1536,2]{0,1:T(2,128)S(1)} %fusion.43), channel_id=1, source_target_pairs={{0,2},{1,3},{2,0},{3,1},{4,6},{5,7},{6,4},{7,5},{8,10},{9,11},{10,... | collective-permute-start | bytes 36872 | tf_op jit(solution)/shard_map/ppermute | solution.py:21
  803.9 30.8 %collective-permute-start.31 = (bf16[4,192,896]{2,1,0:T(8,128)(2,1)}, bf16[4,192,896]{2,1,0:T(8,128)(2,1)}, u32[]{:S(2)}, u32[]{:S(2)}) collective-permute-start(bf16[4,192,896]{2,1,0:T(8,128)(2,1)} %get-tuple-element.162), channel_id=1, source_target_pairs={{0,4},{4,0},{1,5},{5,1},{2,6},{6,2},{3,7},{7,3},{8,12},{12,8},{9,1... | collective-permute-start | bytes 4128776 | tf_op jit(solution)/shard_map/ppermute | solution.py:21
  (71 other events, 850.4 us)
Sparse Core Ops, SparseCore 0:
  73.7 70.5 all-gather.6
  145.8 88.1 all-gather.8
  235.6 107.4 all-gather.10
  386.1 82.4 reduce-scatter.5
  494.8 39.9 reduce-scatter.9
  536.9 40.6 reduce-scatter.7
  683.9 56.2 reduce-scatter.11
  837.6 33.2 reduce-scatter.13

commit v7 on v6

--- a/solution.py
+++ b/solution.py
@@ -487,8 +487,6 @@
 ):
     step = pl.program_id(0)
     core, far, side = partners_of()
-    half = own.shape[0] // 2
-    low, high = pl.ds(0, half), pl.ds(half, half)
     remote = remote_copy(send, recv)
     to_far = remote(own, branch.at[2], 0, far)
     to_near = remote(own, branch.at[1], 1, core)
@@ -496,10 +494,7 @@
     keep = pltpu.make_async_copy(own, branch.at[0], load.at[0])
     loading = pltpu.make_async_copy(gate, held, load.at[1])
     cores = [remote(parts.at[7 - 2 * k], core_in.at[k], 3 + k, core) for k in range(4)]
-    across = [
-        remote(parts.at[6, low], across_in.at[0], 7, far),
-        remote(parts.at[6, high], across_in.at[1], 8, side),
-    ]
+    across = remote(parts.at[6], across_in, 7, side)
     stores = [
         pltpu.make_async_copy(parts.at[4], mlp_side, load.at[2]),
         pltpu.make_async_copy(parts.at[2], mlp_far, load.at[3]),
@@ -532,8 +527,9 @@
             cores[k].wait_recv()
             parts[slot] = (parts[slot].astype(WIDE) + core_in[k].astype(WIDE)).astype(LOW)
             if k == 0:
-                for copy in across:
-                    copy.start()
+                across.start()
+            if k == 1:
+                stores[0].start()
             if k == 3:
                 stores[2].start()
 
@@ -553,16 +549,13 @@
     def _():
         to_near.wait_recv()
         to_cross.wait_recv()
-        for i, (slot, here) in enumerate(((4, low), (2, high))):
-            across[i].wait_recv()
-            parts[slot, here] = (
-                parts[slot, here].astype(WIDE) + across_in[i].astype(WIDE)
-            ).astype(LOW)
-            stores[i].start()
+        across.wait_recv()
+        parts[2] = (parts[2].astype(WIDE) + across_in[...].astype(WIDE)).astype(LOW)
+        stores[1].start()
         keep.wait()
         for copy in stores:
             copy.wait()
-        for copy in (to_far, to_near, to_cross, *cores, *across):
+        for copy in (to_far, to_near, to_cross, *cores, across):
             copy.wait_send()
 
 
@@ -611,10 +604,10 @@
             pltpu.VMEM((length, width), LOW),
             pltpu.VMEM((slots, length, width), LOW),
             pltpu.VMEM((4, length, width), LOW),
-            pltpu.VMEM((2, length // 2, width), LOW),
+            pltpu.VMEM((length, width), LOW),
             pltpu.VMEM((tokens, cols), LOW),
-            pltpu.SemaphoreType.DMA((9,)),
-            pltpu.SemaphoreType.DMA((9,)),
+            pltpu.SemaphoreType.DMA((8,)),
+            pltpu.SemaphoreType.DMA((8,)),
             pltpu.SemaphoreType.DMA((5,)),
         ],
         compiler_params=pltpu.CompilerParams(
@@ -625,8 +618,8 @@
 
 
 def line_kernel(
-    slots, tiles, line, weight, own_in, grad_middle, gain, rows_one, line_all, block, share,
-    gain_grad, attn_out, bias_out, home, parts, core_in, far_in, total, send, recv, load
+    slots, tiles, line, weight, own_in, grad_middle, gain, gain_two, rows_one, line_all, block, share,
+    gain_grad, attn_out, bias_out, home, parts, core_in, far_in, total, gains, gains_in, send, recv, load
 ):
     step = pl.program_id(0)
     core, far, _ = partners_of()
@@ -640,23 +633,27 @@
     to_far = remote(parts.at[2], far_in, 2, far)
     leave = remote(block, home, 3, target)
     keep = pltpu.make_async_copy(block, home, load)
+    cross = {"tp": tensor_rank ^ 3}
+    gain_copies = [
+        remote(gains, gains_in.at[i], 4 + i, partner) for i, partner in enumerate((core, far, cross))
+    ]
 
     @pl.when(step == 0)
     def _():
         barrier = pltpu.get_barrier_semaphore()
-        for partner in (core, far):
+        for partner in (core, far, cross):
             pl.semaphore_signal(barrier, inc=1, device_id=partner, device_id_type=MESH_ID)
 
         @pl.when(stays)
         def _():
-            pl.semaphore_wait(barrier, 2)
+            pl.semaphore_wait(barrier, 3)
             keep.start()
 
         @pl.when(jnp.logical_not(stays))
         def _():
             for partner in (target, source):
                 pl.semaphore_signal(barrier, inc=1, device_id=partner, device_id_type=MESH_ID)
-            pl.semaphore_wait(barrier, 4)
+            pl.semaphore_wait(barrier, 5)
             leave.start()
 
     @pl.when(step < slots)
@@ -692,9 +689,16 @@
         upstream = total[...] + core_in[1].astype(WIDE) + far_in[...].astype(WIDE)
         values = own_in[...].astype(WIDE)
         inverse = lax.rsqrt(jnp.mean(values * values, axis=-1, keepdims=True) + EPS)
-        grad_in, gain_grad[...] = norm_backward(values, inverse, gain[...], upstream)
+        grad_in, gain_one = norm_backward(values, inverse, gain[...], upstream)
+        gains[0:1] = gain_one
+        gains[1:2] = gain_two[...]
+        for copy in gain_copies:
+            copy.start()
         share[...] = (grad_middle[...] + grad_in).astype(LOW)
-        for copy in (*cores, to_far):
+        for copy in gain_copies:
+            copy.wait_recv()
+        gain_grad[...] = (gains[...] + gains_in[0]) + (gains_in[1] + gains_in[2])
+        for copy in (*cores, to_far, *gain_copies):
             copy.wait_send()
         pl.when(stays)(keep.wait)
 
@@ -704,7 +708,7 @@
             leave.wait_send()
 
 
-def finish_rows(line, weight, own_in, grad_middle, gain, rows_one, block):
+def finish_rows(line, weight, own_in, grad_middle, gain, gain_two, rows_one, block):
     length, width = own_in.shape
     near_tokens, line_cols = line.shape
     slots, tile = near_tokens // length, 256
@@ -722,20 +726,21 @@
             once,
             once,
             whole_spec(1, width),
+            whole_spec(1, width),
             by_column(near_tokens),
             whole_spec(near_tokens, line_cols, once=True),
             ANYWHERE,
         ],
         out_specs=[
             whole_spec(length, width),
-            whole_spec(1, width),
+            whole_spec(2, width),
             pl.BlockSpec((tile, attn_cols), lambda i: (column(i), 0)),
             whole_spec(1, line_cols),
             ANYWHERE,
         ],
         out_shape=[
             jax.ShapeDtypeStruct((length, width), LOW),
-            jax.ShapeDtypeStruct((1, width), WIDE),
+            jax.ShapeDtypeStruct((2, width), WIDE),
             jax.ShapeDtypeStruct((width, attn_cols), LOW),
             jax.ShapeDtypeStruct((1, line_cols), WIDE),
             jax.ShapeDtypeStruct((length, width), LOW),
@@ -745,15 +750,17 @@
             pltpu.VMEM((2, length, width), LOW),
             pltpu.VMEM((length, width), LOW),
             pltpu.VMEM((length, width), WIDE),
-            pltpu.SemaphoreType.DMA((4,)),
-            pltpu.SemaphoreType.DMA((4,)),
+            pltpu.VMEM((2, width), WIDE),
+            pltpu.VMEM((3, 2, width), WIDE),
+            pltpu.SemaphoreType.DMA((7,)),
+            pltpu.SemaphoreType.DMA((7,)),
             pltpu.SemaphoreType.DMA,
         ],
         compiler_params=pltpu.CompilerParams(
             vmem_limit_bytes=63 << 20, collective_id=3, has_side_effects=True
         ),
         cost_estimate=estimate(2 * near_tokens * width * attn_cols, 10 * near_tokens * width),
-    )(line, weight, own_in, grad_middle, gain, rows_one, line, block)
+    )(line, weight, own_in, grad_middle, gain, gain_two, rows_one, line, block)
 
 
 def place_kernel(count, info, *refs):
@@ -1343,7 +1350,7 @@
 
         leaving_units, own_units = in_parts(1 - ctx_rank), in_parts(ctx_rank)
         slot_pick = lax.dynamic_index_in_dim(cotangent, tensor_rank, 0, keepdims=False)
-        small = after(small, outgoing, cosine, sine, info, pick_info, leaving_units, own_units, slot_pick)
+        small = after(small, outgoing, leaving_units)
         small_both = in_order(small, from_partner(small, "ctx", 1))
         arriving_units = from_partner(after(leaving_units, small_both), "ctx", 1)
         other_own = from_partner(after(slot_pick, arriving_units), "ctx", 1)
@@ -1356,7 +1363,8 @@
         small_both, unit_both, half_units = small, jnp.concatenate(shards, axis=1), units_pad
     far_in = from_partner(own_in, "tp", 2)
     near_in = from_partner(own_in, "tp", 1)
-    cross_in = from_partner(far_in, "tp", 1)
+    ready = (cosine, sine, info, pick_info, own_units, slot_pick) if split else (cosine, sine, info)
+    cross_in = from_partner(after(far_in, *ready), "tp", 1)
     grad_slots = [lax.dynamic_index_in_dim(cotangent, s, 0, keepdims=False) for s in slot_now]
 
     near_full = all_rows(small_both, own_in)
@@ -1548,14 +1556,28 @@
         project_full, query_cols + parity * head_dim, head_dim, axis=1
     )
     back_full = jnp.concatenate([project_full[:, :query_cols], own_weight], axis=1)
+    def scatter_units(grad):
+        if not split:
+            return scatter_sum(grad, ctx_rank, LOW)
+        return lax.psum_scatter(grad, "fsdp", scatter_dimension=0, tiled=True)
+
+    unit_grads = (grad_a, down_b, up_grad_b, gate_grad_b) if split else (down_grad, gate_grad, up_grad)
+    unit_sums = [scatter_units(unit_grads[0])]
+    if split:
+        unit_sums += [scatter_units(after(g, unit_sums[0])) for g in unit_grads[1:3]]
+        unit_sums += [scatter_units(after(unit_grads[3], unit_sums[0]))]
+    else:
+        unit_sums += [scatter_units(g) for g in unit_grads[1:]]
+
     normed_flat = normed_one.reshape(token_count, model_width)
     if split:
-        input_share, gain_one, attn_grad, bias_grad, block_home = finish_rows(
+        input_share, gain_grad, attn_grad, bias_grad, block_home = finish_rows(
             line_grad,
-            back_full,
+            after(back_full, *unit_sums),
             own_in,
             grad_middle,
             gains_now[0:1],
+            gain_two,
             normed_flat,
             block_share,
         )
@@ -1579,69 +1601,56 @@
         )
         bias_grad = jnp.sum(line_grad.astype(WIDE), axis=0)
 
-    def scatter_units(grad):
-        if not split:
-            return scatter_sum(grad, ctx_rank, LOW)
-        return lax.psum_scatter(grad, "fsdp", scatter_dimension=0, tiled=True)
-
-    unit_grads = (grad_a, down_b, up_grad_b, gate_grad_b) if split else (down_grad, gate_grad, up_grad)
-    unit_sums = [scatter_units(unit_grads[0])]
+    shard_count = fsdp_count * ctx_count
+    share = head_dim // shard_count
+    if not split:
+        gain_grad = jnp.concatenate([gain_one, gain_two], axis=0)
+        gain_grad = gain_grad + from_partner(gain_grad, "tp", 1)
+        gain_grad = gain_grad + from_partner(gain_grad, "tp", 2)
+    bias_cols = jnp.transpose(bias_grad.reshape(heads + 1, shard_count, share), (1, 2, 0))
+    bias_cols = jnp.pad(bias_cols, ((0, 0), (0, (model_width - head_dim) // shard_count), (0, 0)))
+    tiny = jnp.concatenate([gain_grad.T, bias_cols.reshape(model_width, heads + 1)], axis=1)
+    tiny = jnp.pad(tiny, ((0, 0), (0, 128 - tiny.shape[1]))).astype(LOW)
+    attn_grad = jnp.concatenate([attn_grad, tiny], axis=1)
     if split:
-        unit_sums += [scatter_units(after(g, unit_sums[0])) for g in unit_grads[1:3]]
-        unit_sums += [scatter_units(after(unit_grads[3], *unit_sums))]
+        attn_blocks = attn_grad.reshape(fsdp_count, ctx_count, -1, attn_grad.shape[1])
+        kept, sent = scatter_ctx(attn_blocks, ctx_rank)
+        attn_held = (kept.astype(WIDE) + from_partner(sent, "ctx", 1).astype(WIDE)).astype(LOW)
+        attn_held = attn_held.reshape(-1, attn_grad.shape[1])
+        attn_end = lax.psum_scatter(after(attn_held, *unit_sums), "fsdp", scatter_dimension=0, tiled=True)
     else:
-        unit_sums += [scatter_units(g) for g in unit_grads[1:]]
-
-    attn_end = scatter_sum(attn_grad, ctx_rank, LOW, *unit_sums)
+        attn_end = scatter_sum(attn_grad, ctx_rank, LOW, *unit_sums)
 
     home_order = jnp.stack(home_now).astype(jnp.int32)
 
     def leave(share):
         return lax.ppermute(share, ("fsdp", "tp"), back)
 
-    def arrive(own):
+    def arrive(own, order):
         far = from_partner(own, "tp", 2)
         near = from_partner(own, "tp", 1)
-        return place_rows((own, near, far, from_partner(far, "tp", 1)), home_order)
+        return place_rows((own, near, far, from_partner(far, "tp", 1)), order)
 
     input_home = leave(input_share)
     if not split:
         block_home = leave(block_share)
-    block_out = arrive(block_home)
-    input_grad = arrive(input_home)
-
-    gain_grad = jnp.concatenate([gain_one, gain_two], axis=0).T
-    gain_grad = gain_grad + from_partner(gain_grad, "tp", 1)
-    gain_grad = gain_grad + from_partner(gain_grad, "tp", 2)
-    shard_count = fsdp_count * ctx_count
-    share = head_dim // shard_count
-    bias_cols = jnp.transpose(bias_grad.reshape(heads + 1, shard_count, share), (1, 2, 0))
-    bias_cols = jnp.pad(bias_cols, ((0, 0), (0, (model_width - head_dim) // shard_count), (0, 0)))
-    tiny = jnp.concatenate([gain_grad, bias_cols.reshape(model_width, heads + 1)], axis=1)
-    tiny = jnp.pad(tiny, ((0, 0), (0, 8 - tiny.shape[1])))
-    tiny = tiny.reshape(fsdp_count, ctx_count, model_width // shard_count, 8)
-    if split:
-        kept, sent = scatter_ctx(tiny, ctx_rank)
-        tiny = kept + from_partner(sent, "ctx", 1)
-    else:
-        tiny = lax.psum_scatter(tiny, "ctx", scatter_dimension=1, tiled=True)
-    tiny = tiny.reshape(fsdp_count, -1, 8)
-    pick = lambda shift: lax.dynamic_index_in_dim(
-        tiny, lax.rem(group_rank + shift, fsdp_count), 0, keepdims=False
-    )
-    tiny_grad = pick(0)
-    for shift in range(1, fsdp_count):
-        pairs = [(f, (f + shift) % fsdp_count) for f in range(fsdp_count)]
-        tiny_grad = tiny_grad + lax.ppermute(pick(shift), "fsdp", pairs)
-
+    block_out = arrive(block_home, home_order)
     if split:
 
         def unit_end(total, *earlier):
             kept, sent = scatter_ctx(total.reshape(1, ctx_count, -1, total.shape[1]), ctx_rank)
             return kept[0], from_partner(after(sent[0], *earlier), "ctx", 1)
 
-        own_a, got_a = unit_end(unit_sums[0], line_grad)
+        own_a, got_a = unit_end(unit_sums[0], grad_branch)
         ends = [unit_end(t, line_grad) for t in unit_sums[1:]]
+        input_home = after(input_home, attn_held)
+        home_order = after(home_order, got_a, *[end[1] for end in ends])
+    input_grad = arrive(input_home, home_order)
+
+    small_at = query_cols + head_dim + query_cols
+    tiny_grad = attn_end[:, small_at:].astype(WIDE)
+
+    if split:
 
         def joined(part, end):
             cols = slice(part * first_units, (part + 1) * first_units)
@@ -1658,7 +1667,7 @@
         input_grad,
         attn_end[:, :query_cols].astype(WIDE),
         attn_end[:, query_cols : query_cols + head_dim].astype(WIDE),
-        attn_end[:, query_cols + head_dim :].astype(WIDE).T,
+        attn_end[:, query_cols + head_dim : small_at].astype(WIDE).T,
         tiny_grad[:, :2].T,
         tiny_grad[:share, 2 : 2 + heads].T,
         tiny_grad[:share, 2 + heads : 3 + heads].T,

time: 892 us -> 805 us (0.902)
  waiting for transfers between devices: 285 us -> 203 us
  Pallas kernels: 414 us -> 404 us
    ppermute x1, waiting for transfers between devices: 62.1 us -> 0.01 us  [leave(): return lax.ppermute(share, ('fsdp', 'tp'), back)]
    ppermute x35 -> x32, waiting for transfers between devices: 210 us -> 170 us  [from_partner(): return lax.ppermute(value, axis, pairs)]
    ppermute x1, waiting for transfers between devices: 0.01 us -> 17.4 us  [local(): own_in = lax.ppermute(outgoing, ('fsdp', 'tp'), there)]
    pallas_call x1, Pallas kernels: 65.6 us -> 55.1 us  [spread_branch(): pl.pallas_call(functools.partial(branch_kernel, slots, tiles), grid=(slot...]
    ppermute x35 -> x32, starting transfers between devices: 41 us -> 44.6 us  [from_partner(): return lax.ppermute(value, axis, pairs)]
  transfers between devices with their start and end apart: 50 -> 44, of which waited for: 22 -> 20; matrix products, arithmetic and copies ran while one was open for 8% -> 9% of each run, Pallas kernels for 47% -> 43%
where the time goes in v7:
time: 805 us; the launch traced here: 794 us
  Pallas kernels  404 us (50%)
  waiting for transfers between devices  203 us (25%)
  starting transfers between devices  59.1 us (7%)
  local copies, waits for them, and re-layouts  45.5 us (6%)
  other arithmetic  42 us (5%)
  between operations  34.7 us (4%)
    ppermute x32, waiting for transfers between devices, from_partner(): return lax.ppermute(value, axis, pairs)  170 us
    pallas_call x1, Pallas kernels, collect_back(): pl.pallas_call(functools.partial(collect_kernel, slots, tiles), grid=(slo...  71.2 us
    pallas_call x1, Pallas kernels, spread_branch(): pl.pallas_call(functools.partial(branch_kernel, slots, tiles), grid=(slot...  55.1 us
    pallas_call x1, Pallas kernels, attend_exchange(): pl.pallas_call(functools.partial(exchange_kernel, heads, head_dim, scale,...  55.1 us
    pallas_call x1, Pallas kernels, finish_rows(): pl.pallas_call(functools.partial(line_kernel, slots, tiles), grid=(slots...  52.9 us
    ppermute x32, starting transfers between devices, from_partner(): return lax.ppermute(value, axis, pairs)  44.6 us
    pallas_call x1, Pallas kernels, full_units(): pl.pallas_call(full_units_kernel, grid=(tokens // step,), in_specs=[by_ro...  36.6 us
    pallas_call x1, Pallas kernels, first_grads(): pl.pallas_call(first_grads_kernel, grid=(3, tiles), in_specs=[pl.BlockSpe...  33.5 us
  transfers between devices with their start and end apart: 44, of which 20 were waited for; matrix products, arithmetic and copies ran while one was open for 9% of the time, Pallas kernels for 43%

profile of v7, /device:TPU:1, one launch (start us, length us, event | category | flops | bytes accessed | tf_op | source)
XLA Modules:
  0.0 794.4 jit_solution(15552132215925390787)
XLA Ops:
  29.9 9.1 %collective-permute-done.4 = bf16[192,1152]{1,0:T(8,128)(2,1)S(1)} collective-permute-done((bf16[192,1152]{1,0:T(8,128)(2,1)S(1)}, bf16[192,1152]{1,0:T(8,128)(2,1)S(1)}, u32[]{:S(2)}, u32[]{:S(2)}) %collective-permute-start.4) | collective-permute-done | bytes 442400 | tf_op jit(solution)/shard_map/ppermute | solution.py:21
  40.1 17.4 %collective-permute-done.x0.own_in = bf16[512,1536]{1,0:T(8,128)(2,1)S(1)} collective-permute-done((bf16[512,1536]{1,0:T(8,128)(2,1)}, bf16[512,1536]{1,0:T(8,128)(2,1)S(1)}, u32[]{:S(2)}, u32[]{:S(2)}) %collective-permute-start) | collective-permute-done | bytes 1572896 | tf_op jit(solution)/shard_map/ppermute | solution.py:1304
  95.7 15.3 %collective-permute-done.5 = bf16[192,3456]{1,0:T(8,128)(2,1)S(1)} collective-permute-done((bf16[192,3456]{1,0:T(8,128)(2,1)}, bf16[192,3456]{1,0:T(8,128)(2,1)S(1)}, u32[]{:S(2)}, u32[]{:S(2)}) %collective-permute-start.5) | collective-permute-done | bytes 1327136 | tf_op jit(solution)/shard_map/ppermute | solution.py:21
  118.9 27.7 %collective-permute-done.6.refs_0_ = bf16[512,1536]{1,0:T(8,128)(2,1)} collective-permute-done((bf16[512,1536]{1,0:T(8,128)(2,1)}, bf16[512,1536]{1,0:T(8,128)(2,1)}, u32[]{:S(2)}, u32[]{:S(2)}) %collective-permute-start.6) | collective-permute-done | bytes 1572896 | tf_op jit(solution)/shard_map/ppermute | solution.py:21
  152.4 12.5 %shard_map.230 = (bf16[4,512,1536]{2,1,0:T(8,128)(2,1)}, bf16[4,512,384]{2,1,0:T(8,128)(2,1)}, bf16[4,512,128]{2,1,0:T(8,128)(2,1)}, bf16[4,512,128]{2,1,0:T(8,128)(2,1)}) custom-call(bf16[512,1536]{1,0:T(8,128)(2,1)} %copy-done.7, bf16[512,1536]{1,0:T(8,128)(2,1)} %copy-done.15, bf16[512,1536]{1,0:T(8,128)(2,1)} %copy-done.14, ...), custom_call_target="tpu_custom_call" | custom-call | flops 4026531840 | bytes 17170432 | tf_op jit(solution)/shard_map/pallas_call | solution.py:836
  171.5 8.0 %collective-permute-done.8.refs_2_ = bf16[512,1536]{1,0:T(8,128)(2,1)} collective-permute-done((bf16[512,1536]{1,0:T(8,128)(2,1)}, bf16[512,1536]{1,0:T(8,128)(2,1)}, u32[]{:S(2)}, u32[]{:S(2)}) %collective-permute-start.8) | collective-permute-done | bytes 1572896 | tf_op jit(solution)/shard_map/ppermute | solution.py:21
  179.5 7.8 collective-permute-done.9.v_past
  188.1 13.6 %shard_map.231 = (bf16[2,512,384]{2,1,0:T(8,128)(2,1)}, f32[2,512,128]{2,1,0:T(8,128)}, bf16[512,1536]{1,0:T(8,128)(2,1)}, bf16[512,1536]{1,0:T(8,128)(2,1)}) custom-call(s32[6]{0:T(128)} %concatenate.78.info, bf16[4,512,384]{2,1,0:T(8,128)(2,1)} %get-tuple-element.84.q, bf16[4,512,128]{2,1,0:T(8,128)(2,1)} %copy-done.23, bf16[4,512,128]{2,1,0:T(8,128)(2,1)} %copy-done.24, ...), custom_call_target="tpu_custom_call" | custom-call | flops 1610612736 | bytes 1572864 | tf_op jit(solution)/shard_map/pallas_call | solution.py:924
  212.6 13.6 %shard_map.232 = (bf16[2,512,384]{2,1,0:T(8,128)(2,1)}, f32[2,512,128]{2,1,0:T(8,128)}, bf16[512,1536]{1,0:T(8,128)(2,1)}, bf16[512,1536]{1,0:T(8,128)(2,1)}) custom-call(s32[6]{0:T(128)} %concatenate.78.info, bf16[4,512,384]{2,1,0:T(8,128)(2,1)} %get-tuple-element.84.q, bf16[4,512,128]{2,1,0:T(8,128)(2,1)} %copy-done.23, bf16[4,512,128]{2,1,0:T(8,128)(2,1)} %copy-done.24, ...), custom_call_target="tpu_custom_call" | custom-call | flops 1610612736 | bytes 1572864 | tf_op jit(solution)/shard_map/pallas_call | solution.py:924
  229.7 18.8 %collective-permute-done.12 = bf16[512,1536]{1,0:T(8,128)(2,1)} collective-permute-done((bf16[512,1536]{1,0:T(8,128)(2,1)}, bf16[512,1536]{1,0:T(8,128)(2,1)}, u32[]{:S(2)}, u32[]{:S(2)}) %collective-permute-start.12) | collective-permute-done | bytes 1572896 | tf_op jit(solution)/shard_map/ppermute | solution.py:21
  257.4 15.6 %shard_map.233 = (bf16[4096,512]{1,0:T(8,128)(2,1)}, bf16[4096,1536]{1,0:T(8,128)(2,1)}) custom-call(s32[8]{0:T(128)} %stack.98.info, bf16[4,512,1536]{2,1,0:T(8,128)(2,1)} %cotangent, bf16[512,1536]{1,0:T(8,128)(2,1)} %collective-permute-done.6.refs_0_, bf16[512,1536]{1,0:T(8,128)(2,1)} %collective-permute-done.15.refs_1_, ...), custom_call_target="tpu_custom_call" | custom-call | flops 6442450944 | bytes 30932992 | tf_op jit(solution)/shard_map/pallas_call | solution.py:226
  273.0 16.3 %collective-permute-done.18.refs_4_ = bf16[512,1536]{1,0:T(8,128)(2,1)S(1)} collective-permute-done((bf16[512,1536]{1,0:T(8,128)(2,1)S(1)}, bf16[512,1536]{1,0:T(8,128)(2,1)S(1)}, u32[]{:S(2)}, u32[]{:S(2)}) %collective-permute-start.18) | collective-permute-done | bytes 1572896 | tf_op jit(solution)/shard_map/ppermute | solution.py:21
  294.5 12.5 %collective-permute-done.21.refs_7_ = bf16[256,1536]{1,0:T(8,128)(2,1)S(1)} collective-permute-done((bf16[256,1536]{1,0:T(8,128)(2,1)S(1)}, bf16[256,1536]{1,0:T(8,128)(2,1)S(1)}, u32[]{:S(2)}, u32[]{:S(2)}) %collective-permute-start.21) | collective-permute-done | bytes 786464 | tf_op jit(solution)/shard_map/ppermute | solution.py:21
  314.4 15.6 %shard_map.234 = (bf16[4096,512]{1,0:T(8,128)(2,1)}, bf16[4096,1536]{1,0:T(8,128)(2,1)}) custom-call(bf16[512,1536]{1,0:T(8,128)(2,1)} %copy-done.16, bf16[512,1536]{1,0:T(8,128)(2,1)} %collective-permute-done.13.refs_1_, bf16[512,1536]{1,0:T(8,128)(2,1)} %collective-permute-done.14.refs_2_, bf16[512,1536]{1,0:T(8,128)(2,1)} %collective-permute-done.17.refs_3_, ...), custom_call_target="tpu_custom_call" | custom-call | flops 6442450944 | bytes 30932992 | tf_op jit(solution)/shard_map/pallas_call | solution.py:121
  330.0 17.8 %shard_map.235 = (bf16[4096,512]{1,0:T(8,128)(2,1)}, bf16[4096,512]{1,0:T(8,128)(2,1)}, bf16[4096,512]{1,0:T(8,128)(2,1)}) custom-call(bf16[4096,1536]{1,0:T(8,128)(2,1)} %get-tuple-element.106.h.right.turned, bf16[1536,1536]{1,0:T(8,128)(2,1)} %bitcast.141, bf16[4096,512]{1,0:T(8,128)(2,1)} %get-tuple-element.101.gate, bf16[4096,512]{1,0:T(8,128)(2,1)} %get-tuple-element.97.grad), custom_call_target="tpu_custom_call" | custom-call | flops 6442450944 | bytes 35127296 | tf_op jit(solution)/shard_map/pallas_call | solution.py:157
  347.7 33.5 %shard_map.236 = bf16[1536,1536]{1,0:T(8,128)(2,1)} custom-call(bf16[4096,1536]{1,0:T(8,128)(2,1)} %get-tuple-element.104.g.left, bf16[4096,1536]{1,0:T(8,128)(2,1)} %get-tuple-element.106.h.right.turned, bf16[4096,512]{1,0:T(8,128)(2,1)} %get-tuple-element.105.hid.hid_a, bf16[4096,512]{1,0:T(8,128)(2,1)} %get-tuple-element.102.gate.gate_a, ...), custom_call_target="tpu_custom_call" | custom-call | flops 19327352832 | bytes 17301504 | tf_op jit(solution)/shard_map/pallas_call | solution.py:294
  381.7 36.6 %shard_map.237 = (bf16[4096,640]{1,0:T(8,128)(2,1)}, bf16[4096,640]{1,0:T(8,128)(2,1)}, bf16[4096,640]{1,0:T(8,128)(2,1)}) custom-call(bf16[4096,1536]{1,0:T(8,128)(2,1)} %get-tuple-element.106.h.right.turned, bf16[4096,1536]{1,0:T(8,128)(2,1)} %get-tuple-element.104.g.left, bf16[1536,1920]{1,0:T(8,128)(2,1)} %bitcast.160, bf16[1536,1920]{1,0:T(8,128)(2,1)} %bitcast.161, ...), custom_call_target="tpu_custom_call" | custom-call | flops 24159191040 | bytes 46792704 | tf_op jit(solution)/shard_map/pallas_call | solution.py:268
  418.4 71.2 %shard_map.238 = (f32[512,1536]{1,0:T(8,128)}, bf16[1536,640]{1,0:T(8,128)(2,1)}, bf16[1536,640]{1,0:T(8,128)(2,1)}) custom-call(bf16[4096,512]{1,0:T(8,128)(2,1)} %get-tuple-element.102.gate.gate_a, bf16[4096,512]{1,0:T(8,128)(2,1)} %get-tuple-element.103.up.up_a, bf16[4096,640]{1,0:T(8,128)(2,1)} %get-tuple-element.108.gate_b.gate, ...), custom_call_target="tpu_custom_call" | custom-call | flops 24159191040 | bytes 26214400 | tf_op jit(solution)/shard_map/pallas_call | solution.py:435
  490.5 55.1 %shard_map.239 = (f32[512,1536]{1,0:T(8,128)}, f32[1,1536]{1,0:T(1,128)}, bf16[1536,640]{1,0:T(8,128)(2,1)}, bf16[4,512,1536]{2,1,0:T(8,128)(2,1)}, bf16[512,153...) custom-call(f32[512,1536]{1,0:T(8,128)} %get-tuple-element.111.total, f32[512,1536]{1,0:T(8,128)} %copy-done.6, ...), custom_call_target="tpu_custom_call" | custom-call | flops 16106127360 | bytes 26214400 | tf_op jit(solution)/shard_map/pallas_call | solution.py:573
  558.3 55.1 %shard_map.240 = (bf16[4,512,512]{2,1,0:T(8,128)(2,1)}, bf16[1536,384]{1,0:T(8,128)(2,1)}, bf16[512,1536]{1,0:T(8,128)(2,1)}) custom-call(s32[6]{0:T(128)} %concatenate.78.info, bf16[4,512,384]{2,1,0:T(8,128)(2,1)} %get-tuple-element.84.q, bf16[4,512,128]{2,1,0:T(8,128)(2,1)} %copy-done.23, bf16[4,512,128]{2,1,0:T(8,128)(2,1)} %copy-done.24, ...), custom_call_target="tpu_custom_call" | custom-call | flops 2415919104 | bytes 7864320 | tf_op jit(solution)/shard_map/pallas_call | solution.py:1191
  613.4 7.4 reduce-scatter.12.cloned.1.call-done
  620.9 52.9 %shard_map.241 = (bf16[512,1536]{1,0:T(8,128)(2,1)}, f32[2,1536]{1,0:T(2,128)}, bf16[1536,512]{1,0:T(8,128)(2,1)}, f32[1,512]{1,0:T(1,128)}, bf16[512,1536]{1,0:T(8,128)(2,1)}) custom-call(bf16[2048,512]{1,0:T(8,128)(2,1)} %bitcast.130, bf16[1536,512]{1,0:T(8,128)(2,1)} %pad_maximum_fusion.1.weight, bf16[512,1536]{1,0:T(8,128)(2,1)} %copy-done.7, ...), custom_call_target="tpu_custom_call" | custom-call | flops 3221225472 | bytes 31457280 | tf_op jit(solution)/shard_map/pallas_call | solution.py:720
  687.1 25.2 %collective-permute-done.32 = bf16[4,192,1024]{2,1,0:T(8,128)(2,1)} collective-permute-done((bf16[4,192,1024]{2,1,0:T(8,128)(2,1)}, bf16[4,192,1024]{2,1,0:T(8,128)(2,1)}, u32[]{:S(2)}, u32[]{:S(2)}) %collective-permute-start.32) | collective-permute-done | bytes 1572896 | tf_op jit(solution)/shard_map/ppermute | solution.py:21
  753.5 13.5 %collective-permute-done.34.refs_2_ = bf16[512,1536]{1,0:T(8,128)(2,1)} collective-permute-done((bf16[512,1536]{1,0:T(8,128)(2,1)S(1)}, bf16[512,1536]{1,0:T(8,128)(2,1)}, u32[]{:S(2)}, u32[]{:S(2)}) %collective-permute-start.34) | collective-permute-done | bytes 1572896 | tf_op jit(solution)/shard_map/ppermute | solution.py:21
  (253 shorter events, 187.4 us)
Async XLA Ops:
  7.2 144.1 %all-gather.7.cloned.1.call-start = ((), (), s32[]{:S(2)}) async-start(), calls=%async_computation.10 | async-start | bytes 4423680 | tf_op jit(solution)/shard_map/all_gather | solution.py:1339
  17.5 39.9 %collective-permute-start = (bf16[512,1536]{1,0:T(8,128)(2,1)}, bf16[512,1536]{1,0:T(8,128)(2,1)S(1)}, u32[]{:S(2)}, u32[]{:S(2)}) collective-permute-start(bf16[512,1536]{1,0:T(8,128)(2,1)} %dynamic-slice_bitcast_fusion.3), channel_id=1, source_target_pairs={{0,0},{1,17},{2,10},{3,27},{8,8},{9,25},{10,18},{11,3},{16,16},{17... | collective-permute-start | bytes 4718600 | tf_op jit(solution)/shard_map/ppermute | solution.py:1304
  57.4 200.0 %all-gather.9.cloned.1.call-start = ((), (), s32[]{:S(2)}) async-start(), calls=%async_computation.11 | async-start | bytes 5898240 | tf_op jit(solution)/shard_map/all_gather | solution.py:1339
  57.5 35.5 %collective-permute-start.2 = (bf16[512,1536]{1,0:T(8,128)(2,1)S(1)}, bf16[512,1536]{1,0:T(8,128)(2,1)S(1)}, u32[]{:S(2)}, u32[]{:S(2)}) collective-permute-start(bf16[512,1536]{1,0:T(8,128)(2,1)S(1)} %collective-permute-done.x0.own_in), channel_id=1, source_target_pairs={{0,2},{1,3},{2,0},{3,1},{4,6},{5,7},{6,4},{7,5},{8,10},{9,11},{10,... | collective-permute-start | bytes 4718600 | tf_op jit(solution)/shard_map/ppermute | solution.py:21
  113.5 268.3 %all-gather.11.cloned.1.call-start = ((), (), s32[]{:S(2)}) async-start(), calls=%async_computation.12 | async-start | bytes 7372800 | tf_op jit(solution)/shard_map/all_gather | solution.py:1339
  113.5 33.1 %collective-permute-start.6 = (bf16[512,1536]{1,0:T(8,128)(2,1)}, bf16[512,1536]{1,0:T(8,128)(2,1)}, u32[]{:S(2)}, u32[]{:S(2)}) collective-permute-start(bf16[512,1536]{1,0:T(8,128)(2,1)} %get-tuple-element.82), channel_id=1, source_target_pairs={{0,4},{4,0},{1,5},{5,1},{2,6},{6,2},{3,7},{7,3},{8,12},{12,8},{9,1... | collective-permute-start | bytes 4718600 | tf_op jit(solution)/shard_map/ppermute | solution.py:21
  114.8 36.5 %collective-permute-start.1 = (bf16[512,1536]{1,0:T(8,128)(2,1)S(1)}, bf16[512,1536]{1,0:T(8,128)(2,1)S(1)}, u32[]{:S(2)}, u32[]{:S(2)}) collective-permute-start(bf16[512,1536]{1,0:T(8,128)(2,1)S(1)} %collective-permute-done.x0.own_in), channel_id=1, source_target_pairs={{0,1},{1,0},{2,3},{3,2},{4,5},{5,4},{6,7},{7,6},{8,9},{9,8},{10,11... | collective-permute-start | bytes 4718600 | tf_op jit(solution)/shard_map/ppermute | solution.py:21
  146.6 32.9 %collective-permute-start.8 = (bf16[512,1536]{1,0:T(8,128)(2,1)}, bf16[512,1536]{1,0:T(8,128)(2,1)}, u32[]{:S(2)}, u32[]{:S(2)}) collective-permute-start(bf16[512,1536]{1,0:T(8,128)(2,1)} %collective-permute-done.6.refs_0_), channel_id=1, source_target_pairs={{0,2},{1,3},{2,0},{3,1},{4,6},{5,7},{6,4},{7,5},{8,10},{9,11},{10,... | collective-permute-start | bytes 4718600 | tf_op jit(solution)/shard_map/ppermute | solution.py:21
  212.6 35.9 %collective-permute-start.12 = (bf16[512,1536]{1,0:T(8,128)(2,1)}, bf16[512,1536]{1,0:T(8,128)(2,1)}, u32[]{:S(2)}, u32[]{:S(2)}) collective-permute-start(bf16[512,1536]{1,0:T(8,128)(2,1)} %add_convert_fusion), channel_id=1, source_target_pairs={{0,2},{1,3},{2,0},{3,1},{4,6},{5,7},{6,4},{7,5},{8,10},{9,11},{10,... | collective-permute-start | bytes 4718600 | tf_op jit(solution)/shard_map/ppermute | solution.py:21
  227.0 262.7 %reduce-scatter.6.cloned.1.call-start = ((), (), s32[]{:S(2)}) async-start(), calls=%async_computation.5 | async-start | bytes 5898240 | tf_op jit(solution)/shard_map/reduce_scatter | solution.py:1562
  253.5 35.7 %collective-permute-start.18 = (bf16[512,1536]{1,0:T(8,128)(2,1)S(1)}, bf16[512,1536]{1,0:T(8,128)(2,1)S(1)}, u32[]{:S(2)}, u32[]{:S(2)}) collective-permute-start(bf16[512,1536]{1,0:T(8,128)(2,1)S(1)} %multiply_convert_fusion.refs_0_), channel_id=1, source_target_pairs={{0,4},{4,0},{1,5},{5,1},{2,6},{6,2},{3,7},{7,3},{8,12},{12,8},{9,1... | collective-permute-start | bytes 4718600 | tf_op jit(solution)/shard_map/ppermute | solution.py:21
  255.6 34.5 %collective-permute-start.14 = (bf16[512,1536]{1,0:T(8,128)(2,1)S(1)}, bf16[512,1536]{1,0:T(8,128)(2,1)}, u32[]{:S(2)}, u32[]{:S(2)}) collective-permute-start(bf16[512,1536]{1,0:T(8,128)(2,1)S(1)} %multiply_convert_fusion.refs_0_), channel_id=1, source_target_pairs={{0,2},{1,3},{2,0},{3,1},{4,6},{5,7},{6,4},{7,5},{8,10},{9,11},{10,... | collective-permute-start | bytes 4718600 | tf_op jit(solution)/shard_map/ppermute | solution.py:21
  255.7 55.9 %collective-permute-start.13 = (bf16[512,1536]{1,0:T(8,128)(2,1)S(1)}, bf16[512,1536]{1,0:T(8,128)(2,1)}, u32[]{:S(2)}, u32[]{:S(2)}) collective-permute-start(bf16[512,1536]{1,0:T(8,128)(2,1)S(1)} %multiply_convert_fusion.refs_0_), channel_id=1, source_target_pairs={{0,1},{1,0},{2,3},{3,2},{4,5},{5,4},{6,7},{7,6},{8,9},{9,8},{10,11... | collective-permute-start | bytes 4718600 | tf_op jit(solution)/shard_map/ppermute | solution.py:21
  381.3 232.1 %reduce-scatter.10.cloned.1.call-start = ((), (), s32[]{:S(2)}) async-start(), calls=%async_computation.7 | async-start | bytes 2457600 | tf_op jit(solution)/shard_map/reduce_scatter | solution.py:1562
  489.7 123.7 %reduce-scatter.8.cloned.1.call-start = ((), (), s32[]{:S(2)}) async-start(), calls=%async_computation.6 | async-start | bytes 2457600 | tf_op jit(solution)/shard_map/reduce_scatter | solution.py:1562
  490.3 130.6 %reduce-scatter.12.cloned.1.call-start = ((), (), s32[]{:S(2)}) async-start(), calls=%async_computation.8 | async-start | bytes 2457600 | tf_op jit(solution)/shard_map/reduce_scatter | solution.py:1562
  545.6 228.7 %reduce-scatter.14.cloned.1.call-start = ((), (), s32[]{:S(2)}) async-start(), calls=%async_computation.9 | async-start | bytes 1966080 | tf_op jit(solution)/shard_map/reduce_scatter | solution.py:1620
  679.9 32.5 %collective-permute-start.32 = (bf16[4,192,1024]{2,1,0:T(8,128)(2,1)}, bf16[4,192,1024]{2,1,0:T(8,128)(2,1)}, u32[]{:S(2)}, u32[]{:S(2)}) collective-permute-start(bf16[4,192,1024]{2,1,0:T(8,128)(2,1)} %dynamic-slice_bitcast_fusion), channel_id=1, source_target_pairs={{0,4},{4,0},{1,5},{5,1},{2,6},{6,2},{3,7},{7,3},{8,12},{12,8},{9,1... | collective-permute-start | bytes 4718600 | tf_op jit(solution)/shard_map/ppermute | solution.py:21
  681.1 49.8 %collective-permute-start.31 = (bf16[512,1536]{1,0:T(8,128)(2,1)}, bf16[512,1536]{1,0:T(8,128)(2,1)S(1)}, u32[]{:S(2)}, u32[]{:S(2)}) collective-permute-start(bf16[512,1536]{1,0:T(8,128)(2,1)} %get-tuple-element.138), channel_id=1, source_target_pairs={{0,0},{17,1},{10,2},{27,3},{8,8},{25,9},{18,10},{3,11},{16,16},{1,... | collective-permute-start | bytes 4718600 | tf_op jit(solution)/shard_map/ppermute | solution.py:1627
  686.7 38.3 %collective-permute-start.27 = (bf16[192,1536]{1,0:T(8,128)(2,1)}, bf16[192,1536]{1,0:T(8,128)(2,1)}, u32[]{:S(2)}, u32[]{:S(2)}) collective-permute-start(bf16[192,1536]{1,0:T(8,128)(2,1)} %get-tuple-element.133), channel_id=1, source_target_pairs={{0,4},{4,0},{1,5},{5,1},{2,6},{6,2},{3,7},{7,3},{8,12},{12,8},{9,1... | collective-permute-start | bytes 1769480 | tf_op jit(solution)/shard_map/ppermute | solution.py:21
  687.1 53.5 %collective-permute-start.25 = (bf16[512,1536]{1,0:T(8,128)(2,1)S(1)}, bf16[512,1536]{1,0:T(8,128)(2,1)}, u32[]{:S(2)}, u32[]{:S(2)}) collective-permute-start(bf16[512,1536]{1,0:T(8,128)(2,1)S(1)} %copy-done.2), channel_id=1, source_target_pairs={{0,2},{1,3},{2,0},{3,1},{4,6},{5,7},{6,4},{7,5},{8,10},{9,11},{10,... | collective-permute-start | bytes 4718600 | tf_op jit(solution)/shard_map/ppermute | solution.py:21
  726.2 43.2 %collective-permute-start.24 = (bf16[512,1536]{1,0:T(8,128)(2,1)S(1)}, bf16[512,1536]{1,0:T(8,128)(2,1)S(1)}, u32[]{:S(2)}, u32[]{:S(2)}) collective-permute-start(bf16[512,1536]{1,0:T(8,128)(2,1)S(1)} %copy-done.2), channel_id=1, source_target_pairs={{0,1},{1,0},{2,3},{3,2},{4,5},{5,4},{6,7},{7,6},{8,9},{9,8},{10,11... | collective-permute-start | bytes 4718600 | tf_op jit(solution)/shard_map/ppermute | solution.py:21
  730.9 36.1 %collective-permute-start.34 = (bf16[512,1536]{1,0:T(8,128)(2,1)S(1)}, bf16[512,1536]{1,0:T(8,128)(2,1)}, u32[]{:S(2)}, u32[]{:S(2)}) collective-permute-start(bf16[512,1536]{1,0:T(8,128)(2,1)S(1)} %collective-permute-done.31.refs_0_), channel_id=1, source_target_pairs={{0,2},{1,3},{2,0},{3,1},{4,6},{5,7},{6,4},{7,5},{8,10},{9,11},{10,... | collective-permute-start | bytes 4718600 | tf_op jit(solution)/shard_map/ppermute | solution.py:21
  740.6 28.7 %collective-permute-start.26 = (bf16[512,1536]{1,0:T(8,128)(2,1)}, bf16[512,1536]{1,0:T(8,128)(2,1)S(1)}, u32[]{:S(2)}, u32[]{:S(2)}) collective-permute-start(bf16[512,1536]{1,0:T(8,128)(2,1)} %collective-permute-done.25.refs_2_), channel_id=1, source_target_pairs={{0,1},{1,0},{2,3},{3,2},{4,5},{5,4},{6,7},{7,6},{8,9},{9,8},{10,11... | collective-permute-start | bytes 4718600 | tf_op jit(solution)/shard_map/ppermute | solution.py:21
  (64 other events, 828.3 us)
Sparse Core Ops, SparseCore 0:
  57.6 71.4 all-gather.6
  130.7 88.1 all-gather.8
  227.1 112.5 all-gather.10
  381.4 87.1 reduce-scatter.5
  489.8 45.1 reduce-scatter.9
  537.1 40.6 reduce-scatter.7
  580.2 40.6 reduce-scatter.11
  716.2 41.7 reduce-scatter.13

commit v8 on v7

--- a/solution.py
+++ b/solution.py
@@ -882,10 +882,9 @@
     return lax.dot_general(left, right, (((0,), (0,)), ((), ())), preferred_element_type=WIDE)
 
 
-def attend_kernel(
-    heads, head_dim, scale, first, total_slots, info, q, k_past, v_past, k_own, v_own, weight, out, lse, *parts
+def attend_rows(
+    heads, head_dim, scale, length, offset, q, k_past, v_past, k_own, v_own, weight, out, lse, put
 ):
-    length, offset = info[first + pl.program_id(0)], info[total_slots]
     past = k_past.shape[1]
     for start, rows in row_blocks(q.shape[1]):
         keys = start + rows
@@ -908,11 +907,22 @@
             out[0, here, cols] = mixed.astype(LOW)
             lse[0, here, h : h + 1] = top + jnp.log(total)
         rows_out = dot_cols(out[0, here], weight[...]).astype(LOW)
+        put(here, rows_out)
+
+
+def attend_kernel(
+    heads, head_dim, scale, first, total_slots, info, q, k_past, v_past, k_own, v_own, weight, out, lse, *parts
+):
+    length, offset = info[first + pl.program_id(0)], info[total_slots]
+
+    def put(here, value):
         for i, part in enumerate(parts):
 
             @pl.when(pl.program_id(0) == i)
             def _():
-                part[here] = rows_out
+                part[here] = value
+
+    attend_rows(heads, head_dim, scale, length, offset, q, k_past, v_past, k_own, v_own, weight, out, lse, put)
 
 
 def attend_forward(info, q, k_past, v_past, k_own, v_own, weight, heads, head_dim, scale, first, count):
@@ -1078,6 +1088,99 @@
         compiler_params=pltpu.CompilerParams(vmem_limit_bytes=56 << 20),
         cost_estimate=estimate(10 * keys * head_dim, 8 * count * length * width, keys),
     )(info, q, k_past, v_past, k_own, v_own, grad, lse, cosine, sine)
+
+
+def attend_sum_kernel(
+    heads, head_dim, scale, slots, info, q, k_past, v_past, k_own, v_own, weight, own_in, gain, out, lse, middle,
+    normed, parts, core_in, far_in, send, recv
+):
+    step = pl.program_id(0)
+    slot = slots - 1 - step
+    core, far, _ = partners_of()
+    remote = remote_copy(send, recv)
+    cores = [remote(parts.at[3 - 2 * k], core_in.at[k], k, core) for k in range(2)]
+    to_far = remote(parts.at[2], far_in, 2, far)
+
+    @pl.when(step == 0)
+    def _():
+        meet((core, far))
+
+    def put(here, value):
+        parts[slot, here] = value
+
+    offset = lax.axis_index("ctx") * q.shape[1]
+    attend_rows(
+        heads, head_dim, scale, info[slot], offset, q, k_past, v_past, k_own, v_own, weight, out, lse, put
+    )
+    for k in range(2):
+        pl.when(step == 2 * k)(cores[k].start)
+
+    @pl.when(step == 1)
+    def _():
+        cores[0].wait_recv()
+        parts[2] = (parts[2].astype(WIDE) + core_in[0].astype(WIDE)).astype(LOW)
+        to_far.start()
+
+    @pl.when(step == slots - 1)
+    def _():
+        cores[1].wait_recv()
+        to_far.wait_recv()
+        rows = own_in[...].astype(WIDE) + parts[0].astype(WIDE)
+        rows = rows + core_in[1].astype(WIDE) + far_in[...].astype(WIDE)
+        middle[...] = rows
+        inverse = lax.rsqrt(jnp.mean(rows * rows, axis=-1, keepdims=True) + EPS)
+        normed[...] = (rows * inverse * gain[...]).astype(LOW)
+        for copy in (*cores, to_far):
+            copy.wait_send()
+
+
+def attend_sum(info, q, k_past, v_past, k_own, v_own, weight, own_in, gain, heads, head_dim, scale):
+    count, length, width = q.shape
+    past, model_width = k_past.shape[1], own_in.shape[1]
+    by_slot = lambda *shape: pl.BlockSpec(
+        (1, *shape), lambda i, info: (count - 1 - i,) + (0,) * len(shape)
+    )
+    keys = count * length * (past + length) * heads
+    return pl.pallas_call(
+        functools.partial(attend_sum_kernel, heads, head_dim, scale, count),
+        grid_spec=pltpu.PrefetchScalarGridSpec(
+            num_scalar_prefetch=1,
+            grid=(count,),
+            in_specs=[
+                by_slot(length, width),
+                by_slot(past, head_dim),
+                by_slot(past, head_dim),
+                by_slot(length, head_dim),
+                by_slot(length, head_dim),
+                whole_spec(*weight.shape, once=True),
+                whole_spec(length, model_width, once=True),
+                whole_spec(1, model_width),
+            ],
+            out_specs=[
+                by_slot(length, width),
+                by_slot(length, 128),
+                whole_spec(length, model_width, once=True),
+                whole_spec(length, model_width, once=True),
+            ],
+            scratch_shapes=[
+                pltpu.VMEM((count, length, model_width), LOW),
+                pltpu.VMEM((2, length, model_width), LOW),
+                pltpu.VMEM((length, model_width), LOW),
+                pltpu.SemaphoreType.DMA((3,)),
+                pltpu.SemaphoreType.DMA((3,)),
+            ],
+        ),
+        out_shape=[
+            jax.ShapeDtypeStruct((count, length, width), LOW),
+            jax.ShapeDtypeStruct((count, length, 128), WIDE),
+            jax.ShapeDtypeStruct((length, model_width), WIDE),
+            jax.ShapeDtypeStruct((length, model_width), LOW),
+        ],
+        compiler_params=pltpu.CompilerParams(
+            vmem_limit_bytes=56 << 20, collective_id=5, has_side_effects=True
+        ),
+        cost_estimate=estimate(4 * keys * head_dim, 4 * count * length * width, keys),
+    )(info, q, k_past, v_past, k_own, v_own, weight, own_in, gain)
 
 
 def exchange_kernel(
@@ -1269,25 +1372,24 @@
     offset = ctx_rank * local_len
     head_pair = tensor_rank // (tensor_count // keyval_heads)
     parity = tensor_rank % 2
-    shifts = jnp.array(DEAL_SHIFT, jnp.int32)
-
-    table = permutation.reshape(fsdp_count, seq_grp)
-    far_group = lax.rem(group_rank + shifts[tensor_rank], fsdp_count)
-    far_row = lax.dynamic_index_in_dim(table, far_group, 0, keepdims=False)
-    leaving = jnp.sum(jnp.where(far_row // seq_grp == group_rank, far_row - group_rank * seq_grp, 0))
-    own_row = lax.dynamic_index_in_dim(table, group_rank, 0, keepdims=False)
-    slot_now, seq_now, home_now = [], [], []
-    for r in range(seq_grp):
-        shift = shifts[tensor_rank ^ r]
-        source = lax.rem(group_rank - shift + fsdp_count, fsdp_count)
-        hit = own_row // seq_grp == source
-        slot_now.append(jnp.sum(jnp.where(hit, jnp.arange(seq_grp), 0)))
-        seq_now.append(jnp.sum(jnp.where(hit, own_row, 0)))
-        target = lax.rem(group_rank + shift, fsdp_count)
-        target_row = lax.dynamic_index_in_dim(table, target, 0, keepdims=False)
-        home_now.append(
-            jnp.sum(jnp.where(target_row // seq_grp == group_rank, target_row - group_rank * seq_grp, 0))
-        )
+    assert DEAL_SHIFT == tuple((t % 2) * 2 + t // 2 for t in range(tensor_count))
+
+    entry = jnp.arange(permutation.shape[0])
+    entry_group, entry_slot = entry // seq_grp, entry % seq_grp
+    home_group, home_slot = lax.div(permutation, seq_grp), lax.rem(permutation, seq_grp)
+    places = jnp.arange(2 * seq_grp)
+    near_places = places < seq_grp
+    slot_rank = tensor_rank ^ (places % seq_grp)
+    shift_of = lambda rank: lax.rem(rank, 2) * 2 + lax.div(rank, 2)
+    target = lax.rem(group_rank + shift_of(tensor_rank), fsdp_count)
+    leaving = jnp.sum(jnp.where((entry_group == target) & (home_group == group_rank), home_slot, 0))
+    source = lax.rem(group_rank + fsdp_count - shift_of(slot_rank), fsdp_count)
+    hit = (entry_group == group_rank)[None] & (home_group[None] == source[:, None])
+    slot_now = jnp.sum(jnp.where(hit, entry_slot[None], 0), axis=1)
+    seq_now = jnp.sum(jnp.where(hit, permutation[None], 0), axis=1)
+    targets = lax.rem(group_rank + shift_of(slot_rank), fsdp_count)
+    back_hit = (entry_group[None] == targets[:, None]) & (home_group == group_rank)[None]
+    home_order = jnp.sum(jnp.where(back_hit, home_slot[None], 0), axis=1)[:seq_grp]
     there = [
         (f * tensor_count + t, (f + DEAL_SHIFT[t]) % fsdp_count * tensor_count + t)
         for f in range(fsdp_count)
@@ -1311,17 +1413,19 @@
         ],
         axis=1,
     )
-    lengths_now = jnp.stack([seq_lengths[s] for s in seq_now])
-    info = jnp.concatenate([lengths_now, jnp.stack([offset, parity])]).astype(jnp.int32)
-    positions_now = jnp.stack(
-        [lax.dynamic_index_in_dim(positions, s, 0, keepdims=False) for s in seq_now]
+    seq_hit = seq_now[:, None] == entry[None]
+    lengths_now = jnp.sum(jnp.where(seq_hit, seq_lengths[None], 0), axis=1)
+    more = jnp.where(places == seq_grp, offset, jnp.where(places == seq_grp + 1, parity, 0))
+    info = jnp.where(near_places, lengths_now, more).astype(jnp.int32)
+    positions_now = jnp.sum(
+        jnp.where(seq_hit[:seq_grp, :, None], positions[None], 0), axis=1
     )
     lane = jnp.arange(head_dim)
     frequency = 1.0 / ROPE_BASE ** ((lane % (head_dim // 2)).astype(WIDE) * 2.0 / head_dim)
     angles = positions_now.astype(WIDE)[..., None] * frequency
     cosine = jnp.cos(angles)
     sine = jnp.sin(angles) * jnp.where(lane < head_dim // 2, -1.0, 1.0)
-    pick_info = jnp.stack(slot_now + [s ^ tensor_rank for s in slot_now]).astype(jnp.int32)
+    pick_info = jnp.where(near_places, slot_now, slot_now ^ tensor_rank).astype(jnp.int32)
     units = gate_weight.shape[1]
     units_pad = -(-units // 256) * 256
     widen = lambda w: jnp.pad(w, ((0, 0), (0, units_pad - units)))
@@ -1350,7 +1454,7 @@
 
         leaving_units, own_units = in_parts(1 - ctx_rank), in_parts(ctx_rank)
         slot_pick = lax.dynamic_index_in_dim(cotangent, tensor_rank, 0, keepdims=False)
-        small = after(small, outgoing, leaving_units)
+        small = after(small, outgoing, leaving_units, cosine, sine, slot_pick)
         small_both = in_order(small, from_partner(small, "ctx", 1))
         arriving_units = from_partner(after(leaving_units, small_both), "ctx", 1)
         other_own = from_partner(after(slot_pick, arriving_units), "ctx", 1)
@@ -1363,9 +1467,8 @@
         small_both, unit_both, half_units = small, jnp.concatenate(shards, axis=1), units_pad
     far_in = from_partner(own_in, "tp", 2)
     near_in = from_partner(own_in, "tp", 1)
-    ready = (cosine, sine, info, pick_info, own_units, slot_pick) if split else (cosine, sine, info)
+    ready = (info, pick_info, own_units, home_order) if split else (cosine, sine, info)
     cross_in = from_partner(after(far_in, *ready), "tp", 1)
-    grad_slots = [lax.dynamic_index_in_dim(cotangent, s, 0, keepdims=False) for s in slot_now]
 
     near_full = all_rows(small_both, own_in)
     if split:
@@ -1398,24 +1501,42 @@
     else:
         key_past = lax.all_gather(key_own, "ctx", axis=1, tiled=True)
         value_past = lax.all_gather(value_own, "ctx", axis=1, tiled=True)
-    attend = lambda first, *held: attend_forward(
-        info, query_rot, *held, key_own, value_own, output_full, heads, head_dim, scale, first, 2
-    )
     in_share = own_in.astype(WIDE)
-
-    mixed_far, lse_far, *attn_far = attend(2, key_past, value_past)
-    attn_wide = collect_far(attn_far[0], attn_far[1])
-    attn_got = from_partner(attn_wide, "tp", 2)
-    mixed_near, lse_near, *attn_near = attend(0, after(key_past, attn_wide), value_past)
-    attn_core = from_partner(attn_near[1], "tp", 1)
-    middle_share = (
-        in_share
-        + attn_near[0].astype(WIDE)
-        + attn_core.astype(WIDE)
-        + attn_got.astype(WIDE)
-    )
-    inv_two = lax.rsqrt(jnp.mean(middle_share * middle_share, axis=-1, keepdims=True) + EPS)
-    normed_share = (middle_share * inv_two * gains_now[1]).astype(LOW)
+    if split:
+        mixed, lse, middle_share, normed_share = attend_sum(
+            info,
+            query_rot,
+            key_past,
+            value_past,
+            key_own,
+            value_own,
+            output_full,
+            own_in,
+            gains_now[1:2],
+            heads,
+            head_dim,
+            scale,
+        )
+    else:
+        attend = lambda first, *held: attend_forward(
+            info, query_rot, *held, key_own, value_own, output_full, heads, head_dim, scale, first, 2
+        )
+
+        mixed_far, lse_far, *attn_far = attend(2, key_past, value_past)
+        attn_wide = collect_far(attn_far[0], attn_far[1])
+        attn_got = from_partner(attn_wide, "tp", 2)
+        mixed_near, lse_near, *attn_near = attend(0, after(key_past, attn_wide), value_past)
+        attn_core = from_partner(attn_near[1], "tp", 1)
+        middle_share = (
+            in_share
+            + attn_near[0].astype(WIDE)
+            + attn_core.astype(WIDE)
+            + attn_got.astype(WIDE)
+        )
+        inv_two = lax.rsqrt(jnp.mean(middle_share * middle_share, axis=-1, keepdims=True) + EPS)
+        normed_share = (middle_share * inv_two * gains_now[1]).astype(LOW)
+        mixed = jnp.concatenate([mixed_near, mixed_far], axis=0)
+        lse = jnp.concatenate([lse_near, lse_far], axis=0)
     half_len = local_len // 2
 
     if split:
@@ -1428,6 +1549,9 @@
             3,
         )
     else:
+        grad_slots = [
+            lax.dynamic_index_in_dim(cotangent, slot_now[r], 0, keepdims=False) for r in range(seq_grp)
+        ]
         grad_hidden, grad_rows = stack_rows([(g,) for g in grad_slots], down_full, 0, 1)
 
     def spread_all(own):
@@ -1446,9 +1570,15 @@
             return [(row,) for row in rows]
         return [(row,) for row in rows[:6]] + [rows[6:8], rows[8:]]
 
+    mixed_flat = mixed.reshape(token_count, query_cols)
+    own_weight = lax.dynamic_slice_in_dim(
+        project_full, query_cols + parity * head_dim, head_dim, axis=1
+    )
+    back_full = jnp.concatenate([project_full[:, :query_cols], own_weight], axis=1)
     normed_slots = in_slots(spread_all(normed_share))
     if split:
-        gate_lin, normed_two = stack_rows(normed_slots, units_a, 1, 3)
+        early = after(units_a, back_full)
+        gate_lin, normed_two = stack_rows(normed_slots, early, 1, 3)
         hidden_a, gate_a, up_a = hidden_units(normed_two, units_a, 2, 3, gate_lin, grad_hidden)
         grad_a = first_grads(grad_rows, normed_two, hidden_a, gate_a, up_a)
         hidden_b, gate_b, up_b = full_units(after(normed_two, grad_a), grad_rows, units_b)
@@ -1485,7 +1615,7 @@
         grad_middle, gain_two, gate_grad_b, grad_branch, *mlp = spread_branch(
             grad_two_share,
             middle_share,
-            grad_slots[0],
+            grad_rows,
             gains_now[1:2],
             hidden_a,
             hidden_b,
@@ -1515,8 +1645,6 @@
         up_grad = contract_rows(normed_two, after(grad_up, branch_own), LOW)
 
     grad_mixed = product(grad_branch, output_full, LOW)
-    mixed_flat = jnp.concatenate([mixed_near, mixed_far], axis=0).reshape(token_count, query_cols)
-    lse = jnp.concatenate([lse_near, lse_far], axis=0)
     attend_args = (
         info,
         query_rot,
@@ -1552,10 +1680,6 @@
         turned = own_sum * cosine - jnp.roll(own_sum, half_lanes, axis=-1) * sine
         own_grad = jnp.where(parity == 0, turned, own_sum).astype(LOW).reshape(token_count, head_dim)
         line_grad = jnp.concatenate([grad_query.reshape(token_count, query_cols), own_grad], axis=1)
-    own_weight = lax.dynamic_slice_in_dim(
-        project_full, query_cols + parity * head_dim, head_dim, axis=1
-    )
-    back_full = jnp.concatenate([project_full[:, :query_cols], own_weight], axis=1)
     def scatter_units(grad):
         if not split:
             return scatter_sum(grad, ctx_rank, LOW)
@@ -1621,7 +1745,6 @@
     else:
         attn_end = scatter_sum(attn_grad, ctx_rank, LOW, *unit_sums)
 
-    home_order = jnp.stack(home_now).astype(jnp.int32)
 
     def leave(share):
         return lax.ppermute(share, ("fsdp", "tp"), back)

time: 805 us -> 776 us (0.964)
  Pallas kernels: 404 us -> 431 us
  local copies, waits for them, and re-layouts: 45.5 us -> 27.9 us
  between operations: 34.7 us -> 17.1 us
  other arithmetic: 42 us -> 31.8 us
    pallas_call x2 -> x1, Pallas kernels: 27.2 us -> 52.3 us  [attend_sum(): pl.pallas_call(functools.partial(attend_sum_kernel, heads, head_dim, scal...]
    ppermute x32 -> x29, starting transfers between devices: 44.6 us -> 39.5 us  [from_partner(): return lax.ppermute(value, axis, pairs)]
    ppermute x32 -> x29, waiting for transfers between devices: 170 us -> 173 us  [from_partner(): return lax.ppermute(value, axis, pairs)]
  transfers between devices with their start and end apart: 44 -> 41, of which waited for: 20 -> 16; matrix products, arithmetic and copies ran while one was open for 9% -> 7% of each run, Pallas kernels for 43% -> 49%
where the time goes in v8:
time: 776 us; the launch traced here: 766 us
  Pallas kernels  431 us (56%)
  waiting for transfers between devices  197 us (25%)
  starting transfers between devices  53.7 us (7%)
  other arithmetic  31.8 us (4%)
  local copies, waits for them, and re-layouts  27.9 us (4%)
  between operations  17.1 us (2%)
    ppermute x29, waiting for transfers between devices, from_partner(): return lax.ppermute(value, axis, pairs)  173 us
    pallas_call x1, Pallas kernels, collect_back(): pl.pallas_call(functools.partial(collect_kernel, slots, tiles), grid=(slo...  71.9 us
    pallas_call x1, Pallas kernels, attend_exchange(): pl.pallas_call(functools.partial(exchange_kernel, heads, head_dim, scale,...  55.4 us
    pallas_call x1, Pallas kernels, spread_branch(): pl.pallas_call(functools.partial(branch_kernel, slots, tiles), grid=(slot...  54.7 us
    pallas_call x1, Pallas kernels, finish_rows(): pl.pallas_call(functools.partial(line_kernel, slots, tiles), grid=(slots...  53 us
    pallas_call x1, Pallas kernels, attend_sum(): pl.pallas_call(functools.partial(attend_sum_kernel, heads, head_dim, scal...  52.3 us
    ppermute x29, starting transfers between devices, from_partner(): return lax.ppermute(value, axis, pairs)  39.5 us
    pallas_call x1, Pallas kernels, full_units(): pl.pallas_call(full_units_kernel, grid=(tokens // step,), in_specs=[by_ro...  37 us
  transfers between devices with their start and end apart: 41, of which 16 were waited for; matrix products, arithmetic and copies ran while one was open for 7% of the time, Pallas kernels for 49%

profile of v8, /device:TPU:1, one launch (start us, length us, event | category | flops | bytes accessed | tf_op | source)
XLA Modules:
  0.0 766.4 jit_solution(1980161820074169601)
XLA Ops:
  33.4 9.1 %collective-permute-done.4 = bf16[192,1152]{1,0:T(8,128)(2,1)S(1)} collective-permute-done((bf16[192,1152]{1,0:T(8,128)(2,1)S(1)}, bf16[192,1152]{1,0:T(8,128)(2,1)S(1)}, u32[]{:S(2)}, u32[]{:S(2)}) %collective-permute-start.4) | collective-permute-done | bytes 442400 | tf_op jit(solution)/shard_map/ppermute | solution.py:21
  43.6 10.7 %collective-permute-done.x0.own_in = bf16[512,1536]{1,0:T(8,128)(2,1)S(1)} collective-permute-done((bf16[512,1536]{1,0:T(8,128)(2,1)}, bf16[512,1536]{1,0:T(8,128)(2,1)S(1)}, u32[]{:S(2)}, u32[]{:S(2)}) %collective-permute-start) | collective-permute-done | bytes 1572896 | tf_op jit(solution)/shard_map/ppermute | solution.py:1406
  58.1 31.0 %collective-permute-done.2.x2 = bf16[512,1536]{1,0:T(8,128)(2,1)} collective-permute-done((bf16[512,1536]{1,0:T(8,128)(2,1)S(1)}, bf16[512,1536]{1,0:T(8,128)(2,1)}, u32[]{:S(2)}, u32[]{:S(2)}) %collective-permute-start.2) | collective-permute-done | bytes 1572896 | tf_op jit(solution)/shard_map/ppermute | solution.py:21
  99.7 31.2 %collective-permute-done.6.refs_0_ = bf16[512,1536]{1,0:T(8,128)(2,1)} collective-permute-done((bf16[512,1536]{1,0:T(8,128)(2,1)}, bf16[512,1536]{1,0:T(8,128)(2,1)}, u32[]{:S(2)}, u32[]{:S(2)}) %collective-permute-start.6) | collective-permute-done | bytes 1572896 | tf_op jit(solution)/shard_map/ppermute | solution.py:21
  132.5 13.3 %shard_map.221 = (bf16[4,512,1536]{2,1,0:T(8,128)(2,1)}, bf16[4,512,384]{2,1,0:T(8,128)(2,1)}, bf16[4,512,128]{2,1,0:T(8,128)(2,1)}, bf16[4,512,128]{2,1,0:T(8,128)(2,1)}) custom-call(bf16[512,1536]{1,0:T(8,128)(2,1)} %copy-done.7, bf16[512,1536]{1,0:T(8,128)(2,1)} %collective-permute-done.1.x1, bf16[512,1536]{1,0:T(8,128)(2,1)} %collective-permute-done.2.x2, ...), custom_call_target="tpu_custom_call" | custom-call | flops 4026531840 | bytes 17170432 | tf_op jit(solution)/shard_map/pallas_call | solution.py:836
  152.9 12.9 %collective-permute-done.8.refs_2_ = bf16[512,1536]{1,0:T(8,128)(2,1)} collective-permute-done((bf16[512,1536]{1,0:T(8,128)(2,1)}, bf16[512,1536]{1,0:T(8,128)(2,1)}, u32[]{:S(2)}, u32[]{:S(2)}) %collective-permute-start.8) | collective-permute-done | bytes 1572896 | tf_op jit(solution)/shard_map/ppermute | solution.py:21
  170.3 52.3 %shard_map.222 = (bf16[4,512,384]{2,1,0:T(8,128)(2,1)}, f32[4,512,128]{2,1,0:T(8,128)}, f32[512,1536]{1,0:T(8,128)}, bf16[512,1536]{1,0:T(8,128)(2,1)}) custom-call(s32[8]{0:T(128)} %compare_select_fusion.14.info, bf16[4,512,384]{2,1,0:T(8,128)(2,1)} %get-tuple-element.80.q, bf16[4,512,128]{2,1,0:T(8,128)(2,1)} %copy-done.13, ...), custom_call_target="tpu_custom_call" | custom-call | flops 3221225472 | bytes 3145728 | tf_op jit(solution)/shard_map/pallas_call | solution.py:1144
  228.4 15.6 %shard_map.223 = (bf16[4096,512]{1,0:T(8,128)(2,1)}, bf16[4096,1536]{1,0:T(8,128)(2,1)}) custom-call(s32[8]{0:T(128)} %compare_select_fusion.13.info, bf16[4,512,1536]{2,1,0:T(8,128)(2,1)} %cotangent, bf16[512,1536]{1,0:T(8,128)(2,1)} %collective-permute-done.6.refs_0_, bf16[512,1536]{1,0:T(8,128)(2,1)} %collective-permute-done.12.refs_1_, ...), custom_call_target="tpu_custom_call" | custom-call | flops 6442450944 | bytes 30932992 | tf_op jit(solution)/shard_map/pallas_call | solution.py:226
  244.0 14.2 %collective-permute-done.15.refs_4_ = bf16[512,1536]{1,0:T(8,128)(2,1)} collective-permute-done((bf16[512,1536]{1,0:T(8,128)(2,1)}, bf16[512,1536]{1,0:T(8,128)(2,1)}, u32[]{:S(2)}, u32[]{:S(2)}) %collective-permute-start.15) | collective-permute-done | bytes 1572896 | tf_op jit(solution)/shard_map/ppermute | solution.py:21
  266.7 14.6 %collective-permute-done.18.refs_7_ = bf16[256,1536]{1,0:T(8,128)(2,1)} collective-permute-done((bf16[256,1536]{1,0:T(8,128)(2,1)S(1)}, bf16[256,1536]{1,0:T(8,128)(2,1)}, u32[]{:S(2)}, u32[]{:S(2)}) %collective-permute-start.18) | collective-permute-done | bytes 786464 | tf_op jit(solution)/shard_map/ppermute | solution.py:21
  287.8 15.8 %shard_map.224 = (bf16[4096,512]{1,0:T(8,128)(2,1)}, bf16[4096,1536]{1,0:T(8,128)(2,1)}) custom-call(bf16[512,1536]{1,0:T(8,128)(2,1)} %get-tuple-element.84.refs_0_, bf16[512,1536]{1,0:T(8,128)(2,1)} %collective-permute-done.10.refs_1_, bf16[512,1536]{1,0:T(8,128)(2,1)} %collective-permute-done.11.refs_2_, ...), custom_call_target="tpu_custom_call" | custom-call | flops 6442450944 | bytes 30932992 | tf_op jit(solution)/shard_map/pallas_call | solution.py:121
  303.5 17.8 %shard_map.225 = (bf16[4096,512]{1,0:T(8,128)(2,1)}, bf16[4096,512]{1,0:T(8,128)(2,1)}, bf16[4096,512]{1,0:T(8,128)(2,1)}) custom-call(bf16[4096,1536]{1,0:T(8,128)(2,1)} %get-tuple-element.99.h.right.turned, bf16[1536,1536]{1,0:T(8,128)(2,1)} %bitcast.102, bf16[4096,512]{1,0:T(8,128)(2,1)} %get-tuple-element.94.gate, bf16[4096,512]{1,0:T(8,128)(2,1)} %get-tuple-element.89.grad), custom_call_target="tpu_custom_call" | custom-call | flops 6442450944 | bytes 35127296 | tf_op jit(solution)/shard_map/pallas_call | solution.py:157
  321.3 33.5 %shard_map.226 = bf16[1536,1536]{1,0:T(8,128)(2,1)} custom-call(bf16[4096,1536]{1,0:T(8,128)(2,1)} %get-tuple-element.97.g.left.own_grad, bf16[4096,1536]{1,0:T(8,128)(2,1)} %get-tuple-element.99.h.right.turned, bf16[4096,512]{1,0:T(8,128)(2,1)} %get-tuple-element.98.hid.hid_a, bf16[4096,512]{1,0:T(8,128)(2,1)} %get-tuple-element.95.gate.gate_a, ...), custom_call_target="tpu_custom_call" | custom-call | flops 19327352832 | bytes 17301504 | tf_op jit(solution)/shard_map/pallas_call | solution.py:294
  354.9 37.0 %shard_map.227 = (bf16[4096,640]{1,0:T(8,128)(2,1)}, bf16[4096,640]{1,0:T(8,128)(2,1)}, bf16[4096,640]{1,0:T(8,128)(2,1)}) custom-call(bf16[4096,1536]{1,0:T(8,128)(2,1)} %get-tuple-element.99.h.right.turned, bf16[4096,1536]{1,0:T(8,128)(2,1)} %get-tuple-element.97.g.left.own_grad, bf16[1536,1920]{1,0:T(8,128)(2,1)} %bitcast.122, ...), custom_call_target="tpu_custom_call" | custom-call | flops 24159191040 | bytes 46792704 | tf_op jit(solution)/shard_map/pallas_call | solution.py:268
  391.9 71.9 %shard_map.228 = (f32[512,1536]{1,0:T(8,128)}, bf16[1536,640]{1,0:T(8,128)(2,1)}, bf16[1536,640]{1,0:T(8,128)(2,1)}) custom-call(bf16[4096,512]{1,0:T(8,128)(2,1)} %get-tuple-element.95.gate.gate_a, bf16[4096,512]{1,0:T(8,128)(2,1)} %get-tuple-element.96.up.up_a, bf16[4096,640]{1,0:T(8,128)(2,1)} %get-tuple-element.101.gate_b.gate, ...), custom_call_target="tpu_custom_call" | custom-call | flops 24159191040 | bytes 26214400 | tf_op jit(solution)/shard_map/pallas_call | solution.py:435
  464.5 54.7 %shard_map.229 = (f32[512,1536]{1,0:T(8,128)}, f32[1,1536]{1,0:T(1,128)}, bf16[1536,640]{1,0:T(8,128)(2,1)}, bf16[4,512,1536]{2,1,0:T(8,128)(2,1)}, bf16[512,153...) custom-call(f32[512,1536]{1,0:T(8,128)} %get-tuple-element.104.total, ...), custom_call_target="tpu_custom_call" | custom-call | flops 16106127360 | bytes 26214400 | tf_op jit(solution)/shard_map/pallas_call | solution.py:573
  519.3 7.7 %convolution_convert_fusion = bf16[2048,384]{1,0:T(8,128)(2,1)} fusion(bf16[2048,1536]{1,0:T(8,128)(2,1)} %bitcast.98, bf16[1536,1152]{1,0:T(8,128)(2,1)} %bitcast.89), kind=kOutput, calls=%fused_computation.5 | convolution fusion | flops 2416705536 | bytes 9043968 | tf_op jit(solution)/shard_map/dot_general | solution.py:25
  526.9 55.4 %shard_map.230 = (bf16[4,512,512]{2,1,0:T(8,128)(2,1)}, bf16[1536,384]{1,0:T(8,128)(2,1)}, bf16[512,1536]{1,0:T(8,128)(2,1)}) custom-call(s32[8]{0:T(128)} %compare_select_fusion.14.info, bf16[4,512,384]{2,1,0:T(8,128)(2,1)} %get-tuple-element.80.q, bf16[4,512,128]{2,1,0:T(8,128)(2,1)} %copy-done.13, bf16[4,512,128]{2,1,0:T(8,128)(2,1)} %collective-permute-done.9.v_past, ...), custom_call_target="tpu_custom_call" | custom-call | flops 2415919104 | bytes 7864320 | tf_op jit(solution)/shard_map/pallas_call | solution.py:1294
  582.4 11.3 %reduce-scatter.12.cloned.1.call-done = bf16[384,640]{1,0:T(8,128)(2,1)} async-done(((bf16[1536,640]{1,0:T(8,128)(2,1)}), bf16[384,640]{1,0:T(8,128)(2,1)}) %reduce-scatter.12.cloned.1.call-update) | async-done | bytes 491536 | tf_op jit(solution)/shard_map/reduce_scatter | solution.py:1686
  593.7 53.0 %shard_map.231 = (bf16[512,1536]{1,0:T(8,128)(2,1)}, f32[2,1536]{1,0:T(2,128)}, bf16[1536,512]{1,0:T(8,128)(2,1)}, f32[1,512]{1,0:T(1,128)}, bf16[512,1536]{1,0:T(8,128)(2,1)}) custom-call(bf16[2048,512]{1,0:T(8,128)(2,1)} %bitcast.94, bf16[1536,512]{1,0:T(8,128)(2,1)} %pad_maximum_fusion.weight, bf16[512,1536]{1,0:T(8,128)(2,1)} %copy-done.7, ...), custom_call_target="tpu_custom_call" | custom-call | flops 3221225472 | bytes 31457280 | tf_op jit(solution)/shard_map/pallas_call | solution.py:720
  659.5 24.8 %collective-permute-done.29 = bf16[4,192,1024]{2,1,0:T(8,128)(2,1)} collective-permute-done((bf16[4,192,1024]{2,1,0:T(8,128)(2,1)}, bf16[4,192,1024]{2,1,0:T(8,128)(2,1)}, u32[]{:S(2)}, u32[]{:S(2)}) %collective-permute-start.29) | collective-permute-done | bytes 1572896 | tf_op jit(solution)/shard_map/ppermute | solution.py:21
  689.4 7.6 collective-permute-done.24
  725.5 13.5 %collective-permute-done.31.refs_2_ = bf16[512,1536]{1,0:T(8,128)(2,1)} collective-permute-done((bf16[512,1536]{1,0:T(8,128)(2,1)S(1)}, bf16[512,1536]{1,0:T(8,128)(2,1)}, u32[]{:S(2)}, u32[]{:S(2)}) %collective-permute-start.31) | collective-permute-done | bytes 1572896 | tf_op jit(solution)/shard_map/ppermute | solution.py:21
  753.1 5.9 shard_map.233
  (205 shorter events, 134.6 us)
Async XLA Ops:
  7.2 125.3 %all-gather.7.cloned.1.call-start = ((), (), s32[]{:S(2)}) async-start(), calls=%async_computation.10 | async-start | bytes 4423680 | tf_op jit(solution)/shard_map/all_gather | solution.py:1443
  14.4 39.9 %collective-permute-start = (bf16[512,1536]{1,0:T(8,128)(2,1)}, bf16[512,1536]{1,0:T(8,128)(2,1)S(1)}, u32[]{:S(2)}, u32[]{:S(2)}) collective-permute-start(bf16[512,1536]{1,0:T(8,128)(2,1)} %get-tuple-element.253), channel_id=1, source_target_pairs={{0,0},{1,17},{2,10},{3,27},{8,8},{9,25},{10,18},{11,3},{16,16},{17... | collective-permute-start | bytes 4718600 | tf_op jit(solution)/shard_map/ppermute | solution.py:1406
  54.3 174.1 %all-gather.9.cloned.1.call-start = ((), (), s32[]{:S(2)}) async-start(), calls=%async_computation.11 | async-start | bytes 5898240 | tf_op jit(solution)/shard_map/all_gather | solution.py:1443
  54.3 34.7 %collective-permute-start.2 = (bf16[512,1536]{1,0:T(8,128)(2,1)S(1)}, bf16[512,1536]{1,0:T(8,128)(2,1)}, u32[]{:S(2)}, u32[]{:S(2)}) collective-permute-start(bf16[512,1536]{1,0:T(8,128)(2,1)S(1)} %collective-permute-done.x0.own_in), channel_id=1, source_target_pairs={{0,2},{1,3},{2,0},{3,1},{4,6},{5,7},{6,4},{7,5},{8,10},{9,11},{10,... | collective-permute-start | bytes 4718600 | tf_op jit(solution)/shard_map/ppermute | solution.py:21
  55.6 35.7 %collective-permute-start.5 = (bf16[192,3456]{1,0:T(8,128)(2,1)}, bf16[192,3456]{1,0:T(8,128)(2,1)S(1)}, u32[]{:S(2)}, u32[]{:S(2)}) collective-permute-start(bf16[192,3456]{1,0:T(8,128)(2,1)} %copy-done.20), channel_id=1, source_target_pairs={{0,4},{4,0},{1,5},{5,1},{2,6},{6,2},{3,7},{7,3},{8,12},{12,8},{9,1... | collective-permute-start | bytes 3981320 | tf_op jit(solution)/shard_map/ppermute | solution.py:21
  94.8 260.1 %all-gather.11.cloned.1.call-start = ((), (), s32[]{:S(2)}) async-start(), calls=%async_computation.12 | async-start | bytes 7372800 | tf_op jit(solution)/shard_map/all_gather | solution.py:1443
  94.8 36.0 %collective-permute-start.6 = (bf16[512,1536]{1,0:T(8,128)(2,1)}, bf16[512,1536]{1,0:T(8,128)(2,1)}, u32[]{:S(2)}, u32[]{:S(2)}) collective-permute-start(bf16[512,1536]{1,0:T(8,128)(2,1)} %get-tuple-element.78), channel_id=1, source_target_pairs={{0,4},{4,0},{1,5},{5,1},{2,6},{6,2},{3,7},{7,3},{8,12},{12,8},{9,1... | collective-permute-start | bytes 4718600 | tf_op jit(solution)/shard_map/ppermute | solution.py:21
  96.2 36.3 %collective-permute-start.1 = (bf16[512,1536]{1,0:T(8,128)(2,1)S(1)}, bf16[512,1536]{1,0:T(8,128)(2,1)}, u32[]{:S(2)}, u32[]{:S(2)}) collective-permute-start(bf16[512,1536]{1,0:T(8,128)(2,1)S(1)} %collective-permute-done.x0.own_in), channel_id=1, source_target_pairs={{0,1},{1,0},{2,3},{3,2},{4,5},{5,4},{6,7},{7,6},{8,9},{9,8},{10,11... | collective-permute-start | bytes 4718600 | tf_op jit(solution)/shard_map/ppermute | solution.py:21
  99.6 364.2 %reduce-scatter.6.cloned.1.call-start = ((), (), s32[]{:S(2)}) async-start(), calls=%async_computation.5 | async-start | bytes 5898240 | tf_op jit(solution)/shard_map/reduce_scatter | solution.py:1686
  130.8 35.0 %collective-permute-start.8 = (bf16[512,1536]{1,0:T(8,128)(2,1)}, bf16[512,1536]{1,0:T(8,128)(2,1)}, u32[]{:S(2)}, u32[]{:S(2)}) collective-permute-start(bf16[512,1536]{1,0:T(8,128)(2,1)} %collective-permute-done.6.refs_0_), channel_id=1, source_target_pairs={{0,2},{1,3},{2,0},{3,1},{4,6},{5,7},{6,4},{7,5},{8,10},{9,11},{10,... | collective-permute-start | bytes 4718600 | tf_op jit(solution)/shard_map/ppermute | solution.py:21
  165.9 62.6 %collective-permute-start.13 = (bf16[512,1536]{1,0:T(8,128)(2,1)}, bf16[512,1536]{1,0:T(8,128)(2,1)}, u32[]{:S(2)}, u32[]{:S(2)}) collective-permute-start(bf16[512,1536]{1,0:T(8,128)(2,1)} %collective-permute-done.8.refs_2_), channel_id=1, source_target_pairs={{0,1},{1,0},{2,3},{3,2},{4,5},{5,4},{6,7},{7,6},{8,9},{9,8},{10,11... | collective-permute-start | bytes 4718600 | tf_op jit(solution)/shard_map/ppermute | solution.py:21
  168.0 60.5 %collective-permute-start.12 = (bf16[512,1536]{1,0:T(8,128)(2,1)}, bf16[512,1536]{1,0:T(8,128)(2,1)}, u32[]{:S(2)}, u32[]{:S(2)}) collective-permute-start(bf16[512,1536]{1,0:T(8,128)(2,1)} %collective-permute-done.6.refs_0_), channel_id=1, source_target_pairs={{0,1},{1,0},{2,3},{3,2},{4,5},{5,4},{6,7},{7,6},{8,9},{9,8},{10,11... | collective-permute-start | bytes 4718600 | tf_op jit(solution)/shard_map/ppermute | solution.py:21
  222.6 35.6 %collective-permute-start.15 = (bf16[512,1536]{1,0:T(8,128)(2,1)}, bf16[512,1536]{1,0:T(8,128)(2,1)}, u32[]{:S(2)}, u32[]{:S(2)}) collective-permute-start(bf16[512,1536]{1,0:T(8,128)(2,1)} %get-tuple-element.84.refs_0_), channel_id=1, source_target_pairs={{0,4},{4,0},{1,5},{5,1},{2,6},{6,2},{3,7},{7,3},{8,12},{12,8},{9,1... | collective-permute-start | bytes 4718600 | tf_op jit(solution)/shard_map/ppermute | solution.py:21
  225.1 38.2 %collective-permute-start.11 = (bf16[512,1536]{1,0:T(8,128)(2,1)}, bf16[512,1536]{1,0:T(8,128)(2,1)}, u32[]{:S(2)}, u32[]{:S(2)}) collective-permute-start(bf16[512,1536]{1,0:T(8,128)(2,1)} %get-tuple-element.84.refs_0_), channel_id=1, source_target_pairs={{0,2},{1,3},{2,0},{3,1},{4,6},{5,7},{6,4},{7,5},{8,10},{9,11},{10,... | collective-permute-start | bytes 4718600 | tf_op jit(solution)/shard_map/ppermute | solution.py:21
  226.4 61.3 %collective-permute-start.10 = (bf16[512,1536]{1,0:T(8,128)(2,1)}, bf16[512,1536]{1,0:T(8,128)(2,1)}, u32[]{:S(2)}, u32[]{:S(2)}) collective-permute-start(bf16[512,1536]{1,0:T(8,128)(2,1)} %get-tuple-element.84.refs_0_), channel_id=1, source_target_pairs={{0,1},{1,0},{2,3},{3,2},{4,5},{5,4},{6,7},{7,6},{8,9},{9,8},{10,11... | collective-permute-start | bytes 4718600 | tf_op jit(solution)/shard_map/ppermute | solution.py:21
  354.8 227.5 %reduce-scatter.8.cloned.1.call-start = ((), (), s32[]{:S(2)}) async-start(), calls=%async_computation.6 | async-start | bytes 2457600 | tf_op jit(solution)/shard_map/reduce_scatter | solution.py:1686
  463.9 118.5 %reduce-scatter.10.cloned.1.call-start = ((), (), s32[]{:S(2)}) async-start(), calls=%async_computation.7 | async-start | bytes 2457600 | tf_op jit(solution)/shard_map/reduce_scatter | solution.py:1686
  464.4 129.2 %reduce-scatter.12.cloned.1.call-start = ((), (), s32[]{:S(2)}) async-start(), calls=%async_computation.8 | async-start | bytes 2457600 | tf_op jit(solution)/shard_map/reduce_scatter | solution.py:1686
  519.2 227.1 %reduce-scatter.14.cloned.1.call-start = ((), (), s32[]{:S(2)}) async-start(), calls=%async_computation.9 | async-start | bytes 1966080 | tf_op jit(solution)/shard_map/reduce_scatter | solution.py:1744
  653.1 49.8 %collective-permute-start.28 = (bf16[512,1536]{1,0:T(8,128)(2,1)}, bf16[512,1536]{1,0:T(8,128)(2,1)S(1)}, u32[]{:S(2)}, u32[]{:S(2)}) collective-permute-start(bf16[512,1536]{1,0:T(8,128)(2,1)} %get-tuple-element.130), channel_id=1, source_target_pairs={{0,0},{17,1},{10,2},{27,3},{8,8},{25,9},{18,10},{3,11},{16,16},{1,... | collective-permute-start | bytes 4718600 | tf_op jit(solution)/shard_map/ppermute | solution.py:1750
  658.7 38.3 %collective-permute-start.24 = (bf16[192,1536]{1,0:T(8,128)(2,1)}, bf16[192,1536]{1,0:T(8,128)(2,1)}, u32[]{:S(2)}, u32[]{:S(2)}) collective-permute-start(bf16[192,1536]{1,0:T(8,128)(2,1)} %get-tuple-element.125), channel_id=1, source_target_pairs={{0,4},{4,0},{1,5},{5,1},{2,6},{6,2},{3,7},{7,3},{8,12},{12,8},{9,1... | collective-permute-start | bytes 1769480 | tf_op jit(solution)/shard_map/ppermute | solution.py:21
  659.5 53.1 %collective-permute-start.22 = (bf16[512,1536]{1,0:T(8,128)(2,1)S(1)}, bf16[512,1536]{1,0:T(8,128)(2,1)}, u32[]{:S(2)}, u32[]{:S(2)}) collective-permute-start(bf16[512,1536]{1,0:T(8,128)(2,1)S(1)} %copy-done.2), channel_id=1, source_target_pairs={{0,2},{1,3},{2,0},{3,1},{4,6},{5,7},{6,4},{7,5},{8,10},{9,11},{10,... | collective-permute-start | bytes 4718600 | tf_op jit(solution)/shard_map/ppermute | solution.py:21
  698.1 43.2 %collective-permute-start.21 = (bf16[512,1536]{1,0:T(8,128)(2,1)S(1)}, bf16[512,1536]{1,0:T(8,128)(2,1)S(1)}, u32[]{:S(2)}, u32[]{:S(2)}) collective-permute-start(bf16[512,1536]{1,0:T(8,128)(2,1)S(1)} %copy-done.2), channel_id=1, source_target_pairs={{0,1},{1,0},{2,3},{3,2},{4,5},{5,4},{6,7},{7,6},{8,9},{9,8},{10,11... | collective-permute-start | bytes 4718600 | tf_op jit(solution)/shard_map/ppermute | solution.py:21
  702.9 36.1 %collective-permute-start.31 = (bf16[512,1536]{1,0:T(8,128)(2,1)S(1)}, bf16[512,1536]{1,0:T(8,128)(2,1)}, u32[]{:S(2)}, u32[]{:S(2)}) collective-permute-start(bf16[512,1536]{1,0:T(8,128)(2,1)S(1)} %collective-permute-done.28.refs_0_), channel_id=1, source_target_pairs={{0,2},{1,3},{2,0},{3,1},{4,6},{5,7},{6,4},{7,5},{8,10},{9,11},{10,... | collective-permute-start | bytes 4718600 | tf_op jit(solution)/shard_map/ppermute | solution.py:21
  (43 other events, 568.9 us)
Sparse Core Ops, SparseCore 0:
  54.4 71.4 all-gather.6
  127.5 88.1 all-gather.8
  217.8 107.4 all-gather.10
  354.9 86.4 reduce-scatter.5
  464.0 43.7 reduce-scatter.7
  509.9 40.6 reduce-scatter.9
  553.0 40.6 reduce-scatter.11
  688.2 41.6 reduce-scatter.13

commit v9 on v8

--- a/solution.py
+++ b/solution.py
@@ -98,7 +98,7 @@
 
 def rows_kernel(groups, *refs):
     slot = pl.program_id(0)
-    weight, lin, stacked = refs[-3:]
+    weight, (lin, stacked) = refs[sum(groups)], refs[-2:]
 
     def run(pieces):
         start = 0
@@ -113,29 +113,33 @@
         first += pieces
 
 
-def stack_rows(slots, weight, part, parts):
+def stack_rows(slots, weight, part, parts, into=None, first=0, total=None):
     groups = [len(s) for s in slots]
     rows = [piece for s in slots for piece in s]
     width, length = rows[0].shape[1], sum(piece.shape[0] for piece in slots[0])
     count, cols = len(slots), weight.shape[1] // parts
+    total = total or count
+    into = into or ()
     return pl.pallas_call(
         functools.partial(rows_kernel, groups),
         grid=(count,),
         in_specs=[whole_spec(*piece.shape, once=True) for piece in rows]
-        + [part_spec(width, cols, part)],
+        + [part_spec(width, cols, part)]
+        + [pl.BlockSpec(memory_space=pl.ANY)] * len(into),
         out_specs=[
-            pl.BlockSpec((length, cols), lambda s: (s, 0)),
-            pl.BlockSpec((length, width), lambda s: (s, 0)),
+            pl.BlockSpec((length, cols), lambda s: (first + s, 0)),
+            pl.BlockSpec((length, width), lambda s: (first + s, 0)),
         ],
         out_shape=[
-            jax.ShapeDtypeStruct((count * length, cols), LOW),
-            jax.ShapeDtypeStruct((count * length, width), LOW),
-        ],
+            jax.ShapeDtypeStruct((total * length, cols), LOW),
+            jax.ShapeDtypeStruct((total * length, width), LOW),
+        ],
+        input_output_aliases={len(rows) + 1 + i: i for i in range(len(into))},
         compiler_params=pltpu.CompilerParams(vmem_limit_bytes=60 << 20),
         cost_estimate=estimate(
             2 * count * length * width * cols, 2 * (count * length * (2 * width + cols) + width * cols)
         ),
-    )(*rows, weight)
+    )(*rows, weight, *into)
 
 
 def units_kernel(h, up, gate, grad, hid, grad_gate, grad_up):
@@ -1184,10 +1188,10 @@
 
 
 def exchange_kernel(
-    heads, head_dim, scale, slots, tiles, info, q, k_past, v_past, k_own, v_own, grad, lse, cosine, sine,
+    heads, head_dim, scale, slots, tiles, info, q, k_past, v_past, k_own, v_own, rows, weight, lse, cosine, sine,
     cosine_all, sine_all, branch, mixed, mlp_far, mlp_side, mlp_own, middle, line, out_grad, block, mine_past,
     mine_own, other_past, other_own, got_past, got_own, side_out, side_in, dk_past, dk_own, dv_past, dv_own,
-    own_rows, last_in, send, recv, load
+    own_rows, last_in, grad, send, recv, load
 ):
     step = pl.program_id(0)
     tensor_rank = lax.axis_index("tp")
@@ -1216,6 +1220,7 @@
         length = info[jnp.minimum(step, slots - 1)]
         for total in (dk_past, dk_own, dv_past, dv_own):
             total[...] = jnp.zeros_like(total)
+        grad[0] = jnp.dot(rows[...], weight[...], preferred_element_type=WIDE).astype(LOW)
         attend_back_rows(
             heads, head_dim, scale, length, offset, q, k_past, v_past, k_own, v_own, grad, lse, cosine,
             sine, lambda here, cols, value: line.__setitem__((step, here, cols), value),
@@ -1277,7 +1282,8 @@
 
 
 def attend_exchange(
-    info, q, k_past, v_past, k_own, v_own, grad, lse, cosine, sine, heads, head_dim, scale, branch, mixed, mlp, middle
+    info, q, k_past, v_past, k_own, v_own, weight, lse, cosine, sine, heads, head_dim, scale, branch, mixed, mlp,
+    middle
 ):
     count, length, width = q.shape
     past = k_past.shape[1]
@@ -1302,7 +1308,8 @@
                 by_slot(past, head_dim),
                 by_slot(length, head_dim),
                 by_slot(length, head_dim),
-                by_slot(length, width),
+                pl.BlockSpec((length, model_width), lambda i, info: (slot(i), 0)),
+                held(*weight.shape),
                 by_slot(length, 128),
                 by_slot(length, head_dim),
                 by_slot(length, head_dim),
@@ -1324,6 +1331,7 @@
             + [
                 pltpu.VMEM((length, model_width), LOW),
                 pltpu.VMEM((2, length, model_width), LOW),
+                pltpu.VMEM((1, length, width), LOW),
                 pltpu.SemaphoreType.DMA((3 * count + 2,)),
                 pltpu.SemaphoreType.DMA((3 * count + 2,)),
                 pltpu.SemaphoreType.DMA,
@@ -1338,7 +1346,7 @@
             vmem_limit_bytes=63 << 20, collective_id=4, has_side_effects=True
         ),
         cost_estimate=estimate(2 * tokens * model_width * width, 10 * tokens * width),
-    )(info, q, k_past, v_past, k_own, v_own, grad, lse, cosine, sine, cosine, sine, branch, mixed, *mlp, middle)
+    )(info, q, k_past, v_past, k_own, v_own, branch, weight, lse, cosine, sine, cosine, sine, branch, mixed, *mlp, middle)
 
 
 def local(
@@ -1562,13 +1570,13 @@
         side = from_partner(own, "ctx", 1)
         held = after(far, grad_hidden), after(side, grad_hidden)
         across = from_partner(held[0][:half_len], "ctx", 1), from_partner(held[1][half_len:], "tp", 2)
-        cores = [from_partner(v, "tp", 1) for v in (*held, *across)]
-        return (own, near, far, cores[0], side, cores[1], *across, *cores[2:])
+        cores = [from_partner(v, "tp", 1) for v in held]
+        return (own, near, far, cores[0], side, cores[1], *across)
 
     def in_slots(rows):
         if not split:
             return [(row,) for row in rows]
-        return [(row,) for row in rows[:6]] + [rows[6:8], rows[8:]]
+        return [(row,) for row in rows[:6]] + [rows[6:]]
 
     mixed_flat = mixed.reshape(token_count, query_cols)
     own_weight = lax.dynamic_slice_in_dim(
@@ -1578,7 +1586,9 @@
     normed_slots = in_slots(spread_all(normed_share))
     if split:
         early = after(units_a, back_full)
-        gate_lin, normed_two = stack_rows(normed_slots, early, 1, 3)
+        ahead = stack_rows(normed_slots[:6], early, 1, 3, total=8)
+        last = [normed_slots[6], tuple(from_partner(after(v, ahead[0]), "tp", 1) for v in normed_slots[6])]
+        gate_lin, normed_two = stack_rows(last, units_a, 1, 3, into=ahead, first=6, total=8)
         hidden_a, gate_a, up_a = hidden_units(normed_two, units_a, 2, 3, gate_lin, grad_hidden)
         grad_a = first_grads(grad_rows, normed_two, hidden_a, gate_a, up_a)
         hidden_b, gate_b, up_b = full_units(after(normed_two, grad_a), grad_rows, units_b)
@@ -1644,7 +1654,7 @@
         grad_branch = jnp.concatenate([branch_own, branch_near, branch_far, branch_cross], axis=0)
         up_grad = contract_rows(normed_two, after(grad_up, branch_own), LOW)
 
-    grad_mixed = product(grad_branch, output_full, LOW)
+    grad_mixed = None if split else product(grad_branch, output_full, LOW)
     attend_args = (
         info,
         query_rot,
@@ -1652,7 +1662,7 @@
         value_past,
         key_own,
         value_own,
-        grad_mixed.reshape(seq_grp, local_len, query_cols),
+        output_full if split else grad_mixed.reshape(seq_grp, local_len, query_cols),
         lse,
         cosine,
         sine,

time: 776 us -> 773 us (level)
    ppermute x29, waiting for transfers between devices: 173 us -> 161 us  [from_partner(): return lax.ppermute(value, axis, pairs)]
    pallas_call x1 -> x2, Pallas kernels: 15.8 us -> 18.2 us  [stack_rows(): pl.pallas_call(functools.partial(rows_kernel, groups), grid=(count,), in_...]
  transfers between devices with their start and end apart: 41 -> 41, of which waited for: 16 -> 18; matrix products, arithmetic and copies ran while one was open for 7% -> 7% of each run, Pallas kernels for 49% -> 49%
where the time goes in v9:
time: 773 us; the launch traced here: 763 us
  Pallas kernels  434 us (56%)
  waiting for transfers between devices  193 us (25%)
  starting transfers between devices  51.8 us (7%)
  other arithmetic  36 us (5%)
  local copies, waits for them, and re-layouts  31.4 us (4%)
  between operations  16.9 us (2%)
    ppermute x29, waiting for transfers between devices, from_partner(): return lax.ppermute(value, axis, pairs)  161 us
    pallas_call x1, Pallas kernels, collect_back(): pl.pallas_call(functools.partial(collect_kernel, slots, tiles), grid=(slo...  71.2 us
    pallas_call x1, Pallas kernels, attend_exchange(): pl.pallas_call(functools.partial(exchange_kernel, heads, head_dim, scale,...  56.6 us
    pallas_call x1, Pallas kernels, spread_branch(): pl.pallas_call(functools.partial(branch_kernel, slots, tiles), grid=(slot...  55.1 us
    pallas_call x1, Pallas kernels, finish_rows(): pl.pallas_call(functools.partial(line_kernel, slots, tiles), grid=(slots...  52.8 us
    pallas_call x1, Pallas kernels, attend_sum(): pl.pallas_call(functools.partial(attend_sum_kernel, heads, head_dim, scal...  52.1 us
    ppermute x29, starting transfers between devices, from_partner(): return lax.ppermute(value, axis, pairs)  37.2 us
    pallas_call x1, Pallas kernels, full_units(): pl.pallas_call(full_units_kernel, grid=(tokens // step,), in_specs=[by_ro...  36.6 us
  transfers between devices with their start and end apart: 41, of which 18 were waited for; matrix products, arithmetic and copies ran while one was open for 7% of the time, Pallas kernels for 49%

profile of v9, /device:TPU:1, one launch (start us, length us, event | category | flops | bytes accessed | tf_op | source)
XLA Modules:
  0.0 762.8 jit_solution(4221915721568988114)
XLA Ops:
  34.6 9.1 %collective-permute-done.4 = bf16[192,1152]{1,0:T(8,128)(2,1)S(1)} collective-permute-done((bf16[192,1152]{1,0:T(8,128)(2,1)S(1)}, bf16[192,1152]{1,0:T(8,128)(2,1)S(1)}, u32[]{:S(2)}, u32[]{:S(2)}) %collective-permute-start.4) | collective-permute-done | bytes 442400 | tf_op jit(solution)/shard_map/ppermute | solution.py:21
  44.8 10.1 %collective-permute-done.x0.own_in = bf16[512,1536]{1,0:T(8,128)(2,1)S(1)} collective-permute-done((bf16[512,1536]{1,0:T(8,128)(2,1)}, bf16[512,1536]{1,0:T(8,128)(2,1)S(1)}, u32[]{:S(2)}, u32[]{:S(2)}) %collective-permute-start) | collective-permute-done | bytes 1572896 | tf_op jit(solution)/shard_map/ppermute | solution.py:1414
  60.7 29.0 %collective-permute-done.2.x2 = bf16[512,1536]{1,0:T(8,128)(2,1)S(1)} collective-permute-done((bf16[512,1536]{1,0:T(8,128)(2,1)S(1)}, bf16[512,1536]{1,0:T(8,128)(2,1)S(1)}, u32[]{:S(2)}, u32[]{:S(2)}) %collective-permute-start.2) | collective-permute-done | bytes 1572896 | tf_op jit(solution)/shard_map/ppermute | solution.py:21
  99.3 32.2 %collective-permute-done.6.refs_0_ = bf16[512,1536]{1,0:T(8,128)(2,1)} collective-permute-done((bf16[512,1536]{1,0:T(8,128)(2,1)}, bf16[512,1536]{1,0:T(8,128)(2,1)}, u32[]{:S(2)}, u32[]{:S(2)}) %collective-permute-start.6) | collective-permute-done | bytes 1572896 | tf_op jit(solution)/shard_map/ppermute | solution.py:21
  135.1 13.2 %shard_map.221 = (bf16[4,512,1536]{2,1,0:T(8,128)(2,1)}, bf16[4,512,384]{2,1,0:T(8,128)(2,1)}, bf16[4,512,128]{2,1,0:T(8,128)(2,1)}, bf16[4,512,128]{2,1,0:T(8,128)(2,1)}) custom-call(bf16[512,1536]{1,0:T(8,128)(2,1)} %copy-done.7, bf16[512,1536]{1,0:T(8,128)(2,1)} %copy-done.12, bf16[512,1536]{1,0:T(8,128)(2,1)} %copy-done.11, ...), custom_call_target="tpu_custom_call" | custom-call | flops 4026531840 | bytes 17170432 | tf_op jit(solution)/shard_map/pallas_call | solution.py:840
  155.8 10.9 %collective-permute-done.8.refs_2_ = bf16[512,1536]{1,0:T(8,128)(2,1)} collective-permute-done((bf16[512,1536]{1,0:T(8,128)(2,1)}, bf16[512,1536]{1,0:T(8,128)(2,1)}, u32[]{:S(2)}, u32[]{:S(2)}) %collective-permute-start.8) | collective-permute-done | bytes 1572896 | tf_op jit(solution)/shard_map/ppermute | solution.py:21
  173.3 52.1 %shard_map.222 = (bf16[4,512,384]{2,1,0:T(8,128)(2,1)}, f32[4,512,128]{2,1,0:T(8,128)}, f32[512,1536]{1,0:T(8,128)}, bf16[512,1536]{1,0:T(8,128)(2,1)}) custom-call(s32[8]{0:T(128)} %compare_select_fusion.14.info, bf16[4,512,384]{2,1,0:T(8,128)(2,1)} %get-tuple-element.84.q, bf16[4,512,128]{2,1,0:T(8,128)(2,1)} %copy-done.21, ...), custom_call_target="tpu_custom_call" | custom-call | flops 3221225472 | bytes 3145728 | tf_op jit(solution)/shard_map/pallas_call | solution.py:1148
  230.9 15.6 %shard_map.223 = (bf16[4096,512]{1,0:T(8,128)(2,1)}, bf16[4096,1536]{1,0:T(8,128)(2,1)}) custom-call(s32[8]{0:T(128)} %compare_select_fusion.13.info, bf16[4,512,1536]{2,1,0:T(8,128)(2,1)} %cotangent, bf16[512,1536]{1,0:T(8,128)(2,1)} %collective-permute-done.6.refs_0_, bf16[512,1536]{1,0:T(8,128)(2,1)} %collective-permute-done.11.refs_1_, ...), custom_call_target="tpu_custom_call" | custom-call | flops 6442450944 | bytes 30932992 | tf_op jit(solution)/shard_map/pallas_call | solution.py:230
  246.6 14.4 %collective-permute-done.14.refs_4_ = bf16[512,1536]{1,0:T(8,128)(2,1)} collective-permute-done((bf16[512,1536]{1,0:T(8,128)(2,1)}, bf16[512,1536]{1,0:T(8,128)(2,1)}, u32[]{:S(2)}, u32[]{:S(2)}) %collective-permute-start.14) | collective-permute-done | bytes 1572896 | tf_op jit(solution)/shard_map/ppermute | solution.py:21
  273.5 12.3 %shard_map.224 = (bf16[4096,512]{1,0:T(8,128)(2,1)}, bf16[4096,1536]{1,0:T(8,128)(2,1)}) custom-call(bf16[512,1536]{1,0:T(8,128)(2,1)} %get-tuple-element.88.refs_0_, bf16[512,1536]{1,0:T(8,128)(2,1)} %collective-permute-done.16.refs_1_, bf16[512,1536]{1,0:T(8,128)(2,1)} %collective-permute-done.10.refs_2_, ...), custom_call_target="tpu_custom_call" | custom-call | flops 4831838208 | bytes 23592960 | tf_op jit(solution)/shard_map/pallas_call | solution.py:123
  295.0 5.9 shard_map.225
  300.9 17.8 %shard_map.226 = (bf16[4096,512]{1,0:T(8,128)(2,1)}, bf16[4096,512]{1,0:T(8,128)(2,1)}, bf16[4096,512]{1,0:T(8,128)(2,1)}) custom-call(bf16[4096,1536]{1,0:T(8,128)(2,1)} %get-tuple-element.107.h.right.turned, bf16[1536,1536]{1,0:T(8,128)(2,1)} %bitcast.94, bf16[4096,512]{1,0:T(8,128)(2,1)} %get-tuple-element.102.gate, bf16[4096,512]{1,0:T(8,128)(2,1)} %get-tuple-element.93.grad), custom_call_target="tpu_custom_call" | custom-call | flops 6442450944 | bytes 35127296 | tf_op jit(solution)/shard_map/pallas_call | solution.py:161
  318.7 33.5 %shard_map.227 = bf16[1536,1536]{1,0:T(8,128)(2,1)} custom-call(bf16[4096,1536]{1,0:T(8,128)(2,1)} %get-tuple-element.105.g.left.own_grad, bf16[4096,1536]{1,0:T(8,128)(2,1)} %get-tuple-element.107.h.right.turned, bf16[4096,512]{1,0:T(8,128)(2,1)} %get-tuple-element.106.hid.hid_a, bf16[4096,512]{1,0:T(8,128)(2,1)} %get-tuple-element.103.gate.gate_a, ...), custom_call_target="tpu_custom_call" | custom-call | flops 19327352832 | bytes 17301504 | tf_op jit(solution)/shard_map/pallas_call | solution.py:298
  352.3 36.6 %shard_map.228 = (bf16[4096,640]{1,0:T(8,128)(2,1)}, bf16[4096,640]{1,0:T(8,128)(2,1)}, bf16[4096,640]{1,0:T(8,128)(2,1)}) custom-call(bf16[4096,1536]{1,0:T(8,128)(2,1)} %get-tuple-element.107.h.right.turned, bf16[4096,1536]{1,0:T(8,128)(2,1)} %get-tuple-element.105.g.left.own_grad, bf16[1536,1920]{1,0:T(8,128)(2,1)} %bitcast.119, ...), custom_call_target="tpu_custom_call" | custom-call | flops 24159191040 | bytes 46792704 | tf_op jit(solution)/shard_map/pallas_call | solution.py:272
  389.0 71.2 %shard_map.229 = (f32[512,1536]{1,0:T(8,128)}, bf16[1536,640]{1,0:T(8,128)(2,1)}, bf16[1536,640]{1,0:T(8,128)(2,1)}) custom-call(bf16[4096,512]{1,0:T(8,128)(2,1)} %get-tuple-element.103.gate.gate_a, bf16[4096,512]{1,0:T(8,128)(2,1)} %get-tuple-element.104.up.up_a, bf16[4096,640]{1,0:T(8,128)(2,1)} %get-tuple-element.109.gate_b.gate, ...), custom_call_target="tpu_custom_call" | custom-call | flops 24159191040 | bytes 26214400 | tf_op jit(solution)/shard_map/pallas_call | solution.py:439
  460.8 55.1 %shard_map.230 = (f32[512,1536]{1,0:T(8,128)}, f32[1,1536]{1,0:T(1,128)}, bf16[1536,640]{1,0:T(8,128)(2,1)}, bf16[4,512,1536]{2,1,0:T(8,128)(2,1)}, bf16[512,153...) custom-call(f32[512,1536]{1,0:T(8,128)} %get-tuple-element.112.total, ...), custom_call_target="tpu_custom_call" | custom-call | flops 16106127360 | bytes 26214400 | tf_op jit(solution)/shard_map/pallas_call | solution.py:577
  516.0 56.6 %shard_map.231 = (bf16[4,512,512]{2,1,0:T(8,128)(2,1)}, bf16[1536,384]{1,0:T(8,128)(2,1)}, bf16[512,1536]{1,0:T(8,128)(2,1)}) custom-call(s32[8]{0:T(128)} %compare_select_fusion.14.info, bf16[4,512,384]{2,1,0:T(8,128)(2,1)} %get-tuple-element.84.q, bf16[4,512,128]{2,1,0:T(8,128)(2,1)} %copy-done.21, bf16[4,512,128]{2,1,0:T(8,128)(2,1)} %collective-permute-done.9.v_past, ...), custom_call_target="tpu_custom_call" | custom-call | flops 2415919104 | bytes 7864320 | tf_op jit(solution)/shard_map/pallas_call | solution.py:1300
  572.7 16.9 %reduce-scatter.12.cloned.1.call-done = bf16[384,640]{1,0:T(8,128)(2,1)} async-done(((bf16[1536,640]{1,0:T(8,128)(2,1)}), bf16[384,640]{1,0:T(8,128)(2,1)}) %reduce-scatter.12.cloned.1.call-update) | async-done | bytes 491536 | tf_op jit(solution)/shard_map/reduce_scatter | solution.py:1696
  589.6 52.8 %shard_map.232 = (bf16[512,1536]{1,0:T(8,128)(2,1)}, f32[2,1536]{1,0:T(2,128)}, bf16[1536,512]{1,0:T(8,128)(2,1)}, f32[1,512]{1,0:T(1,128)}, bf16[512,1536]{1,0:T(8,128)(2,1)}) custom-call(bf16[2048,512]{1,0:T(8,128)(2,1)} %bitcast.100, bf16[1536,512]{1,0:T(8,128)(2,1)} %pad_maximum_fusion.weight, bf16[512,1536]{1,0:T(8,128)(2,1)} %copy-done.7, ...), custom_call_target="tpu_custom_call" | custom-call | flops 3221225472 | bytes 31457280 | tf_op jit(solution)/shard_map/pallas_call | solution.py:724
  655.7 25.3 %collective-permute-done.29 = bf16[4,192,1024]{2,1,0:T(8,128)(2,1)} collective-permute-done((bf16[4,192,1024]{2,1,0:T(8,128)(2,1)}, bf16[4,192,1024]{2,1,0:T(8,128)(2,1)}, u32[]{:S(2)}, u32[]{:S(2)}) %collective-permute-start.29) | collective-permute-done | bytes 1572896 | tf_op jit(solution)/shard_map/ppermute | solution.py:21
  686.0 7.6 collective-permute-done.24
  702.2 5.7 collective-permute-done.25
  722.1 13.5 %collective-permute-done.31.refs_2_ = bf16[512,1536]{1,0:T(8,128)(2,1)} collective-permute-done((bf16[512,1536]{1,0:T(8,128)(2,1)S(1)}, bf16[512,1536]{1,0:T(8,128)(2,1)}, u32[]{:S(2)}, u32[]{:S(2)}) %collective-permute-start.31) | collective-permute-done | bytes 1572896 | tf_op jit(solution)/shard_map/ppermute | solution.py:21
  749.8 5.9 shard_map.234
  (227 shorter events, 142.6 us)
Async XLA Ops:
  7.2 126.8 %all-gather.7.cloned.1.call-start = ((), (), s32[]{:S(2)}) async-start(), calls=%async_computation.10 | async-start | bytes 4423680 | tf_op jit(solution)/shard_map/all_gather | solution.py:1451
  14.9 40.0 %collective-permute-start = (bf16[512,1536]{1,0:T(8,128)(2,1)}, bf16[512,1536]{1,0:T(8,128)(2,1)S(1)}, u32[]{:S(2)}, u32[]{:S(2)}) collective-permute-start(bf16[512,1536]{1,0:T(8,128)(2,1)} %get-tuple-element.261), channel_id=1, source_target_pairs={{0,0},{1,17},{2,10},{3,27},{8,8},{9,25},{10,18},{11,3},{16,16},{17... | collective-permute-start | bytes 4718600 | tf_op jit(solution)/shard_map/ppermute | solution.py:1414
  54.9 176.0 %all-gather.9.cloned.1.call-start = ((), (), s32[]{:S(2)}) async-start(), calls=%async_computation.11 | async-start | bytes 5898240 | tf_op jit(solution)/shard_map/all_gather | solution.py:1451
  55.0 34.7 %collective-permute-start.2 = (bf16[512,1536]{1,0:T(8,128)(2,1)S(1)}, bf16[512,1536]{1,0:T(8,128)(2,1)S(1)}, u32[]{:S(2)}, u32[]{:S(2)}) collective-permute-start(bf16[512,1536]{1,0:T(8,128)(2,1)S(1)} %collective-permute-done.x0.own_in), channel_id=1, source_target_pairs={{0,2},{1,3},{2,0},{3,1},{4,6},{5,7},{6,4},{7,5},{8,10},{9,11},{10,... | collective-permute-start | bytes 4718600 | tf_op jit(solution)/shard_map/ppermute | solution.py:21
  56.9 35.0 %collective-permute-start.5 = (bf16[192,3456]{1,0:T(8,128)(2,1)}, bf16[192,3456]{1,0:T(8,128)(2,1)S(1)}, u32[]{:S(2)}, u32[]{:S(2)}) collective-permute-start(bf16[192,3456]{1,0:T(8,128)(2,1)} %copy-done.28), channel_id=1, source_target_pairs={{0,4},{4,0},{1,5},{5,1},{2,6},{6,2},{3,7},{7,3},{8,12},{12,8},{9,1... | collective-permute-start | bytes 3981320 | tf_op jit(solution)/shard_map/ppermute | solution.py:21
  95.2 257.1 %all-gather.11.cloned.1.call-start = ((), (), s32[]{:S(2)}) async-start(), calls=%async_computation.12 | async-start | bytes 7372800 | tf_op jit(solution)/shard_map/all_gather | solution.py:1451
  95.3 36.2 %collective-permute-start.6 = (bf16[512,1536]{1,0:T(8,128)(2,1)}, bf16[512,1536]{1,0:T(8,128)(2,1)}, u32[]{:S(2)}, u32[]{:S(2)}) collective-permute-start(bf16[512,1536]{1,0:T(8,128)(2,1)} %get-tuple-element.82), channel_id=1, source_target_pairs={{0,4},{4,0},{1,5},{5,1},{2,6},{6,2},{3,7},{7,3},{8,12},{12,8},{9,1... | collective-permute-start | bytes 4718600 | tf_op jit(solution)/shard_map/ppermute | solution.py:21
  96.6 37.3 %collective-permute-start.1 = (bf16[512,1536]{1,0:T(8,128)(2,1)S(1)}, bf16[512,1536]{1,0:T(8,128)(2,1)S(1)}, u32[]{:S(2)}, u32[]{:S(2)}) collective-permute-start(bf16[512,1536]{1,0:T(8,128)(2,1)S(1)} %collective-permute-done.x0.own_in), channel_id=1, source_target_pairs={{0,1},{1,0},{2,3},{3,2},{4,5},{5,4},{6,7},{7,6},{8,9},{9,8},{10,11... | collective-permute-start | bytes 4718600 | tf_op jit(solution)/shard_map/ppermute | solution.py:21
  131.5 35.2 %collective-permute-start.8 = (bf16[512,1536]{1,0:T(8,128)(2,1)}, bf16[512,1536]{1,0:T(8,128)(2,1)}, u32[]{:S(2)}, u32[]{:S(2)}) collective-permute-start(bf16[512,1536]{1,0:T(8,128)(2,1)} %collective-permute-done.6.refs_0_), channel_id=1, source_target_pairs={{0,2},{1,3},{2,0},{3,1},{4,6},{5,7},{6,4},{7,5},{8,10},{9,11},{10,... | collective-permute-start | bytes 4718600 | tf_op jit(solution)/shard_map/ppermute | solution.py:21
  133.9 326.3 %reduce-scatter.6.cloned.1.call-start = ((), (), s32[]{:S(2)}) async-start(), calls=%async_computation.5 | async-start | bytes 5898240 | tf_op jit(solution)/shard_map/reduce_scatter | solution.py:1696
  166.7 64.2 %collective-permute-start.12 = (bf16[512,1536]{1,0:T(8,128)(2,1)}, bf16[512,1536]{1,0:T(8,128)(2,1)}, u32[]{:S(2)}, u32[]{:S(2)}) collective-permute-start(bf16[512,1536]{1,0:T(8,128)(2,1)} %collective-permute-done.8.refs_2_), channel_id=1, source_target_pairs={{0,1},{1,0},{2,3},{3,2},{4,5},{5,4},{6,7},{7,6},{8,9},{9,8},{10,11... | collective-permute-start | bytes 4718600 | tf_op jit(solution)/shard_map/ppermute | solution.py:21
  168.6 62.3 %collective-permute-start.11 = (bf16[512,1536]{1,0:T(8,128)(2,1)}, bf16[512,1536]{1,0:T(8,128)(2,1)}, u32[]{:S(2)}, u32[]{:S(2)}) collective-permute-start(bf16[512,1536]{1,0:T(8,128)(2,1)} %collective-permute-done.6.refs_0_), channel_id=1, source_target_pairs={{0,1},{1,0},{2,3},{3,2},{4,5},{5,4},{6,7},{7,6},{8,9},{9,8},{10,11... | collective-permute-start | bytes 4718600 | tf_op jit(solution)/shard_map/ppermute | solution.py:21
  225.4 35.6 %collective-permute-start.14 = (bf16[512,1536]{1,0:T(8,128)(2,1)}, bf16[512,1536]{1,0:T(8,128)(2,1)}, u32[]{:S(2)}, u32[]{:S(2)}) collective-permute-start(bf16[512,1536]{1,0:T(8,128)(2,1)} %get-tuple-element.88.refs_0_), channel_id=1, source_target_pairs={{0,4},{4,0},{1,5},{5,1},{2,6},{6,2},{3,7},{7,3},{8,12},{12,8},{9,1... | collective-permute-start | bytes 4718600 | tf_op jit(solution)/shard_map/ppermute | solution.py:21
  227.7 35.7 %collective-permute-start.10 = (bf16[512,1536]{1,0:T(8,128)(2,1)}, bf16[512,1536]{1,0:T(8,128)(2,1)}, u32[]{:S(2)}, u32[]{:S(2)}) collective-permute-start(bf16[512,1536]{1,0:T(8,128)(2,1)} %get-tuple-element.88.refs_0_), channel_id=1, source_target_pairs={{0,2},{1,3},{2,0},{3,1},{4,6},{5,7},{6,4},{7,5},{8,10},{9,11},{10,... | collective-permute-start | bytes 4718600 | tf_op jit(solution)/shard_map/ppermute | solution.py:21
  228.9 44.5 %collective-permute-start.16 = (bf16[512,1536]{1,0:T(8,128)(2,1)}, bf16[512,1536]{1,0:T(8,128)(2,1)}, u32[]{:S(2)}, u32[]{:S(2)}) collective-permute-start(bf16[512,1536]{1,0:T(8,128)(2,1)} %get-tuple-element.88.refs_0_), channel_id=1, source_target_pairs={{0,1},{1,0},{2,3},{3,2},{4,5},{5,4},{6,7},{7,6},{8,9},{9,8},{10,11... | collective-permute-start | bytes 4718600 | tf_op jit(solution)/shard_map/ppermute | solution.py:21
  352.2 220.4 %reduce-scatter.8.cloned.1.call-start = ((), (), s32[]{:S(2)}) async-start(), calls=%async_computation.6 | async-start | bytes 2457600 | tf_op jit(solution)/shard_map/reduce_scatter | solution.py:1696
  460.2 112.5 %reduce-scatter.10.cloned.1.call-start = ((), (), s32[]{:S(2)}) async-start(), calls=%async_computation.7 | async-start | bytes 2457600 | tf_op jit(solution)/shard_map/reduce_scatter | solution.py:1696
  460.8 128.9 %reduce-scatter.12.cloned.1.call-start = ((), (), s32[]{:S(2)}) async-start(), calls=%async_computation.8 | async-start | bytes 2457600 | tf_op jit(solution)/shard_map/reduce_scatter | solution.py:1696
  516.0 227.0 %reduce-scatter.14.cloned.1.call-start = ((), (), s32[]{:S(2)}) async-start(), calls=%async_computation.9 | async-start | bytes 1966080 | tf_op jit(solution)/shard_map/reduce_scatter | solution.py:1754
  649.7 49.8 %collective-permute-start.28 = (bf16[512,1536]{1,0:T(8,128)(2,1)}, bf16[512,1536]{1,0:T(8,128)(2,1)S(1)}, u32[]{:S(2)}, u32[]{:S(2)}) collective-permute-start(bf16[512,1536]{1,0:T(8,128)(2,1)} %get-tuple-element.138), channel_id=1, source_target_pairs={{0,0},{17,1},{10,2},{27,3},{8,8},{25,9},{18,10},{3,11},{16,16},{1,... | collective-permute-start | bytes 4718600 | tf_op jit(solution)/shard_map/ppermute | solution.py:1760
  655.3 38.3 %collective-permute-start.24 = (bf16[192,1536]{1,0:T(8,128)(2,1)}, bf16[192,1536]{1,0:T(8,128)(2,1)}, u32[]{:S(2)}, u32[]{:S(2)}) collective-permute-start(bf16[192,1536]{1,0:T(8,128)(2,1)} %get-tuple-element.133), channel_id=1, source_target_pairs={{0,4},{4,0},{1,5},{5,1},{2,6},{6,2},{3,7},{7,3},{8,12},{12,8},{9,1... | collective-permute-start | bytes 1769480 | tf_op jit(solution)/shard_map/ppermute | solution.py:21
  655.7 53.5 %collective-permute-start.22 = (bf16[512,1536]{1,0:T(8,128)(2,1)S(1)}, bf16[512,1536]{1,0:T(8,128)(2,1)}, u32[]{:S(2)}, u32[]{:S(2)}) collective-permute-start(bf16[512,1536]{1,0:T(8,128)(2,1)S(1)} %copy-done.2), channel_id=1, source_target_pairs={{0,2},{1,3},{2,0},{3,1},{4,6},{5,7},{6,4},{7,5},{8,10},{9,11},{10,... | collective-permute-start | bytes 4718600 | tf_op jit(solution)/shard_map/ppermute | solution.py:21
  694.8 43.2 %collective-permute-start.21 = (bf16[512,1536]{1,0:T(8,128)(2,1)S(1)}, bf16[512,1536]{1,0:T(8,128)(2,1)S(1)}, u32[]{:S(2)}, u32[]{:S(2)}) collective-permute-start(bf16[512,1536]{1,0:T(8,128)(2,1)S(1)} %copy-done.2), channel_id=1, source_target_pairs={{0,1},{1,0},{2,3},{3,2},{4,5},{5,4},{6,7},{7,6},{8,9},{9,8},{10,11... | collective-permute-start | bytes 4718600 | tf_op jit(solution)/shard_map/ppermute | solution.py:21
  699.6 36.1 %collective-permute-start.31 = (bf16[512,1536]{1,0:T(8,128)(2,1)S(1)}, bf16[512,1536]{1,0:T(8,128)(2,1)}, u32[]{:S(2)}, u32[]{:S(2)}) collective-permute-start(bf16[512,1536]{1,0:T(8,128)(2,1)S(1)} %collective-permute-done.28.refs_0_), channel_id=1, source_target_pairs={{0,2},{1,3},{2,0},{3,1},{4,6},{5,7},{6,4},{7,5},{8,10},{9,11},{10,... | collective-permute-start | bytes 4718600 | tf_op jit(solution)/shard_map/ppermute | solution.py:21
  (54 other events, 590.9 us)
Sparse Core Ops, SparseCore 0:
  55.1 71.4 all-gather.6
  128.7 88.1 all-gather.8
  218.5 107.5 all-gather.10
  352.4 85.7 reduce-scatter.5
  460.3 43.3 reduce-scatter.7
  505.9 40.6 reduce-scatter.9
  548.9 40.6 reduce-scatter.11
  684.9 41.6 reduce-scatter.13

commit v10 on v9

--- a/solution.py
+++ b/solution.py
@@ -1451,7 +1451,7 @@
             full = lax.all_gather(after(both, *earlier), "fsdp", axis=0, tiled=False)
             return full.reshape(-1, both.shape[-1])
 
-        first_units = half_units // 2 // 256 * 256
+        first_units = half_units - half_units // 2 // 256 * 256
         first_cols = 3 * first_units
 
         def in_parts(c):
@@ -1759,26 +1759,29 @@
     def leave(share):
         return lax.ppermute(share, ("fsdp", "tp"), back)
 
-    def arrive(own, order):
+    def arrive(own):
         far = from_partner(own, "tp", 2)
         near = from_partner(own, "tp", 1)
-        return place_rows((own, near, far, from_partner(far, "tp", 1)), order)
+        return (own, near, far, from_partner(far, "tp", 1))
 
     input_home = leave(input_share)
     if not split:
         block_home = leave(block_share)
-    block_out = arrive(block_home, home_order)
+    block_out = place_rows(arrive(block_home), home_order)
     if split:
 
         def unit_end(total, *earlier):
             kept, sent = scatter_ctx(total.reshape(1, ctx_count, -1, total.shape[1]), ctx_rank)
             return kept[0], from_partner(after(sent[0], *earlier), "ctx", 1)
 
-        own_a, got_a = unit_end(unit_sums[0], grad_branch)
-        ends = [unit_end(t, line_grad) for t in unit_sums[1:]]
         input_home = after(input_home, attn_held)
+        input_rows = arrive(input_home)
+        own_a, got_a = unit_end(unit_sums[0], input_rows[1])
+        ends = [unit_end(t, input_rows[1]) for t in unit_sums[1:]]
         home_order = after(home_order, got_a, *[end[1] for end in ends])
-    input_grad = arrive(input_home, home_order)
+    else:
+        input_rows = arrive(input_home)
+    input_grad = place_rows(input_rows, home_order)
 
     small_at = query_cols + head_dim + query_cols
     tiny_grad = attn_end[:, small_at:].astype(WIDE)

time: 773 us -> 764 us (0.988)
  starting transfers between devices: 51.8 us -> 42.9 us
  waiting for transfers between devices: 193 us -> 185 us
    pallas_call x1, Pallas kernels: 36.6 us -> 26.7 us  [full_units(): pl.pallas_call(full_units_kernel, grid=(tokens // step,), in_specs=[by_ro...]
    reduce_scatter x4, waiting for transfers between devices: 17 us -> 7.13 us  [scatter_units(): return lax.psum_scatter(grad, 'fsdp', scatter_dimension=0, tiled=True)]
    ppermute x29, starting transfers between devices: 37.2 us -> 27.7 us  [from_partner(): return lax.ppermute(value, axis, pairs)]
    pallas_call x1, Pallas kernels: 33.5 us -> 41.7 us  [first_grads(): pl.pallas_call(first_grads_kernel, grid=(3, tiles), in_specs=[pl.BlockSpe...]
  transfers between devices with their start and end apart: 41 -> 41, of which waited for: 18 -> 18; matrix products, arithmetic and copies ran while one was open for 7% -> 6% of each run, Pallas kernels for 49% -> 51%
where the time goes in v10:
time: 764 us; the launch traced here: 754 us
  Pallas kernels  440 us (58%)
  waiting for transfers between devices  185 us (24%)
  starting transfers between devices  42.9 us (6%)
  other arithmetic  35.3 us (5%)
  local copies, waits for them, and re-layouts  33.3 us (4%)
  between operations  16.9 us (2%)
    ppermute x29, waiting for transfers between devices, from_partner(): return lax.ppermute(value, axis, pairs)  158 us
    pallas_call x1, Pallas kernels, collect_back(): pl.pallas_call(functools.partial(collect_kernel, slots, tiles), grid=(slo...  70.8 us
    pallas_call x1, Pallas kernels, attend_exchange(): pl.pallas_call(functools.partial(exchange_kernel, heads, head_dim, scale,...  56.9 us
    pallas_call x1, Pallas kernels, spread_branch(): pl.pallas_call(functools.partial(branch_kernel, slots, tiles), grid=(slot...  54.7 us
    pallas_call x1, Pallas kernels, attend_sum(): pl.pallas_call(functools.partial(attend_sum_kernel, heads, head_dim, scal...  52.4 us
    pallas_call x1, Pallas kernels, finish_rows(): pl.pallas_call(functools.partial(line_kernel, slots, tiles), grid=(slots...  52 us
    pallas_call x1, Pallas kernels, first_grads(): pl.pallas_call(first_grads_kernel, grid=(3, tiles), in_specs=[pl.BlockSpe...  41.7 us
    ppermute x29, starting transfers between devices, from_partner(): return lax.ppermute(value, axis, pairs)  27.7 us
  transfers between devices with their start and end apart: 41, of which 18 were waited for; matrix products, arithmetic and copies ran while one was open for 6% of the time, Pallas kernels for 51%

profile of v10, /device:TPU:1, one launch (start us, length us, event | category | flops | bytes accessed | tf_op | source)
XLA Modules:
  0.0 754.1 jit_solution(12309160785846409599)
XLA Ops:
  14.9 5.2 collective-permute-start
  31.0 5.6 fusion.3
  37.8 9.1 %collective-permute-done.4 = bf16[192,1152]{1,0:T(8,128)(2,1)S(1)} collective-permute-done((bf16[192,1152]{1,0:T(8,128)(2,1)S(1)}, bf16[192,1152]{1,0:T(8,128)(2,1)S(1)}, u32[]{:S(2)}, u32[]{:S(2)}) %collective-permute-start.4) | collective-permute-done | bytes 442400 | tf_op jit(solution)/shard_map/ppermute | solution.py:21
  48.1 6.8 collective-permute-done.x0.own_in
  58.8 30.9 %collective-permute-done.2.x2 = bf16[512,1536]{1,0:T(8,128)(2,1)S(1)} collective-permute-done((bf16[512,1536]{1,0:T(8,128)(2,1)S(1)}, bf16[512,1536]{1,0:T(8,128)(2,1)S(1)}, u32[]{:S(2)}, u32[]{:S(2)}) %collective-permute-start.2) | collective-permute-done | bytes 1572896 | tf_op jit(solution)/shard_map/ppermute | solution.py:21
  98.0 34.1 %collective-permute-done.6.refs_0_ = bf16[512,1536]{1,0:T(8,128)(2,1)} collective-permute-done((bf16[512,1536]{1,0:T(8,128)(2,1)}, bf16[512,1536]{1,0:T(8,128)(2,1)}, u32[]{:S(2)}, u32[]{:S(2)}) %collective-permute-start.6) | collective-permute-done | bytes 1572896 | tf_op jit(solution)/shard_map/ppermute | solution.py:21
  136.7 13.0 %shard_map.221 = (bf16[4,512,1536]{2,1,0:T(8,128)(2,1)}, bf16[4,512,384]{2,1,0:T(8,128)(2,1)}, bf16[4,512,128]{2,1,0:T(8,128)(2,1)}, bf16[4,512,128]{2,1,0:T(8,128)(2,1)}) custom-call(bf16[512,1536]{1,0:T(8,128)(2,1)} %copy-done.8, bf16[512,1536]{1,0:T(8,128)(2,1)} %copy-done.13, bf16[512,1536]{1,0:T(8,128)(2,1)} %copy-done.12, ...), custom_call_target="tpu_custom_call" | custom-call | flops 4026531840 | bytes 17170432 | tf_op jit(solution)/shard_map/pallas_call | solution.py:840
  156.1 11.5 %collective-permute-done.8.refs_2_ = bf16[512,1536]{1,0:T(8,128)(2,1)} collective-permute-done((bf16[512,1536]{1,0:T(8,128)(2,1)}, bf16[512,1536]{1,0:T(8,128)(2,1)}, u32[]{:S(2)}, u32[]{:S(2)}) %collective-permute-start.8) | collective-permute-done | bytes 1572896 | tf_op jit(solution)/shard_map/ppermute | solution.py:21
  175.4 52.4 %shard_map.222 = (bf16[4,512,384]{2,1,0:T(8,128)(2,1)}, f32[4,512,128]{2,1,0:T(8,128)}, f32[512,1536]{1,0:T(8,128)}, bf16[512,1536]{1,0:T(8,128)(2,1)}) custom-call(s32[8]{0:T(128)} %compare_select_fusion.14.info, bf16[4,512,384]{2,1,0:T(8,128)(2,1)} %get-tuple-element.84.q, bf16[4,512,128]{2,1,0:T(8,128)(2,1)} %copy-done.20, ...), custom_call_target="tpu_custom_call" | custom-call | flops 3221225472 | bytes 3145728 | tf_op jit(solution)/shard_map/pallas_call | solution.py:1148
  236.5 18.6 %shard_map.223 = (bf16[4096,640]{1,0:T(8,128)(2,1)}, bf16[4096,1536]{1,0:T(8,128)(2,1)}) custom-call(s32[8]{0:T(128)} %compare_select_fusion.13.info, bf16[4,512,1536]{2,1,0:T(8,128)(2,1)} %cotangent, bf16[512,1536]{1,0:T(8,128)(2,1)} %collective-permute-done.6.refs_0_, bf16[512,1536]{1,0:T(8,128)(2,1)} %collective-permute-done.11.refs_1_, ...), custom_call_target="tpu_custom_call" | custom-call | flops 8053063680 | bytes 32374784 | tf_op jit(solution)/shard_map/pallas_call | solution.py:230
  255.1 8.4 %collective-permute-done.14.refs_4_ = bf16[512,1536]{1,0:T(8,128)(2,1)} collective-permute-done((bf16[512,1536]{1,0:T(8,128)(2,1)}, bf16[512,1536]{1,0:T(8,128)(2,1)}, u32[]{:S(2)}, u32[]{:S(2)}) %collective-permute-start.14) | collective-permute-done | bytes 1572896 | tf_op jit(solution)/shard_map/ppermute | solution.py:21
  275.3 14.5 %shard_map.224 = (bf16[4096,640]{1,0:T(8,128)(2,1)}, bf16[4096,1536]{1,0:T(8,128)(2,1)}) custom-call(bf16[512,1536]{1,0:T(8,128)(2,1)} %get-tuple-element.88.refs_0_, bf16[512,1536]{1,0:T(8,128)(2,1)} %collective-permute-done.16.refs_1_, bf16[512,1536]{1,0:T(8,128)(2,1)} %collective-permute-done.10.refs_2_, ...), custom_call_target="tpu_custom_call" | custom-call | flops 6039797760 | bytes 24772608 | tf_op jit(solution)/shard_map/pallas_call | solution.py:123
  298.0 6.8 shard_map.225
  304.8 20.9 %shard_map.226 = (bf16[4096,640]{1,0:T(8,128)(2,1)}, bf16[4096,640]{1,0:T(8,128)(2,1)}, bf16[4096,640]{1,0:T(8,128)(2,1)}) custom-call(bf16[4096,1536]{1,0:T(8,128)(2,1)} %get-tuple-element.107.h.right.turned, bf16[1536,1920]{1,0:T(8,128)(2,1)} %bitcast.87, bf16[4096,640]{1,0:T(8,128)(2,1)} %get-tuple-element.102.gate, bf16[4096,640]{1,0:T(8,128)(2,1)} %get-tuple-element.93.grad), custom_call_target="tpu_custom_call" | custom-call | flops 8053063680 | bytes 40763392 | tf_op jit(solution)/shard_map/pallas_call | solution.py:161
  325.7 41.7 %shard_map.227 = bf16[1536,1920]{1,0:T(8,128)(2,1)} custom-call(bf16[4096,1536]{1,0:T(8,128)(2,1)} %get-tuple-element.105.g.left.own_grad, bf16[4096,1536]{1,0:T(8,128)(2,1)} %get-tuple-element.107.h.right.turned, bf16[4096,640]{1,0:T(8,128)(2,1)} %get-tuple-element.106.hid.hid_a, bf16[4096,640]{1,0:T(8,128)(2,1)} %get-tuple-element.103.gate.gate_a, ...), custom_call_target="tpu_custom_call" | custom-call | flops 24159191040 | bytes 21626880 | tf_op jit(solution)/shard_map/pallas_call | solution.py:298
  367.4 26.7 %shard_map.228 = (bf16[4096,512]{1,0:T(8,128)(2,1)}, bf16[4096,512]{1,0:T(8,128)(2,1)}, bf16[4096,512]{1,0:T(8,128)(2,1)}) custom-call(bf16[4096,1536]{1,0:T(8,128)(2,1)} %get-tuple-element.107.h.right.turned, bf16[4096,1536]{1,0:T(8,128)(2,1)} %get-tuple-element.105.g.left.own_grad, bf16[1536,1536]{1,0:T(8,128)(2,1)} %bitcast.91, ...), custom_call_target="tpu_custom_call" | custom-call | flops 19327352832 | bytes 42467328 | tf_op jit(solution)/shard_map/pallas_call | solution.py:272
  394.2 70.8 %shard_map.229 = (f32[512,1536]{1,0:T(8,128)}, bf16[1536,512]{1,0:T(8,128)(2,1)}, bf16[1536,512]{1,0:T(8,128)(2,1)}) custom-call(bf16[4096,640]{1,0:T(8,128)(2,1)} %get-tuple-element.103.gate.gate_a, bf16[4096,640]{1,0:T(8,128)(2,1)} %get-tuple-element.104.up.up_a, bf16[4096,512]{1,0:T(8,128)(2,1)} %get-tuple-element.109.gate_b.gate, ...), custom_call_target="tpu_custom_call" | custom-call | flops 19327352832 | bytes 20971520 | tf_op jit(solution)/shard_map/pallas_call | solution.py:439
  465.0 7.1 reduce-scatter.6.cloned.1.call-done
  472.7 54.7 %shard_map.230 = (f32[512,1536]{1,0:T(8,128)}, f32[1,1536]{1,0:T(1,128)}, bf16[1536,512]{1,0:T(8,128)(2,1)}, bf16[4,512,1536]{2,1,0:T(8,128)(2,1)}, bf16[512,153...) custom-call(f32[512,1536]{1,0:T(8,128)} %get-tuple-element.112.total, ...), custom_call_target="tpu_custom_call" | custom-call | flops 12884901888 | bytes 20971520 | tf_op jit(solution)/shard_map/pallas_call | solution.py:577
  527.5 56.9 %shard_map.231 = (bf16[4,512,512]{2,1,0:T(8,128)(2,1)}, bf16[1536,384]{1,0:T(8,128)(2,1)}, bf16[512,1536]{1,0:T(8,128)(2,1)}) custom-call(s32[8]{0:T(128)} %compare_select_fusion.14.info, bf16[4,512,384]{2,1,0:T(8,128)(2,1)} %get-tuple-element.84.q, bf16[4,512,128]{2,1,0:T(8,128)(2,1)} %copy-done.20, bf16[4,512,128]{2,1,0:T(8,128)(2,1)} %copy-done.21, ...), custom_call_target="tpu_custom_call" | custom-call | flops 2415919104 | bytes 7864320 | tf_op jit(solution)/shard_map/pallas_call | solution.py:1300
  584.5 52.0 %shard_map.232 = (bf16[512,1536]{1,0:T(8,128)(2,1)}, f32[2,1536]{1,0:T(2,128)}, bf16[1536,512]{1,0:T(8,128)(2,1)}, f32[1,512]{1,0:T(1,128)}, bf16[512,1536]{1,0:T(8,128)(2,1)}) custom-call(bf16[2048,512]{1,0:T(8,128)(2,1)} %bitcast.106, bf16[1536,512]{1,0:T(8,128)(2,1)} %pad_maximum_fusion.weight, bf16[512,1536]{1,0:T(8,128)(2,1)} %copy-done.8, ...), custom_call_target="tpu_custom_call" | custom-call | flops 3221225472 | bytes 31457280 | tf_op jit(solution)/shard_map/pallas_call | solution.py:724
  648.3 26.7 %collective-permute-done.25 = bf16[4,192,1024]{2,1,0:T(8,128)(2,1)S(1)} collective-permute-done((bf16[4,192,1024]{2,1,0:T(8,128)(2,1)}, bf16[4,192,1024]{2,1,0:T(8,128)(2,1)S(1)}, u32[]{:S(2)}, u32[]{:S(2)}) %collective-permute-start.25) | collective-permute-done | bytes 1572896 | tf_op jit(solution)/shard_map/ppermute | solution.py:21
  690.9 29.9 %collective-permute-done.31.refs_2_ = bf16[512,1536]{1,0:T(8,128)(2,1)} collective-permute-done((bf16[512,1536]{1,0:T(8,128)(2,1)S(1)}, bf16[512,1536]{1,0:T(8,128)(2,1)}, u32[]{:S(2)}, u32[]{:S(2)}) %collective-permute-start.31) | collective-permute-done | bytes 1572896 | tf_op jit(solution)/shard_map/ppermute | solution.py:21
  721.7 6.4 shard_map.233
  (229 shorter events, 126.5 us)
Async XLA Ops:
  7.2 128.4 %all-gather.7.cloned.1.call-start = ((), (), s32[]{:S(2)}) async-start(), calls=%async_computation.10 | async-start | bytes 4423680 | tf_op jit(solution)/shard_map/all_gather | solution.py:1451
  14.9 40.0 %collective-permute-start = (bf16[512,1536]{1,0:T(8,128)(2,1)}, bf16[512,1536]{1,0:T(8,128)(2,1)S(1)}, u32[]{:S(2)}, u32[]{:S(2)}) collective-permute-start(bf16[512,1536]{1,0:T(8,128)(2,1)} %get-tuple-element.261), channel_id=1, source_target_pairs={{0,0},{1,17},{2,10},{3,27},{8,8},{9,25},{10,18},{11,3},{16,16},{17... | collective-permute-start | bytes 4718600 | tf_op jit(solution)/shard_map/ppermute | solution.py:1414
  54.9 181.6 %all-gather.9.cloned.1.call-start = ((), (), s32[]{:S(2)}) async-start(), calls=%async_computation.11 | async-start | bytes 7372800 | tf_op jit(solution)/shard_map/all_gather | solution.py:1451
  56.2 35.6 %collective-permute-start.5 = (bf16[192,3456]{1,0:T(8,128)(2,1)}, bf16[192,3456]{1,0:T(8,128)(2,1)S(1)}, u32[]{:S(2)}, u32[]{:S(2)}) collective-permute-start(bf16[192,3456]{1,0:T(8,128)(2,1)} %get-tuple-element.81), channel_id=1, source_target_pairs={{0,4},{4,0},{1,5},{5,1},{2,6},{6,2},{3,7},{7,3},{8,12},{12,8},{9,1... | collective-permute-start | bytes 3981320 | tf_op jit(solution)/shard_map/ppermute | solution.py:21
  95.7 271.7 %all-gather.11.cloned.1.call-start = ((), (), s32[]{:S(2)}) async-start(), calls=%async_computation.12 | async-start | bytes 5898240 | tf_op jit(solution)/shard_map/all_gather | solution.py:1451
  95.7 36.4 %collective-permute-start.6 = (bf16[512,1536]{1,0:T(8,128)(2,1)}, bf16[512,1536]{1,0:T(8,128)(2,1)}, u32[]{:S(2)}, u32[]{:S(2)}) collective-permute-start(bf16[512,1536]{1,0:T(8,128)(2,1)} %get-tuple-element.82), channel_id=1, source_target_pairs={{0,4},{4,0},{1,5},{5,1},{2,6},{6,2},{3,7},{7,3},{8,12},{12,8},{9,1... | collective-permute-start | bytes 4718600 | tf_op jit(solution)/shard_map/ppermute | solution.py:21
  97.1 38.5 %collective-permute-start.1 = (bf16[512,1536]{1,0:T(8,128)(2,1)S(1)}, bf16[512,1536]{1,0:T(8,128)(2,1)S(1)}, u32[]{:S(2)}, u32[]{:S(2)}) collective-permute-start(bf16[512,1536]{1,0:T(8,128)(2,1)S(1)} %collective-permute-done.x0.own_in), channel_id=1, source_target_pairs={{0,1},{1,0},{2,3},{3,2},{4,5},{5,4},{6,7},{7,6},{8,9},{9,8},{10,11... | collective-permute-start | bytes 4718600 | tf_op jit(solution)/shard_map/ppermute | solution.py:21
  132.1 35.4 %collective-permute-start.8 = (bf16[512,1536]{1,0:T(8,128)(2,1)}, bf16[512,1536]{1,0:T(8,128)(2,1)}, u32[]{:S(2)}, u32[]{:S(2)}) collective-permute-start(bf16[512,1536]{1,0:T(8,128)(2,1)} %collective-permute-done.6.refs_0_), channel_id=1, source_target_pairs={{0,2},{1,3},{2,0},{3,1},{4,6},{5,7},{6,4},{7,5},{8,10},{9,11},{10,... | collective-permute-start | bytes 4718600 | tf_op jit(solution)/shard_map/ppermute | solution.py:21
  167.5 65.6 %collective-permute-start.11 = (bf16[512,1536]{1,0:T(8,128)(2,1)}, bf16[512,1536]{1,0:T(8,128)(2,1)}, u32[]{:S(2)}, u32[]{:S(2)}) collective-permute-start(bf16[512,1536]{1,0:T(8,128)(2,1)} %collective-permute-done.6.refs_0_), channel_id=1, source_target_pairs={{0,1},{1,0},{2,3},{3,2},{4,5},{5,4},{6,7},{7,6},{8,9},{9,8},{10,11... | collective-permute-start | bytes 4718600 | tf_op jit(solution)/shard_map/ppermute | solution.py:21
  169.2 63.9 %collective-permute-start.12 = (bf16[512,1536]{1,0:T(8,128)(2,1)}, bf16[512,1536]{1,0:T(8,128)(2,1)}, u32[]{:S(2)}, u32[]{:S(2)}) collective-permute-start(bf16[512,1536]{1,0:T(8,128)(2,1)} %collective-permute-done.8.refs_2_), channel_id=1, source_target_pairs={{0,1},{1,0},{2,3},{3,2},{4,5},{5,4},{6,7},{7,6},{8,9},{9,8},{10,11... | collective-permute-start | bytes 4718600 | tf_op jit(solution)/shard_map/ppermute | solution.py:21
  227.8 35.7 %collective-permute-start.14 = (bf16[512,1536]{1,0:T(8,128)(2,1)}, bf16[512,1536]{1,0:T(8,128)(2,1)}, u32[]{:S(2)}, u32[]{:S(2)}) collective-permute-start(bf16[512,1536]{1,0:T(8,128)(2,1)} %get-tuple-element.88.refs_0_), channel_id=1, source_target_pairs={{0,4},{4,0},{1,5},{5,1},{2,6},{6,2},{3,7},{7,3},{8,12},{12,8},{9,1... | collective-permute-start | bytes 4718600 | tf_op jit(solution)/shard_map/ppermute | solution.py:21
  230.8 241.2 %reduce-scatter.6.cloned.1.call-start = ((), (), s32[]{:S(2)}) async-start(), calls=%async_computation.5 | async-start | bytes 7372800 | tf_op jit(solution)/shard_map/reduce_scatter | solution.py:1696
  231.1 44.2 %collective-permute-start.16 = (bf16[512,1536]{1,0:T(8,128)(2,1)}, bf16[512,1536]{1,0:T(8,128)(2,1)}, u32[]{:S(2)}, u32[]{:S(2)}) collective-permute-start(bf16[512,1536]{1,0:T(8,128)(2,1)} %get-tuple-element.88.refs_0_), channel_id=1, source_target_pairs={{0,1},{1,0},{2,3},{3,2},{4,5},{5,4},{6,7},{7,6},{8,9},{9,8},{10,11... | collective-permute-start | bytes 4718600 | tf_op jit(solution)/shard_map/ppermute | solution.py:21
  367.4 217.1 %reduce-scatter.10.cloned.1.call-start = ((), (), s32[]{:S(2)}) async-start(), calls=%async_computation.7 | async-start | bytes 1966080 | tf_op jit(solution)/shard_map/reduce_scatter | solution.py:1696
  472.1 112.4 %reduce-scatter.8.cloned.1.call-start = ((), (), s32[]{:S(2)}) async-start(), calls=%async_computation.6 | async-start | bytes 1966080 | tf_op jit(solution)/shard_map/reduce_scatter | solution.py:1696
  472.6 111.9 %reduce-scatter.12.cloned.1.call-start = ((), (), s32[]{:S(2)}) async-start(), calls=%async_computation.8 | async-start | bytes 1966080 | tf_op jit(solution)/shard_map/reduce_scatter | solution.py:1696
  527.5 205.2 %reduce-scatter.14.cloned.1.call-start = ((), (), s32[]{:S(2)}) async-start(), calls=%async_computation.9 | async-start | bytes 1966080 | tf_op jit(solution)/shard_map/reduce_scatter | solution.py:1754
  643.7 39.4 %collective-permute-start.24 = (bf16[512,1536]{1,0:T(8,128)(2,1)}, bf16[512,1536]{1,0:T(8,128)(2,1)S(1)}, u32[]{:S(2)}, u32[]{:S(2)}) collective-permute-start(bf16[512,1536]{1,0:T(8,128)(2,1)} %get-tuple-element.133), channel_id=1, source_target_pairs={{0,0},{17,1},{10,2},{27,3},{8,8},{25,9},{18,10},{3,11},{16,16},{1,... | collective-permute-start | bytes 4718600 | tf_op jit(solution)/shard_map/ppermute | solution.py:1760
  648.2 37.7 %collective-permute-start.22 = (bf16[512,1536]{1,0:T(8,128)(2,1)}, bf16[512,1536]{1,0:T(8,128)(2,1)}, u32[]{:S(2)}, u32[]{:S(2)}) collective-permute-start(bf16[512,1536]{1,0:T(8,128)(2,1)} %get-tuple-element.132.refs_0_), channel_id=1, source_target_pairs={{0,2},{1,3},{2,0},{3,1},{4,6},{5,7},{6,4},{7,5},{8,10},{9,11},{10,... | collective-permute-start | bytes 4718600 | tf_op jit(solution)/shard_map/ppermute | solution.py:21
  683.6 37.2 %collective-permute-start.31 = (bf16[512,1536]{1,0:T(8,128)(2,1)S(1)}, bf16[512,1536]{1,0:T(8,128)(2,1)}, u32[]{:S(2)}, u32[]{:S(2)}) collective-permute-start(bf16[512,1536]{1,0:T(8,128)(2,1)S(1)} %collective-permute-done.24.refs_0_), channel_id=1, source_target_pairs={{0,2},{1,3},{2,0},{3,1},{4,6},{5,7},{6,4},{7,5},{8,10},{9,11},{10,... | collective-permute-start | bytes 4718600 | tf_op jit(solution)/shard_map/ppermute | solution.py:21
  685.9 35.0 %collective-permute-start.23 = (bf16[512,1536]{1,0:T(8,128)(2,1)}, bf16[512,1536]{1,0:T(8,128)(2,1)}, u32[]{:S(2)}, u32[]{:S(2)}) collective-permute-start(bf16[512,1536]{1,0:T(8,128)(2,1)} %collective-permute-done.22.refs_2_), channel_id=1, source_target_pairs={{0,1},{1,0},{2,3},{3,2},{4,5},{5,4},{6,7},{7,6},{8,9},{9,8},{10,11... | collective-permute-start | bytes 4718600 | tf_op jit(solution)/shard_map/ppermute | solution.py:21
  688.7 39.5 %collective-permute-start.27 = (bf16[192,1920]{1,0:T(8,128)(2,1)S(1)}, bf16[192,1920]{1,0:T(8,128)(2,1)S(1)}, u32[]{:S(2)}, u32[]{:S(2)}) collective-permute-start(bf16[192,1920]{1,0:T(8,128)(2,1)S(1)} %get-tuple-element.139), channel_id=1, source_target_pairs={{0,4},{4,0},{1,5},{5,1},{2,6},{6,2},{3,7},{7,3},{8,12},{12,8},{9,1... | collective-permute-start | bytes 2211848 | tf_op jit(solution)/shard_map/ppermute | solution.py:21
  689.4 38.8 %collective-permute-start.28 = (bf16[192,512]{1,0:T(8,128)(2,1)S(1)}, bf16[192,512]{1,0:T(8,128)(2,1)S(1)}, u32[]{:S(2)}, u32[]{:S(2)}) collective-permute-start(bf16[192,512]{1,0:T(8,128)(2,1)S(1)} %get-tuple-element.140), channel_id=1, source_target_pairs={{0,4},{4,0},{1,5},{5,1},{2,6},{6,2},{3,7},{7,3},{8,12},{12,8},{9,1... | collective-permute-start | bytes 589832 | tf_op jit(solution)/shard_map/ppermute | solution.py:21
  690.4 37.8 %collective-permute-start.29 = (bf16[192,512]{1,0:T(8,128)(2,1)S(1)}, bf16[192,512]{1,0:T(8,128)(2,1)S(1)}, u32[]{:S(2)}, u32[]{:S(2)}) collective-permute-start(bf16[192,512]{1,0:T(8,128)(2,1)S(1)} %get-tuple-element.141), channel_id=1, source_target_pairs={{0,4},{4,0},{1,5},{5,1},{2,6},{6,2},{3,7},{7,3},{8,12},{12,8},{9,1... | collective-permute-start | bytes 589832 | tf_op jit(solution)/shard_map/ppermute | solution.py:21
  (55 other events, 569.8 us)
Sparse Core Ops, SparseCore 0:
  55.1 71.4 all-gather.6
  128.7 107.7 all-gather.8
  238.1 87.5 all-gather.10
  367.5 104.5 reduce-scatter.5
  474.2 35.5 reduce-scatter.9
  512.0 34.2 reduce-scatter.7
  548.6 34.2 reduce-scatter.11
  686.4 32.6 reduce-scatter.13

commit v11 on v10

--- a/solution.py
+++ b/solution.py
@@ -622,11 +622,13 @@
 
 
 def line_kernel(
-    slots, tiles, line, weight, own_in, grad_middle, gain, gain_two, rows_one, line_all, block, share,
-    gain_grad, attn_out, bias_out, home, parts, core_in, far_in, total, gains, gains_in, send, recv, load
+    slots, tiles, count, line, weight, own_in, grad_middle, gain, gain_two, rows_one, line_all, block, *refs
 ):
+    sums, (share, gain_grad, attn_out, bias_out, home) = refs[:count], refs[count : count + 5]
+    gots = refs[count + 5 : 2 * count + 5]
+    parts, core_in, far_in, total, gains, gains_in, send, recv, load = refs[2 * count + 5 :]
     step = pl.program_id(0)
-    core, far, _ = partners_of()
+    core, far, side = partners_of()
     tensor_rank, group = lax.axis_index("tp"), lax.axis_index("fsdp")
     shift = (tensor_rank % 2) * 2 + tensor_rank // 2
     target = {"fsdp": (group + slots - shift) % slots}
@@ -641,24 +643,32 @@
     gain_copies = [
         remote(gains, gains_in.at[i], 4 + i, partner) for i, partner in enumerate((core, far, cross))
     ]
+    rows = gots[0].shape[0]
+    there = pl.multiple_of((1 - lax.axis_index("ctx")) * rows, rows)
+    sides = [
+        remote(held.at[pl.ds(there, rows)], got, 7 + i, side) for i, (held, got) in enumerate(zip(sums, gots))
+    ]
 
     @pl.when(step == 0)
     def _():
         barrier = pltpu.get_barrier_semaphore()
-        for partner in (core, far, cross):
+        for partner in (core, far, cross, side):
             pl.semaphore_signal(barrier, inc=1, device_id=partner, device_id_type=MESH_ID)
 
         @pl.when(stays)
         def _():
-            pl.semaphore_wait(barrier, 3)
+            pl.semaphore_wait(barrier, 4)
             keep.start()
 
         @pl.when(jnp.logical_not(stays))
         def _():
             for partner in (target, source):
                 pl.semaphore_signal(barrier, inc=1, device_id=partner, device_id_type=MESH_ID)
-            pl.semaphore_wait(barrier, 5)
+            pl.semaphore_wait(barrier, 6)
             leave.start()
+
+        for copy in sides:
+            copy.start()
 
     @pl.when(step < slots)
     def _():
@@ -702,7 +712,9 @@
         for copy in gain_copies:
             copy.wait_recv()
         gain_grad[...] = (gains[...] + gains_in[0]) + (gains_in[1] + gains_in[2])
-        for copy in (*cores, to_far, *gain_copies):
+        for copy in sides:
+            copy.wait_recv()
+        for copy in (*cores, to_far, *gain_copies, *sides):
             copy.wait_send()
         pl.when(stays)(keep.wait)
 
@@ -712,7 +724,7 @@
             leave.wait_send()
 
 
-def finish_rows(line, weight, own_in, grad_middle, gain, gain_two, rows_one, block):
+def finish_rows(line, weight, own_in, grad_middle, gain, gain_two, rows_one, block, sums):
     length, width = own_in.shape
     near_tokens, line_cols = line.shape
     slots, tile = near_tokens // length, 256
@@ -722,7 +734,7 @@
     by_column = lambda n: pl.BlockSpec((n, tile), lambda i: (0, column(i)))
     attn_cols = line_cols
     return pl.pallas_call(
-        functools.partial(line_kernel, slots, tiles),
+        functools.partial(line_kernel, slots, tiles, len(sums)),
         grid=(slots + tiles,),
         in_specs=[
             pl.BlockSpec((length, line_cols), lambda i: (jnp.maximum(slots - 1 - i, 0), 0)),
@@ -734,21 +746,24 @@
             by_column(near_tokens),
             whole_spec(near_tokens, line_cols, once=True),
             ANYWHERE,
-        ],
+        ]
+        + [ANYWHERE] * len(sums),
         out_specs=[
             whole_spec(length, width),
             whole_spec(2, width),
             pl.BlockSpec((tile, attn_cols), lambda i: (column(i), 0)),
             whole_spec(1, line_cols),
             ANYWHERE,
-        ],
+        ]
+        + [ANYWHERE] * len(sums),
         out_shape=[
             jax.ShapeDtypeStruct((length, width), LOW),
             jax.ShapeDtypeStruct((2, width), WIDE),
             jax.ShapeDtypeStruct((width, attn_cols), LOW),
             jax.ShapeDtypeStruct((1, line_cols), WIDE),
             jax.ShapeDtypeStruct((length, width), LOW),
-        ],
+        ]
+        + [jax.ShapeDtypeStruct((t.shape[0] // 2, t.shape[1]), LOW) for t in sums],
         scratch_shapes=[
             pltpu.VMEM((slots, length, width), LOW),
             pltpu.VMEM((2, length, width), LOW),
@@ -756,15 +771,15 @@
             pltpu.VMEM((length, width), WIDE),
             pltpu.VMEM((2, width), WIDE),
             pltpu.VMEM((3, 2, width), WIDE),
-            pltpu.SemaphoreType.DMA((7,)),
-            pltpu.SemaphoreType.DMA((7,)),
+            pltpu.SemaphoreType.DMA((7 + len(sums),)),
+            pltpu.SemaphoreType.DMA((7 + len(sums),)),
             pltpu.SemaphoreType.DMA,
         ],
         compiler_params=pltpu.CompilerParams(
             vmem_limit_bytes=63 << 20, collective_id=3, has_side_effects=True
         ),
         cost_estimate=estimate(2 * near_tokens * width * attn_cols, 10 * near_tokens * width),
-    )(line, weight, own_in, grad_middle, gain, gain_two, rows_one, line, block)
+    )(line, weight, own_in, grad_middle, gain, gain_two, rows_one, line, block, *sums)
 
 
 def place_kernel(count, info, *refs):
@@ -1705,15 +1720,16 @@
 
     normed_flat = normed_one.reshape(token_count, model_width)
     if split:
-        input_share, gain_grad, attn_grad, bias_grad, block_home = finish_rows(
+        input_share, gain_grad, attn_grad, bias_grad, block_home, *unit_gots = finish_rows(
             line_grad,
-            after(back_full, *unit_sums),
+            back_full,
             own_in,
             grad_middle,
             gains_now[0:1],
             gain_two,
             normed_flat,
             block_share,
+            unit_sums,
         )
         attn_grad = jnp.concatenate([attn_grad, output_grad], axis=1)
     else:
@@ -1769,16 +1785,8 @@
         block_home = leave(block_share)
     block_out = place_rows(arrive(block_home), home_order)
     if split:
-
-        def unit_end(total, *earlier):
-            kept, sent = scatter_ctx(total.reshape(1, ctx_count, -1, total.shape[1]), ctx_rank)
-            return kept[0], from_partner(after(sent[0], *earlier), "ctx", 1)
-
         input_home = after(input_home, attn_held)
         input_rows = arrive(input_home)
-        own_a, got_a = unit_end(unit_sums[0], input_rows[1])
-        ends = [unit_end(t, input_rows[1]) for t in unit_sums[1:]]
-        home_order = after(home_order, got_a, *[end[1] for end in ends])
     else:
         input_rows = arrive(input_home)
     input_grad = place_rows(input_rows, home_order)
@@ -1787,6 +1795,12 @@
     tiny_grad = attn_end[:, small_at:].astype(WIDE)
 
     if split:
+
+        def own_half(total):
+            rows = total.shape[0] // 2
+            return lax.dynamic_slice_in_dim(total, ctx_rank * rows, rows, axis=0)
+
+        (own_a, got_a), *ends = [(own_half(t), got) for t, got in zip(unit_sums, unit_gots)]
 
         def joined(part, end):
             cols = slice(part * first_units, (part + 1) * first_units)

time: 764 us -> 757 us (level)
    ppermute x29 -> x25, starting transfers between devices: 27.7 us -> 30.2 us  [from_partner(): return lax.ppermute(value, axis, pairs)]
    ppermute x29 -> x25, waiting for transfers between devices: 158 us -> 157 us  [from_partner(): return lax.ppermute(value, axis, pairs)]
  transfers between devices with their start and end apart: 41 -> 37, of which waited for: 18 -> 16; matrix products, arithmetic and copies ran while one was open for 6% -> 6% of each run, Pallas kernels for 51% -> 51%
where the time goes in v11:
time: 757 us; the launch traced here: 747 us
  Pallas kernels  440 us (58%)
  waiting for transfers between devices  182 us (24%)
  starting transfers between devices  45.3 us (6%)
  other arithmetic  31.7 us (4%)
  local copies, waits for them, and re-layouts  30.4 us (4%)
  between operations  17 us (2%)
    ppermute x25, waiting for transfers between devices, from_partner(): return lax.ppermute(value, axis, pairs)  157 us
    pallas_call x1, Pallas kernels, collect_back(): pl.pallas_call(functools.partial(collect_kernel, slots, tiles), grid=(slo...  71.2 us
    pallas_call x1, Pallas kernels, attend_exchange(): pl.pallas_call(functools.partial(exchange_kernel, heads, head_dim, scale,...  56.9 us
    pallas_call x1, Pallas kernels, spread_branch(): pl.pallas_call(functools.partial(branch_kernel, slots, tiles), grid=(slot...  54.8 us
    pallas_call x1, Pallas kernels, finish_rows(): pl.pallas_call(functools.partial(line_kernel, slots, tiles, len(sums)), g...  52.1 us
    pallas_call x1, Pallas kernels, attend_sum(): pl.pallas_call(functools.partial(attend_sum_kernel, heads, head_dim, scal...  52 us
    pallas_call x1, Pallas kernels, first_grads(): pl.pallas_call(first_grads_kernel, grid=(3, tiles), in_specs=[pl.BlockSpe...  41.7 us
    ppermute x25, starting transfers between devices, from_partner(): return lax.ppermute(value, axis, pairs)  30.2 us
  transfers between devices with their start and end apart: 37, of which 16 were waited for; matrix products, arithmetic and copies ran while one was open for 6% of the time, Pallas kernels for 51%

profile of v11, /device:TPU:1, one launch (start us, length us, event | category | flops | bytes accessed | tf_op | source)
XLA Modules:
  0.0 747.3 jit_solution(10255971799168657467)
XLA Ops:
  14.4 5.0 collective-permute-start
  27.4 5.6 fusion.3
  34.2 9.1 %collective-permute-done.4 = bf16[192,1152]{1,0:T(8,128)(2,1)S(1)} collective-permute-done((bf16[192,1152]{1,0:T(8,128)(2,1)S(1)}, bf16[192,1152]{1,0:T(8,128)(2,1)S(1)}, u32[]{:S(2)}, u32[]{:S(2)}) %collective-permute-start.4) | collective-permute-done | bytes 442400 | tf_op jit(solution)/shard_map/ppermute | solution.py:21
  44.4 9.9 %collective-permute-done.x0.own_in = bf16[512,1536]{1,0:T(8,128)(2,1)S(1)} collective-permute-done((bf16[512,1536]{1,0:T(8,128)(2,1)}, bf16[512,1536]{1,0:T(8,128)(2,1)S(1)}, u32[]{:S(2)}, u32[]{:S(2)}) %collective-permute-start) | collective-permute-done | bytes 1572896 | tf_op jit(solution)/shard_map/ppermute | solution.py:1429
  58.1 31.0 %collective-permute-done.2.x2 = bf16[512,1536]{1,0:T(8,128)(2,1)} collective-permute-done((bf16[512,1536]{1,0:T(8,128)(2,1)S(1)}, bf16[512,1536]{1,0:T(8,128)(2,1)}, u32[]{:S(2)}, u32[]{:S(2)}) %collective-permute-start.2) | collective-permute-done | bytes 1572896 | tf_op jit(solution)/shard_map/ppermute | solution.py:21
  97.5 34.1 %collective-permute-done.6.refs_0_ = bf16[512,1536]{1,0:T(8,128)(2,1)} collective-permute-done((bf16[512,1536]{1,0:T(8,128)(2,1)}, bf16[512,1536]{1,0:T(8,128)(2,1)}, u32[]{:S(2)}, u32[]{:S(2)}) %collective-permute-start.6) | collective-permute-done | bytes 1572896 | tf_op jit(solution)/shard_map/ppermute | solution.py:21
  135.0 13.3 %shard_map.221 = (bf16[4,512,1536]{2,1,0:T(8,128)(2,1)}, bf16[4,512,384]{2,1,0:T(8,128)(2,1)}, bf16[4,512,128]{2,1,0:T(8,128)(2,1)}, bf16[4,512,128]{2,1,0:T(8,128)(2,1)}) custom-call(bf16[512,1536]{1,0:T(8,128)(2,1)} %copy-done.7, bf16[512,1536]{1,0:T(8,128)(2,1)} %collective-permute-done.1.x1, bf16[512,1536]{1,0:T(8,128)(2,1)} %collective-permute-done.2.x2, ...), custom_call_target="tpu_custom_call" | custom-call | flops 4026531840 | bytes 17170432 | tf_op jit(solution)/shard_map/pallas_call | solution.py:855
  154.7 12.3 %collective-permute-done.8.refs_2_ = bf16[512,1536]{1,0:T(8,128)(2,1)} collective-permute-done((bf16[512,1536]{1,0:T(8,128)(2,1)}, bf16[512,1536]{1,0:T(8,128)(2,1)}, u32[]{:S(2)}, u32[]{:S(2)}) %collective-permute-start.8) | collective-permute-done | bytes 1572896 | tf_op jit(solution)/shard_map/ppermute | solution.py:21
  174.0 52.0 %shard_map.222 = (bf16[4,512,384]{2,1,0:T(8,128)(2,1)}, f32[4,512,128]{2,1,0:T(8,128)}, f32[512,1536]{1,0:T(8,128)}, bf16[512,1536]{1,0:T(8,128)(2,1)}) custom-call(s32[8]{0:T(128)} %compare_select_fusion.14.info, bf16[4,512,384]{2,1,0:T(8,128)(2,1)} %get-tuple-element.82.q, bf16[4,512,128]{2,1,0:T(8,128)(2,1)} %copy-done.22, ...), custom_call_target="tpu_custom_call" | custom-call | flops 3221225472 | bytes 3145728 | tf_op jit(solution)/shard_map/pallas_call | solution.py:1163
  235.9 18.6 %shard_map.223 = (bf16[4096,640]{1,0:T(8,128)(2,1)}, bf16[4096,1536]{1,0:T(8,128)(2,1)}) custom-call(s32[8]{0:T(128)} %compare_select_fusion.13.info, bf16[4,512,1536]{2,1,0:T(8,128)(2,1)} %cotangent, bf16[512,1536]{1,0:T(8,128)(2,1)} %collective-permute-done.6.refs_0_, bf16[512,1536]{1,0:T(8,128)(2,1)} %collective-permute-done.11.refs_1_, ...), custom_call_target="tpu_custom_call" | custom-call | flops 8053063680 | bytes 32374784 | tf_op jit(solution)/shard_map/pallas_call | solution.py:230
  254.5 7.1 collective-permute-done.14.refs_4_
  273.9 14.5 %shard_map.224 = (bf16[4096,640]{1,0:T(8,128)(2,1)}, bf16[4096,1536]{1,0:T(8,128)(2,1)}) custom-call(bf16[512,1536]{1,0:T(8,128)(2,1)} %get-tuple-element.86.refs_0_, bf16[512,1536]{1,0:T(8,128)(2,1)} %collective-permute-done.16.refs_1_, bf16[512,1536]{1,0:T(8,128)(2,1)} %collective-permute-done.10.refs_2_, ...), custom_call_target="tpu_custom_call" | custom-call | flops 6039797760 | bytes 24772608 | tf_op jit(solution)/shard_map/pallas_call | solution.py:123
  296.6 6.8 shard_map.225
  303.4 20.9 %shard_map.226 = (bf16[4096,640]{1,0:T(8,128)(2,1)}, bf16[4096,640]{1,0:T(8,128)(2,1)}, bf16[4096,640]{1,0:T(8,128)(2,1)}) custom-call(bf16[4096,1536]{1,0:T(8,128)(2,1)} %get-tuple-element.105.h.right.turned, bf16[1536,1920]{1,0:T(8,128)(2,1)} %bitcast.67, bf16[4096,640]{1,0:T(8,128)(2,1)} %get-tuple-element.100.gate, bf16[4096,640]{1,0:T(8,128)(2,1)} %get-tuple-element.91.grad), custom_call_target="tpu_custom_call" | custom-call | flops 8053063680 | bytes 40763392 | tf_op jit(solution)/shard_map/pallas_call | solution.py:161
  324.3 41.7 %shard_map.227 = bf16[1536,1920]{1,0:T(8,128)(2,1)} custom-call(bf16[4096,1536]{1,0:T(8,128)(2,1)} %get-tuple-element.103.g.left.own_grad, bf16[4096,1536]{1,0:T(8,128)(2,1)} %get-tuple-element.105.h.right.turned, bf16[4096,640]{1,0:T(8,128)(2,1)} %get-tuple-element.104.hid.hid_a, bf16[4096,640]{1,0:T(8,128)(2,1)} %get-tuple-element.101.gate.gate_a, ...), custom_call_target="tpu_custom_call" | custom-call | flops 24159191040 | bytes 21626880 | tf_op jit(solution)/shard_map/pallas_call | solution.py:298
  366.1 26.7 %shard_map.228 = (bf16[4096,512]{1,0:T(8,128)(2,1)}, bf16[4096,512]{1,0:T(8,128)(2,1)}, bf16[4096,512]{1,0:T(8,128)(2,1)}) custom-call(bf16[4096,1536]{1,0:T(8,128)(2,1)} %get-tuple-element.105.h.right.turned, bf16[4096,1536]{1,0:T(8,128)(2,1)} %get-tuple-element.103.g.left.own_grad, bf16[1536,1536]{1,0:T(8,128)(2,1)} %bitcast.71, ...), custom_call_target="tpu_custom_call" | custom-call | flops 19327352832 | bytes 42467328 | tf_op jit(solution)/shard_map/pallas_call | solution.py:272
  392.8 71.2 %shard_map.229 = (f32[512,1536]{1,0:T(8,128)}, bf16[1536,512]{1,0:T(8,128)(2,1)}, bf16[1536,512]{1,0:T(8,128)(2,1)}) custom-call(bf16[4096,640]{1,0:T(8,128)(2,1)} %get-tuple-element.101.gate.gate_a, bf16[4096,640]{1,0:T(8,128)(2,1)} %get-tuple-element.102.up.up_a, bf16[4096,512]{1,0:T(8,128)(2,1)} %get-tuple-element.107.gate_b.gate, ...), custom_call_target="tpu_custom_call" | custom-call | flops 19327352832 | bytes 20971520 | tf_op jit(solution)/shard_map/pallas_call | solution.py:439
  464.0 6.6 reduce-scatter.6.cloned.1.call-done.refs_0_
  471.2 54.8 %shard_map.230 = (f32[512,1536]{1,0:T(8,128)}, f32[1,1536]{1,0:T(1,128)}, bf16[1536,512]{1,0:T(8,128)(2,1)}, bf16[4,512,1536]{2,1,0:T(8,128)(2,1)}, bf16[512,153...) custom-call(f32[512,1536]{1,0:T(8,128)} %get-tuple-element.110.total, ...), custom_call_target="tpu_custom_call" | custom-call | flops 12884901888 | bytes 20971520 | tf_op jit(solution)/shard_map/pallas_call | solution.py:577
  526.1 56.9 %shard_map.231 = (bf16[4,512,512]{2,1,0:T(8,128)(2,1)}, bf16[1536,384]{1,0:T(8,128)(2,1)}, bf16[512,1536]{1,0:T(8,128)(2,1)}) custom-call(s32[8]{0:T(128)} %compare_select_fusion.14.info, bf16[4,512,384]{2,1,0:T(8,128)(2,1)} %get-tuple-element.82.q, bf16[4,512,128]{2,1,0:T(8,128)(2,1)} %copy-done.22, bf16[4,512,128]{2,1,0:T(8,128)(2,1)} %copy-done.23, ...), custom_call_target="tpu_custom_call" | custom-call | flops 2415919104 | bytes 7864320 | tf_op jit(solution)/shard_map/pallas_call | solution.py:1315
  583.1 52.1 %shard_map.232 = (bf16[512,1536]{1,0:T(8,128)(2,1)}, f32[2,1536]{1,0:T(2,128)}, bf16[1536,512]{1,0:T(8,128)(2,1)}, f32[1,512]{1,0:T(1,128)}, bf16[512,1536]{1,0:...) custom-call(bf16[2048,512]{1,0:T(8,128)(2,1)} %bitcast.86, ...), custom_call_target="tpu_custom_call" | custom-call | flops 3221225472 | bytes 31457280 | tf_op jit(solution)/shard_map/pallas_call | solution.py:736
  646.1 26.7 %collective-permute-done.25 = bf16[4,192,1024]{2,1,0:T(8,128)(2,1)} collective-permute-done((bf16[4,192,1024]{2,1,0:T(8,128)(2,1)}, bf16[4,192,1024]{2,1,0:T(8,128)(2,1)}, u32[]{:S(2)}, u32[]{:S(2)}) %collective-permute-start.25) | collective-permute-done | bytes 1572896 | tf_op jit(solution)/shard_map/ppermute | solution.py:21
  689.5 30.7 %collective-permute-done.27.refs_2_ = bf16[512,1536]{1,0:T(8,128)(2,1)} collective-permute-done((bf16[512,1536]{1,0:T(8,128)(2,1)S(1)}, bf16[512,1536]{1,0:T(8,128)(2,1)}, u32[]{:S(2)}, u32[]{:S(2)}) %collective-permute-start.27) | collective-permute-done | bytes 1572896 | tf_op jit(solution)/shard_map/ppermute | solution.py:21
  734.3 5.9 shard_map.234
  (214 shorter events, 117.0 us)
Async XLA Ops:
  7.2 127.8 %all-gather.7.cloned.1.call-start = ((), (), s32[]{:S(2)}) async-start(), calls=%async_computation.10 | async-start | bytes 4423680 | tf_op jit(solution)/shard_map/all_gather | solution.py:1466
  14.4 39.9 %collective-permute-start = (bf16[512,1536]{1,0:T(8,128)(2,1)}, bf16[512,1536]{1,0:T(8,128)(2,1)S(1)}, u32[]{:S(2)}, u32[]{:S(2)}) collective-permute-start(bf16[512,1536]{1,0:T(8,128)(2,1)} %get-tuple-element.260), channel_id=1, source_target_pairs={{0,0},{1,17},{2,10},{3,27},{8,8},{9,25},{10,18},{11,3},{16,16},{17... | collective-permute-start | bytes 4718600 | tf_op jit(solution)/shard_map/ppermute | solution.py:1429
  54.3 181.6 %all-gather.9.cloned.1.call-start = ((), (), s32[]{:S(2)}) async-start(), calls=%async_computation.11 | async-start | bytes 7372800 | tf_op jit(solution)/shard_map/all_gather | solution.py:1466
  54.4 34.7 %collective-permute-start.2 = (bf16[512,1536]{1,0:T(8,128)(2,1)S(1)}, bf16[512,1536]{1,0:T(8,128)(2,1)}, u32[]{:S(2)}, u32[]{:S(2)}) collective-permute-start(bf16[512,1536]{1,0:T(8,128)(2,1)S(1)} %collective-permute-done.x0.own_in), channel_id=1, source_target_pairs={{0,2},{1,3},{2,0},{3,1},{4,6},{5,7},{6,4},{7,5},{8,10},{9,11},{10,... | collective-permute-start | bytes 4718600 | tf_op jit(solution)/shard_map/ppermute | solution.py:21
  55.6 35.7 %collective-permute-start.5 = (bf16[192,3456]{1,0:T(8,128)(2,1)}, bf16[192,3456]{1,0:T(8,128)(2,1)S(1)}, u32[]{:S(2)}, u32[]{:S(2)}) collective-permute-start(bf16[192,3456]{1,0:T(8,128)(2,1)} %get-tuple-element.79), channel_id=1, source_target_pairs={{0,4},{4,0},{1,5},{5,1},{2,6},{6,2},{3,7},{7,3},{8,12},{12,8},{9,1... | collective-permute-start | bytes 3981320 | tf_op jit(solution)/shard_map/ppermute | solution.py:21
  95.1 271.0 %all-gather.11.cloned.1.call-start = ((), (), s32[]{:S(2)}) async-start(), calls=%async_computation.12 | async-start | bytes 5898240 | tf_op jit(solution)/shard_map/all_gather | solution.py:1466
  95.2 36.4 %collective-permute-start.6 = (bf16[512,1536]{1,0:T(8,128)(2,1)}, bf16[512,1536]{1,0:T(8,128)(2,1)}, u32[]{:S(2)}, u32[]{:S(2)}) collective-permute-start(bf16[512,1536]{1,0:T(8,128)(2,1)} %get-tuple-element.80), channel_id=1, source_target_pairs={{0,4},{4,0},{1,5},{5,1},{2,6},{6,2},{3,7},{7,3},{8,12},{12,8},{9,1... | collective-permute-start | bytes 4718600 | tf_op jit(solution)/shard_map/ppermute | solution.py:21
  96.5 38.5 %collective-permute-start.1 = (bf16[512,1536]{1,0:T(8,128)(2,1)S(1)}, bf16[512,1536]{1,0:T(8,128)(2,1)}, u32[]{:S(2)}, u32[]{:S(2)}) collective-permute-start(bf16[512,1536]{1,0:T(8,128)(2,1)S(1)} %collective-permute-done.x0.own_in), channel_id=1, source_target_pairs={{0,1},{1,0},{2,3},{3,2},{4,5},{5,4},{6,7},{7,6},{8,9},{9,8},{10,11... | collective-permute-start | bytes 4718600 | tf_op jit(solution)/shard_map/ppermute | solution.py:21
  131.5 35.4 %collective-permute-start.8 = (bf16[512,1536]{1,0:T(8,128)(2,1)}, bf16[512,1536]{1,0:T(8,128)(2,1)}, u32[]{:S(2)}, u32[]{:S(2)}) collective-permute-start(bf16[512,1536]{1,0:T(8,128)(2,1)} %collective-permute-done.6.refs_0_), channel_id=1, source_target_pairs={{0,2},{1,3},{2,0},{3,1},{4,6},{5,7},{6,4},{7,5},{8,10},{9,11},{10,... | collective-permute-start | bytes 4718600 | tf_op jit(solution)/shard_map/ppermute | solution.py:21
  166.9 64.7 %collective-permute-start.11 = (bf16[512,1536]{1,0:T(8,128)(2,1)}, bf16[512,1536]{1,0:T(8,128)(2,1)}, u32[]{:S(2)}, u32[]{:S(2)}) collective-permute-start(bf16[512,1536]{1,0:T(8,128)(2,1)} %collective-permute-done.6.refs_0_), channel_id=1, source_target_pairs={{0,1},{1,0},{2,3},{3,2},{4,5},{5,4},{6,7},{7,6},{8,9},{9,8},{10,11... | collective-permute-start | bytes 4718600 | tf_op jit(solution)/shard_map/ppermute | solution.py:21
  168.6 63.0 %collective-permute-start.12 = (bf16[512,1536]{1,0:T(8,128)(2,1)}, bf16[512,1536]{1,0:T(8,128)(2,1)}, u32[]{:S(2)}, u32[]{:S(2)}) collective-permute-start(bf16[512,1536]{1,0:T(8,128)(2,1)} %collective-permute-done.8.refs_2_), channel_id=1, source_target_pairs={{0,1},{1,0},{2,3},{3,2},{4,5},{5,4},{6,7},{7,6},{8,9},{9,8},{10,11... | collective-permute-start | bytes 4718600 | tf_op jit(solution)/shard_map/ppermute | solution.py:21
  226.1 35.5 %collective-permute-start.14 = (bf16[512,1536]{1,0:T(8,128)(2,1)}, bf16[512,1536]{1,0:T(8,128)(2,1)}, u32[]{:S(2)}, u32[]{:S(2)}) collective-permute-start(bf16[512,1536]{1,0:T(8,128)(2,1)} %get-tuple-element.86.refs_0_), channel_id=1, source_target_pairs={{0,4},{4,0},{1,5},{5,1},{2,6},{6,2},{3,7},{7,3},{8,12},{12,8},{9,1... | collective-permute-start | bytes 4718600 | tf_op jit(solution)/shard_map/ppermute | solution.py:21
  229.4 241.1 %reduce-scatter.6.cloned.1.call-start = ((), (), s32[]{:S(2)}) async-start(), calls=%async_computation.5 | async-start | bytes 7372800 | tf_op jit(solution)/shard_map/reduce_scatter | solution.py:1711
  229.7 44.2 %collective-permute-start.16 = (bf16[512,1536]{1,0:T(8,128)(2,1)}, bf16[512,1536]{1,0:T(8,128)(2,1)}, u32[]{:S(2)}, u32[]{:S(2)}) collective-permute-start(bf16[512,1536]{1,0:T(8,128)(2,1)} %get-tuple-element.86.refs_0_), channel_id=1, source_target_pairs={{0,1},{1,0},{2,3},{3,2},{4,5},{5,4},{6,7},{7,6},{8,9},{9,8},{10,11... | collective-permute-start | bytes 4718600 | tf_op jit(solution)/shard_map/ppermute | solution.py:21
  366.0 217.0 %reduce-scatter.10.cloned.1.call-start = ((), (), s32[]{:S(2)}) async-start(), calls=%async_computation.7 | async-start | bytes 1966080 | tf_op jit(solution)/shard_map/reduce_scatter | solution.py:1711
  470.6 112.5 %reduce-scatter.8.cloned.1.call-start = ((), (), s32[]{:S(2)}) async-start(), calls=%async_computation.6 | async-start | bytes 1966080 | tf_op jit(solution)/shard_map/reduce_scatter | solution.py:1711
  471.1 111.9 %reduce-scatter.12.cloned.1.call-start = ((), (), s32[]{:S(2)}) async-start(), calls=%async_computation.8 | async-start | bytes 1966080 | tf_op jit(solution)/shard_map/reduce_scatter | solution.py:1711
  526.0 201.4 %reduce-scatter.14.cloned.1.call-start = ((), (), s32[]{:S(2)}) async-start(), calls=%async_computation.9 | async-start | bytes 1966080 | tf_op jit(solution)/shard_map/reduce_scatter | solution.py:1770
  641.5 42.4 %collective-permute-start.24 = (bf16[512,1536]{1,0:T(8,128)(2,1)}, bf16[512,1536]{1,0:T(8,128)(2,1)S(1)}, u32[]{:S(2)}, u32[]{:S(2)}) collective-permute-start(bf16[512,1536]{1,0:T(8,128)(2,1)} %get-tuple-element.130), channel_id=1, source_target_pairs={{0,0},{17,1},{10,2},{27,3},{8,8},{25,9},{18,10},{3,11},{16,16},{1,... | collective-permute-start | bytes 4718600 | tf_op jit(solution)/shard_map/ppermute | solution.py:1776
  646.0 39.8 %collective-permute-start.22 = (bf16[512,1536]{1,0:T(8,128)(2,1)S(1)}, bf16[512,1536]{1,0:T(8,128)(2,1)}, u32[]{:S(2)}, u32[]{:S(2)}) collective-permute-start(bf16[512,1536]{1,0:T(8,128)(2,1)S(1)} %copy-done.2), channel_id=1, source_target_pairs={{0,2},{1,3},{2,0},{3,1},{4,6},{5,7},{6,4},{7,5},{8,10},{9,11},{10,... | collective-permute-start | bytes 4718600 | tf_op jit(solution)/shard_map/ppermute | solution.py:21
  677.9 44.5 %collective-permute-start.21 = (bf16[512,1536]{1,0:T(8,128)(2,1)S(1)}, bf16[512,1536]{1,0:T(8,128)(2,1)S(1)}, u32[]{:S(2)}, u32[]{:S(2)}) collective-permute-start(bf16[512,1536]{1,0:T(8,128)(2,1)S(1)} %copy-done.2), channel_id=1, source_target_pairs={{0,1},{1,0},{2,3},{3,2},{4,5},{5,4},{6,7},{7,6},{8,9},{9,8},{10,11... | collective-permute-start | bytes 4718600 | tf_op jit(solution)/shard_map/ppermute | solution.py:21
  683.9 36.3 %collective-permute-start.27 = (bf16[512,1536]{1,0:T(8,128)(2,1)S(1)}, bf16[512,1536]{1,0:T(8,128)(2,1)}, u32[]{:S(2)}, u32[]{:S(2)}) collective-permute-start(bf16[512,1536]{1,0:T(8,128)(2,1)S(1)} %collective-permute-done.24.refs_0_), channel_id=1, source_target_pairs={{0,2},{1,3},{2,0},{3,1},{4,6},{5,7},{6,4},{7,5},{8,10},{9,11},{10,... | collective-permute-start | bytes 4718600 | tf_op jit(solution)/shard_map/ppermute | solution.py:21
  685.8 36.7 %collective-permute-start.23 = (bf16[512,1536]{1,0:T(8,128)(2,1)}, bf16[512,1536]{1,0:T(8,128)(2,1)S(1)}, u32[]{:S(2)}, u32[]{:S(2)}) collective-permute-start(bf16[512,1536]{1,0:T(8,128)(2,1)} %collective-permute-done.22.refs_2_), channel_id=1, source_target_pairs={{0,1},{1,0},{2,3},{3,2},{4,5},{5,4},{6,7},{7,6},{8,9},{9,8},{10,11... | collective-permute-start | bytes 4718600 | tf_op jit(solution)/shard_map/ppermute | solution.py:21
  689.2 43.6 %collective-permute-start.26 = (bf16[512,1536]{1,0:T(8,128)(2,1)S(1)}, bf16[512,1536]{1,0:T(8,128)(2,1)}, u32[]{:S(2)}, u32[]{:S(2)}) collective-permute-start(bf16[512,1536]{1,0:T(8,128)(2,1)S(1)} %collective-permute-done.24.refs_0_), channel_id=1, source_target_pairs={{0,1},{1,0},{2,3},{3,2},{4,5},{5,4},{6,7},{7,6},{8,9},{9,8},{10,11... | collective-permute-start | bytes 4718600 | tf_op jit(solution)/shard_map/ppermute | solution.py:21
  (48 other events, 565.9 us)
Sparse Core Ops, SparseCore 0:
  54.5 71.4 all-gather.6
  128.1 107.7 all-gather.8
  237.5 87.5 all-gather.10
  366.1 104.3 reduce-scatter.5
  472.7 35.5 reduce-scatter.9
  510.5 34.2 reduce-scatter.7
  547.1 34.2 reduce-scatter.11
  676.7 38.8 reduce-scatter.13

commit v12 on v11

--- a/solution.py
+++ b/solution.py
@@ -1524,6 +1524,10 @@
     else:
         key_past = lax.all_gather(key_own, "ctx", axis=1, tiled=True)
         value_past = lax.all_gather(value_own, "ctx", axis=1, tiled=True)
+    own_weight = lax.dynamic_slice_in_dim(
+        project_full, query_cols + parity * head_dim, head_dim, axis=1
+    )
+    back_full = jnp.concatenate([project_full[:, :query_cols], own_weight], axis=1)
     in_share = own_in.astype(WIDE)
     if split:
         mixed, lse, middle_share, normed_share = attend_sum(
@@ -1533,7 +1537,7 @@
             value_past,
             key_own,
             value_own,
-            output_full,
+            after(output_full, back_full),
             own_in,
             gains_now[1:2],
             heads,
@@ -1594,14 +1598,9 @@
         return [(row,) for row in rows[:6]] + [rows[6:]]
 
     mixed_flat = mixed.reshape(token_count, query_cols)
-    own_weight = lax.dynamic_slice_in_dim(
-        project_full, query_cols + parity * head_dim, head_dim, axis=1
-    )
-    back_full = jnp.concatenate([project_full[:, :query_cols], own_weight], axis=1)
     normed_slots = in_slots(spread_all(normed_share))
     if split:
-        early = after(units_a, back_full)
-        ahead = stack_rows(normed_slots[:6], early, 1, 3, total=8)
+        ahead = stack_rows(normed_slots[:6], units_a, 1, 3, total=8)
         last = [normed_slots[6], tuple(from_partner(after(v, ahead[0]), "tp", 1) for v in normed_slots[6])]
         gate_lin, normed_two = stack_rows(last, units_a, 1, 3, into=ahead, first=6, total=8)
         hidden_a, gate_a, up_a = hidden_units(normed_two, units_a, 2, 3, gate_lin, grad_hidden)
@@ -1775,10 +1774,10 @@
     def leave(share):
         return lax.ppermute(share, ("fsdp", "tp"), back)
 
-    def arrive(own):
+    def arrive(own, *earlier):
         far = from_partner(own, "tp", 2)
         near = from_partner(own, "tp", 1)
-        return (own, near, far, from_partner(far, "tp", 1))
+        return (own, near, far, from_partner(after(far, *earlier), "tp", 1))
 
     input_home = leave(input_share)
     if not split:
@@ -1786,7 +1785,7 @@
     block_out = place_rows(arrive(block_home), home_order)
     if split:
         input_home = after(input_home, attn_held)
-        input_rows = arrive(input_home)
+        input_rows = arrive(input_home, block_out)
     else:
         input_rows = arrive(input_home)
     input_grad = place_rows(input_rows, home_order)

time: 757 us -> 753 us (level)
  waiting for transfers between devices: 182 us -> 169 us
    ppermute x25, waiting for transfers between devices: 157 us -> 150 us  [from_partner(): return lax.ppermute(value, axis, pairs)]
  transfers between devices with their start and end apart: 37 -> 37, of which waited for: 16 -> 16; matrix products, arithmetic and copies ran while one was open for 6% -> 7% of each run, Pallas kernels for 51% -> 51%
where the time goes in v12:
time: 753 us; the launch traced here: 743 us
  Pallas kernels  440 us (58%)
  waiting for transfers between devices  169 us (22%)
  starting transfers between devices  45.5 us (6%)
  other arithmetic  35.8 us (5%)
  local copies, waits for them, and re-layouts  35.7 us (5%)
  between operations  17.2 us (2%)
    ppermute x25, waiting for transfers between devices, from_partner(): return lax.ppermute(value, axis, pairs)  150 us
    pallas_call x1, Pallas kernels, collect_back(): pl.pallas_call(functools.partial(collect_kernel, slots, tiles), grid=(slo...  71.3 us
    pallas_call x1, Pallas kernels, attend_exchange(): pl.pallas_call(functools.partial(exchange_kernel, heads, head_dim, scale,...  56.9 us
    pallas_call x1, Pallas kernels, spread_branch(): pl.pallas_call(functools.partial(branch_kernel, slots, tiles), grid=(slot...  54.5 us
    pallas_call x1, Pallas kernels, finish_rows(): pl.pallas_call(functools.partial(line_kernel, slots, tiles, len(sums)), g...  52.3 us
    pallas_call x1, Pallas kernels, attend_sum(): pl.pallas_call(functools.partial(attend_sum_kernel, heads, head_dim, scal...  51.8 us
    pallas_call x1, Pallas kernels, first_grads(): pl.pallas_call(first_grads_kernel, grid=(3, tiles), in_specs=[pl.BlockSpe...  41.7 us
    ppermute x25, starting transfers between devices, from_partner(): return lax.ppermute(value, axis, pairs)  30.4 us
  transfers between devices with their start and end apart: 37, of which 16 were waited for; matrix products, arithmetic and copies ran while one was open for 7% of the time, Pallas kernels for 51%

profile of v12, /device:TPU:1, one launch (start us, length us, event | category | flops | bytes accessed | tf_op | source)
XLA Modules:
  0.0 743.0 jit_solution(7489402186906542531)
XLA Ops:
  14.9 5.2 collective-permute-start
  31.0 5.6 fusion.3
  37.9 9.1 %collective-permute-done.4 = bf16[192,1152]{1,0:T(8,128)(2,1)S(1)} collective-permute-done((bf16[192,1152]{1,0:T(8,128)(2,1)S(1)}, bf16[192,1152]{1,0:T(8,128)(2,1)S(1)}, u32[]{:S(2)}, u32[]{:S(2)}) %collective-permute-start.4) | collective-permute-done | bytes 442400 | tf_op jit(solution)/shard_map/ppermute | solution.py:21
  48.1 6.8 collective-permute-done.x0.own_in
  58.8 30.9 %collective-permute-done.2.x2 = bf16[512,1536]{1,0:T(8,128)(2,1)S(1)} collective-permute-done((bf16[512,1536]{1,0:T(8,128)(2,1)S(1)}, bf16[512,1536]{1,0:T(8,128)(2,1)S(1)}, u32[]{:S(2)}, u32[]{:S(2)}) %collective-permute-start.2) | collective-permute-done | bytes 1572896 | tf_op jit(solution)/shard_map/ppermute | solution.py:21
  100.5 31.6 %collective-permute-done.6.refs_0_ = bf16[512,1536]{1,0:T(8,128)(2,1)} collective-permute-done((bf16[512,1536]{1,0:T(8,128)(2,1)}, bf16[512,1536]{1,0:T(8,128)(2,1)}, u32[]{:S(2)}, u32[]{:S(2)}) %collective-permute-start.6) | collective-permute-done | bytes 1572896 | tf_op jit(solution)/shard_map/ppermute | solution.py:21
  137.4 12.8 %shard_map.221 = (bf16[4,512,1536]{2,1,0:T(8,128)(2,1)}, bf16[4,512,384]{2,1,0:T(8,128)(2,1)}, bf16[4,512,128]{2,1,0:T(8,128)(2,1)}, bf16[4,512,128]{2,1,0:T(8,128)(2,1)}) custom-call(bf16[512,1536]{1,0:T(8,128)(2,1)} %copy-done.7, bf16[512,1536]{1,0:T(8,128)(2,1)} %copy-done.12, bf16[512,1536]{1,0:T(8,128)(2,1)} %copy-done.11, ...), custom_call_target="tpu_custom_call" | custom-call | flops 4026531840 | bytes 17170432 | tf_op jit(solution)/shard_map/pallas_call | solution.py:855
  157.3 10.2 %collective-permute-done.8.refs_2_ = bf16[512,1536]{1,0:T(8,128)(2,1)} collective-permute-done((bf16[512,1536]{1,0:T(8,128)(2,1)}, bf16[512,1536]{1,0:T(8,128)(2,1)}, u32[]{:S(2)}, u32[]{:S(2)}) %collective-permute-start.8) | collective-permute-done | bytes 1572896 | tf_op jit(solution)/shard_map/ppermute | solution.py:21
  176.1 51.8 %shard_map.222 = (bf16[4,512,384]{2,1,0:T(8,128)(2,1)}, f32[4,512,128]{2,1,0:T(8,128)}, f32[512,1536]{1,0:T(8,128)}, bf16[512,1536]{1,0:T(8,128)(2,1)}) custom-call(s32[8]{0:T(128)} %compare_select_fusion.14.info, bf16[4,512,384]{2,1,0:T(8,128)(2,1)} %get-tuple-element.83.q, bf16[4,512,128]{2,1,0:T(8,128)(2,1)} %copy-done.20, ...), custom_call_target="tpu_custom_call" | custom-call | flops 3221225472 | bytes 3145728 | tf_op jit(solution)/shard_map/pallas_call | solution.py:1163
  235.9 18.6 %shard_map.223 = (bf16[4096,640]{1,0:T(8,128)(2,1)}, bf16[4096,1536]{1,0:T(8,128)(2,1)}) custom-call(s32[8]{0:T(128)} %compare_select_fusion.13.info, bf16[4,512,1536]{2,1,0:T(8,128)(2,1)} %cotangent, bf16[512,1536]{1,0:T(8,128)(2,1)} %collective-permute-done.6.refs_0_, bf16[512,1536]{1,0:T(8,128)(2,1)} %collective-permute-done.11.refs_1_, ...), custom_call_target="tpu_custom_call" | custom-call | flops 8053063680 | bytes 32374784 | tf_op jit(solution)/shard_map/pallas_call | solution.py:230
  254.5 8.9 %collective-permute-done.14.refs_4_ = bf16[512,1536]{1,0:T(8,128)(2,1)} collective-permute-done((bf16[512,1536]{1,0:T(8,128)(2,1)}, bf16[512,1536]{1,0:T(8,128)(2,1)}, u32[]{:S(2)}, u32[]{:S(2)}) %collective-permute-start.14) | collective-permute-done | bytes 1572896 | tf_op jit(solution)/shard_map/ppermute | solution.py:21
  272.8 14.4 %shard_map.224 = (bf16[4096,640]{1,0:T(8,128)(2,1)}, bf16[4096,1536]{1,0:T(8,128)(2,1)}) custom-call(bf16[512,1536]{1,0:T(8,128)(2,1)} %get-tuple-element.88.refs_0_, bf16[512,1536]{1,0:T(8,128)(2,1)} %collective-permute-done.16.refs_1_, bf16[512,1536]{1,0:T(8,128)(2,1)} %collective-permute-done.10.refs_2_, ...), custom_call_target="tpu_custom_call" | custom-call | flops 6039797760 | bytes 24772608 | tf_op jit(solution)/shard_map/pallas_call | solution.py:123
  295.0 6.8 shard_map.225
  301.8 21.1 %shard_map.226 = (bf16[4096,640]{1,0:T(8,128)(2,1)}, bf16[4096,640]{1,0:T(8,128)(2,1)}, bf16[4096,640]{1,0:T(8,128)(2,1)}) custom-call(bf16[4096,1536]{1,0:T(8,128)(2,1)} %get-tuple-element.106.h.right.turned, bf16[1536,1920]{1,0:T(8,128)(2,1)} %bitcast.67, bf16[4096,640]{1,0:T(8,128)(2,1)} %get-tuple-element.101.gate, bf16[4096,640]{1,0:T(8,128)(2,1)} %get-tuple-element.93.grad), custom_call_target="tpu_custom_call" | custom-call | flops 8053063680 | bytes 40763392 | tf_op jit(solution)/shard_map/pallas_call | solution.py:161
  322.9 41.7 %shard_map.227 = bf16[1536,1920]{1,0:T(8,128)(2,1)} custom-call(bf16[4096,1536]{1,0:T(8,128)(2,1)} %get-tuple-element.104.g.left.own_grad, bf16[4096,1536]{1,0:T(8,128)(2,1)} %get-tuple-element.106.h.right.turned, bf16[4096,640]{1,0:T(8,128)(2,1)} %get-tuple-element.105.hid.hid_a, bf16[4096,640]{1,0:T(8,128)(2,1)} %get-tuple-element.102.gate.gate_a, ...), custom_call_target="tpu_custom_call" | custom-call | flops 24159191040 | bytes 21626880 | tf_op jit(solution)/shard_map/pallas_call | solution.py:298
  364.7 26.9 %shard_map.228 = (bf16[4096,512]{1,0:T(8,128)(2,1)}, bf16[4096,512]{1,0:T(8,128)(2,1)}, bf16[4096,512]{1,0:T(8,128)(2,1)}) custom-call(bf16[4096,1536]{1,0:T(8,128)(2,1)} %get-tuple-element.106.h.right.turned, bf16[4096,1536]{1,0:T(8,128)(2,1)} %get-tuple-element.104.g.left.own_grad, bf16[1536,1536]{1,0:T(8,128)(2,1)} %bitcast.71, ...), custom_call_target="tpu_custom_call" | custom-call | flops 19327352832 | bytes 42467328 | tf_op jit(solution)/shard_map/pallas_call | solution.py:272
  391.6 71.3 %shard_map.229 = (f32[512,1536]{1,0:T(8,128)}, bf16[1536,512]{1,0:T(8,128)(2,1)}, bf16[1536,512]{1,0:T(8,128)(2,1)}) custom-call(bf16[4096,640]{1,0:T(8,128)(2,1)} %get-tuple-element.102.gate.gate_a, bf16[4096,640]{1,0:T(8,128)(2,1)} %get-tuple-element.103.up.up_a, bf16[4096,512]{1,0:T(8,128)(2,1)} %get-tuple-element.108.gate_b.gate, ...), custom_call_target="tpu_custom_call" | custom-call | flops 19327352832 | bytes 20971520 | tf_op jit(solution)/shard_map/pallas_call | solution.py:439
  462.9 5.9 reduce-scatter.6.cloned.1.call-done.refs_0_
  469.5 54.5 %shard_map.230 = (f32[512,1536]{1,0:T(8,128)}, f32[1,1536]{1,0:T(1,128)}, bf16[1536,512]{1,0:T(8,128)(2,1)}, bf16[4,512,1536]{2,1,0:T(8,128)(2,1)}, bf16[512,153...) custom-call(f32[512,1536]{1,0:T(8,128)} %get-tuple-element.111.total, ...), custom_call_target="tpu_custom_call" | custom-call | flops 12884901888 | bytes 20971520 | tf_op jit(solution)/shard_map/pallas_call | solution.py:577
  524.1 56.9 %shard_map.231 = (bf16[4,512,512]{2,1,0:T(8,128)(2,1)}, bf16[1536,384]{1,0:T(8,128)(2,1)}, bf16[512,1536]{1,0:T(8,128)(2,1)}) custom-call(s32[8]{0:T(128)} %compare_select_fusion.14.info, bf16[4,512,384]{2,1,0:T(8,128)(2,1)} %get-tuple-element.83.q, bf16[4,512,128]{2,1,0:T(8,128)(2,1)} %copy-done.20, bf16[4,512,128]{2,1,0:T(8,128)(2,1)} %copy-done.21, ...), custom_call_target="tpu_custom_call" | custom-call | flops 2415919104 | bytes 7864320 | tf_op jit(solution)/shard_map/pallas_call | solution.py:1315
  581.1 52.3 %shard_map.232 = (bf16[512,1536]{1,0:T(8,128)(2,1)}, f32[2,1536]{1,0:T(2,128)}, bf16[1536,512]{1,0:T(8,128)(2,1)}, f32[1,512]{1,0:T(1,128)}, bf16[512,1536]{1,0:...) custom-call(bf16[2048,512]{1,0:T(8,128)(2,1)} %bitcast.86, ...), custom_call_target="tpu_custom_call" | custom-call | flops 3221225472 | bytes 31457280 | tf_op jit(solution)/shard_map/pallas_call | solution.py:736
  645.2 26.7 %collective-permute-done.25 = bf16[4,192,1024]{2,1,0:T(8,128)(2,1)} collective-permute-done((bf16[4,192,1024]{2,1,0:T(8,128)(2,1)}, bf16[4,192,1024]{2,1,0:T(8,128)(2,1)}, u32[]{:S(2)}, u32[]{:S(2)}) %collective-permute-start.25) | collective-permute-done | bytes 1572896 | tf_op jit(solution)/shard_map/ppermute | solution.py:21
  695.6 24.5 %collective-permute-done.27.refs_2_ = bf16[512,1536]{1,0:T(8,128)(2,1)} collective-permute-done((bf16[512,1536]{1,0:T(8,128)(2,1)S(1)}, bf16[512,1536]{1,0:T(8,128)(2,1)}, u32[]{:S(2)}, u32[]{:S(2)}) %collective-permute-start.27) | collective-permute-done | bytes 1572896 | tf_op jit(solution)/shard_map/ppermute | solution.py:21
  730.2 5.5 shard_map.234
  (220 shorter events, 125.8 us)
Async XLA Ops:
  7.2 125.9 %all-gather.7.cloned.1.call-start = ((), (), s32[]{:S(2)}) async-start(), calls=%async_computation.10 | async-start | bytes 4423680 | tf_op jit(solution)/shard_map/all_gather | solution.py:1466
  14.9 40.0 %collective-permute-start = (bf16[512,1536]{1,0:T(8,128)(2,1)}, bf16[512,1536]{1,0:T(8,128)(2,1)S(1)}, u32[]{:S(2)}, u32[]{:S(2)}) collective-permute-start(bf16[512,1536]{1,0:T(8,128)(2,1)} %get-tuple-element.262), channel_id=1, source_target_pairs={{0,0},{1,17},{2,10},{3,27},{8,8},{9,25},{10,18},{11,3},{16,16},{17... | collective-permute-start | bytes 4718600 | tf_op jit(solution)/shard_map/ppermute | solution.py:1429
  54.9 181.0 %all-gather.9.cloned.1.call-start = ((), (), s32[]{:S(2)}) async-start(), calls=%async_computation.11 | async-start | bytes 7372800 | tf_op jit(solution)/shard_map/all_gather | solution.py:1466
  55.0 34.7 %collective-permute-start.2 = (bf16[512,1536]{1,0:T(8,128)(2,1)S(1)}, bf16[512,1536]{1,0:T(8,128)(2,1)S(1)}, u32[]{:S(2)}, u32[]{:S(2)}) collective-permute-start(bf16[512,1536]{1,0:T(8,128)(2,1)S(1)} %collective-permute-done.x0.own_in), channel_id=1, source_target_pairs={{0,2},{1,3},{2,0},{3,1},{4,6},{5,7},{6,4},{7,5},{8,10},{9,11},{10,... | collective-permute-start | bytes 4718600 | tf_op jit(solution)/shard_map/ppermute | solution.py:21
  56.2 35.6 %collective-permute-start.5 = (bf16[192,3456]{1,0:T(8,128)(2,1)}, bf16[192,3456]{1,0:T(8,128)(2,1)S(1)}, u32[]{:S(2)}, u32[]{:S(2)}) collective-permute-start(bf16[192,3456]{1,0:T(8,128)(2,1)} %get-tuple-element.80), channel_id=1, source_target_pairs={{0,4},{4,0},{1,5},{5,1},{2,6},{6,2},{3,7},{7,3},{8,12},{12,8},{9,1... | collective-permute-start | bytes 3981320 | tf_op jit(solution)/shard_map/ppermute | solution.py:21
  95.7 269.0 %all-gather.11.cloned.1.call-start = ((), (), s32[]{:S(2)}) async-start(), calls=%async_computation.12 | async-start | bytes 5898240 | tf_op jit(solution)/shard_map/all_gather | solution.py:1466
  95.7 36.4 %collective-permute-start.6 = (bf16[512,1536]{1,0:T(8,128)(2,1)}, bf16[512,1536]{1,0:T(8,128)(2,1)}, u32[]{:S(2)}, u32[]{:S(2)}) collective-permute-start(bf16[512,1536]{1,0:T(8,128)(2,1)} %get-tuple-element.81), channel_id=1, source_target_pairs={{0,4},{4,0},{1,5},{5,1},{2,6},{6,2},{3,7},{7,3},{8,12},{12,8},{9,1... | collective-permute-start | bytes 4718600 | tf_op jit(solution)/shard_map/ppermute | solution.py:21
  97.1 39.2 %collective-permute-start.1 = (bf16[512,1536]{1,0:T(8,128)(2,1)S(1)}, bf16[512,1536]{1,0:T(8,128)(2,1)S(1)}, u32[]{:S(2)}, u32[]{:S(2)}) collective-permute-start(bf16[512,1536]{1,0:T(8,128)(2,1)S(1)} %collective-permute-done.x0.own_in), channel_id=1, source_target_pairs={{0,1},{1,0},{2,3},{3,2},{4,5},{5,4},{6,7},{7,6},{8,9},{9,8},{10,11... | collective-permute-start | bytes 4718600 | tf_op jit(solution)/shard_map/ppermute | solution.py:21
  132.1 35.4 %collective-permute-start.8 = (bf16[512,1536]{1,0:T(8,128)(2,1)}, bf16[512,1536]{1,0:T(8,128)(2,1)}, u32[]{:S(2)}, u32[]{:S(2)}) collective-permute-start(bf16[512,1536]{1,0:T(8,128)(2,1)} %collective-permute-done.6.refs_0_), channel_id=1, source_target_pairs={{0,2},{1,3},{2,0},{3,1},{4,6},{5,7},{6,4},{7,5},{8,10},{9,11},{10,... | collective-permute-start | bytes 4718600 | tf_op jit(solution)/shard_map/ppermute | solution.py:21
  167.5 66.2 %collective-permute-start.11 = (bf16[512,1536]{1,0:T(8,128)(2,1)}, bf16[512,1536]{1,0:T(8,128)(2,1)}, u32[]{:S(2)}, u32[]{:S(2)}) collective-permute-start(bf16[512,1536]{1,0:T(8,128)(2,1)} %collective-permute-done.6.refs_0_), channel_id=1, source_target_pairs={{0,1},{1,0},{2,3},{3,2},{4,5},{5,4},{6,7},{7,6},{8,9},{9,8},{10,11... | collective-permute-start | bytes 4718600 | tf_op jit(solution)/shard_map/ppermute | solution.py:21
  169.2 64.5 %collective-permute-start.12 = (bf16[512,1536]{1,0:T(8,128)(2,1)}, bf16[512,1536]{1,0:T(8,128)(2,1)}, u32[]{:S(2)}, u32[]{:S(2)}) collective-permute-start(bf16[512,1536]{1,0:T(8,128)(2,1)} %collective-permute-done.8.refs_2_), channel_id=1, source_target_pairs={{0,1},{1,0},{2,3},{3,2},{4,5},{5,4},{6,7},{7,6},{8,9},{9,8},{10,11... | collective-permute-start | bytes 4718600 | tf_op jit(solution)/shard_map/ppermute | solution.py:21
  227.9 35.5 %collective-permute-start.14 = (bf16[512,1536]{1,0:T(8,128)(2,1)}, bf16[512,1536]{1,0:T(8,128)(2,1)}, u32[]{:S(2)}, u32[]{:S(2)}) collective-permute-start(bf16[512,1536]{1,0:T(8,128)(2,1)} %get-tuple-element.88.refs_0_), channel_id=1, source_target_pairs={{0,4},{4,0},{1,5},{5,1},{2,6},{6,2},{3,7},{7,3},{8,12},{12,8},{9,1... | collective-permute-start | bytes 4718600 | tf_op jit(solution)/shard_map/ppermute | solution.py:21
  230.1 34.2 %collective-permute-start.10 = (bf16[512,1536]{1,0:T(8,128)(2,1)}, bf16[512,1536]{1,0:T(8,128)(2,1)}, u32[]{:S(2)}, u32[]{:S(2)}) collective-permute-start(bf16[512,1536]{1,0:T(8,128)(2,1)} %get-tuple-element.88.refs_0_), channel_id=1, source_target_pairs={{0,2},{1,3},{2,0},{3,1},{4,6},{5,7},{6,4},{7,5},{8,10},{9,11},{10,... | collective-permute-start | bytes 4718600 | tf_op jit(solution)/shard_map/ppermute | solution.py:21
  231.5 237.4 %reduce-scatter.6.cloned.1.call-start = ((), (), s32[]{:S(2)}) async-start(), calls=%async_computation.5 | async-start | bytes 7372800 | tf_op jit(solution)/shard_map/reduce_scatter | solution.py:1710
  231.8 39.4 %collective-permute-start.16 = (bf16[512,1536]{1,0:T(8,128)(2,1)}, bf16[512,1536]{1,0:T(8,128)(2,1)}, u32[]{:S(2)}, u32[]{:S(2)}) collective-permute-start(bf16[512,1536]{1,0:T(8,128)(2,1)} %get-tuple-element.88.refs_0_), channel_id=1, source_target_pairs={{0,1},{1,0},{2,3},{3,2},{4,5},{5,4},{6,7},{7,6},{8,9},{9,8},{10,11... | collective-permute-start | bytes 4718600 | tf_op jit(solution)/shard_map/ppermute | solution.py:21
  364.6 216.4 %reduce-scatter.10.cloned.1.call-start = ((), (), s32[]{:S(2)}) async-start(), calls=%async_computation.7 | async-start | bytes 1966080 | tf_op jit(solution)/shard_map/reduce_scatter | solution.py:1710
  468.9 112.2 %reduce-scatter.8.cloned.1.call-start = ((), (), s32[]{:S(2)}) async-start(), calls=%async_computation.6 | async-start | bytes 1966080 | tf_op jit(solution)/shard_map/reduce_scatter | solution.py:1710
  469.4 111.6 %reduce-scatter.12.cloned.1.call-start = ((), (), s32[]{:S(2)}) async-start(), calls=%async_computation.8 | async-start | bytes 1966080 | tf_op jit(solution)/shard_map/reduce_scatter | solution.py:1710
  524.1 198.2 %reduce-scatter.14.cloned.1.call-start = ((), (), s32[]{:S(2)}) async-start(), calls=%async_computation.9 | async-start | bytes 1966080 | tf_op jit(solution)/shard_map/reduce_scatter | solution.py:1769
  639.5 32.5 %collective-permute-start.25 = (bf16[4,192,1024]{2,1,0:T(8,128)(2,1)}, bf16[4,192,1024]{2,1,0:T(8,128)(2,1)}, u32[]{:S(2)}, u32[]{:S(2)}) collective-permute-start(bf16[4,192,1024]{2,1,0:T(8,128)(2,1)} %dynamic-slice_bitcast_fusion), channel_id=1, source_target_pairs={{0,4},{4,0},{1,5},{5,1},{2,6},{6,2},{3,7},{7,3},{8,12},{12,8},{9,1... | collective-permute-start | bytes 4718600 | tf_op jit(solution)/shard_map/ppermute | solution.py:21
  640.6 43.1 %collective-permute-start.24 = (bf16[512,1536]{1,0:T(8,128)(2,1)}, bf16[512,1536]{1,0:T(8,128)(2,1)S(1)}, u32[]{:S(2)}, u32[]{:S(2)}) collective-permute-start(bf16[512,1536]{1,0:T(8,128)(2,1)} %get-tuple-element.131), channel_id=1, source_target_pairs={{0,0},{17,1},{10,2},{27,3},{8,8},{25,9},{18,10},{3,11},{16,16},{1,... | collective-permute-start | bytes 4718600 | tf_op jit(solution)/shard_map/ppermute | solution.py:1775
  645.1 40.2 %collective-permute-start.22 = (bf16[512,1536]{1,0:T(8,128)(2,1)S(1)}, bf16[512,1536]{1,0:T(8,128)(2,1)}, u32[]{:S(2)}, u32[]{:S(2)}) collective-permute-start(bf16[512,1536]{1,0:T(8,128)(2,1)S(1)} %copy-done.2), channel_id=1, source_target_pairs={{0,2},{1,3},{2,0},{3,1},{4,6},{5,7},{6,4},{7,5},{8,10},{9,11},{10,... | collective-permute-start | bytes 4718600 | tf_op jit(solution)/shard_map/ppermute | solution.py:21
  683.6 36.5 %collective-permute-start.27 = (bf16[512,1536]{1,0:T(8,128)(2,1)S(1)}, bf16[512,1536]{1,0:T(8,128)(2,1)}, u32[]{:S(2)}, u32[]{:S(2)}) collective-permute-start(bf16[512,1536]{1,0:T(8,128)(2,1)S(1)} %collective-permute-done.24.refs_0_), channel_id=1, source_target_pairs={{0,2},{1,3},{2,0},{3,1},{4,6},{5,7},{6,4},{7,5},{8,10},{9,11},{10,... | collective-permute-start | bytes 4718600 | tf_op jit(solution)/shard_map/ppermute | solution.py:21
  690.3 37.3 %collective-permute-start.26 = (bf16[512,1536]{1,0:T(8,128)(2,1)S(1)}, bf16[512,1536]{1,0:T(8,128)(2,1)}, u32[]{:S(2)}, u32[]{:S(2)}) collective-permute-start(bf16[512,1536]{1,0:T(8,128)(2,1)S(1)} %collective-permute-done.24.refs_0_), channel_id=1, source_target_pairs={{0,1},{1,0},{2,3},{3,2},{4,5},{5,4},{6,7},{7,6},{8,9},{9,8},{10,11... | collective-permute-start | bytes 4718600 | tf_op jit(solution)/shard_map/ppermute | solution.py:21
  (51 other events, 429.7 us)
Sparse Core Ops, SparseCore 0:
  55.1 71.4 all-gather.6
  128.2 107.7 all-gather.8
  237.5 87.5 all-gather.10
  364.8 104.0 reduce-scatter.5
  471.0 35.5 reduce-scatter.9
  508.8 34.2 reduce-scatter.7
  545.4 34.2 reduce-scatter.11
  675.8 38.8 reduce-scatter.13

commit v13 on v12

--- a/solution.py
+++ b/solution.py
@@ -1500,7 +1500,6 @@
     else:
         down_full = all_rows(unit_both[..., :half_units], cross_in)
         gate_up_full = all_rows(unit_both[..., half_units:], cross_in)
-    project_full = near_full[:, : query_cols + head_width]
     output_full = near_full[:, near_cols:]
     bias_head = lax.dynamic_slice_in_dim(bias_keyval, head_pair * 2, 2, axis=0)
     bias_row = jnp.concatenate([bias_query.reshape(1, -1), bias_head.reshape(1, -1)], axis=1).astype(WIDE)
@@ -1524,6 +1523,7 @@
     else:
         key_past = lax.all_gather(key_own, "ctx", axis=1, tiled=True)
         value_past = lax.all_gather(value_own, "ctx", axis=1, tiled=True)
+    project_full = after(near_full, query_rot)[:, : query_cols + head_width]
     own_weight = lax.dynamic_slice_in_dim(
         project_full, query_cols + parity * head_dim, head_dim, axis=1
     )

time: 753 us -> 753 us (level)
  transfers between devices with their start and end apart: 37 -> 37, of which waited for: 16 -> 16; matrix products, arithmetic and copies ran while one was open for 7% -> 6% of each run, Pallas kernels for 51% -> 51%
where the time goes in v13:
time: 753 us; the launch traced here: 743 us
  Pallas kernels  440 us (58%)
  waiting for transfers between devices  173 us (23%)
  starting transfers between devices  44.5 us (6%)
  other arithmetic  35.8 us (5%)
  local copies, waits for them, and re-layouts  32.6 us (4%)
  between operations  17.2 us (2%)
    ppermute x25, waiting for transfers between devices, from_partner(): return lax.ppermute(value, axis, pairs)  153 us
    pallas_call x1, Pallas kernels, collect_back(): pl.pallas_call(functools.partial(collect_kernel, slots, tiles), grid=(slo...  70.8 us
    pallas_call x1, Pallas kernels, attend_exchange(): pl.pallas_call(functools.partial(exchange_kernel, heads, head_dim, scale,...  56.9 us
    pallas_call x1, Pallas kernels, spread_branch(): pl.pallas_call(functools.partial(branch_kernel, slots, tiles), grid=(slot...  54.6 us
    pallas_call x1, Pallas kernels, attend_sum(): pl.pallas_call(functools.partial(attend_sum_kernel, heads, head_dim, scal...  52.4 us
    pallas_call x1, Pallas kernels, finish_rows(): pl.pallas_call(functools.partial(line_kernel, slots, tiles, len(sums)), g...  52.3 us
    pallas_call x1, Pallas kernels, first_grads(): pl.pallas_call(first_grads_kernel, grid=(3, tiles), in_specs=[pl.BlockSpe...  41.7 us
    ppermute x25, starting transfers between devices, from_partner(): return lax.ppermute(value, axis, pairs)  29.5 us
  transfers between devices with their start and end apart: 37, of which 16 were waited for; matrix products, arithmetic and copies ran while one was open for 6% of the time, Pallas kernels for 51%

profile of v13, /device:TPU:1, one launch (start us, length us, event | category | flops | bytes accessed | tf_op | source)
XLA Modules:
  0.0 742.7 jit_solution(7530495352115628452)
XLA Ops:
  14.9 5.2 collective-permute-start
  31.0 5.6 fusion.3
  37.8 9.1 %collective-permute-done.4 = bf16[192,1152]{1,0:T(8,128)(2,1)S(1)} collective-permute-done((bf16[192,1152]{1,0:T(8,128)(2,1)S(1)}, bf16[192,1152]{1,0:T(8,128)(2,1)S(1)}, u32[]{:S(2)}, u32[]{:S(2)}) %collective-permute-start.4) | collective-permute-done | bytes 442400 | tf_op jit(solution)/shard_map/ppermute | solution.py:21
  48.1 6.8 collective-permute-done.x0.own_in
  58.8 30.9 %collective-permute-done.2.x2 = bf16[512,1536]{1,0:T(8,128)(2,1)S(1)} collective-permute-done((bf16[512,1536]{1,0:T(8,128)(2,1)S(1)}, bf16[512,1536]{1,0:T(8,128)(2,1)S(1)}, u32[]{:S(2)}, u32[]{:S(2)}) %collective-permute-start.2) | collective-permute-done | bytes 1572896 | tf_op jit(solution)/shard_map/ppermute | solution.py:21
  98.0 34.1 %collective-permute-done.6.refs_0_ = bf16[512,1536]{1,0:T(8,128)(2,1)} collective-permute-done((bf16[512,1536]{1,0:T(8,128)(2,1)}, bf16[512,1536]{1,0:T(8,128)(2,1)}, u32[]{:S(2)}, u32[]{:S(2)}) %collective-permute-start.6) | collective-permute-done | bytes 1572896 | tf_op jit(solution)/shard_map/ppermute | solution.py:21
  136.7 13.0 %shard_map.221 = (bf16[4,512,1536]{2,1,0:T(8,128)(2,1)}, bf16[4,512,384]{2,1,0:T(8,128)(2,1)}, bf16[4,512,128]{2,1,0:T(8,128)(2,1)}, bf16[4,512,128]{2,1,0:T(8,128)(2,1)}) custom-call(bf16[512,1536]{1,0:T(8,128)(2,1)} %copy-done.7, bf16[512,1536]{1,0:T(8,128)(2,1)} %copy-done.12, bf16[512,1536]{1,0:T(8,128)(2,1)} %copy-done.11, ...), custom_call_target="tpu_custom_call" | custom-call | flops 4026531840 | bytes 17170432 | tf_op jit(solution)/shard_map/pallas_call | solution.py:855
  155.8 11.7 %collective-permute-done.8.refs_2_ = bf16[512,1536]{1,0:T(8,128)(2,1)} collective-permute-done((bf16[512,1536]{1,0:T(8,128)(2,1)}, bf16[512,1536]{1,0:T(8,128)(2,1)}, u32[]{:S(2)}, u32[]{:S(2)}) %collective-permute-start.8) | collective-permute-done | bytes 1572896 | tf_op jit(solution)/shard_map/ppermute | solution.py:21
  175.3 52.4 %shard_map.222 = (bf16[4,512,384]{2,1,0:T(8,128)(2,1)}, f32[4,512,128]{2,1,0:T(8,128)}, f32[512,1536]{1,0:T(8,128)}, bf16[512,1536]{1,0:T(8,128)(2,1)}) custom-call(s32[8]{0:T(128)} %compare_select_fusion.14.info, bf16[4,512,384]{2,1,0:T(8,128)(2,1)} %get-tuple-element.84.q, bf16[4,512,128]{2,1,0:T(8,128)(2,1)} %copy-done.21, ...), custom_call_target="tpu_custom_call" | custom-call | flops 3221225472 | bytes 3145728 | tf_op jit(solution)/shard_map/pallas_call | solution.py:1163
  236.5 18.6 %shard_map.223 = (bf16[4096,640]{1,0:T(8,128)(2,1)}, bf16[4096,1536]{1,0:T(8,128)(2,1)}) custom-call(s32[8]{0:T(128)} %compare_select_fusion.13.info, bf16[4,512,1536]{2,1,0:T(8,128)(2,1)} %cotangent, bf16[512,1536]{1,0:T(8,128)(2,1)} %collective-permute-done.6.refs_0_, bf16[512,1536]{1,0:T(8,128)(2,1)} %collective-permute-done.11.refs_1_, ...), custom_call_target="tpu_custom_call" | custom-call | flops 8053063680 | bytes 32374784 | tf_op jit(solution)/shard_map/pallas_call | solution.py:230
  255.1 8.3 %collective-permute-done.14.refs_4_ = bf16[512,1536]{1,0:T(8,128)(2,1)} collective-permute-done((bf16[512,1536]{1,0:T(8,128)(2,1)}, bf16[512,1536]{1,0:T(8,128)(2,1)}, u32[]{:S(2)}, u32[]{:S(2)}) %collective-permute-start.14) | collective-permute-done | bytes 1572896 | tf_op jit(solution)/shard_map/ppermute | solution.py:21
  272.7 14.4 %shard_map.224 = (bf16[4096,640]{1,0:T(8,128)(2,1)}, bf16[4096,1536]{1,0:T(8,128)(2,1)}) custom-call(bf16[512,1536]{1,0:T(8,128)(2,1)} %get-tuple-element.90.refs_0_, bf16[512,1536]{1,0:T(8,128)(2,1)} %collective-permute-done.16.refs_1_, bf16[512,1536]{1,0:T(8,128)(2,1)} %collective-permute-done.10.refs_2_, ...), custom_call_target="tpu_custom_call" | custom-call | flops 6039797760 | bytes 24772608 | tf_op jit(solution)/shard_map/pallas_call | solution.py:123
  294.3 6.8 shard_map.225
  301.2 21.1 %shard_map.226 = (bf16[4096,640]{1,0:T(8,128)(2,1)}, bf16[4096,640]{1,0:T(8,128)(2,1)}, bf16[4096,640]{1,0:T(8,128)(2,1)}) custom-call(bf16[4096,1536]{1,0:T(8,128)(2,1)} %get-tuple-element.108.h.right.turned, bf16[1536,1920]{1,0:T(8,128)(2,1)} %bitcast.67, bf16[4096,640]{1,0:T(8,128)(2,1)} %get-tuple-element.103.gate, bf16[4096,640]{1,0:T(8,128)(2,1)} %get-tuple-element.95.grad), custom_call_target="tpu_custom_call" | custom-call | flops 8053063680 | bytes 40763392 | tf_op jit(solution)/shard_map/pallas_call | solution.py:161
  322.3 41.7 %shard_map.227 = bf16[1536,1920]{1,0:T(8,128)(2,1)} custom-call(bf16[4096,1536]{1,0:T(8,128)(2,1)} %get-tuple-element.106.g.left.own_grad, bf16[4096,1536]{1,0:T(8,128)(2,1)} %get-tuple-element.108.h.right.turned, bf16[4096,640]{1,0:T(8,128)(2,1)} %get-tuple-element.107.hid.hid_a, bf16[4096,640]{1,0:T(8,128)(2,1)} %get-tuple-element.104.gate.gate_a, ...), custom_call_target="tpu_custom_call" | custom-call | flops 24159191040 | bytes 21626880 | tf_op jit(solution)/shard_map/pallas_call | solution.py:298
  364.1 26.9 %shard_map.228 = (bf16[4096,512]{1,0:T(8,128)(2,1)}, bf16[4096,512]{1,0:T(8,128)(2,1)}, bf16[4096,512]{1,0:T(8,128)(2,1)}) custom-call(bf16[4096,1536]{1,0:T(8,128)(2,1)} %get-tuple-element.108.h.right.turned, bf16[4096,1536]{1,0:T(8,128)(2,1)} %get-tuple-element.106.g.left.own_grad, bf16[1536,1536]{1,0:T(8,128)(2,1)} %bitcast.71, ...), custom_call_target="tpu_custom_call" | custom-call | flops 19327352832 | bytes 42467328 | tf_op jit(solution)/shard_map/pallas_call | solution.py:272
  391.0 70.8 %shard_map.229 = (f32[512,1536]{1,0:T(8,128)}, bf16[1536,512]{1,0:T(8,128)(2,1)}, bf16[1536,512]{1,0:T(8,128)(2,1)}) custom-call(bf16[4096,640]{1,0:T(8,128)(2,1)} %get-tuple-element.104.gate.gate_a, bf16[4096,640]{1,0:T(8,128)(2,1)} %get-tuple-element.105.up.up_a, bf16[4096,512]{1,0:T(8,128)(2,1)} %get-tuple-element.110.gate_b.gate, ...), custom_call_target="tpu_custom_call" | custom-call | flops 19327352832 | bytes 20971520 | tf_op jit(solution)/shard_map/pallas_call | solution.py:439
  461.8 6.8 reduce-scatter.6.cloned.1.call-done.refs_0_
  469.2 54.6 %shard_map.230 = (f32[512,1536]{1,0:T(8,128)}, f32[1,1536]{1,0:T(1,128)}, bf16[1536,512]{1,0:T(8,128)(2,1)}, bf16[4,512,1536]{2,1,0:T(8,128)(2,1)}, bf16[512,153...) custom-call(f32[512,1536]{1,0:T(8,128)} %get-tuple-element.113.total, ...), custom_call_target="tpu_custom_call" | custom-call | flops 12884901888 | bytes 20971520 | tf_op jit(solution)/shard_map/pallas_call | solution.py:577
  523.9 56.9 %shard_map.231 = (bf16[4,512,512]{2,1,0:T(8,128)(2,1)}, bf16[1536,384]{1,0:T(8,128)(2,1)}, bf16[512,1536]{1,0:T(8,128)(2,1)}) custom-call(s32[8]{0:T(128)} %compare_select_fusion.14.info, bf16[4,512,384]{2,1,0:T(8,128)(2,1)} %get-tuple-element.84.q, bf16[4,512,128]{2,1,0:T(8,128)(2,1)} %copy-done.21, bf16[4,512,128]{2,1,0:T(8,128)(2,1)} %copy-done.22, ...), custom_call_target="tpu_custom_call" | custom-call | flops 2415919104 | bytes 7864320 | tf_op jit(solution)/shard_map/pallas_call | solution.py:1315
  580.8 52.3 %shard_map.232 = (bf16[512,1536]{1,0:T(8,128)(2,1)}, f32[2,1536]{1,0:T(2,128)}, bf16[1536,512]{1,0:T(8,128)(2,1)}, f32[1,512]{1,0:T(1,128)}, bf16[512,1536]{1,0:...) custom-call(bf16[2048,512]{1,0:T(8,128)(2,1)} %bitcast.87, ...), custom_call_target="tpu_custom_call" | custom-call | flops 3221225472 | bytes 31457280 | tf_op jit(solution)/shard_map/pallas_call | solution.py:736
  645.0 26.7 %collective-permute-done.25 = bf16[4,192,1024]{2,1,0:T(8,128)(2,1)} collective-permute-done((bf16[4,192,1024]{2,1,0:T(8,128)(2,1)}, bf16[4,192,1024]{2,1,0:T(8,128)(2,1)}, u32[]{:S(2)}, u32[]{:S(2)}) %collective-permute-start.25) | collective-permute-done | bytes 1572896 | tf_op jit(solution)/shard_map/ppermute | solution.py:21
  695.2 24.4 %collective-permute-done.27.refs_2_ = bf16[512,1536]{1,0:T(8,128)(2,1)} collective-permute-done((bf16[512,1536]{1,0:T(8,128)(2,1)S(1)}, bf16[512,1536]{1,0:T(8,128)(2,1)}, u32[]{:S(2)}, u32[]{:S(2)}) %collective-permute-start.27) | collective-permute-done | bytes 1572896 | tf_op jit(solution)/shard_map/ppermute | solution.py:21
  729.9 5.5 shard_map.234
  (223 shorter events, 120.9 us)
Async XLA Ops:
  7.2 128.4 %all-gather.7.cloned.1.call-start = ((), (), s32[]{:S(2)}) async-start(), calls=%async_computation.10 | async-start | bytes 4423680 | tf_op jit(solution)/shard_map/all_gather | solution.py:1466
  14.9 40.0 %collective-permute-start = (bf16[512,1536]{1,0:T(8,128)(2,1)}, bf16[512,1536]{1,0:T(8,128)(2,1)S(1)}, u32[]{:S(2)}, u32[]{:S(2)}) collective-permute-start(bf16[512,1536]{1,0:T(8,128)(2,1)} %get-tuple-element.262), channel_id=1, source_target_pairs={{0,0},{1,17},{2,10},{3,27},{8,8},{9,25},{10,18},{11,3},{16,16},{17... | collective-permute-start | bytes 4718600 | tf_op jit(solution)/shard_map/ppermute | solution.py:1429
  54.9 181.6 %all-gather.9.cloned.1.call-start = ((), (), s32[]{:S(2)}) async-start(), calls=%async_computation.11 | async-start | bytes 7372800 | tf_op jit(solution)/shard_map/all_gather | solution.py:1466
  55.0 34.7 %collective-permute-start.2 = (bf16[512,1536]{1,0:T(8,128)(2,1)S(1)}, bf16[512,1536]{1,0:T(8,128)(2,1)S(1)}, u32[]{:S(2)}, u32[]{:S(2)}) collective-permute-start(bf16[512,1536]{1,0:T(8,128)(2,1)S(1)} %collective-permute-done.x0.own_in), channel_id=1, source_target_pairs={{0,2},{1,3},{2,0},{3,1},{4,6},{5,7},{6,4},{7,5},{8,10},{9,11},{10,... | collective-permute-start | bytes 4718600 | tf_op jit(solution)/shard_map/ppermute | solution.py:21
  56.2 35.6 %collective-permute-start.5 = (bf16[192,3456]{1,0:T(8,128)(2,1)}, bf16[192,3456]{1,0:T(8,128)(2,1)S(1)}, u32[]{:S(2)}, u32[]{:S(2)}) collective-permute-start(bf16[192,3456]{1,0:T(8,128)(2,1)} %get-tuple-element.81), channel_id=1, source_target_pairs={{0,4},{4,0},{1,5},{5,1},{2,6},{6,2},{3,7},{7,3},{8,12},{12,8},{9,1... | collective-permute-start | bytes 3981320 | tf_op jit(solution)/shard_map/ppermute | solution.py:21
  95.7 268.4 %all-gather.11.cloned.1.call-start = ((), (), s32[]{:S(2)}) async-start(), calls=%async_computation.12 | async-start | bytes 5898240 | tf_op jit(solution)/shard_map/all_gather | solution.py:1466
  95.7 36.4 %collective-permute-start.6 = (bf16[512,1536]{1,0:T(8,128)(2,1)}, bf16[512,1536]{1,0:T(8,128)(2,1)}, u32[]{:S(2)}, u32[]{:S(2)}) collective-permute-start(bf16[512,1536]{1,0:T(8,128)(2,1)} %get-tuple-element.82), channel_id=1, source_target_pairs={{0,4},{4,0},{1,5},{5,1},{2,6},{6,2},{3,7},{7,3},{8,12},{12,8},{9,1... | collective-permute-start | bytes 4718600 | tf_op jit(solution)/shard_map/ppermute | solution.py:21
  97.1 38.5 %collective-permute-start.1 = (bf16[512,1536]{1,0:T(8,128)(2,1)S(1)}, bf16[512,1536]{1,0:T(8,128)(2,1)S(1)}, u32[]{:S(2)}, u32[]{:S(2)}) collective-permute-start(bf16[512,1536]{1,0:T(8,128)(2,1)S(1)} %collective-permute-done.x0.own_in), channel_id=1, source_target_pairs={{0,1},{1,0},{2,3},{3,2},{4,5},{5,4},{6,7},{7,6},{8,9},{9,8},{10,11... | collective-permute-start | bytes 4718600 | tf_op jit(solution)/shard_map/ppermute | solution.py:21
  132.1 35.4 %collective-permute-start.8 = (bf16[512,1536]{1,0:T(8,128)(2,1)}, bf16[512,1536]{1,0:T(8,128)(2,1)}, u32[]{:S(2)}, u32[]{:S(2)}) collective-permute-start(bf16[512,1536]{1,0:T(8,128)(2,1)} %collective-permute-done.6.refs_0_), channel_id=1, source_target_pairs={{0,2},{1,3},{2,0},{3,1},{4,6},{5,7},{6,4},{7,5},{8,10},{9,11},{10,... | collective-permute-start | bytes 4718600 | tf_op jit(solution)/shard_map/ppermute | solution.py:21
  167.5 65.7 %collective-permute-start.11 = (bf16[512,1536]{1,0:T(8,128)(2,1)}, bf16[512,1536]{1,0:T(8,128)(2,1)}, u32[]{:S(2)}, u32[]{:S(2)}) collective-permute-start(bf16[512,1536]{1,0:T(8,128)(2,1)} %collective-permute-done.6.refs_0_), channel_id=1, source_target_pairs={{0,1},{1,0},{2,3},{3,2},{4,5},{5,4},{6,7},{7,6},{8,9},{9,8},{10,11... | collective-permute-start | bytes 4718600 | tf_op jit(solution)/shard_map/ppermute | solution.py:21
  169.2 64.0 %collective-permute-start.12 = (bf16[512,1536]{1,0:T(8,128)(2,1)}, bf16[512,1536]{1,0:T(8,128)(2,1)}, u32[]{:S(2)}, u32[]{:S(2)}) collective-permute-start(bf16[512,1536]{1,0:T(8,128)(2,1)} %collective-permute-done.8.refs_2_), channel_id=1, source_target_pairs={{0,1},{1,0},{2,3},{3,2},{4,5},{5,4},{6,7},{7,6},{8,9},{9,8},{10,11... | collective-permute-start | bytes 4718600 | tf_op jit(solution)/shard_map/ppermute | solution.py:21
  227.7 35.7 %collective-permute-start.14 = (bf16[512,1536]{1,0:T(8,128)(2,1)}, bf16[512,1536]{1,0:T(8,128)(2,1)}, u32[]{:S(2)}, u32[]{:S(2)}) collective-permute-start(bf16[512,1536]{1,0:T(8,128)(2,1)} %get-tuple-element.90.refs_0_), channel_id=1, source_target_pairs={{0,4},{4,0},{1,5},{5,1},{2,6},{6,2},{3,7},{7,3},{8,12},{12,8},{9,1... | collective-permute-start | bytes 4718600 | tf_op jit(solution)/shard_map/ppermute | solution.py:21
  229.9 34.4 %collective-permute-start.10 = (bf16[512,1536]{1,0:T(8,128)(2,1)}, bf16[512,1536]{1,0:T(8,128)(2,1)}, u32[]{:S(2)}, u32[]{:S(2)}) collective-permute-start(bf16[512,1536]{1,0:T(8,128)(2,1)} %get-tuple-element.90.refs_0_), channel_id=1, source_target_pairs={{0,2},{1,3},{2,0},{3,1},{4,6},{5,7},{6,4},{7,5},{8,10},{9,11},{10,... | collective-permute-start | bytes 4718600 | tf_op jit(solution)/shard_map/ppermute | solution.py:21
  230.8 237.8 %reduce-scatter.6.cloned.1.call-start = ((), (), s32[]{:S(2)}) async-start(), calls=%async_computation.5 | async-start | bytes 7372800 | tf_op jit(solution)/shard_map/reduce_scatter | solution.py:1710
  231.1 39.4 %collective-permute-start.16 = (bf16[512,1536]{1,0:T(8,128)(2,1)}, bf16[512,1536]{1,0:T(8,128)(2,1)}, u32[]{:S(2)}, u32[]{:S(2)}) collective-permute-start(bf16[512,1536]{1,0:T(8,128)(2,1)} %get-tuple-element.90.refs_0_), channel_id=1, source_target_pairs={{0,1},{1,0},{2,3},{3,2},{4,5},{5,4},{6,7},{7,6},{8,9},{9,8},{10,11... | collective-permute-start | bytes 4718600 | tf_op jit(solution)/shard_map/ppermute | solution.py:21
  364.0 216.8 %reduce-scatter.10.cloned.1.call-start = ((), (), s32[]{:S(2)}) async-start(), calls=%async_computation.7 | async-start | bytes 1966080 | tf_op jit(solution)/shard_map/reduce_scatter | solution.py:1710
  468.6 112.2 %reduce-scatter.8.cloned.1.call-start = ((), (), s32[]{:S(2)}) async-start(), calls=%async_computation.6 | async-start | bytes 1966080 | tf_op jit(solution)/shard_map/reduce_scatter | solution.py:1710
  469.2 111.7 %reduce-scatter.12.cloned.1.call-start = ((), (), s32[]{:S(2)}) async-start(), calls=%async_computation.8 | async-start | bytes 1966080 | tf_op jit(solution)/shard_map/reduce_scatter | solution.py:1710
  523.8 198.1 %reduce-scatter.14.cloned.1.call-start = ((), (), s32[]{:S(2)}) async-start(), calls=%async_computation.9 | async-start | bytes 1966080 | tf_op jit(solution)/shard_map/reduce_scatter | solution.py:1769
  639.2 32.5 %collective-permute-start.25 = (bf16[4,192,1024]{2,1,0:T(8,128)(2,1)}, bf16[4,192,1024]{2,1,0:T(8,128)(2,1)}, u32[]{:S(2)}, u32[]{:S(2)}) collective-permute-start(bf16[4,192,1024]{2,1,0:T(8,128)(2,1)} %dynamic-slice_bitcast_fusion), channel_id=1, source_target_pairs={{0,4},{4,0},{1,5},{5,1},{2,6},{6,2},{3,7},{7,3},{8,12},{12,8},{9,1... | collective-permute-start | bytes 4718600 | tf_op jit(solution)/shard_map/ppermute | solution.py:21
  640.3 43.1 %collective-permute-start.24 = (bf16[512,1536]{1,0:T(8,128)(2,1)}, bf16[512,1536]{1,0:T(8,128)(2,1)S(1)}, u32[]{:S(2)}, u32[]{:S(2)}) collective-permute-start(bf16[512,1536]{1,0:T(8,128)(2,1)} %get-tuple-element.133), channel_id=1, source_target_pairs={{0,0},{17,1},{10,2},{27,3},{8,8},{25,9},{18,10},{3,11},{16,16},{1,... | collective-permute-start | bytes 4718600 | tf_op jit(solution)/shard_map/ppermute | solution.py:1775
  644.9 40.1 %collective-permute-start.22 = (bf16[512,1536]{1,0:T(8,128)(2,1)S(1)}, bf16[512,1536]{1,0:T(8,128)(2,1)}, u32[]{:S(2)}, u32[]{:S(2)}) collective-permute-start(bf16[512,1536]{1,0:T(8,128)(2,1)S(1)} %copy-done.2), channel_id=1, source_target_pairs={{0,2},{1,3},{2,0},{3,1},{4,6},{5,7},{6,4},{7,5},{8,10},{9,11},{10,... | collective-permute-start | bytes 4718600 | tf_op jit(solution)/shard_map/ppermute | solution.py:21
  683.4 36.2 %collective-permute-start.27 = (bf16[512,1536]{1,0:T(8,128)(2,1)S(1)}, bf16[512,1536]{1,0:T(8,128)(2,1)}, u32[]{:S(2)}, u32[]{:S(2)}) collective-permute-start(bf16[512,1536]{1,0:T(8,128)(2,1)S(1)} %collective-permute-done.24.refs_0_), channel_id=1, source_target_pairs={{0,2},{1,3},{2,0},{3,1},{4,6},{5,7},{6,4},{7,5},{8,10},{9,11},{10,... | collective-permute-start | bytes 4718600 | tf_op jit(solution)/shard_map/ppermute | solution.py:21
  690.0 37.3 %collective-permute-start.26 = (bf16[512,1536]{1,0:T(8,128)(2,1)S(1)}, bf16[512,1536]{1,0:T(8,128)(2,1)}, u32[]{:S(2)}, u32[]{:S(2)}) collective-permute-start(bf16[512,1536]{1,0:T(8,128)(2,1)S(1)} %collective-permute-done.24.refs_0_), channel_id=1, source_target_pairs={{0,1},{1,0},{2,3},{3,2},{4,5},{5,4},{6,7},{7,6},{8,9},{9,8},{10,11... | collective-permute-start | bytes 4718600 | tf_op jit(solution)/shard_map/ppermute | solution.py:21
  (52 other events, 462.3 us)
Sparse Core Ops, SparseCore 0:
  55.1 71.4 all-gather.6
  128.7 107.7 all-gather.8
  238.1 87.5 all-gather.10
  364.1 104.4 reduce-scatter.5
  470.7 35.5 reduce-scatter.9
  508.5 34.2 reduce-scatter.7
  545.1 34.2 reduce-scatter.11
  675.5 38.8 reduce-scatter.13

commit v14 on v13

--- a/solution.py
+++ b/solution.py
@@ -149,7 +149,7 @@
     sigmoid = 1.0 / (1.0 + jnp.exp(-gate_lin))
     silu = gate_lin * sigmoid
     hid[...] = (silu * up_lin).astype(LOW)
-    grad_gate[...] = (grad_hidden * up_lin * sigmoid * (1.0 + gate_lin * (1.0 - sigmoid))).astype(LOW)
+    grad_gate[...] = (grad_hidden * up_lin * (sigmoid + silu * (1.0 - sigmoid))).astype(LOW)
     grad_up[...] = (grad_hidden * silu).astype(LOW)
 
 
@@ -260,7 +260,7 @@
     sigmoid = 1.0 / (1.0 + jnp.exp(-gate_lin))
     silu = gate_lin * sigmoid
     hid[...] = (silu * up_lin).astype(LOW)
-    grad_gate[...] = (grad_hidden * up_lin * sigmoid * (1.0 + gate_lin * (1.0 - sigmoid))).astype(LOW)
+    grad_gate[...] = (grad_hidden * up_lin * (sigmoid + silu * (1.0 - sigmoid))).astype(LOW)
     grad_up[...] = (grad_hidden * silu).astype(LOW)
 
 

time: 753 us -> 752 us (level)
  no operation moved by 1% of the time
where the time goes in v14:
time: 752 us; the launch traced here: 742 us
  Pallas kernels  439 us (58%)
  waiting for transfers between devices  173 us (23%)
  starting transfers between devices  44.8 us (6%)
  other arithmetic  35.8 us (5%)
  local copies, waits for them, and re-layouts  32.6 us (4%)
  between operations  16.9 us (2%)
    ppermute x25, waiting for transfers between devices, from_partner(): return lax.ppermute(value, axis, pairs)  153 us
    pallas_call x1, Pallas kernels, collect_back(): pl.pallas_call(functools.partial(collect_kernel, slots, tiles), grid=(slo...  70.8 us
    pallas_call x1, Pallas kernels, attend_exchange(): pl.pallas_call(functools.partial(exchange_kernel, heads, head_dim, scale,...  56.9 us
    pallas_call x1, Pallas kernels, spread_branch(): pl.pallas_call(functools.partial(branch_kernel, slots, tiles), grid=(slot...  54.8 us
    pallas_call x1, Pallas kernels, attend_sum(): pl.pallas_call(functools.partial(attend_sum_kernel, heads, head_dim, scal...  52.3 us
    pallas_call x1, Pallas kernels, finish_rows(): pl.pallas_call(functools.partial(line_kernel, slots, tiles, len(sums)), g...  52.1 us
    pallas_call x1, Pallas kernels, first_grads(): pl.pallas_call(first_grads_kernel, grid=(3, tiles), in_specs=[pl.BlockSpe...  41.7 us
    ppermute x25, starting transfers between devices, from_partner(): return lax.ppermute(value, axis, pairs)  29.6 us
  transfers between devices with their start and end apart: 37, of which 16 were waited for; matrix products, arithmetic and copies ran while one was open for 6% of the time, Pallas kernels for 51%

profile of v14, /device:TPU:1, one launch (start us, length us, event | category | flops | bytes accessed | tf_op | source)
XLA Modules:
  0.0 742.0 jit_solution(2809578598020973102)
XLA Ops:
  14.9 5.2 collective-permute-start
  31.0 5.6 fusion.3
  37.8 9.1 %collective-permute-done.4 = bf16[192,1152]{1,0:T(8,128)(2,1)S(1)} collective-permute-done((bf16[192,1152]{1,0:T(8,128)(2,1)S(1)}, bf16[192,1152]{1,0:T(8,128)(2,1)S(1)}, u32[]{:S(2)}, u32[]{:S(2)}) %collective-permute-start.4) | collective-permute-done | bytes 442400 | tf_op jit(solution)/shard_map/ppermute | solution.py:21
  48.1 6.8 collective-permute-done.x0.own_in
  58.8 30.9 %collective-permute-done.2.x2 = bf16[512,1536]{1,0:T(8,128)(2,1)S(1)} collective-permute-done((bf16[512,1536]{1,0:T(8,128)(2,1)S(1)}, bf16[512,1536]{1,0:T(8,128)(2,1)S(1)}, u32[]{:S(2)}, u32[]{:S(2)}) %collective-permute-start.2) | collective-permute-done | bytes 1572896 | tf_op jit(solution)/shard_map/ppermute | solution.py:21
  98.0 34.1 %collective-permute-done.6.refs_0_ = bf16[512,1536]{1,0:T(8,128)(2,1)} collective-permute-done((bf16[512,1536]{1,0:T(8,128)(2,1)}, bf16[512,1536]{1,0:T(8,128)(2,1)}, u32[]{:S(2)}, u32[]{:S(2)}) %collective-permute-start.6) | collective-permute-done | bytes 1572896 | tf_op jit(solution)/shard_map/ppermute | solution.py:21
  136.7 13.0 %shard_map.221 = (bf16[4,512,1536]{2,1,0:T(8,128)(2,1)}, bf16[4,512,384]{2,1,0:T(8,128)(2,1)}, bf16[4,512,128]{2,1,0:T(8,128)(2,1)}, bf16[4,512,128]{2,1,0:T(8,128)(2,1)}) custom-call(bf16[512,1536]{1,0:T(8,128)(2,1)} %copy-done.7, bf16[512,1536]{1,0:T(8,128)(2,1)} %copy-done.12, bf16[512,1536]{1,0:T(8,128)(2,1)} %copy-done.11, ...), custom_call_target="tpu_custom_call" | custom-call | flops 4026531840 | bytes 17170432 | tf_op jit(solution)/shard_map/pallas_call | solution.py:855
  156.1 11.4 %collective-permute-done.8.refs_2_ = bf16[512,1536]{1,0:T(8,128)(2,1)} collective-permute-done((bf16[512,1536]{1,0:T(8,128)(2,1)}, bf16[512,1536]{1,0:T(8,128)(2,1)}, u32[]{:S(2)}, u32[]{:S(2)}) %collective-permute-start.8) | collective-permute-done | bytes 1572896 | tf_op jit(solution)/shard_map/ppermute | solution.py:21
  175.3 52.3 %shard_map.222 = (bf16[4,512,384]{2,1,0:T(8,128)(2,1)}, f32[4,512,128]{2,1,0:T(8,128)}, f32[512,1536]{1,0:T(8,128)}, bf16[512,1536]{1,0:T(8,128)(2,1)}) custom-call(s32[8]{0:T(128)} %compare_select_fusion.14.info, bf16[4,512,384]{2,1,0:T(8,128)(2,1)} %get-tuple-element.84.q, bf16[4,512,128]{2,1,0:T(8,128)(2,1)} %copy-done.21, ...), custom_call_target="tpu_custom_call" | custom-call | flops 3221225472 | bytes 3145728 | tf_op jit(solution)/shard_map/pallas_call | solution.py:1163
  236.5 18.6 %shard_map.223 = (bf16[4096,640]{1,0:T(8,128)(2,1)}, bf16[4096,1536]{1,0:T(8,128)(2,1)}) custom-call(s32[8]{0:T(128)} %compare_select_fusion.13.info, bf16[4,512,1536]{2,1,0:T(8,128)(2,1)} %cotangent, bf16[512,1536]{1,0:T(8,128)(2,1)} %collective-permute-done.6.refs_0_, bf16[512,1536]{1,0:T(8,128)(2,1)} %collective-permute-done.11.refs_1_, ...), custom_call_target="tpu_custom_call" | custom-call | flops 8053063680 | bytes 32374784 | tf_op jit(solution)/shard_map/pallas_call | solution.py:230
  255.1 8.3 %collective-permute-done.14.refs_4_ = bf16[512,1536]{1,0:T(8,128)(2,1)} collective-permute-done((bf16[512,1536]{1,0:T(8,128)(2,1)}, bf16[512,1536]{1,0:T(8,128)(2,1)}, u32[]{:S(2)}, u32[]{:S(2)}) %collective-permute-start.14) | collective-permute-done | bytes 1572896 | tf_op jit(solution)/shard_map/ppermute | solution.py:21
  272.7 14.4 %shard_map.224 = (bf16[4096,640]{1,0:T(8,128)(2,1)}, bf16[4096,1536]{1,0:T(8,128)(2,1)}) custom-call(bf16[512,1536]{1,0:T(8,128)(2,1)} %get-tuple-element.90.refs_0_, bf16[512,1536]{1,0:T(8,128)(2,1)} %collective-permute-done.16.refs_1_, bf16[512,1536]{1,0:T(8,128)(2,1)} %collective-permute-done.10.refs_2_, ...), custom_call_target="tpu_custom_call" | custom-call | flops 6039797760 | bytes 24772608 | tf_op jit(solution)/shard_map/pallas_call | solution.py:123
  294.4 6.8 shard_map.225
  301.2 20.7 %shard_map.226 = (bf16[4096,640]{1,0:T(8,128)(2,1)}, bf16[4096,640]{1,0:T(8,128)(2,1)}, bf16[4096,640]{1,0:T(8,128)(2,1)}) custom-call(bf16[4096,1536]{1,0:T(8,128)(2,1)} %get-tuple-element.108.h.right.turned, bf16[1536,1920]{1,0:T(8,128)(2,1)} %bitcast.67, bf16[4096,640]{1,0:T(8,128)(2,1)} %get-tuple-element.103.gate, bf16[4096,640]{1,0:T(8,128)(2,1)} %get-tuple-element.95.grad), custom_call_target="tpu_custom_call" | custom-call | flops 8053063680 | bytes 40763392 | tf_op jit(solution)/shard_map/pallas_call | solution.py:161
  321.9 41.7 %shard_map.227 = bf16[1536,1920]{1,0:T(8,128)(2,1)} custom-call(bf16[4096,1536]{1,0:T(8,128)(2,1)} %get-tuple-element.106.g.left.own_grad, bf16[4096,1536]{1,0:T(8,128)(2,1)} %get-tuple-element.108.h.right.turned, bf16[4096,640]{1,0:T(8,128)(2,1)} %get-tuple-element.107.hid.hid_a, bf16[4096,640]{1,0:T(8,128)(2,1)} %get-tuple-element.104.gate.gate_a, ...), custom_call_target="tpu_custom_call" | custom-call | flops 24159191040 | bytes 21626880 | tf_op jit(solution)/shard_map/pallas_call | solution.py:298
  363.7 26.3 %shard_map.228 = (bf16[4096,512]{1,0:T(8,128)(2,1)}, bf16[4096,512]{1,0:T(8,128)(2,1)}, bf16[4096,512]{1,0:T(8,128)(2,1)}) custom-call(bf16[4096,1536]{1,0:T(8,128)(2,1)} %get-tuple-element.108.h.right.turned, bf16[4096,1536]{1,0:T(8,128)(2,1)} %get-tuple-element.106.g.left.own_grad, bf16[1536,1536]{1,0:T(8,128)(2,1)} %bitcast.71, ...), custom_call_target="tpu_custom_call" | custom-call | flops 19327352832 | bytes 42467328 | tf_op jit(solution)/shard_map/pallas_call | solution.py:272
  390.0 70.8 %shard_map.229 = (f32[512,1536]{1,0:T(8,128)}, bf16[1536,512]{1,0:T(8,128)(2,1)}, bf16[1536,512]{1,0:T(8,128)(2,1)}) custom-call(bf16[4096,640]{1,0:T(8,128)(2,1)} %get-tuple-element.104.gate.gate_a, bf16[4096,640]{1,0:T(8,128)(2,1)} %get-tuple-element.105.up.up_a, bf16[4096,512]{1,0:T(8,128)(2,1)} %get-tuple-element.110.gate_b.gate, ...), custom_call_target="tpu_custom_call" | custom-call | flops 19327352832 | bytes 20971520 | tf_op jit(solution)/shard_map/pallas_call | solution.py:439
  460.8 7.4 reduce-scatter.6.cloned.1.call-done.refs_0_
  468.8 54.8 %shard_map.230 = (f32[512,1536]{1,0:T(8,128)}, f32[1,1536]{1,0:T(1,128)}, bf16[1536,512]{1,0:T(8,128)(2,1)}, bf16[4,512,1536]{2,1,0:T(8,128)(2,1)}, bf16[512,153...) custom-call(f32[512,1536]{1,0:T(8,128)} %get-tuple-element.113.total, ...), custom_call_target="tpu_custom_call" | custom-call | flops 12884901888 | bytes 20971520 | tf_op jit(solution)/shard_map/pallas_call | solution.py:577
  523.6 56.9 %shard_map.231 = (bf16[4,512,512]{2,1,0:T(8,128)(2,1)}, bf16[1536,384]{1,0:T(8,128)(2,1)}, bf16[512,1536]{1,0:T(8,128)(2,1)}) custom-call(s32[8]{0:T(128)} %compare_select_fusion.14.info, bf16[4,512,384]{2,1,0:T(8,128)(2,1)} %get-tuple-element.84.q, bf16[4,512,128]{2,1,0:T(8,128)(2,1)} %copy-done.21, bf16[4,512,128]{2,1,0:T(8,128)(2,1)} %copy-done.22, ...), custom_call_target="tpu_custom_call" | custom-call | flops 2415919104 | bytes 7864320 | tf_op jit(solution)/shard_map/pallas_call | solution.py:1315
  580.6 52.1 %shard_map.232 = (bf16[512,1536]{1,0:T(8,128)(2,1)}, f32[2,1536]{1,0:T(2,128)}, bf16[1536,512]{1,0:T(8,128)(2,1)}, f32[1,512]{1,0:T(1,128)}, bf16[512,1536]{1,0:...) custom-call(bf16[2048,512]{1,0:T(8,128)(2,1)} %bitcast.87, ...), custom_call_target="tpu_custom_call" | custom-call | flops 3221225472 | bytes 31457280 | tf_op jit(solution)/shard_map/pallas_call | solution.py:736
  644.5 26.7 %collective-permute-done.25 = bf16[4,192,1024]{2,1,0:T(8,128)(2,1)} collective-permute-done((bf16[4,192,1024]{2,1,0:T(8,128)(2,1)}, bf16[4,192,1024]{2,1,0:T(8,128)(2,1)}, u32[]{:S(2)}, u32[]{:S(2)}) %collective-permute-start.25) | collective-permute-done | bytes 1572896 | tf_op jit(solution)/shard_map/ppermute | solution.py:21
  694.8 24.4 %collective-permute-done.27.refs_2_ = bf16[512,1536]{1,0:T(8,128)(2,1)} collective-permute-done((bf16[512,1536]{1,0:T(8,128)(2,1)S(1)}, bf16[512,1536]{1,0:T(8,128)(2,1)}, u32[]{:S(2)}, u32[]{:S(2)}) %collective-permute-start.27) | collective-permute-done | bytes 1572896 | tf_op jit(solution)/shard_map/ppermute | solution.py:21
  729.4 5.5 shard_map.234
  (223 shorter events, 121.3 us)
Async XLA Ops:
  7.2 128.4 %all-gather.7.cloned.1.call-start = ((), (), s32[]{:S(2)}) async-start(), calls=%async_computation.10 | async-start | bytes 4423680 | tf_op jit(solution)/shard_map/all_gather | solution.py:1466
  14.9 40.0 %collective-permute-start = (bf16[512,1536]{1,0:T(8,128)(2,1)}, bf16[512,1536]{1,0:T(8,128)(2,1)S(1)}, u32[]{:S(2)}, u32[]{:S(2)}) collective-permute-start(bf16[512,1536]{1,0:T(8,128)(2,1)} %get-tuple-element.262), channel_id=1, source_target_pairs={{0,0},{1,17},{2,10},{3,27},{8,8},{9,25},{10,18},{11,3},{16,16},{17... | collective-permute-start | bytes 4718600 | tf_op jit(solution)/shard_map/ppermute | solution.py:1429
  54.9 181.6 %all-gather.9.cloned.1.call-start = ((), (), s32[]{:S(2)}) async-start(), calls=%async_computation.11 | async-start | bytes 7372800 | tf_op jit(solution)/shard_map/all_gather | solution.py:1466
  55.0 34.7 %collective-permute-start.2 = (bf16[512,1536]{1,0:T(8,128)(2,1)S(1)}, bf16[512,1536]{1,0:T(8,128)(2,1)S(1)}, u32[]{:S(2)}, u32[]{:S(2)}) collective-permute-start(bf16[512,1536]{1,0:T(8,128)(2,1)S(1)} %collective-permute-done.x0.own_in), channel_id=1, source_target_pairs={{0,2},{1,3},{2,0},{3,1},{4,6},{5,7},{6,4},{7,5},{8,10},{9,11},{10,... | collective-permute-start | bytes 4718600 | tf_op jit(solution)/shard_map/ppermute | solution.py:21
  56.2 35.6 %collective-permute-start.5 = (bf16[192,3456]{1,0:T(8,128)(2,1)}, bf16[192,3456]{1,0:T(8,128)(2,1)S(1)}, u32[]{:S(2)}, u32[]{:S(2)}) collective-permute-start(bf16[192,3456]{1,0:T(8,128)(2,1)} %get-tuple-element.81), channel_id=1, source_target_pairs={{0,4},{4,0},{1,5},{5,1},{2,6},{6,2},{3,7},{7,3},{8,12},{12,8},{9,1... | collective-permute-start | bytes 3981320 | tf_op jit(solution)/shard_map/ppermute | solution.py:21
  95.7 268.0 %all-gather.11.cloned.1.call-start = ((), (), s32[]{:S(2)}) async-start(), calls=%async_computation.12 | async-start | bytes 5898240 | tf_op jit(solution)/shard_map/all_gather | solution.py:1466
  95.7 36.4 %collective-permute-start.6 = (bf16[512,1536]{1,0:T(8,128)(2,1)}, bf16[512,1536]{1,0:T(8,128)(2,1)}, u32[]{:S(2)}, u32[]{:S(2)}) collective-permute-start(bf16[512,1536]{1,0:T(8,128)(2,1)} %get-tuple-element.82), channel_id=1, source_target_pairs={{0,4},{4,0},{1,5},{5,1},{2,6},{6,2},{3,7},{7,3},{8,12},{12,8},{9,1... | collective-permute-start | bytes 4718600 | tf_op jit(solution)/shard_map/ppermute | solution.py:21
  97.1 38.5 %collective-permute-start.1 = (bf16[512,1536]{1,0:T(8,128)(2,1)S(1)}, bf16[512,1536]{1,0:T(8,128)(2,1)S(1)}, u32[]{:S(2)}, u32[]{:S(2)}) collective-permute-start(bf16[512,1536]{1,0:T(8,128)(2,1)S(1)} %collective-permute-done.x0.own_in), channel_id=1, source_target_pairs={{0,1},{1,0},{2,3},{3,2},{4,5},{5,4},{6,7},{7,6},{8,9},{9,8},{10,11... | collective-permute-start | bytes 4718600 | tf_op jit(solution)/shard_map/ppermute | solution.py:21
  132.1 35.4 %collective-permute-start.8 = (bf16[512,1536]{1,0:T(8,128)(2,1)}, bf16[512,1536]{1,0:T(8,128)(2,1)}, u32[]{:S(2)}, u32[]{:S(2)}) collective-permute-start(bf16[512,1536]{1,0:T(8,128)(2,1)} %collective-permute-done.6.refs_0_), channel_id=1, source_target_pairs={{0,2},{1,3},{2,0},{3,1},{4,6},{5,7},{6,4},{7,5},{8,10},{9,11},{10,... | collective-permute-start | bytes 4718600 | tf_op jit(solution)/shard_map/ppermute | solution.py:21
  167.5 65.6 %collective-permute-start.11 = (bf16[512,1536]{1,0:T(8,128)(2,1)}, bf16[512,1536]{1,0:T(8,128)(2,1)}, u32[]{:S(2)}, u32[]{:S(2)}) collective-permute-start(bf16[512,1536]{1,0:T(8,128)(2,1)} %collective-permute-done.6.refs_0_), channel_id=1, source_target_pairs={{0,1},{1,0},{2,3},{3,2},{4,5},{5,4},{6,7},{7,6},{8,9},{9,8},{10,11... | collective-permute-start | bytes 4718600 | tf_op jit(solution)/shard_map/ppermute | solution.py:21
  169.2 63.9 %collective-permute-start.12 = (bf16[512,1536]{1,0:T(8,128)(2,1)}, bf16[512,1536]{1,0:T(8,128)(2,1)}, u32[]{:S(2)}, u32[]{:S(2)}) collective-permute-start(bf16[512,1536]{1,0:T(8,128)(2,1)} %collective-permute-done.8.refs_2_), channel_id=1, source_target_pairs={{0,1},{1,0},{2,3},{3,2},{4,5},{5,4},{6,7},{7,6},{8,9},{9,8},{10,11... | collective-permute-start | bytes 4718600 | tf_op jit(solution)/shard_map/ppermute | solution.py:21
  227.6 35.7 %collective-permute-start.14 = (bf16[512,1536]{1,0:T(8,128)(2,1)}, bf16[512,1536]{1,0:T(8,128)(2,1)}, u32[]{:S(2)}, u32[]{:S(2)}) collective-permute-start(bf16[512,1536]{1,0:T(8,128)(2,1)} %get-tuple-element.90.refs_0_), channel_id=1, source_target_pairs={{0,4},{4,0},{1,5},{5,1},{2,6},{6,2},{3,7},{7,3},{8,12},{12,8},{9,1... | collective-permute-start | bytes 4718600 | tf_op jit(solution)/shard_map/ppermute | solution.py:21
  229.9 34.4 %collective-permute-start.10 = (bf16[512,1536]{1,0:T(8,128)(2,1)}, bf16[512,1536]{1,0:T(8,128)(2,1)}, u32[]{:S(2)}, u32[]{:S(2)}) collective-permute-start(bf16[512,1536]{1,0:T(8,128)(2,1)} %get-tuple-element.90.refs_0_), channel_id=1, source_target_pairs={{0,2},{1,3},{2,0},{3,1},{4,6},{5,7},{6,4},{7,5},{8,10},{9,11},{10,... | collective-permute-start | bytes 4718600 | tf_op jit(solution)/shard_map/ppermute | solution.py:21
  230.8 237.3 %reduce-scatter.6.cloned.1.call-start = ((), (), s32[]{:S(2)}) async-start(), calls=%async_computation.5 | async-start | bytes 7372800 | tf_op jit(solution)/shard_map/reduce_scatter | solution.py:1710
  231.0 39.5 %collective-permute-start.16 = (bf16[512,1536]{1,0:T(8,128)(2,1)}, bf16[512,1536]{1,0:T(8,128)(2,1)}, u32[]{:S(2)}, u32[]{:S(2)}) collective-permute-start(bf16[512,1536]{1,0:T(8,128)(2,1)} %get-tuple-element.90.refs_0_), channel_id=1, source_target_pairs={{0,1},{1,0},{2,3},{3,2},{4,5},{5,4},{6,7},{7,6},{8,9},{9,8},{10,11... | collective-permute-start | bytes 4718600 | tf_op jit(solution)/shard_map/ppermute | solution.py:21
  363.6 216.9 %reduce-scatter.10.cloned.1.call-start = ((), (), s32[]{:S(2)}) async-start(), calls=%async_computation.7 | async-start | bytes 1966080 | tf_op jit(solution)/shard_map/reduce_scatter | solution.py:1710
  468.2 112.4 %reduce-scatter.8.cloned.1.call-start = ((), (), s32[]{:S(2)}) async-start(), calls=%async_computation.6 | async-start | bytes 1966080 | tf_op jit(solution)/shard_map/reduce_scatter | solution.py:1710
  468.7 111.9 %reduce-scatter.12.cloned.1.call-start = ((), (), s32[]{:S(2)}) async-start(), calls=%async_computation.8 | async-start | bytes 1966080 | tf_op jit(solution)/shard_map/reduce_scatter | solution.py:1710
  523.6 197.9 %reduce-scatter.14.cloned.1.call-start = ((), (), s32[]{:S(2)}) async-start(), calls=%async_computation.9 | async-start | bytes 1966080 | tf_op jit(solution)/shard_map/reduce_scatter | solution.py:1769
  638.8 32.5 %collective-permute-start.25 = (bf16[4,192,1024]{2,1,0:T(8,128)(2,1)}, bf16[4,192,1024]{2,1,0:T(8,128)(2,1)}, u32[]{:S(2)}, u32[]{:S(2)}) collective-permute-start(bf16[4,192,1024]{2,1,0:T(8,128)(2,1)} %dynamic-slice_bitcast_fusion), channel_id=1, source_target_pairs={{0,4},{4,0},{1,5},{5,1},{2,6},{6,2},{3,7},{7,3},{8,12},{12,8},{9,1... | collective-permute-start | bytes 4718600 | tf_op jit(solution)/shard_map/ppermute | solution.py:21
  639.9 43.1 %collective-permute-start.24 = (bf16[512,1536]{1,0:T(8,128)(2,1)}, bf16[512,1536]{1,0:T(8,128)(2,1)S(1)}, u32[]{:S(2)}, u32[]{:S(2)}) collective-permute-start(bf16[512,1536]{1,0:T(8,128)(2,1)} %get-tuple-element.133), channel_id=1, source_target_pairs={{0,0},{17,1},{10,2},{27,3},{8,8},{25,9},{18,10},{3,11},{16,16},{1,... | collective-permute-start | bytes 4718600 | tf_op jit(solution)/shard_map/ppermute | solution.py:1775
  644.4 40.1 %collective-permute-start.22 = (bf16[512,1536]{1,0:T(8,128)(2,1)S(1)}, bf16[512,1536]{1,0:T(8,128)(2,1)}, u32[]{:S(2)}, u32[]{:S(2)}) collective-permute-start(bf16[512,1536]{1,0:T(8,128)(2,1)S(1)} %copy-done.2), channel_id=1, source_target_pairs={{0,2},{1,3},{2,0},{3,1},{4,6},{5,7},{6,4},{7,5},{8,10},{9,11},{10,... | collective-permute-start | bytes 4718600 | tf_op jit(solution)/shard_map/ppermute | solution.py:21
  683.0 36.3 %collective-permute-start.27 = (bf16[512,1536]{1,0:T(8,128)(2,1)S(1)}, bf16[512,1536]{1,0:T(8,128)(2,1)}, u32[]{:S(2)}, u32[]{:S(2)}) collective-permute-start(bf16[512,1536]{1,0:T(8,128)(2,1)S(1)} %collective-permute-done.24.refs_0_), channel_id=1, source_target_pairs={{0,2},{1,3},{2,0},{3,1},{4,6},{5,7},{6,4},{7,5},{8,10},{9,11},{10,... | collective-permute-start | bytes 4718600 | tf_op jit(solution)/shard_map/ppermute | solution.py:21
  689.6 37.3 %collective-permute-start.26 = (bf16[512,1536]{1,0:T(8,128)(2,1)S(1)}, bf16[512,1536]{1,0:T(8,128)(2,1)}, u32[]{:S(2)}, u32[]{:S(2)}) collective-permute-start(bf16[512,1536]{1,0:T(8,128)(2,1)S(1)} %collective-permute-done.24.refs_0_), channel_id=1, source_target_pairs={{0,1},{1,0},{2,3},{3,2},{4,5},{5,4},{6,7},{7,6},{8,9},{9,8},{10,11... | collective-permute-start | bytes 4718600 | tf_op jit(solution)/shard_map/ppermute | solution.py:21
  (52 other events, 462.4 us)
Sparse Core Ops, SparseCore 0:
  55.1 71.4 all-gather.6
  128.7 107.7 all-gather.8
  238.1 87.5 all-gather.10
  363.7 104.3 reduce-scatter.5
  470.3 35.5 reduce-scatter.9
  508.1 34.2 reduce-scatter.7
  544.6 34.2 reduce-scatter.11
  675.1 38.8 reduce-scatter.13
